TPU v7x, 32 devices: a whole 2x2x4 slice. The times are simulated.
32 devices in a mesh: row: 8 (over y, x, core), col: 4 (over z).
Axes of the slice: x: 2, y: 2, z: 4, core: 2. Of those that a mesh axis runs over, the one named last changes fastest.
Arguments:
- object_field: float32 [2, 2048, 1024], P(None, 'row', 'col'), may hold values from -5 to 5
- probe_field: float32 [2, 128, 128], replicated, may hold values from -5 to 5
- intensities: int32 [8, 4, 4, 128, 128], P('row', 'col'), may hold values from 0 to 2047
- off_rows: int32 [8, 4, 4], P('row', 'col'), may hold values from 0 to 255
- off_cols: int32 [8, 4, 4], P('row', 'col'), may hold values from 0 to 255
- counts: int32 [8, 4], P('row', 'col'), may hold values from 0 to 4, as said below
Outputs:
- object_out: float32 [2, 2048, 1024], P(None, 'row', 'col')
- probe_out: float32 [2, 128, 128], replicated
Inputs may be any that keep to these rules, and one draw needn't show every extreme that they name: The counts of tile (r, c) and of tile (r + 4, c) add up to exactly 4; some tile owns 4 positions.
All inputs are finite; a program needn't handle non-finite values.
Results may differ from a plain program's by a relative error of at most 0.0003.
Values sent between devices are 32-bit elements; how exact they have to be, the bound alone decides.
No kernel may reach another device: no remote copies, remote signals or barrier semaphores. Data moves between devices by JAX's collectives and lax.ppermute only.
A program may use at most 64 MiB of HBM per device.

v0:
```python
import math

import jax
import jax.numpy as jnp
from jax import lax
from jax.sharding import PartitionSpec as P

ITERS = 2


STEP_SIZE = 0.25
PROBE_STEP = 1.0
REGULARIZER = 1.0
COUNT_SCALE = 1.0 / 1024.0
HIGHEST_PRECISION = lax.Precision.HIGHEST


def from_behind(value, axis, steps):
    count = lax.axis_size(axis)
    first, last = (max(0, -steps), min(count, count - steps))
    return lax.ppermute(value, axis, [(source, source + steps) for source in range(first, last)])


def dft_tables(length):
    points = jnp.arange(length, dtype=jnp.int32)
    phases = points[:, None] * points[None, :] % length
    angles = phases.astype(jnp.float32) * (2.0 * math.pi / length)
    factor = 1.0 / math.sqrt(length)
    return (jnp.cos(angles) * factor, jnp.sin(angles) * factor)


def right_product(table, values):
    return jnp.einsum("bij,jk->bik", values, table, precision=HIGHEST_PRECISION)


def left_product(table, values):
    return jnp.einsum("ij,bjk->bik", table, values, precision=HIGHEST_PRECISION)


def transform(real_part, imag_part, cosine_table, sine_table, direction_sign):
    mid_real = right_product(cosine_table, real_part) - direction_sign * right_product(
        sine_table, imag_part
    )
    mid_imag = right_product(cosine_table, imag_part) + direction_sign * right_product(
        sine_table, real_part
    )
    out_real = left_product(cosine_table, mid_real) - direction_sign * left_product(
        sine_table, mid_imag
    )
    out_imag = left_product(cosine_table, mid_imag) + direction_sign * left_product(
        sine_table, mid_real
    )
    return (out_real, out_imag)


def position_terms(patches, measured, weights, probe_now, cosine_table, sine_table):
    probe_real = probe_now[0]
    probe_imag = probe_now[1]
    patch_real = patches[:, 0]
    patch_imag = patches[:, 1]
    exit_real = probe_real * patch_real - probe_imag * patch_imag
    exit_imag = probe_real * patch_imag + probe_imag * patch_real
    freq_real, freq_imag = transform(exit_real, exit_imag, cosine_table, sine_table, -1.0)
    residual = freq_real * freq_real + freq_imag * freq_imag - COUNT_SCALE * measured
    back_real, back_imag = transform(
        residual * freq_real, residual * freq_imag, cosine_table, sine_table, 1.0
    )
    weight_grid = weights[:, None, None]
    back_real = back_real * weight_grid
    back_imag = back_imag * weight_grid
    object_real = probe_real * back_real + probe_imag * back_imag
    object_imag = probe_real * back_imag - probe_imag * back_real
    lit_grid = weight_grid * (probe_real * probe_real + probe_imag * probe_imag)
    probe_grad = jnp.stack(
        [
            jnp.sum(patch_real * back_real + patch_imag * back_imag, axis=0),
            jnp.sum(patch_real * back_imag - patch_imag * back_real, axis=0),
        ]
    )
    probe_light = jnp.sum(weight_grid * (patch_real * patch_real + patch_imag * patch_imag), axis=0)
    term_stack = jnp.stack([object_real, object_imag, lit_grid], axis=1)
    return (term_stack, probe_grad, probe_light)


def extract(extended, row_list, col_list, length):

    def window(row_start, col_start):
        return lax.dynamic_slice(
            extended, (jnp.int32(0), row_start, col_start), (2, length, length)
        )

    return jax.vmap(window)(row_list, col_list)


def deposit(term_stack, row_list, col_list, height, width):
    channels = term_stack.shape[1]
    length = term_stack.shape[2]

    def add_one(index, total):
        anchor = (jnp.int32(0), row_list[index], col_list[index])
        current = lax.dynamic_slice(total, anchor, (channels, length, length))
        return lax.dynamic_update_slice(total, current + term_stack[index], anchor)

    return lax.fori_loop(
        0, term_stack.shape[0], add_one, jnp.zeros((channels, height, width), jnp.float32)
    )


def local(object_field, probe_field, intensities, off_rows, off_cols, counts):
    tile_rows = object_field.shape[1]
    tile_cols = object_field.shape[2]
    length = probe_field.shape[1]
    slots = off_rows.shape[2]
    row_list = off_rows.reshape(slots)
    col_list = off_cols.reshape(slots)
    count_own = counts[0, 0]
    measured = intensities.reshape(slots, length, length).astype(jnp.float32)
    axis_length = lax.axis_size("row")
    upper_half = lax.axis_index("row") < axis_length // 2
    slot_index = jnp.arange(slots, dtype=jnp.int32)
    valid_mask = jnp.where(
        upper_half, slot_index < count_own, slot_index >= slots - count_own
    ).astype(jnp.float32)
    cosine_table, sine_table = dft_tables(length)
    tile_field = object_field
    probe_now = probe_field
    for step in range(ITERS):
        below_rows = from_behind(tile_field[:, :length, :], "row", -1)
        right_cols = from_behind(tile_field[:, :, :length], "col", -1)
        corner = from_behind(below_rows[:, :, :length], "col", -1)
        extended = jnp.concatenate(
            [
                jnp.concatenate([tile_field, right_cols], 2),
                jnp.concatenate([below_rows, corner], 2),
            ],
            1,
        )
        patches = extract(extended, row_list, col_list, length)
        full_terms, probe_grad, probe_light = position_terms(
            patches, measured, valid_mask, probe_now, cosine_table, sine_table
        )
        deposits = deposit(full_terms, row_list, col_list, tile_rows + length, tile_cols + length)
        right_part = from_behind(deposits[:, :tile_rows, tile_cols:], "col", 1)
        bottom_part = from_behind(deposits[:, tile_rows:, :], "row", 1)
        corner_part = from_behind(bottom_part[:, :, tile_cols:], "col", 1)
        gathered = deposits[:, :tile_rows, :tile_cols]
        gathered = gathered.at[:, :, :length].add(right_part)
        gathered = gathered.at[:, :length, :].add(bottom_part[:, :, :tile_cols])
        gathered = gathered.at[:, :length, :length].add(corner_part)
        grad_total, light_total = lax.psum((probe_grad, probe_light), ("row", "col"))
        tile_field = tile_field - STEP_SIZE * gathered[:2] / (gathered[2] + REGULARIZER)
        probe_now = probe_now - PROBE_STEP * grad_total / (light_total + REGULARIZER)
    return (tile_field, probe_now)


def solution(mesh):
    placed = (
        P(None, "row", "col"),
        P(),
        P("row", "col", None, None, None),
        P("row", "col", None),
        P("row", "col", None),
        P("row", "col"),
    )
    return jax.shard_map(
        local, mesh=mesh, in_specs=placed, out_specs=(P(None, "row", "col"), P()), check_vma=False
    )
```

profile of v0, /device:TPU:0, one launch (start us, length us, event | category | flops | bytes accessed | tf_op | source)
XLA Modules:
  0.0 417.8 jit_solution(13762809415248948394)
XLA Ops:
  7.3 1.0 slice.242
  8.3 1.3 collective-permute-start.1
  9.6 1.0 slice.241
  10.6 1.3 collective-permute-start
  11.9 0.9 slice_bitcast_fusion.3
  12.8 1.3 collective-permute-start.2
  15.3 7.0 %collective-permute-done = f32[2,256,128]{2,1,0:T(8,128)S(1)} collective-permute-done((f32[2,256,128]{2,1,0:T(8,128)S(1)}, f32[2,256,128]{2,1,0:T(8,128)S(1)}, u32[]{:S(2)}, u32[]{:S(2)}) %collective-permute-start) | collective-permute-done | bytes 262176 | tf_op jit(solution)/shard_map/ppermute | solution.py:21
  22.3 2.8 collective-permute-done.2
  25.2 9.1 %while.36 = (s32[]{:T(128)}, f32[2,384,384]{2,1,0:T(8,128)S(1)}, s32[4,3]{1,0:T(4,128)S(1)}, f32[4,2,128,128]{2,3,0,1:T(8,128)S(1)}, s32[]{:T(128)}) while((s32[]{:T(128)}, f32[2,384,384]{2,1,0:T(8,128)S(1)}, s32[4,3]{1,0:T(4,128)S(1)}, f32[4,2,128,128]{2,3,0,1:T(8,128)S(1)}, s32[]{:T(128)}) %tuple.134), condition=%wide.while_cond.6, body=%wide.while_body.6.sunk | while | flops 2 | bytes 786549 | solution.py:88
  25.9 1.4 dynamic-slice_bitcast_fusion.4
  28.2 1.4 dynamic-slice_bitcast_fusion.4
  30.5 1.4 dynamic-slice_bitcast_fusion.4
  32.7 1.4 dynamic-slice_bitcast_fusion.4
  42.7 0.8 convolution_add_fusion.3
  45.6 1.6 fusion.39
  48.2 124.4 %all-reduce.7.cloned.1.call-done = (f32[2,128,128]{1,2,0:T(8,128)}, f32[128,128]{0,1:T(8,128)}) async-done(((f32[2,128,128]{1,2,0:T(8,128)}, f32[128,128]{0,1:T(8,128)}), (f32[2,128,128]{1,2,0:T(8,128)}, f32[128,128]{0,1:T(8,128)})) %all-reduce.7.cloned.1.call-update) | async-done | bytes 196624 | tf_op jit(solution)/shard_map/psum | solution.py:150
  172.6 0.8 broadcast_add_fusion.1
  173.5 0.9 divide_subtract_fusion.1
  174.5 0.9 pad_maximum_fusion
  175.6 37.2 %while.34 = (s32[]{:T(128)}, f32[3,384,384]{2,1,0:T(8,128)S(1)}, s32[4]{0:T(128)S(1)}, s32[4]{0:T(128)S(1)}, f32[4,3,128,128]{2,3,0,1:T(8,128)}, /*index=5*/s32[]{:T(128)}, s32[]{:T(128)}, s32[]{:T(128)}) while((s32[]{:T(128)}, f32[3,384,384]{2,1,0:T(8,128)S(1)}, s32[4]{0:T(128)S(1)}, s32[4]{0:T(128)S(1)}, f32[4,3,128,128]{2,3,0,1:T(8,128)}, ...), condition=%wide.region_1.2_spmd, body=%wide.region_0.1_spmd.sunk | while | flops 49160 | bytes 1769665 | solution.py:104
  180.7 1.0 constant_dynamic-slice_fusion.8
  181.9 3.1 dynamic_update_slice.16
  190.0 1.0 constant_dynamic-slice_fusion.8
  191.2 3.1 dynamic_update_slice.16
  199.4 1.0 constant_dynamic-slice_fusion.8
  200.6 2.9 dynamic_update_slice.16
  208.6 1.0 constant_dynamic-slice_fusion.8
  209.8 3.0 dynamic_update_slice.16
  212.8 5.0 %collective-permute-start.3 = (f32[3,256,128]{2,1,0:T(8,128)S(1)}, f32[3,256,128]{2,1,0:T(8,128)S(1)}, u32[]{:S(2)}, u32[]{:S(2)}) collective-permute-start(f32[3,256,128]{2,1,0:T(8,128)S(1)} %slice.249), channel_id=1, source_target_pairs={{0,1},{1,2},{2,3},{4,5},{5,6},{6,7},{8,9},{9,10},{10,11},{12,13},{... | collective-permute-start | bytes 1179656 | tf_op jit(solution)/shard_map/ppermute | solution.py:21
  217.9 1.3 collective-permute-start.4
  219.3 5.5 %collective-permute-done.3 = f32[3,256,128]{2,1,0:T(8,128)S(1)} collective-permute-done((f32[3,256,128]{2,1,0:T(8,128)S(1)}, f32[3,256,128]{2,1,0:T(8,128)S(1)}, u32[]{:S(2)}, u32[]{:S(2)}) %collective-permute-start.3) | collective-permute-done | bytes 393248 | tf_op jit(solution)/shard_map/ppermute | solution.py:21
  224.9 4.4 %collective-permute-start.5 = (f32[3,128,128]{2,1,0:T(8,128)S(1)}, f32[3,128,128]{2,1,0:T(8,128)S(1)}, u32[]{:S(2)}, u32[]{:S(2)}) collective-permute-start(f32[3,128,128]{2,1,0:T(8,128)S(1)} %slice.308), channel_id=1, source_target_pairs={{0,1},{1,2},{2,3},{4,5},{5,6},{6,7},{8,9},{9,10},{10,11},{12,13},{... | collective-permute-start | bytes 589832 | tf_op jit(solution)/shard_map/ppermute | solution.py:21
  229.4 4.5 %collective-permute-done.5 = f32[3,128,128]{2,1,0:T(8,128)S(1)} collective-permute-done((f32[3,128,128]{2,1,0:T(8,128)S(1)}, f32[3,128,128]{2,1,0:T(8,128)S(1)}, u32[]{:S(2)}, u32[]{:S(2)}) %collective-permute-start.5) | collective-permute-done | bytes 196640 | tf_op jit(solution)/shard_map/ppermute | solution.py:21
  234.1 1.3 collective-permute-start.7
  235.4 1.3 collective-permute-start.6
  236.7 1.1 collective-permute-done.7
  237.8 1.3 collective-permute-start.8
  239.1 7.5 %collective-permute-done.6 = f32[2,256,128]{2,1,0:T(8,128)S(1)} collective-permute-done((f32[2,256,128]{2,1,0:T(8,128)S(1)}, f32[2,256,128]{2,1,0:T(8,128)S(1)}, u32[]{:S(2)}, u32[]{:S(2)}) %collective-permute-start.6) | collective-permute-done | bytes 262176 | tf_op jit(solution)/shard_map/ppermute | solution.py:21
  246.6 1.8 collective-permute-done.8
  248.5 8.7 %while.37 = (s32[]{:T(128)}, f32[2,384,384]{2,1,0:T(8,128)S(1)}, s32[4,3]{1,0:T(4,128)S(1)}, f32[4,2,128,128]{2,3,0,1:T(8,128)S(1)}, s32[]{:T(128)}) while((s32[]{:T(128)}, f32[2,384,384]{2,1,0:T(8,128)S(1)}, s32[4,3]{1,0:T(4,128)S(1)}, f32[4,2,128,128]{2,3,0,1:T(8,128)S(1)}, s32[]{:T(128)}) %tuple.152), condition=%wide.while_cond.7, body=%wide.while_body.7.sunk | while | flops 2 | bytes 786549 | solution.py:88
  249.2 1.4 dynamic-slice_bitcast_fusion.5
  251.3 1.4 dynamic-slice_bitcast_fusion.5
  253.5 1.4 dynamic-slice_bitcast_fusion.5
  255.7 1.4 dynamic-slice_bitcast_fusion.5
  263.2 0.8 fusion.78
  265.5 0.8 convolution_add_fusion.1
  268.5 1.6 fusion.28
  271.0 35.2 %while.35 = (s32[]{:T(128)}, f32[3,384,384]{2,1,0:T(8,128)S(1)}, s32[4]{0:T(128)S(1)}, s32[4]{0:T(128)S(1)}, f32[4,3,128,128]{2,3,0,1:T(8,128)S(1)}, /*index=5*/s32[]{:T(128)}, s32[]{:T(128)}, s32[]{:T(128)}) while((s32[]{:T(128)}, f32[3,384,384]{2,1,0:T(8,128)S(1)}, s32[4]{0:T(128)S(1)}, s32[4]{0:T(128)S(1)}, ...), condition=%wide.region_8.9_spmd, body=%wide.region_7.8_spmd.sunk | while | flops 49160 | bytes 1769665 | solution.py:104
  276.8 3.1 dynamic_update_slice.17
  285.7 3.1 dynamic_update_slice.17
  294.6 2.9 dynamic_update_slice.17
  303.3 3.0 dynamic_update_slice.17
  307.1 0.9 slice.268
  307.9 4.7 %collective-permute-start.9 = (f32[3,256,128]{2,1,0:T(8,128)}, f32[3,256,128]{2,1,0:T(8,128)}, u32[]{:S(2)}, u32[]{:S(2)}) collective-permute-start(f32[3,256,128]{2,1,0:T(8,128)} %slice.266), channel_id=1, source_target_pairs={{0,1},{1,2},{2,3},{4,5},{5,6},{6,7},{8,9},{9,10},{10,11},{12,13},{... | collective-permute-start | bytes 1179656 | tf_op jit(solution)/shard_map/ppermute | solution.py:21
  312.6 3.8 collective-permute-start.10
  316.5 80.7 %all-reduce.5.cloned.1.call-done = (f32[2,128,128]{1,2,0:T(8,128)}, f32[128,128]{0,1:T(8,128)}) async-done(((f32[2,128,128]{1,2,0:T(8,128)}, f32[128,128]{0,1:T(8,128)}), (f32[2,128,128]{1,2,0:T(8,128)}, f32[128,128]{0,1:T(8,128)})) %all-reduce.5.cloned.1.call-update) | async-done | bytes 196624 | tf_op jit(solution)/shard_map/psum | solution.py:150
  397.1 0.8 broadcast_add_fusion
  398.0 0.9 divide_subtract_fusion
  399.7 1.0 add_dynamic-update-slice_fusion
  400.7 0.9 slice.319
  401.7 5.2 %collective-permute-start.11 = (f32[3,128,128]{2,1,0:T(8,128)S(1)}, f32[3,128,128]{2,1,0:T(8,128)S(1)}, u32[]{:S(2)}, u32[]{:S(2)}) collective-permute-start(f32[3,128,128]{2,1,0:T(8,128)S(1)} %slice.319), channel_id=1, source_target_pairs={{0,1},{1,2},{2,3},{4,5},{5,6},{6,7},{8,9},{9,10},{10,11},{12,13},{... | collective-permute-start | bytes 589832 | tf_op jit(solution)/shard_map/ppermute | solution.py:21
  406.9 1.1 constant_dynamic-update-slice_fusion.2
  408.1 2.0 collective-permute-done.11
  410.1 0.9 fusion.20
  (157 shorter events, 43.3 us)
Async XLA Ops:
  7.2 18.0 %copy-start = (f32[2,256,256]{2,1,0:T(8,128)S(1)}, f32[2,256,256]{2,1,0:T(8,128)}, u32[]{:S(2)}) copy-start(f32[2,256,256]{2,1,0:T(8,128)} %param.22) | copy-start | bytes 1572868
  7.2 5.6 %copy-start.5 = (s32[1,1,4]{2,1,0:T(1,128)S(1)}, s32[1,1,4]{2,1,0:T(1,128)}, u32[]{:S(2)}) copy-start(s32[1,1,4]{2,1,0:T(1,128)} %param.25) | copy-start | bytes 52
  7.2 5.6 %copy-start.6 = (s32[1,1,4]{2,1,0:T(1,128)S(1)}, s32[1,1,4]{2,1,0:T(1,128)}, u32[]{:S(2)}) copy-start(s32[1,1,4]{2,1,0:T(1,128)} %param.26) | copy-start | bytes 52
  7.2 7.3 %copy-start.4 = (s32[1,1,4,128,128]{4,3,2,1,0:T(8,128)S(1)}, s32[1,1,4,128,128]{4,3,2,1,0:T(8,128)}, u32[]{:S(2)}) copy-start(s32[1,1,4,128,128]{4,3,2,1,0:T(8,128)} %param.24) | copy-start | bytes 786436
  7.2 165.4 %all-reduce.7.cloned.1.call-start = ((), (), s32[]{:S(2)}) async-start(), calls=%async_computation.1 | async-start | bytes 393216 | tf_op jit(solution)/shard_map/psum | solution.py:150
  8.3 4.5 %collective-permute-start.1 = (f32[2,128,256]{2,1,0:T(8,128)S(1)}, f32[2,128,256]{2,1,0:T(8,128)S(1)}, u32[]{:S(2)}, u32[]{:S(2)}) collective-permute-start(f32[2,128,256]{2,1,0:T(8,128)S(1)} %slice.242), channel_id=1, source_target_pairs={{4,0},{8,4},{12,8},{16,12},{20,16},{24,20},{28,24},{5,1},{9,5},{13... | collective-permute-start | bytes 786440 | tf_op jit(solution)/shard_map/ppermute | solution.py:21
  10.6 11.7 %collective-permute-start = (f32[2,256,128]{2,1,0:T(8,128)S(1)}, f32[2,256,128]{2,1,0:T(8,128)S(1)}, u32[]{:S(2)}, u32[]{:S(2)}) collective-permute-start(f32[2,256,128]{2,1,0:T(8,128)S(1)} %slice.241), channel_id=1, source_target_pairs={{1,0},{2,1},{3,2},{5,4},{6,5},{7,6},{9,8},{10,9},{11,10},{13,12},{... | collective-permute-start | bytes 786440 | tf_op jit(solution)/shard_map/ppermute | solution.py:21
  12.8 12.3 %collective-permute-start.2 = (f32[2,128,128]{2,1,0:T(8,128)S(1)}, f32[2,128,128]{2,1,0:T(8,128)S(1)}, u32[]{:S(2)}, u32[]{:S(2)}) collective-permute-start(f32[2,128,128]{2,1,0:T(8,128)S(1)} %slice.304), channel_id=1, source_target_pairs={{1,0},{2,1},{3,2},{5,4},{6,5},{7,6},{9,8},{10,9},{11,10},{13,12},{... | collective-permute-start | bytes 393224 | tf_op jit(solution)/shard_map/ppermute | solution.py:21
  45.6 2.3 copy-start.3
  47.9 349.2 %all-reduce.5.cloned.1.call-start = ((), (), s32[]{:S(2)}) async-start(), calls=%async_computation | async-start | bytes 393216 | tf_op jit(solution)/shard_map/psum | solution.py:150
  174.4 1.1 copy-start.1
  212.8 12.0 %collective-permute-start.3 = (f32[3,256,128]{2,1,0:T(8,128)S(1)}, f32[3,256,128]{2,1,0:T(8,128)S(1)}, u32[]{:S(2)}, u32[]{:S(2)}) collective-permute-start(f32[3,256,128]{2,1,0:T(8,128)S(1)} %slice.249), channel_id=1, source_target_pairs={{0,1},{1,2},{2,3},{4,5},{5,6},{6,7},{8,9},{9,10},{10,11},{12,13},{... | collective-permute-start | bytes 1179656 | tf_op jit(solution)/shard_map/ppermute | solution.py:21
  217.9 7.0 %collective-permute-start.4 = (f32[3,128,384]{2,1,0:T(8,128)S(1)}, f32[3,128,384]{2,1,0:T(8,128)S(1)}, u32[]{:S(2)}, u32[]{:S(2)}) collective-permute-start(f32[3,128,384]{2,1,0:T(8,128)S(1)} %slice.251), channel_id=1, source_target_pairs={{0,4},{4,8},{8,12},{12,16},{16,20},{20,24},{24,28},{1,5},{5,9},{9,... | collective-permute-start | bytes 1769480 | tf_op jit(solution)/shard_map/ppermute | solution.py:21
  224.9 9.0 %collective-permute-start.5 = (f32[3,128,128]{2,1,0:T(8,128)S(1)}, f32[3,128,128]{2,1,0:T(8,128)S(1)}, u32[]{:S(2)}, u32[]{:S(2)}) collective-permute-start(f32[3,128,128]{2,1,0:T(8,128)S(1)} %slice.308), channel_id=1, source_target_pairs={{0,1},{1,2},{2,3},{4,5},{5,6},{6,7},{8,9},{9,10},{10,11},{12,13},{... | collective-permute-start | bytes 589832 | tf_op jit(solution)/shard_map/ppermute | solution.py:21
  234.1 3.7 collective-permute-start.7
  235.4 11.2 %collective-permute-start.6 = (f32[2,256,128]{2,1,0:T(8,128)S(1)}, f32[2,256,128]{2,1,0:T(8,128)S(1)}, u32[]{:S(2)}, u32[]{:S(2)}) collective-permute-start(f32[2,256,128]{2,1,0:T(8,128)S(1)} %slice.312), channel_id=1, source_target_pairs={{1,0},{2,1},{3,2},{5,4},{6,5},{7,6},{9,8},{10,9},{11,10},{13,12},{... | collective-permute-start | bytes 786440 | tf_op jit(solution)/shard_map/ppermute | solution.py:21
  237.8 10.6 %collective-permute-start.8 = (f32[2,128,128]{2,1,0:T(8,128)S(1)}, f32[2,128,128]{2,1,0:T(8,128)S(1)}, u32[]{:S(2)}, u32[]{:S(2)}) collective-permute-start(f32[2,128,128]{2,1,0:T(8,128)S(1)} %slice.314), channel_id=1, source_target_pairs={{1,0},{2,1},{3,2},{5,4},{6,5},{7,6},{9,8},{10,9},{11,10},{13,12},{... | collective-permute-start | bytes 393224 | tf_op jit(solution)/shard_map/ppermute | solution.py:21
  307.0 91.0 %copy-start.2 = (f32[2,128,128]{1,2,0:T(8,128)S(1)}, f32[2,128,128]{1,2,0:T(8,128)}, u32[]{:S(2)}) copy-start(f32[2,128,128]{1,2,0:T(8,128)} %copy-done.1) | copy-start | bytes 393220
  307.9 91.7 %collective-permute-start.9 = (f32[3,256,128]{2,1,0:T(8,128)}, f32[3,256,128]{2,1,0:T(8,128)}, u32[]{:S(2)}, u32[]{:S(2)}) collective-permute-start(f32[3,256,128]{2,1,0:T(8,128)} %slice.266), channel_id=1, source_target_pairs={{0,1},{1,2},{2,3},{4,5},{5,6},{6,7},{8,9},{9,10},{10,11},{12,13},{... | collective-permute-start | bytes 1179656 | tf_op jit(solution)/shard_map/ppermute | solution.py:21
  312.6 88.1 %collective-permute-start.10 = (f32[3,128,384]{2,1,0:T(8,128)}, f32[3,128,384]{2,1,0:T(8,128)}, u32[]{:S(2)}, u32[]{:S(2)}) collective-permute-start(f32[3,128,384]{2,1,0:T(8,128)} %slice.268), channel_id=1, source_target_pairs={{0,4},{4,8},{8,12},{12,16},{16,20},{20,24},{24,28},{1,5},{5,9},{9,... | collective-permute-start | bytes 1769480 | tf_op jit(solution)/shard_map/ppermute | solution.py:21
  401.7 8.4 %collective-permute-start.11 = (f32[3,128,128]{2,1,0:T(8,128)S(1)}, f32[3,128,128]{2,1,0:T(8,128)S(1)}, u32[]{:S(2)}, u32[]{:S(2)}) collective-permute-start(f32[3,128,128]{2,1,0:T(8,128)S(1)} %slice.319), channel_id=1, source_target_pairs={{0,1},{1,2},{2,3},{4,5},{5,6},{6,7},{8,9},{9,10},{10,11},{12,13},{... | collective-permute-start | bytes 589832 | tf_op jit(solution)/shard_map/ppermute | solution.py:21
Sparse Core Ops, SparseCore 0:
  48.0 124.5 all-reduce.6
  271.0 126.0 all-reduce.4
where the time goes:
time: 419 us; the launch traced here: 418 us
  waiting for transfers between devices  237 us (57%)
  local copies, waits for them, and re-layouts  62.9 us (15%)
  loops' own time  32.8 us (8%)
  starting transfers between devices  32.4 us (8%)
  matrix products  25.5 us (6%)
  between operations  15.4 us (4%)
  other arithmetic  11.5 us (3%)
    psum x2, waiting for transfers between devices, local(): lax.psum((probe_grad, probe_light), ('row', 'col'))  205 us
    another operation x2, loops' own time, deposit(): lax.fori_loop(0, term_stack.shape[0], add_one, jnp.zeros((channels, heigh...  32.5 us
    ppermute x12, starting transfers between devices, from_behind(): lax.ppermute(value, axis, [(source, source + steps) for source in range(f...  32.3 us
    ppermute x12, waiting for transfers between devices, from_behind(): lax.ppermute(value, axis, [(source, source + steps) for source in range(f...  32.2 us
    dynamic_update_slice x8, local copies, waits for them, and re-layouts, add_one(): return lax.dynamic_update_slice(total, current + term_stack[index], anchor)  23.9 us
    gather x40, local copies, waits for them, and re-layouts  17.4 us
    dot_general x16, matrix products, left_product(): return jnp.einsum('ij,bjk->bik', table, values, precision=HIGHEST_PRECISION)  13.2 us
    dot_general x16, matrix products, right_product(): return jnp.einsum('bij,jk->bik', values, table, precision=HIGHEST_PRECISION)  12.3 us
  transfers between devices with their start and end apart: 14, of which 10 were waited for; matrix products, arithmetic and copies ran while one was open for 7% of the time, Pallas kernels for 0%

commit v1 on v0

v1 whole, which is shorter than its diff:
```python
import math

import jax
import jax.numpy as jnp
import numpy as np
from jax import lax
from jax.experimental import pallas as pl
from jax.experimental.pallas import tpu as pltpu
from jax.sharding import PartitionSpec as P

STEP_SIZE = 0.25
PROBE_STEP = 1.0
REGULARIZER = 1.0
COUNT_SCALE = 1.0 / 1024.0
LANES = 128
VMEM_BYTES = 24 * 1024 * 1024


def dft_parts(length):
    points = np.arange(length)
    angles = (points[:, None] * points[None, :] % length) * (2.0 * math.pi / length)
    cosine = np.cos(angles) / math.sqrt(length)
    sine = np.sin(angles) / math.sqrt(length)
    forward = np.block([[cosine, -sine], [sine, cosine]]).astype(np.float32)
    parts = []
    for table in (forward, forward.T):
        high = table.astype(jnp.bfloat16)
        low = (table - high.astype(np.float32)).astype(jnp.bfloat16)
        parts += [high, low]
    return np.stack(parts)


def split(values):
    high = values.astype(jnp.bfloat16)
    low = (values - high.astype(jnp.float32)).astype(jnp.bfloat16)
    return high, low


def dot(left, right):
    return jnp.dot(left, right, preferred_element_type=jnp.float32)


def right_table(values, table_high, table_low):
    high, low = split(values)
    return dot(high, table_high) + (dot(high, table_low) + dot(low, table_high))


def left_table(table_high, table_low, values):
    high, low = split(values)
    return dot(table_high, high) + (dot(table_low, high) + dot(table_high, low))


def slot_weight(counts_ref, slot, slots):
    count = counts_ref[0, 0]
    upper = lax.axis_index("row") < lax.axis_size("row") // 2
    inside = jnp.where(upper, slot < count, slot >= slots - count)
    return jnp.where(inside, 1.0, 0.0).astype(jnp.float32)


def lane_index(length):
    return lax.broadcasted_iota(jnp.int32, (length, LANES), 1)


def take_patch(ext_ref, channel, row, col, length):
    block = col // LANES
    shift = col % LANES
    turn = (LANES - shift) % LANES
    first = pltpu.roll(ext_ref[channel, block, pl.ds(row, length), :], turn, 1)
    second = pltpu.roll(ext_ref[channel, block + 1, pl.ds(row, length), :], turn, 1)
    return jnp.where(lane_index(length) < LANES - shift, first, second)


def add_patch(dep_ref, channel, row, col, values, length):
    block = col // LANES
    shift = col % LANES
    turned = pltpu.roll(values, shift, 1)
    late = lane_index(length) >= shift
    window = pl.ds(row, length)
    dep_ref[block, channel, window, :] += jnp.where(late, turned, 0.0)
    dep_ref[block + 1, channel, window, :] += jnp.where(late, 0.0, turned)


def position_terms(patches, probe_real, probe_imag, measured_ref, tables_ref, weights, slots, length):
    forward_high, forward_low = tables_ref[0], tables_ref[1]
    backward_high, backward_low = tables_ref[2], tables_ref[3]
    exits = []
    for patch_real, patch_imag in patches:
        exits.append(
            jnp.concatenate(
                [
                    probe_real * patch_real - probe_imag * patch_imag,
                    probe_real * patch_imag + probe_imag * patch_real,
                ],
                axis=1,
            )
        )
    mid = right_table(jnp.concatenate(exits, axis=0), forward_high, forward_low)
    mid = jnp.concatenate(
        [
            jnp.concatenate(
                [
                    mid[s * length : (s + 1) * length, :length],
                    mid[s * length : (s + 1) * length, length:],
                ],
                axis=0,
            )
            for s in range(slots)
        ],
        axis=1,
    )
    freq = left_table(backward_high, backward_low, mid)
    scaled = []
    for s in range(slots):
        freq_real = freq[:length, s * length : (s + 1) * length]
        freq_imag = freq[length:, s * length : (s + 1) * length]
        measured = measured_ref[s].astype(jnp.float32)
        residual = freq_real * freq_real + freq_imag * freq_imag - COUNT_SCALE * measured
        scaled.append(jnp.concatenate([residual * freq_real, residual * freq_imag], axis=0))
    mid = left_table(forward_high, forward_low, jnp.concatenate(scaled, axis=1))
    mid = jnp.concatenate(
        [
            jnp.concatenate(
                [
                    mid[:length, s * length : (s + 1) * length],
                    mid[length:, s * length : (s + 1) * length],
                ],
                axis=1,
            )
            for s in range(slots)
        ],
        axis=0,
    )
    back = right_table(mid, backward_high, backward_low)
    updates = []
    for s in range(slots):
        rows = slice(s * length, (s + 1) * length)
        updates.append((back[rows, :length] * weights[s], back[rows, length:] * weights[s]))
    return updates


def finish_terms(
    patches, updates, probe_real, probe_imag, weights, rows_ref, cols_ref, keep_ref, send_ref, dep_ref, sum_ref, length
):
    slots = len(patches)
    grad_real = jnp.zeros((length, length), jnp.float32)
    grad_imag = grad_real
    light = grad_real
    for s in range(slots):
        (patch_real, patch_imag), (back_real, back_imag) = patches[s], updates[s]
        grad_real += patch_real * back_real + patch_imag * back_imag
        grad_imag += patch_real * back_imag - patch_imag * back_real
        light += weights[s] * (patch_real * patch_real + patch_imag * patch_imag)
    sum_ref[0] = grad_real
    sum_ref[1] = grad_imag
    sum_ref[2] = light
    half = length // 2
    side = lax.axis_index("row") % 2
    keep_ref[...] = sum_ref[:, pl.ds(pl.multiple_of(side * half, half), half), :]
    send_ref[...] = sum_ref[:, pl.ds(pl.multiple_of((1 - side) * half, half), half), :]
    power = probe_real * probe_real + probe_imag * probe_imag
    dep_ref[...] = jnp.zeros_like(dep_ref)
    for s in range(slots):
        back_real, back_imag = updates[s]
        row, col = rows_ref[0, 0, s], cols_ref[0, 0, s]
        add_patch(dep_ref, 0, row, col, probe_real * back_real + probe_imag * back_imag, length)
        add_patch(dep_ref, 1, row, col, probe_real * back_imag - probe_imag * back_real, length)
        add_patch(dep_ref, 2, row, col, weights[s] * power, length)


def first_kernel(
    rows_ref, cols_ref, counts_ref, tile_ref, right_ref, below_ref, corner_ref, probe_ref, measured_ref, tables_ref,
    ext_ref, keep_ref, send_ref, left_out, middle_out, right_out, dep_ref, sum_ref,
):
    length = probe_ref.shape[1]
    slots = measured_ref.shape[0]
    tall = tile_ref.shape[1]
    blocks = tile_ref.shape[2] // LANES
    for channel in range(2):
        for block in range(blocks):
            lanes = slice(block * LANES, (block + 1) * LANES)
            ext_ref[channel, block, :tall, :] = tile_ref[channel, :, lanes]
            ext_ref[channel, block, tall:, :] = below_ref[channel, :, lanes]
        ext_ref[channel, blocks, :tall, :] = right_ref[channel]
        ext_ref[channel, blocks, tall:, :] = corner_ref[channel]
    probe_real, probe_imag = probe_ref[0], probe_ref[1]
    weights = [slot_weight(counts_ref, s, slots) for s in range(slots)]
    patches = [
        [take_patch(ext_ref, channel, rows_ref[0, 0, s], cols_ref[0, 0, s], length) for channel in range(2)]
        for s in range(slots)
    ]
    updates = position_terms(
        patches, probe_real, probe_imag, measured_ref, tables_ref, weights, slots, length
    )
    finish_terms(
        patches, updates, probe_real, probe_imag, weights, rows_ref, cols_ref, keep_ref, send_ref, dep_ref, sum_ref, length
    )
    left_out[...] = dep_ref[0]
    middle_out[...] = dep_ref[1]
    right_out[...] = dep_ref[2]


def strips_kernel(left_ref, middle_ref, right_ref, from_left, from_right, left_out, right_out, top_out, bottom_out):
    left_out[...] = left_ref[...] + from_left[...]
    right_out[...] = right_ref[...] + from_right[...]
    length = top_out.shape[2]
    tall = left_ref.shape[1] - length
    for index, part in enumerate((left_out, middle_ref, right_out)):
        top_out[index] = part[:, :length, :]
        bottom_out[index] = part[:, tall:, :]


def object_kernel(
    rows_ref, cols_ref, ext_ref, left_ref, middle_ref, right_ref, from_above, from_below, tile_out, patches_out, new_ref
):
    length = patches_out.shape[2]
    slots = patches_out.shape[0]
    tall = ext_ref.shape[2] - length
    blocks = tile_out.shape[1]
    inside_row = jnp.where(lax.axis_index("row") < lax.axis_size("row") - 1, 1.0, 0.0).astype(jnp.float32)
    inside_col = jnp.where(lax.axis_index("col") < lax.axis_size("col") - 1, 1.0, 0.0).astype(jnp.float32)
    for block, part in enumerate((left_ref, middle_ref, right_ref)):
        for piece, start, stop in ((0, 0, length), (1, length, tall), (2, tall, tall + length)):
            if start == stop:
                continue
            totals = [part[channel, start:stop, :] for channel in range(3)]
            if piece == 0:
                totals = [totals[channel] + from_above[block, channel] for channel in range(3)]
            if piece == 2:
                totals = [totals[channel] + from_below[block, channel] for channel in range(3)]
            scale = STEP_SIZE / (totals[2] + REGULARIZER)
            if piece == 2:
                scale = scale * inside_row
            if block == blocks:
                scale = scale * inside_col
            for channel in range(2):
                new_ref[channel, block, start:stop, :] = (
                    ext_ref[channel, block, start:stop, :] - scale * totals[channel]
                )
    for channel in range(2):
        tile_out[channel] = new_ref[channel, :blocks, :tall, :]
        for s in range(slots):
            patches_out[s, channel] = take_patch(new_ref, channel, rows_ref[0, 0, s], cols_ref[0, 0, s], length)


def assemble_probe(half_ref, other_ref, side):
    first = side == 0
    return [
        jnp.concatenate(
            [
                jnp.where(first, half_ref[channel], other_ref[channel]),
                jnp.where(first, other_ref[channel], half_ref[channel]),
            ],
            axis=0,
        )
        for channel in range(2)
    ]


def second_kernel(
    rows_ref, cols_ref, counts_ref, patches_ref, half_ref, other_ref, measured_ref, tables_ref,
    keep_ref, send_ref, left_out, middle_out, right_out, dep_ref, sum_ref,
):
    slots = measured_ref.shape[0]
    length = measured_ref.shape[1]
    probe_real, probe_imag = assemble_probe(half_ref, other_ref, lax.axis_index("row") % 2)
    weights = [slot_weight(counts_ref, s, slots) for s in range(slots)]
    patches = [[patches_ref[s, channel] for channel in range(2)] for s in range(slots)]
    updates = position_terms(
        patches, probe_real, probe_imag, measured_ref, tables_ref, weights, slots, length
    )
    finish_terms(
        patches, updates, probe_real, probe_imag, weights, rows_ref, cols_ref, keep_ref, send_ref, dep_ref, sum_ref, length
    )
    left_out[...] = dep_ref[0]
    middle_out[...] = dep_ref[1]
    right_out[...] = dep_ref[2]


def final_kernel(tile_ref, left_ref, middle_ref, from_left, from_above, object_out):
    tall = tile_ref.shape[2]
    length = from_above.shape[2]
    for block in range(tile_ref.shape[1]):
        for start, stop in ((0, length), (length, tall)):
            if block == 0:
                totals = [left_ref[channel, start:stop, :] + from_left[channel, start:stop, :] for channel in range(3)]
            else:
                totals = [middle_ref[channel, start:stop, :] for channel in range(3)]
            if start == 0:
                totals = [totals[channel] + from_above[block, channel] for channel in range(3)]
            scale = STEP_SIZE / (totals[2] + REGULARIZER)
            for channel in range(2):
                object_out[channel, start:stop, block * LANES : (block + 1) * LANES] = (
                    tile_ref[channel, block, start:stop, :] - scale * totals[channel]
                )


def shift(value, axis, steps):
    count = lax.axis_size(axis)
    pairs = [(source, source + steps) for source in range(count) if 0 <= source + steps < count]
    return lax.ppermute(value, axis, pairs)


def flip(value, axis, mask):
    count = lax.axis_size(axis)
    return lax.ppermute(value, axis, [(source, source ^ mask) for source in range(count)])


def sum_over(value, axis, bit):
    count = lax.axis_size(axis)
    while bit < count:
        if 2 * bit < count:
            one, two, three = (flip(value, axis, mask * bit) for mask in (1, 2, 3))
            value = (value + one) + (two + three)
            bit *= 4
        else:
            value = value + flip(value, axis, bit)
            bit *= 2
    return value


def probe_half(half, keep, send):
    total = keep + flip(send, "row", 1)
    total = sum_over(total, "row", 2)
    total = sum_over(total, "col", 1)
    return half - PROBE_STEP * total[:2] / (total[2] + REGULARIZER)


def call(kernel, outs, scratch, args, scalars):
    vmem = pl.BlockSpec(memory_space=pltpu.VMEM)
    smem = pl.BlockSpec(memory_space=pltpu.SMEM)
    return pl.pallas_call(
        kernel,
        out_shape=[jax.ShapeDtypeStruct(shape, jnp.float32) for shape in outs],
        in_specs=[smem] * scalars + [vmem] * (len(args) - scalars),
        out_specs=[vmem] * len(outs),
        scratch_shapes=[pltpu.VMEM(shape, jnp.float32) for shape in scratch],
        compiler_params=pltpu.CompilerParams(vmem_limit_bytes=VMEM_BYTES),
    )(*args)


def local(object_field, probe_field, intensities, off_rows, off_cols, counts):
    tall, wide = object_field.shape[1:]
    length = probe_field.shape[1]
    slots = off_rows.shape[2]
    half = length // 2
    high = tall + length
    blocks = wide // LANES
    tables = jnp.asarray(dft_parts(length))
    measured = intensities.reshape(slots, length, length)
    count_rows, count_cols = lax.axis_size("row"), lax.axis_size("col")

    below = shift(object_field[:, :length, :], "row", -1)
    right = shift(object_field[:, :, :length], "col", -1)
    corner = lax.ppermute(
        object_field[:, :length, :length],
        ("row", "col"),
        [
            ((r + 1) * count_cols + c + 1, r * count_cols + c)
            for r in range(count_rows - 1)
            for c in range(count_cols - 1)
        ],
    )
    strip = (3, high, LANES)
    partial = (3, half, length)
    ext, keep, send, left_part, middle_part, right_part = call(
        first_kernel,
        [(2, blocks + 1, high, LANES), partial, partial, strip, strip, strip],
        [(blocks + 1, 3, high, LANES), (3, length, length)],
        [off_rows, off_cols, counts, object_field, right, below, corner, probe_field, measured, tables],
        3,
    )
    side = lax.axis_index("row") % 2
    own = lax.dynamic_slice(probe_field, (jnp.int32(0), side * half, jnp.int32(0)), (2, half, length))
    new_half = probe_half(own, keep, send)
    new_other = flip(new_half, "row", 1)
    from_right = shift(left_part, "col", -1)
    from_left = shift(right_part, "col", 1)
    edge = (blocks + 1, 3, length, LANES)
    left_part, right_part, top, bottom = call(
        strips_kernel,
        [strip, strip, edge, edge],
        [],
        [left_part, middle_part, right_part, from_left, from_right],
        0,
    )
    from_below = shift(top, "row", -1)
    from_above = shift(bottom, "row", 1)
    tile, patches = call(
        object_kernel,
        [(2, blocks, tall, LANES), (slots, 2, length, length)],
        [(2, blocks + 1, high, LANES)],
        [off_rows, off_cols, ext, left_part, middle_part, right_part, from_above, from_below],
        2,
    )
    keep, send, left_part, middle_part, right_part = call(
        second_kernel,
        [partial, partial, strip, strip, strip],
        [(blocks + 1, 3, high, LANES), (3, length, length)],
        [off_rows, off_cols, counts, patches, new_half, new_other, measured, tables],
        3,
    )
    last_half = probe_half(new_half, keep, send)
    last_other = flip(last_half, "row", 1)
    from_left = shift(right_part, "col", 1)
    bottom = jnp.stack([left_part[:, tall:, :] + from_left[:, tall:, :], middle_part[:, tall:, :]])
    from_above = shift(bottom, "row", 1)
    (object_out,) = call(
        final_kernel,
        [(2, tall, wide)],
        [],
        [tile, left_part, middle_part, from_left, from_above],
        0,
    )
    first = side == 0
    probe_out = jnp.concatenate(
        [jnp.where(first, last_half, last_other), jnp.where(first, last_other, last_half)], axis=1
    )
    return object_out, probe_out


def solution(mesh):
    placed = (
        P(None, "row", "col"),
        P(),
        P("row", "col", None, None, None),
        P("row", "col", None),
        P("row", "col", None),
        P("row", "col"),
    )
    return jax.shard_map(
        local, mesh=mesh, in_specs=placed, out_specs=(P(None, "row", "col"), P()), check_vma=False
    )
```

time: 419 us -> 111 us (0.26)
  the two profiles are of different devices: /device:TPU:0 before, /device:TPU:20 now
where the time goes in v1:
time: 111 us
  waiting for transfers between devices  53.8 us (48%)
  starting transfers between devices  40.8 us (37%)
  Pallas kernels  9.82 us (9%)
  local copies, waits for them, and re-layouts  3.9 us (4%)
  between operations  1.65 us (1%)
    ppermute x8, waiting for transfers between devices, shift(): return lax.ppermute(value, axis, pairs)  36.4 us
    ppermute x8, starting transfers between devices, shift(): return lax.ppermute(value, axis, pairs)  23 us
    ppermute x16, starting transfers between devices, flip(): lax.ppermute(value, axis, [(source, source ^ mask) for source in range(co...  15.1 us
    ppermute x16, waiting for transfers between devices, flip(): lax.ppermute(value, axis, [(source, source ^ mask) for source in range(co...  14.2 us
    pallas_call x5, Pallas kernels, call(): pl.pallas_call(kernel, out_shape=[jax.ShapeDtypeStruct(shape, jnp.float32...  9.82 us
    ppermute x1, waiting for transfers between devices, local(): lax.ppermute(object_field[:, :length, :length], ('row', 'col'), [((r + 1)...  3.32 us
    ppermute x1, starting transfers between devices, local(): lax.ppermute(object_field[:, :length, :length], ('row', 'col'), [((r + 1)...  2.75 us
  transfers between devices with their start and end apart: 25, of which 13 were waited for; matrix products, arithmetic and copies ran while one was open for 2% of the time, Pallas kernels for 2%

profile of v1, /device:TPU:20, one launch (start us, length us, event | category | flops | bytes accessed | tf_op | source)
XLA Modules:
  0.0 110.9 jit_solution(11390769397894335253)
XLA Ops:
  0.6 0.0 copy-start.1
  0.6 0.0 copy-start
  0.7 1.1 slice.30
  1.8 2.4 %collective-permute-start = (f32[2,256,128]{2,1,0:T(8,128)S(1)}, f32[2,256,128]{2,1,0:T(8,128)S(1)}, u32[]{:S(2)}, u32[]{:S(2)}) collective-permute-start(f32[2,256,128]{2,1,0:T(8,128)S(1)} %slice.30), channel_id=1, source_target_pairs={{1,0},{2,1},{3,2},{5,4},{6,5},{7,6},{9,8},{10,9},{11,10},{13,12},{... | collective-permute-start | bytes 786440 | tf_op jit(solution)/shard_map/ppermute | solution.py:300
  4.1 1.0 slice.31
  5.1 2.5 %collective-permute-start.1 = (f32[2,128,256]{2,1,0:T(8,128)S(1)}, f32[2,128,256]{2,1,0:T(8,128)S(1)}, u32[]{:S(2)}, u32[]{:S(2)}) collective-permute-start(f32[2,128,256]{2,1,0:T(8,128)S(1)} %slice.31), channel_id=1, source_target_pairs={{4,0},{8,4},{12,8},{16,12},{20,16},{24,20},{28,24},{5,1},{9,5},{13... | collective-permute-start | bytes 786440 | tf_op jit(solution)/shard_map/ppermute | solution.py:300
  7.6 0.9 slice.32
  8.5 2.8 %collective-permute-start.2 = (f32[2,128,128]{2,1,0:T(8,128)S(1)}, f32[2,128,128]{2,1,0:T(8,128)S(1)}, u32[]{:S(2)}, u32[]{:S(2)}) collective-permute-start(f32[2,128,128]{2,1,0:T(8,128)S(1)} %slice.32), channel_id=1, source_target_pairs={{5,0},{6,1},{7,2},{9,4},{10,5},{11,6},{13,8},{14,9},{15,10},{17,12... | collective-permute-start | bytes 393224 | tf_op jit(solution)/shard_map/ppermute | solution.py:354
  11.9 3.3 %collective-permute-done.2.corner_ref = f32[2,128,128]{2,1,0:T(8,128)S(1)} collective-permute-done((f32[2,128,128]{2,1,0:T(8,128)S(1)}, f32[2,128,128]{2,1,0:T(8,128)S(1)}, u32[]{:S(2)}, u32[]{:S(2)}) %collective-permute-start.2) | collective-permute-done | bytes 131104 | tf_op jit(solution)/shard_map/ppermute | solution.py:354
  15.3 0.0 collective-permute-done.right_ref
  15.3 0.0 collective-permute-done.1.below_ref
  15.3 0.0 copy-done.1
  15.3 0.0 copy-start.3
  15.3 0.9 copy-done.3
  16.2 3.6 %shard_map.86 = (f32[2,3,384,128]{3,2,1,0:T(8,128)S(1)}, f32[3,64,128]{2,1,0:T(8,128)S(1)}, f32[3,64,128]{2,1,0:T(8,128)S(1)}, f32[3,384,128]{2,1,0:T(8,128)S(1)...) custom-call(s32[1,1,4]{2,1,0:T(1,128)S(1)} %copy-done.5, s32[1,1,4]{2,1,0:T(1,128)S(1)} %copy-done.6, ...), custom_call_target="tpu_custom_call" | custom-call | tf_op jit(solution)/shard_map/pallas_call | solution.py:331
  19.8 2.3 %collective-permute-start.4 = (f32[3,384,128]{2,1,0:T(8,128)S(1)}, f32[3,384,128]{2,1,0:T(8,128)}, u32[]{:S(2)}, u32[]{:S(2)}) collective-permute-start(f32[3,384,128]{2,1,0:T(8,128)S(1)} %get-tuple-element.20.left_ref), channel_id=1, source_target_pairs={{1,0},{2,1},{3,2},{5,4},{6,5},{7,6},{9,8},{10,9},{11,10},{13,12},{... | collective-permute-start | bytes 1769480 | tf_op jit(solution)/shard_map/ppermute | solution.py:300
  22.2 4.3 %collective-permute-start.3 = (f32[3,384,128]{2,1,0:T(8,128)}, f32[3,384,128]{2,1,0:T(8,128)}, u32[]{:S(2)}, u32[]{:S(2)}) collective-permute-start(f32[3,384,128]{2,1,0:T(8,128)} %get-tuple-element.22.right_ref), channel_id=1, source_target_pairs={{0,1},{1,2},{2,3},{4,5},{5,6},{6,7},{8,9},{9,10},{10,11},{12,13},{... | collective-permute-start | bytes 1769480 | tf_op jit(solution)/shard_map/ppermute | solution.py:300
  26.5 0.6 collective-permute-start.7
  27.1 0.9 collective-permute-done.7
  28.1 2.1 %collective-permute-start.10 = (f32[3,64,128]{2,1,0:T(8,128)S(1)}, f32[3,64,128]{2,1,0:T(8,128)S(1)}, u32[]{:S(2)}, u32[]{:S(2)}) collective-permute-start(f32[3,64,128]{2,1,0:T(8,128)S(1)} %add.62), channel_id=1, source_target_pairs={{0,24},{4,28},{8,16},{12,20},{16,8},{20,12},{24,0},{28,4},{1,25},{... | collective-permute-start | bytes 294920 | tf_op jit(solution)/shard_map/ppermute | solution.py:305
  30.2 0.5 collective-permute-start.9
  30.7 1.0 collective-permute-start.8
  31.7 2.6 %collective-permute-done.10 = f32[3,64,128]{2,1,0:T(8,128)S(1)} collective-permute-done((f32[3,64,128]{2,1,0:T(8,128)S(1)}, f32[3,64,128]{2,1,0:T(8,128)S(1)}, u32[]{:S(2)}, u32[]{:S(2)}) %collective-permute-start.10) | collective-permute-done | bytes 98336 | tf_op jit(solution)/shard_map/ppermute | solution.py:305
  34.2 2.0 %collective-permute-done.9 = f32[3,64,128]{2,1,0:T(8,128)S(1)} collective-permute-done((f32[3,64,128]{2,1,0:T(8,128)S(1)}, f32[3,64,128]{2,1,0:T(8,128)S(1)}, u32[]{:S(2)}, u32[]{:S(2)}) %collective-permute-start.9) | collective-permute-done | bytes 98336 | tf_op jit(solution)/shard_map/ppermute | solution.py:305
  36.2 0.0 collective-permute-done.8
  36.3 0.1 collective-permute-start.13
  36.3 2.0 %collective-permute-start.12 = (f32[3,64,128]{2,1,0:T(8,128)S(1)}, f32[3,64,128]{2,1,0:T(8,128)S(1)}, u32[]{:S(2)}, u32[]{:S(2)}) collective-permute-start(f32[3,64,128]{2,1,0:T(8,128)S(1)} %add_add_fusion.3), channel_id=1, source_target_pairs={{0,2},{1,3},{2,0},{3,1},{4,6},{5,7},{6,4},{7,5},{8,10},{9,11},{10,... | collective-permute-start | bytes 294920 | tf_op jit(solution)/shard_map/ppermute | solution.py:305
  38.4 1.5 %collective-permute-start.11 = (f32[3,64,128]{2,1,0:T(8,128)S(1)}, f32[3,64,128]{2,1,0:T(8,128)S(1)}, u32[]{:S(2)}, u32[]{:S(2)}) collective-permute-start(f32[3,64,128]{2,1,0:T(8,128)S(1)} %add_add_fusion.3), channel_id=1, source_target_pairs={{0,1},{1,0},{2,3},{3,2},{4,5},{5,4},{6,7},{7,6},{8,9},{9,8},{10,11... | collective-permute-start | bytes 294920 | tf_op jit(solution)/shard_map/ppermute | solution.py:305
  39.8 0.0 collective-permute-done.4.from_right
  39.8 5.0 %collective-permute-done.3.from_left = f32[3,384,128]{2,1,0:T(8,128)} collective-permute-done((f32[3,384,128]{2,1,0:T(8,128)}, f32[3,384,128]{2,1,0:T(8,128)}, u32[]{:S(2)}, u32[]{:S(2)}) %collective-permute-start.3) | collective-permute-done | bytes 589856 | tf_op jit(solution)/shard_map/ppermute | solution.py:300
  44.8 1.6 %shard_map.87 = (f32[3,384,128]{2,1,0:T(8,128)S(1)}, f32[3,384,128]{2,1,0:T(8,128)S(1)}, f32[3,3,128,128]{3,2,1,0:T(8,128)S(1)}, f32[3,3,128,128]{3,2,1,0:T(8,128)S(1)}) custom-call(f32[3,384,128]{2,1,0:T(8,128)S(1)} %get-tuple-element.20.left_ref, f32[3,384,128]{2,1,0:T(8,128)S(1)} %get-tuple-element.21.middle_ref, ...), custom_call_target="tpu_custom_call" | custom-call | tf_op jit(solution)/shard_map/pallas_call | solution.py:331
  46.5 1.9 %collective-permute-start.5 = (f32[3,3,128,128]{3,2,1,0:T(8,128)S(1)}, f32[3,3,128,128]{3,2,1,0:T(8,128)S(1)}, u32[]{:S(2)}, u32[]{:S(2)}) collective-permute-start(f32[3,3,128,128]{3,2,1,0:T(8,128)S(1)} %get-tuple-element.25), channel_id=1, source_target_pairs={{0,4},{4,8},{8,12},{12,16},{16,20},{20,24},{24,28},{1,5},{5,9},{9,... | collective-permute-start | bytes 1769480 | tf_op jit(solution)/shard_map/ppermute | solution.py:300
  48.4 4.5 %collective-permute-start.6 = (f32[3,3,128,128]{3,2,1,0:T(8,128)S(1)}, f32[3,3,128,128]{3,2,1,0:T(8,128)S(1)}, u32[]{:S(2)}, u32[]{:S(2)}) collective-permute-start(f32[3,3,128,128]{3,2,1,0:T(8,128)S(1)} %get-tuple-element.26), channel_id=1, source_target_pairs={{4,0},{8,4},{12,8},{16,12},{20,16},{24,20},{28,24},{5,1},{9,5},{13... | collective-permute-start | bytes 1769480 | tf_op jit(solution)/shard_map/ppermute | solution.py:300
  52.9 0.0 collective-permute-done.13
  53.0 0.0 collective-permute-done.12
  53.0 0.0 collective-permute-done.11
  53.1 0.1 collective-permute-start.14
  53.1 10.2 %collective-permute-done.5.from_above = f32[3,3,128,128]{3,2,1,0:T(8,128)S(1)} collective-permute-done((f32[3,3,128,128]{3,2,1,0:T(8,128)S(1)}, f32[3,3,128,128]{3,2,1,0:T(8,128)S(1)}, u32[]{:S(2)}, u32[]{:S(2)}) %collective-permute-start.5) | collective-permute-done | bytes 589856 | tf_op jit(solution)/shard_map/ppermute | solution.py:300
  63.3 0.0 collective-permute-done.6.from_below
  63.3 1.1 shard_map.88
  64.4 0.0 collective-permute-done.14.other_ref
  64.5 2.6 %shard_map.89 = (f32[3,64,128]{2,1,0:T(8,128)S(1)}, f32[3,64,128]{2,1,0:T(8,128)S(1)}, f32[3,384,128]{2,1,0:T(8,128)S(1)}, f32[3,384,128]{2,1,0:T(8,128)S(1)}, f32[3,384,128]{2,1,0:T(8,128)S(1)}) custom-call(s32[1,1,4]{2,1,0:T(1,128)S(1)} %copy-done.5, s32[1,1,4]{2,1,0:T(1,128)S(1)} %copy-done.6, s32[1,1]{1,0:T(1,128)S(6)} %copy.9.counts_ref, ...), custom_call_target="tpu_custom_call" | custom-call | tf_op jit(solution)/shard_map/pallas_call | solution.py:331
  67.0 0.1 collective-permute-start.17
  67.1 1.3 %collective-permute-done.17 = f32[3,64,128]{2,1,0:T(8,128)S(1)} collective-permute-done((f32[3,64,128]{2,1,0:T(8,128)S(1)}, f32[3,64,128]{2,1,0:T(8,128)S(1)}, u32[]{:S(2)}, u32[]{:S(2)}) %collective-permute-start.17) | collective-permute-done | bytes 98336 | tf_op jit(solution)/shard_map/ppermute | solution.py:305
  68.4 1.2 %collective-permute-start.20 = (f32[3,64,128]{2,1,0:T(8,128)S(1)}, f32[3,64,128]{2,1,0:T(8,128)S(1)}, u32[]{:S(2)}, u32[]{:S(2)}) collective-permute-start(f32[3,64,128]{2,1,0:T(8,128)S(1)} %add.71), channel_id=1, source_target_pairs={{0,24},{4,28},{8,16},{12,20},{16,8},{20,12},{24,0},{28,4},{1,25},{... | collective-permute-start | bytes 294920 | tf_op jit(solution)/shard_map/ppermute | solution.py:305
  69.6 0.6 collective-permute-start.19
  70.1 1.8 %collective-permute-start.18 = (f32[3,64,128]{2,1,0:T(8,128)S(1)}, f32[3,64,128]{2,1,0:T(8,128)S(1)}, u32[]{:S(2)}, u32[]{:S(2)}) collective-permute-start(f32[3,64,128]{2,1,0:T(8,128)S(1)} %add.71), channel_id=1, source_target_pairs={{0,8},{4,12},{8,0},{12,4},{16,24},{20,28},{24,16},{28,20},{1,9},{5... | collective-permute-start | bytes 294920 | tf_op jit(solution)/shard_map/ppermute | solution.py:305
  72.0 3.0 %collective-permute-done.20 = f32[3,64,128]{2,1,0:T(8,128)S(1)} collective-permute-done((f32[3,64,128]{2,1,0:T(8,128)S(1)}, f32[3,64,128]{2,1,0:T(8,128)S(1)}, u32[]{:S(2)}, u32[]{:S(2)}) %collective-permute-start.20) | collective-permute-done | bytes 98336 | tf_op jit(solution)/shard_map/ppermute | solution.py:305
  75.0 1.3 %collective-permute-done.19 = f32[3,64,128]{2,1,0:T(8,128)S(1)} collective-permute-done((f32[3,64,128]{2,1,0:T(8,128)S(1)}, f32[3,64,128]{2,1,0:T(8,128)S(1)}, u32[]{:S(2)}, u32[]{:S(2)}) %collective-permute-start.19) | collective-permute-done | bytes 98336 | tf_op jit(solution)/shard_map/ppermute | solution.py:305
  76.2 0.5 collective-permute-done.18
  76.7 0.1 collective-permute-start.23
  76.8 2.6 %collective-permute-start.22 = (f32[3,64,128]{2,1,0:T(8,128)S(1)}, f32[3,64,128]{2,1,0:T(8,128)S(1)}, u32[]{:S(2)}, u32[]{:S(2)}) collective-permute-start(f32[3,64,128]{2,1,0:T(8,128)S(1)} %add_add_fusion.1), channel_id=1, source_target_pairs={{0,2},{1,3},{2,0},{3,1},{4,6},{5,7},{6,4},{7,5},{8,10},{9,11},{10,... | collective-permute-start | bytes 294920 | tf_op jit(solution)/shard_map/ppermute | solution.py:305
  79.5 0.8 collective-permute-start.21
  80.3 3.1 %collective-permute-start.15 = (f32[3,384,128]{2,1,0:T(8,128)S(1)}, f32[3,384,128]{2,1,0:T(8,128)S(1)}, u32[]{:S(2)}, u32[]{:S(2)}) collective-permute-start(f32[3,384,128]{2,1,0:T(8,128)S(1)} %get-tuple-element.33), channel_id=1, source_target_pairs={{0,1},{1,2},{2,3},{4,5},{5,6},{6,7},{8,9},{9,10},{10,11},{12,13},{... | collective-permute-start | bytes 1769480 | tf_op jit(solution)/shard_map/ppermute | solution.py:300
  83.4 2.6 %collective-permute-done.23 = f32[3,64,128]{2,1,0:T(8,128)S(1)} collective-permute-done((f32[3,64,128]{2,1,0:T(8,128)S(1)}, f32[3,64,128]{2,1,0:T(8,128)S(1)}, u32[]{:S(2)}, u32[]{:S(2)}) %collective-permute-start.23) | collective-permute-done | bytes 98336 | tf_op jit(solution)/shard_map/ppermute | solution.py:305
  86.0 0.0 collective-permute-done.22
  86.0 0.0 collective-permute-done.21
  86.1 0.1 collective-permute-start.24
  86.2 13.8 %collective-permute-done.15.from_left = f32[3,384,128]{2,1,0:T(8,128)S(1)} collective-permute-done((f32[3,384,128]{2,1,0:T(8,128)S(1)}, f32[3,384,128]{2,1,0:T(8,128)S(1)}, u32[]{:S(2)}, u32[]{:S(2)}) %collective-permute-start.15) | collective-permute-done | bytes 589856 | tf_op jit(solution)/shard_map/ppermute | solution.py:300
  100.1 1.9 %collective-permute-start.16 = (f32[2,3,128,128]{3,2,1,0:T(8,128)S(1)}, f32[2,3,128,128]{3,2,1,0:T(8,128)S(1)}, u32[]{:S(2)}, u32[]{:S(2)}) collective-permute-start(f32[2,3,128,128]{3,2,1,0:T(8,128)S(1)} %pad_maximum_fusion), channel_id=1, source_target_pairs={{0,4},{4,8},{8,12},{12,16},{16,20},{20,24},{24,28},{1,5},{5,9},{9,... | collective-permute-start | bytes 1179656 | tf_op jit(solution)/shard_map/ppermute | solution.py:300
  102.0 0.0 collective-permute-done.24
  102.0 0.7 pad_maximum_fusion.1
  102.7 7.4 %collective-permute-done.16.from_above = f32[2,3,128,128]{3,2,1,0:T(8,128)S(1)} collective-permute-done((f32[2,3,128,128]{3,2,1,0:T(8,128)S(1)}, f32[2,3,128,128]{3,2,1,0:T(8,128)S(1)}, u32[]{:S(2)}, u32[]{:S(2)}) %collective-permute-start.16) | collective-permute-done | bytes 393248 | tf_op jit(solution)/shard_map/ppermute | solution.py:300
  110.0 0.9 shard_map.90
  (23 shorter events, 0.3 us)
Async XLA Ops:
  0.6 14.6 %copy-start.1 = (bf16[4,256,256]{2,1,0:T(8,128)(2,1)S(1)}, bf16[4,256,256]{2,1,0:T(8,128)(2,1)}, u32[]{:S(2)}) copy-start(bf16[4,256,256]{2,1,0:T(8,128)(2,1)} %constant.28.clone.tables_ref) | copy-start | bytes 1572868
  0.6 14.6 %copy-start = (f32[2,256,256]{2,1,0:T(8,128)S(1)}, f32[2,256,256]{2,1,0:T(8,128)}, u32[]{:S(2)}) copy-start(f32[2,256,256]{2,1,0:T(8,128)} %tile_ref.1) | copy-start | bytes 1572868
  0.7 14.6 %copy-start.6 = (s32[1,1,4]{2,1,0:T(1,128)S(1)}, s32[1,1,4]{2,1,0:T(1,128)}, u32[]{:S(2)}) copy-start(s32[1,1,4]{2,1,0:T(1,128)} %cols_ref.5) | copy-start | bytes 52
  0.7 14.6 %copy-start.5 = (s32[1,1,4]{2,1,0:T(1,128)S(1)}, s32[1,1,4]{2,1,0:T(1,128)}, u32[]{:S(2)}) copy-start(s32[1,1,4]{2,1,0:T(1,128)} %rows_ref.5) | copy-start | bytes 52
  0.7 14.6 %copy-start.2 = (s32[1,1,4,128,128]{4,3,2,1,0:T(8,128)S(1)}, s32[1,1,4,128,128]{4,3,2,1,0:T(8,128)}, u32[]{:S(2)}) copy-start(s32[1,1,4,128,128]{4,3,2,1,0:T(8,128)} %param.9) | copy-start | bytes 786436
  1.8 13.5 %collective-permute-start = (f32[2,256,128]{2,1,0:T(8,128)S(1)}, f32[2,256,128]{2,1,0:T(8,128)S(1)}, u32[]{:S(2)}, u32[]{:S(2)}) collective-permute-start(f32[2,256,128]{2,1,0:T(8,128)S(1)} %slice.30), channel_id=1, source_target_pairs={{1,0},{2,1},{3,2},{5,4},{6,5},{7,6},{9,8},{10,9},{11,10},{13,12},{... | collective-permute-start | bytes 786440 | tf_op jit(solution)/shard_map/ppermute | solution.py:300
  5.1 10.2 %collective-permute-start.1 = (f32[2,128,256]{2,1,0:T(8,128)S(1)}, f32[2,128,256]{2,1,0:T(8,128)S(1)}, u32[]{:S(2)}, u32[]{:S(2)}) collective-permute-start(f32[2,128,256]{2,1,0:T(8,128)S(1)} %slice.31), channel_id=1, source_target_pairs={{4,0},{8,4},{12,8},{16,12},{20,16},{24,20},{28,24},{5,1},{9,5},{13... | collective-permute-start | bytes 786440 | tf_op jit(solution)/shard_map/ppermute | solution.py:300
  8.5 6.7 %collective-permute-start.2 = (f32[2,128,128]{2,1,0:T(8,128)S(1)}, f32[2,128,128]{2,1,0:T(8,128)S(1)}, u32[]{:S(2)}, u32[]{:S(2)}) collective-permute-start(f32[2,128,128]{2,1,0:T(8,128)S(1)} %slice.32), channel_id=1, source_target_pairs={{5,0},{6,1},{7,2},{9,4},{10,5},{11,6},{13,8},{14,9},{15,10},{17,12... | collective-permute-start | bytes 393224 | tf_op jit(solution)/shard_map/ppermute | solution.py:354
  15.3 0.9 copy-start.3
  19.8 20.0 %collective-permute-start.4 = (f32[3,384,128]{2,1,0:T(8,128)S(1)}, f32[3,384,128]{2,1,0:T(8,128)}, u32[]{:S(2)}, u32[]{:S(2)}) collective-permute-start(f32[3,384,128]{2,1,0:T(8,128)S(1)} %get-tuple-element.20.left_ref), channel_id=1, source_target_pairs={{1,0},{2,1},{3,2},{5,4},{6,5},{7,6},{9,8},{10,9},{11,10},{13,12},{... | collective-permute-start | bytes 1769480 | tf_op jit(solution)/shard_map/ppermute | solution.py:300
  22.2 22.6 %collective-permute-start.3 = (f32[3,384,128]{2,1,0:T(8,128)}, f32[3,384,128]{2,1,0:T(8,128)}, u32[]{:S(2)}, u32[]{:S(2)}) collective-permute-start(f32[3,384,128]{2,1,0:T(8,128)} %get-tuple-element.22.right_ref), channel_id=1, source_target_pairs={{0,1},{1,2},{2,3},{4,5},{5,6},{6,7},{8,9},{9,10},{10,11},{12,13},{... | collective-permute-start | bytes 1769480 | tf_op jit(solution)/shard_map/ppermute | solution.py:300
  26.5 1.6 %collective-permute-start.7 = (f32[3,64,128]{2,1,0:T(8,128)S(1)}, f32[3,64,128]{2,1,0:T(8,128)S(1)}, u32[]{:S(2)}, u32[]{:S(2)}) collective-permute-start(f32[3,64,128]{2,1,0:T(8,128)S(1)} %get-tuple-element.30), channel_id=1, source_target_pairs={{0,4},{4,0},{8,12},{12,8},{16,20},{20,16},{24,28},{28,24},{1,5},{5... | collective-permute-start | bytes 294920 | tf_op jit(solution)/shard_map/ppermute | solution.py:305
  28.1 6.1 %collective-permute-start.10 = (f32[3,64,128]{2,1,0:T(8,128)S(1)}, f32[3,64,128]{2,1,0:T(8,128)S(1)}, u32[]{:S(2)}, u32[]{:S(2)}) collective-permute-start(f32[3,64,128]{2,1,0:T(8,128)S(1)} %add.62), channel_id=1, source_target_pairs={{0,24},{4,28},{8,16},{12,20},{16,8},{20,12},{24,0},{28,4},{1,25},{... | collective-permute-start | bytes 294920 | tf_op jit(solution)/shard_map/ppermute | solution.py:305
  30.2 6.0 %collective-permute-start.9 = (f32[3,64,128]{2,1,0:T(8,128)S(1)}, f32[3,64,128]{2,1,0:T(8,128)S(1)}, u32[]{:S(2)}, u32[]{:S(2)}) collective-permute-start(f32[3,64,128]{2,1,0:T(8,128)S(1)} %add.62), channel_id=1, source_target_pairs={{0,16},{4,20},{8,24},{12,28},{16,0},{20,4},{24,8},{28,12},{1,17},{... | collective-permute-start | bytes 294920 | tf_op jit(solution)/shard_map/ppermute | solution.py:305
  30.7 5.5 %collective-permute-start.8 = (f32[3,64,128]{2,1,0:T(8,128)S(1)}, f32[3,64,128]{2,1,0:T(8,128)S(1)}, u32[]{:S(2)}, u32[]{:S(2)}) collective-permute-start(f32[3,64,128]{2,1,0:T(8,128)S(1)} %add.62), channel_id=1, source_target_pairs={{0,8},{4,12},{8,0},{12,4},{16,24},{20,28},{24,16},{28,20},{1,9},{5... | collective-permute-start | bytes 294920 | tf_op jit(solution)/shard_map/ppermute | solution.py:305
  36.3 16.7 %collective-permute-start.13 = (f32[3,64,128]{2,1,0:T(8,128)S(1)}, f32[3,64,128]{2,1,0:T(8,128)S(1)}, u32[]{:S(2)}, u32[]{:S(2)}) collective-permute-start(f32[3,64,128]{2,1,0:T(8,128)S(1)} %add_add_fusion.3), channel_id=1, source_target_pairs={{0,3},{1,2},{2,1},{3,0},{4,7},{5,6},{6,5},{7,4},{8,11},{9,10},{10,... | collective-permute-start | bytes 294920 | tf_op jit(solution)/shard_map/ppermute | solution.py:305
  36.3 16.6 %collective-permute-start.12 = (f32[3,64,128]{2,1,0:T(8,128)S(1)}, f32[3,64,128]{2,1,0:T(8,128)S(1)}, u32[]{:S(2)}, u32[]{:S(2)}) collective-permute-start(f32[3,64,128]{2,1,0:T(8,128)S(1)} %add_add_fusion.3), channel_id=1, source_target_pairs={{0,2},{1,3},{2,0},{3,1},{4,6},{5,7},{6,4},{7,5},{8,10},{9,11},{10,... | collective-permute-start | bytes 294920 | tf_op jit(solution)/shard_map/ppermute | solution.py:305
  38.4 14.6 %collective-permute-start.11 = (f32[3,64,128]{2,1,0:T(8,128)S(1)}, f32[3,64,128]{2,1,0:T(8,128)S(1)}, u32[]{:S(2)}, u32[]{:S(2)}) collective-permute-start(f32[3,64,128]{2,1,0:T(8,128)S(1)} %add_add_fusion.3), channel_id=1, source_target_pairs={{0,1},{1,0},{2,3},{3,2},{4,5},{5,4},{6,7},{7,6},{8,9},{9,8},{10,11... | collective-permute-start | bytes 294920 | tf_op jit(solution)/shard_map/ppermute | solution.py:305
  44.8 8.2 %copy-start.4 = (f32[2,128,128]{2,1,0:T(8,128)S(1)}, f32[2,128,128]{2,1,0:T(8,128)}, u32[]{:S(2)}) copy-start(f32[2,128,128]{2,1,0:T(8,128)} %probe_ref.1) | copy-start | bytes 393220
  46.5 16.9 %collective-permute-start.5 = (f32[3,3,128,128]{3,2,1,0:T(8,128)S(1)}, f32[3,3,128,128]{3,2,1,0:T(8,128)S(1)}, u32[]{:S(2)}, u32[]{:S(2)}) collective-permute-start(f32[3,3,128,128]{3,2,1,0:T(8,128)S(1)} %get-tuple-element.25), channel_id=1, source_target_pairs={{0,4},{4,8},{8,12},{12,16},{16,20},{20,24},{24,28},{1,5},{5,9},{9,... | collective-permute-start | bytes 1769480 | tf_op jit(solution)/shard_map/ppermute | solution.py:300
  48.4 14.9 %collective-permute-start.6 = (f32[3,3,128,128]{3,2,1,0:T(8,128)S(1)}, f32[3,3,128,128]{3,2,1,0:T(8,128)S(1)}, u32[]{:S(2)}, u32[]{:S(2)}) collective-permute-start(f32[3,3,128,128]{3,2,1,0:T(8,128)S(1)} %get-tuple-element.26), channel_id=1, source_target_pairs={{4,0},{8,4},{12,8},{16,12},{20,16},{24,20},{28,24},{5,1},{9,5},{13... | collective-permute-start | bytes 1769480 | tf_op jit(solution)/shard_map/ppermute | solution.py:300
  53.1 11.4 %collective-permute-start.14 = (f32[2,64,128]{2,1,0:T(8,128)S(1)}, f32[2,64,128]{2,1,0:T(8,128)S(1)}, u32[]{:S(2)}, u32[]{:S(2)}) collective-permute-start(f32[2,64,128]{2,1,0:T(8,128)S(1)} %fusion.2.half_ref), channel_id=1, source_target_pairs={{0,4},{4,0},{8,12},{12,8},{16,20},{20,16},{24,28},{28,24},{1,5},{5... | collective-permute-start | bytes 196616 | tf_op jit(solution)/shard_map/ppermute | solution.py:305
  67.0 1.4 %collective-permute-start.17 = (f32[3,64,128]{2,1,0:T(8,128)S(1)}, f32[3,64,128]{2,1,0:T(8,128)S(1)}, u32[]{:S(2)}, u32[]{:S(2)}) collective-permute-start(f32[3,64,128]{2,1,0:T(8,128)S(1)} %get-tuple-element.35), channel_id=1, source_target_pairs={{0,4},{4,0},{8,12},{12,8},{16,20},{20,16},{24,28},{28,24},{1,5},{5... | collective-permute-start | bytes 294920 | tf_op jit(solution)/shard_map/ppermute | solution.py:305
  68.4 6.6 %collective-permute-start.20 = (f32[3,64,128]{2,1,0:T(8,128)S(1)}, f32[3,64,128]{2,1,0:T(8,128)S(1)}, u32[]{:S(2)}, u32[]{:S(2)}) collective-permute-start(f32[3,64,128]{2,1,0:T(8,128)S(1)} %add.71), channel_id=1, source_target_pairs={{0,24},{4,28},{8,16},{12,20},{16,8},{20,12},{24,0},{28,4},{1,25},{... | collective-permute-start | bytes 294920 | tf_op jit(solution)/shard_map/ppermute | solution.py:305
  69.6 6.7 %collective-permute-start.19 = (f32[3,64,128]{2,1,0:T(8,128)S(1)}, f32[3,64,128]{2,1,0:T(8,128)S(1)}, u32[]{:S(2)}, u32[]{:S(2)}) collective-permute-start(f32[3,64,128]{2,1,0:T(8,128)S(1)} %add.71), channel_id=1, source_target_pairs={{0,16},{4,20},{8,24},{12,28},{16,0},{20,4},{24,8},{28,12},{1,17},{... | collective-permute-start | bytes 294920 | tf_op jit(solution)/shard_map/ppermute | solution.py:305
  70.1 6.6 %collective-permute-start.18 = (f32[3,64,128]{2,1,0:T(8,128)S(1)}, f32[3,64,128]{2,1,0:T(8,128)S(1)}, u32[]{:S(2)}, u32[]{:S(2)}) collective-permute-start(f32[3,64,128]{2,1,0:T(8,128)S(1)} %add.71), channel_id=1, source_target_pairs={{0,8},{4,12},{8,0},{12,4},{16,24},{20,28},{24,16},{28,20},{1,9},{5... | collective-permute-start | bytes 294920 | tf_op jit(solution)/shard_map/ppermute | solution.py:305
  76.7 9.3 %collective-permute-start.23 = (f32[3,64,128]{2,1,0:T(8,128)S(1)}, f32[3,64,128]{2,1,0:T(8,128)S(1)}, u32[]{:S(2)}, u32[]{:S(2)}) collective-permute-start(f32[3,64,128]{2,1,0:T(8,128)S(1)} %add_add_fusion.1), channel_id=1, source_target_pairs={{0,3},{1,2},{2,1},{3,0},{4,7},{5,6},{6,5},{7,4},{8,11},{9,10},{10,... | collective-permute-start | bytes 294920 | tf_op jit(solution)/shard_map/ppermute | solution.py:305
  76.8 9.2 %collective-permute-start.22 = (f32[3,64,128]{2,1,0:T(8,128)S(1)}, f32[3,64,128]{2,1,0:T(8,128)S(1)}, u32[]{:S(2)}, u32[]{:S(2)}) collective-permute-start(f32[3,64,128]{2,1,0:T(8,128)S(1)} %add_add_fusion.1), channel_id=1, source_target_pairs={{0,2},{1,3},{2,0},{3,1},{4,6},{5,7},{6,4},{7,5},{8,10},{9,11},{10,... | collective-permute-start | bytes 294920 | tf_op jit(solution)/shard_map/ppermute | solution.py:305
  79.5 6.6 %collective-permute-start.21 = (f32[3,64,128]{2,1,0:T(8,128)S(1)}, f32[3,64,128]{2,1,0:T(8,128)S(1)}, u32[]{:S(2)}, u32[]{:S(2)}) collective-permute-start(f32[3,64,128]{2,1,0:T(8,128)S(1)} %add_add_fusion.1), channel_id=1, source_target_pairs={{0,1},{1,0},{2,3},{3,2},{4,5},{5,4},{6,7},{7,6},{8,9},{9,8},{10,11... | collective-permute-start | bytes 294920 | tf_op jit(solution)/shard_map/ppermute | solution.py:305
  80.3 19.7 %collective-permute-start.15 = (f32[3,384,128]{2,1,0:T(8,128)S(1)}, f32[3,384,128]{2,1,0:T(8,128)S(1)}, u32[]{:S(2)}, u32[]{:S(2)}) collective-permute-start(f32[3,384,128]{2,1,0:T(8,128)S(1)} %get-tuple-element.33), channel_id=1, source_target_pairs={{0,1},{1,2},{2,3},{4,5},{5,6},{6,7},{8,9},{9,10},{10,11},{12,13},{... | collective-permute-start | bytes 1769480 | tf_op jit(solution)/shard_map/ppermute | solution.py:300
  86.1 15.9 %collective-permute-start.24 = (f32[2,64,128]{2,1,0:T(8,128)S(1)}, f32[2,64,128]{2,1,0:T(8,128)S(1)}, u32[]{:S(2)}, u32[]{:S(2)}) collective-permute-start(f32[2,64,128]{2,1,0:T(8,128)S(1)} %fusion.1), channel_id=1, source_target_pairs={{0,4},{4,0},{8,12},{12,8},{16,20},{20,16},{24,28},{28,24},{1,5},{5... | collective-permute-start | bytes 196616 | tf_op jit(solution)/shard_map/ppermute | solution.py:305
  100.1 10.0 %collective-permute-start.16 = (f32[2,3,128,128]{3,2,1,0:T(8,128)S(1)}, f32[2,3,128,128]{3,2,1,0:T(8,128)S(1)}, u32[]{:S(2)}, u32[]{:S(2)}) collective-permute-start(f32[2,3,128,128]{3,2,1,0:T(8,128)S(1)} %pad_maximum_fusion), channel_id=1, source_target_pairs={{0,4},{4,8},{8,12},{12,16},{16,20},{20,24},{24,28},{1,5},{5,9},{9,... | collective-permute-start | bytes 1179656 | tf_op jit(solution)/shard_map/ppermute | solution.py:300

commit v2 on v1

v2 whole, which is shorter than its diff:
```python
import functools
import math

import jax
import jax.numpy as jnp
import numpy as np
from jax import lax
from jax.experimental import pallas as pl
from jax.experimental.pallas import tpu as pltpu
from jax.sharding import PartitionSpec as P

STEP_SIZE = 0.25
PROBE_STEP = 1.0
REGULARIZER = 1.0
COUNT_SCALE = 1.0 / 1024.0
LANES = 128
INFO = 8
VMEM_BYTES = 12 * 1024 * 1024


def dft_parts(length):
    points = np.arange(length)
    angles = (points[:, None] * points[None, :] % length) * (2.0 * math.pi / length)
    cosine = np.cos(angles) / math.sqrt(length)
    sine = np.sin(angles) / math.sqrt(length)
    forward = np.block([[cosine, -sine], [sine, cosine]]).astype(np.float32)
    parts = []
    for table in (forward, forward.T):
        high = table.astype(jnp.bfloat16)
        low = (table - high.astype(np.float32)).astype(jnp.bfloat16)
        parts += [high, low]
    return np.stack(parts)


def split(values):
    high = values.astype(jnp.bfloat16)
    low = (values - high.astype(jnp.float32)).astype(jnp.bfloat16)
    return high, low


def dot(left, right):
    return jnp.dot(left, right, preferred_element_type=jnp.float32)


def right_table(values, table_high, table_low):
    high, low = split(values)
    return dot(high, table_high) + (dot(high, table_low) + dot(low, table_high))


def left_table(table_high, table_low, values):
    high, low = split(values)
    return dot(table_high, high) + (dot(table_low, high) + dot(table_high, low))


def parity(axis):
    return lax.axis_index(axis) % 2


def slot_place(info_ref, index, slot, slots):
    row = info_ref[index, 0, slot].astype(jnp.int32)
    col = info_ref[index, 0, slots + slot].astype(jnp.int32)
    return row, col, info_ref[index, 0, 2 * slots + slot]


def lane_index(length):
    return lax.broadcasted_iota(jnp.int32, (length, LANES), 1)


def take_patch(ext_ref, channel, row, col, length):
    block = col // LANES
    shift = col % LANES
    turn = (LANES - shift) % LANES
    first = pltpu.roll(ext_ref[channel, block, pl.ds(row, length), :], turn, 1)
    second = pltpu.roll(ext_ref[channel, block + 1, pl.ds(row, length), :], turn, 1)
    return jnp.where(lane_index(length) < LANES - shift, first, second)


def add_patch(acc_ref, row, col, values, length):
    block = col // LANES
    shift = col % LANES
    turned = pltpu.roll(values, shift, 1)
    late = lane_index(length) >= shift
    window = pl.ds(row, length)
    acc_ref[block, window, :] += jnp.where(late, turned, 0.0)
    acc_ref[block + 1, window, :] += jnp.where(late, 0.0, turned)


def add_light(light_ref, power_ref, row, col, weight, length):
    row, col = row + length, col + length
    inside = (row > 0) & (row < light_ref.shape[1] - length) & (col > 0) & (col < (light_ref.shape[0] - 1) * LANES)

    @pl.when(inside & (weight > 0.0))
    def _():
        add_patch(light_ref, row, col, power_ref[...], length)


def all_light(light_ref, power_ref, info_ref, tall, wide, slots, length):
    across = 1 - 2 * parity("col")
    down = 1 - 2 * parity("row")
    places = [(0, 0), (0, across), (0, -across)]
    places += [(down, step) for step in (-1, 0, 1)] + [(-down, step) for step in (-1, 0, 1)]
    for index, (row_step, col_step) in enumerate(places):
        for s in range(slots):
            row, col, weight = slot_place(info_ref, index, s, slots)
            add_light(light_ref, power_ref, row + row_step * tall, col + col_step * wide, weight, length)


def fill_info(rows_ref, cols_ref, counts_ref, slots):
    lanes = lax.broadcasted_iota(jnp.int32, (INFO, LANES), 1)
    info = jnp.zeros((INFO, LANES), jnp.float32)
    count = counts_ref[0, 0]
    upper = lax.axis_index("row") < lax.axis_size("row") // 2
    for s in range(slots):
        inside = jnp.where(upper, s < count, s >= slots - count)
        weight = jnp.where(inside, 1.0, 0.0).astype(jnp.float32)
        info = jnp.where(lanes == s, rows_ref[0, 0, s].astype(jnp.float32), info)
        info = jnp.where(lanes == slots + s, cols_ref[0, 0, s].astype(jnp.float32), info)
        info = jnp.where(lanes == 2 * slots + s, weight, info)
    return info


def position_terms(patches, probe_real, probe_imag, measured_ref, tables_ref, weights, slots, length):
    forward_high, forward_low = tables_ref[0], tables_ref[1]
    backward_high, backward_low = tables_ref[2], tables_ref[3]
    exits = []
    for patch_real, patch_imag in patches:
        exits.append(
            jnp.concatenate(
                [
                    probe_real * patch_real - probe_imag * patch_imag,
                    probe_real * patch_imag + probe_imag * patch_real,
                ],
                axis=1,
            )
        )
    mid = right_table(jnp.concatenate(exits, axis=0), forward_high, forward_low)
    mid = jnp.concatenate(
        [
            jnp.concatenate(
                [
                    mid[s * length : (s + 1) * length, :length],
                    mid[s * length : (s + 1) * length, length:],
                ],
                axis=0,
            )
            for s in range(slots)
        ],
        axis=1,
    )
    freq = left_table(backward_high, backward_low, mid)
    scaled = []
    for s in range(slots):
        freq_real = freq[:length, s * length : (s + 1) * length]
        freq_imag = freq[length:, s * length : (s + 1) * length]
        measured = measured_ref[s].astype(jnp.float32)
        residual = freq_real * freq_real + freq_imag * freq_imag - COUNT_SCALE * measured
        scaled.append(jnp.concatenate([residual * freq_real, residual * freq_imag], axis=0))
    mid = left_table(forward_high, forward_low, jnp.concatenate(scaled, axis=1))
    mid = jnp.concatenate(
        [
            jnp.concatenate(
                [
                    mid[:length, s * length : (s + 1) * length],
                    mid[length:, s * length : (s + 1) * length],
                ],
                axis=1,
            )
            for s in range(slots)
        ],
        axis=0,
    )
    back = right_table(mid, backward_high, backward_low)
    updates = []
    for s in range(slots):
        rows = slice(s * length, (s + 1) * length)
        updates.append((back[rows, :length] * weights[s], back[rows, length:] * weights[s]))
    return updates


def finish_terms(patches, updates, probe_real, probe_imag, places, keep_ref, send_ref, dep_ref, sum_ref, length):
    slots = len(patches)
    grad_real = jnp.zeros((length, length), jnp.float32)
    grad_imag = grad_real
    light = grad_real
    for s in range(slots):
        (patch_real, patch_imag), (back_real, back_imag) = patches[s], updates[s]
        grad_real += patch_real * back_real + patch_imag * back_imag
        grad_imag += patch_real * back_imag - patch_imag * back_real
        light += places[s][2] * (patch_real * patch_real + patch_imag * patch_imag)
    sum_ref[0] = grad_real
    sum_ref[1] = grad_imag
    sum_ref[2] = light
    half = length // 2
    side = parity("row")
    keep_ref[...] = sum_ref[:, pl.ds(pl.multiple_of(side * half, half), half), :]
    send_ref[...] = sum_ref[:, pl.ds(pl.multiple_of((1 - side) * half, half), half), :]
    dep_ref[...] = jnp.zeros_like(dep_ref)
    high = dep_ref.shape[1] // 2
    for s in range(slots):
        back_real, back_imag = updates[s]
        row, col, _ = places[s]
        add_patch(dep_ref, row, col, probe_real * back_real + probe_imag * back_imag, length)
        add_patch(dep_ref, row + high, col, probe_real * back_imag - probe_imag * back_real, length)


def start_all(pairs, sems):
    copies = [pltpu.make_async_copy(source, target, sems.at[i]) for i, (source, target) in enumerate(pairs)]
    for copy in copies:
        copy.start()
    return copies


def wait_all(copies):
    for copy in copies:
        copy.wait()


def halo_kernel(
    field_ref, probe_ref, measured_ref, tables_ref, rows_ref, cols_ref, counts_ref,
    ext_ref, right_out, below_out, corner_out, probe_out, half_out, measured_out, tables_out, info_out,
    rows_at, cols_at, counts_at, sems,
):
    length = corner_out.shape[1]
    half = half_out.shape[1]
    blocks = ext_ref.shape[1] - 1
    tall = field_ref.shape[1]
    start = pl.multiple_of(parity("row") * half, half)
    pairs = [
        (rows_ref, rows_at),
        (cols_ref, cols_at),
        (counts_ref, counts_at),
        (field_ref.at[:, :, pl.ds(0, length)], right_out),
        (field_ref.at[:, pl.ds(0, length), :], below_out),
        (field_ref.at[:, pl.ds(0, length), pl.ds(0, length)], corner_out),
        (probe_ref, probe_out),
        (probe_ref.at[:, pl.ds(start, half), :], half_out),
        (measured_ref, measured_out),
        (tables_ref, tables_out),
    ]
    for block in range(blocks):
        for channel in range(2):
            pairs.append(
                (
                    field_ref.at[channel, :, pl.ds(block * LANES, LANES)],
                    ext_ref.at[channel, block, pl.ds(0, tall), :],
                )
            )
    copies = start_all(pairs, sems)
    wait_all(copies[:3])
    info_out[...] = fill_info(rows_at, cols_at, counts_at, rows_at.shape[2])
    wait_all(copies[3:])


def split_sides(inner_out, outer_out, dep_ref):
    size = dep_ref.shape[1]
    side = parity("col")
    inner_out[:size] = dep_ref[2 - 2 * side]
    outer_out[:size] = dep_ref[2 * side]


def first_kernel(
    start_ref, right_ref, below_ref, corner_ref, probe_ref, measured_ref, tables_ref, info_ref,
    ext_ref, keep_ref, send_ref, inner_out, middle_out, outer_out, dep_ref, sum_ref, info_at, sems,
):
    copies = start_all([(info_ref, info_at.at[0])], sems)
    length = probe_ref.shape[1]
    slots = measured_ref.shape[0]
    tall = right_ref.shape[1]
    blocks = below_ref.shape[2] // LANES
    for channel in range(2):
        for block in range(blocks):
            lanes = slice(block * LANES, (block + 1) * LANES)
            ext_ref[channel, block, tall:, :] = below_ref[channel, :, lanes]
        ext_ref[channel, blocks, :tall, :] = right_ref[channel]
        ext_ref[channel, blocks, tall:, :] = corner_ref[channel]
    probe_real, probe_imag = probe_ref[0], probe_ref[1]
    wait_all(copies)
    places = [slot_place(info_at, 0, s, slots) for s in range(slots)]
    patches = [
        [take_patch(ext_ref, channel, places[s][0], places[s][1], length) for channel in range(2)] for s in range(slots)
    ]
    weights = [place[2] for place in places]
    updates = position_terms(
        patches, probe_real, probe_imag, measured_ref, tables_ref, weights, slots, length
    )
    finish_terms(patches, updates, probe_real, probe_imag, places, keep_ref, send_ref, dep_ref, sum_ref, length)
    size = dep_ref.shape[1]
    middle_out[...] = dep_ref[1]
    split_sides(inner_out, outer_out, dep_ref)
    inner_out[size:] = info_ref[...]
    outer_out[size:] = info_ref[...]


def strips_kernel(
    inner_ref, middle_ref, outer_ref, from_inner, from_outer, total_out, inner_out, outer_out, infos_out
):
    size = middle_ref.shape[0]
    high = size // 2
    length = (inner_out.shape[0] - 3 * INFO) // 6
    tall = high - length
    side = parity("col")
    total_out[2 - 2 * side] = inner_ref[:size] + from_inner[:size]
    total_out[1] = middle_ref[...]
    total_out[2 * side] = outer_ref[:size] + from_outer[:size]
    side_row = parity("row")
    for block in range(3):
        for channel in range(2):
            rows = slice((2 * block + channel) * length, (2 * block + channel + 1) * length)
            start = channel * high + tall - side_row * tall
            inner_out[rows] = total_out[block, pl.ds(pl.multiple_of(start, 8), length), :]
            start = channel * high + side_row * tall
            outer_out[rows] = total_out[block, pl.ds(pl.multiple_of(start, 8), length), :]
    own, inner, outer = inner_ref[size:], from_inner[size:], from_outer[size:]
    infos_out[0], infos_out[1], infos_out[2] = own, inner, outer
    left = jnp.where(side == 0, outer, inner)
    right = jnp.where(side == 0, inner, outer)
    for index, info in enumerate((left, own, right)):
        rows = slice(6 * length + index * INFO, 6 * length + (index + 1) * INFO)
        inner_out[rows] = info
        outer_out[rows] = info


def object_kernel(
    ext_ref, probe_ref, total_ref, infos_ref, from_inner, from_outer,
    tile_out, patches_out, info_out, new_ref, light_ref, power_ref, info_at, sems,
):
    length = patches_out.shape[2]
    slots = patches_out.shape[0]
    high = ext_ref.shape[2]
    tall = high - length
    blocks = tile_out.shape[1]
    edge = 6 * length
    info_out[0:3] = infos_ref[...]
    for index in range(3):
        info_out[3 + index] = from_inner[edge + index * INFO : edge + (index + 1) * INFO]
        info_out[6 + index] = from_outer[edge + index * INFO : edge + (index + 1) * INFO]
    copies = start_all([(info_out, info_at)], sems)
    power_ref[...] = probe_ref[0] * probe_ref[0] + probe_ref[1] * probe_ref[1]
    light_ref[...] = jnp.zeros_like(light_ref)
    wait_all(copies)
    all_light(light_ref, power_ref, info_at, tall, blocks * LANES, slots, length)
    inside_row = jnp.where(lax.axis_index("row") < lax.axis_size("row") - 1, 1.0, 0.0).astype(jnp.float32)
    inside_col = jnp.where(lax.axis_index("col") < lax.axis_size("col") - 1, 1.0, 0.0).astype(jnp.float32)
    even = parity("row") == 0
    for block in range(blocks + 1):
        for piece, start, stop in ((0, 0, length), (1, length, tall), (2, tall, high)):
            light = light_ref[block + 1, start + length : stop + length, :]
            scale = STEP_SIZE / (light + REGULARIZER)
            if piece == 2:
                scale = scale * inside_row
            if block == blocks:
                scale = scale * inside_col
            for channel in range(2):
                total = total_ref[block, channel * high + start : channel * high + stop]
                rows = slice((2 * block + channel) * length, (2 * block + channel + 1) * length)
                if piece == 0:
                    total = total + jnp.where(even, from_outer[rows], from_inner[rows])
                if piece == 2:
                    total = total + jnp.where(even, from_inner[rows], from_outer[rows])
                new_ref[channel, block, start:stop, :] = ext_ref[channel, block, start:stop, :] - scale * total
    for channel in range(2):
        tile_out[channel] = new_ref[channel, :blocks, :tall, :]
    for s in range(slots):
        row, col, _ = slot_place(info_at, 0, s, slots)
        for channel in range(2):
            patches_out[s, channel] = take_patch(new_ref, channel, row, col, length)


def assemble_probe(half_ref, other_ref, side):
    first = side == 0
    return [
        jnp.concatenate(
            [
                jnp.where(first, half_ref[channel], other_ref[channel]),
                jnp.where(first, other_ref[channel], half_ref[channel]),
            ],
            axis=0,
        )
        for channel in range(2)
    ]


def second_kernel(
    patches_ref, half_ref, other_ref, measured_ref, tables_ref, info_ref,
    keep_ref, send_ref, left_out, middle_out, right_out, dep_ref, sum_ref, info_at, sems,
):
    copies = start_all([(info_ref, info_at.at[0])], sems)
    slots = measured_ref.shape[0]
    length = measured_ref.shape[1]
    probe_real, probe_imag = assemble_probe(half_ref, other_ref, parity("row"))
    patches = [[patches_ref[s, channel] for channel in range(2)] for s in range(slots)]
    wait_all(copies)
    places = [slot_place(info_at, 0, s, slots) for s in range(slots)]
    weights = [place[2] for place in places]
    updates = position_terms(
        patches, probe_real, probe_imag, measured_ref, tables_ref, weights, slots, length
    )
    finish_terms(patches, updates, probe_real, probe_imag, places, keep_ref, send_ref, dep_ref, sum_ref, length)
    left_out[...] = dep_ref[0]
    middle_out[...] = dep_ref[1]
    right_out[...] = dep_ref[2]


def light_kernel(slots, infos_ref, half_ref, other_ref, light_out, light_ref, power_ref, info_at, sems):
    copies = start_all([(infos_ref, info_at)], sems)
    length = power_ref.shape[0]
    tall = light_out.shape[1]
    blocks = light_out.shape[0]
    probe_real, probe_imag = assemble_probe(half_ref, other_ref, parity("row"))
    power_ref[...] = probe_real * probe_real + probe_imag * probe_imag
    light_ref[...] = jnp.zeros_like(light_ref)
    wait_all(copies)
    all_light(light_ref, power_ref, info_at, tall, blocks * LANES, slots, length)
    light_out[...] = STEP_SIZE / (light_ref[1 : 1 + blocks, length : length + tall, :] + REGULARIZER)


def push_kernel(left_ref, middle_ref, from_left, left_out, bottom_out):
    size = middle_ref.shape[0]
    high = size // 2
    length = bottom_out.shape[1] // 2
    tall = high - length
    left_out[...] = left_ref[...] + from_left[...]
    for block, part in enumerate((left_out, middle_ref)):
        for channel in range(2):
            bottom_out[block, channel * length : (channel + 1) * length] = part[
                channel * high + tall : (channel + 1) * high
            ]


def final_kernel(tile_ref, light_ref, left_ref, middle_ref, from_above, half_ref, other_ref, object_out, probe_out):
    tall = tile_ref.shape[2]
    length = from_above.shape[1] // 2
    high = tall + length
    for block, part in enumerate((left_ref, middle_ref)):
        lanes = slice(block * LANES, (block + 1) * LANES)
        for channel in range(2):
            for start, stop in ((0, length), (length, tall)):
                total = part[channel * high + start : channel * high + stop]
                if start == 0:
                    total = total + from_above[block, channel * length : (channel + 1) * length]
                object_out[channel, start:stop, lanes] = (
                    tile_ref[channel, block, start:stop, :] - light_ref[block, start:stop, :] * total
                )
    probe_out[0], probe_out[1] = assemble_probe(half_ref, other_ref, parity("row"))


def shift(value, axis, steps):
    count = lax.axis_size(axis)
    pairs = [(source, source + steps) for source in range(count) if 0 <= source + steps < count]
    return lax.ppermute(value, axis, pairs)


def swap(value, axis, first):
    count = lax.axis_size(axis)
    pairs = []
    for low in range(first, count - 1, 2):
        pairs += [(low, low + 1), (low + 1, low)]
    return lax.ppermute(value, axis, pairs)


def flip(value, axis, mask):
    count = lax.axis_size(axis)
    return lax.ppermute(value, axis, [(source, source ^ mask) for source in range(count)])


def sum_over(value, axis, bit):
    count = lax.axis_size(axis)
    while bit < count:
        value = value + flip(value, axis, bit)
        bit *= 2
    return value


def probe_half(half, keep, send, *gates):
    total = keep + flip(send, "row", 1)
    total = sum_over(total, "row", 2)
    total = sum_over(total, "col", 1)
    return half - PROBE_STEP * total[:2] / (total[2] + REGULARIZER), *gates


def shape_of(spec):
    return spec if isinstance(spec, jax.ShapeDtypeStruct) else jax.ShapeDtypeStruct(spec, jnp.float32)


def call(kernel, outs, scratch, args, aliases={}, space=pltpu.VMEM):
    vmem = pl.BlockSpec(memory_space=pltpu.VMEM)
    return pl.pallas_call(
        kernel,
        out_shape=[shape_of(spec) for spec in outs],
        in_specs=[pl.BlockSpec(memory_space=space)] * len(args),
        out_specs=[vmem] * len(outs),
        scratch_shapes=[pltpu.VMEM(shape, jnp.float32) if isinstance(shape, tuple) else shape for shape in scratch],
        compiler_params=pltpu.CompilerParams(vmem_limit_bytes=VMEM_BYTES),
        input_output_aliases=aliases,
    )(*args)


def local(object_field, probe_field, intensities, off_rows, off_cols, counts):
    tall, wide = object_field.shape[1:]
    length = probe_field.shape[1]
    slots = off_rows.shape[2]
    half = length // 2
    high = tall + length
    blocks = wide // LANES
    tables = jnp.asarray(dft_parts(length))
    measured = intensities.reshape(slots, length, length)
    count_rows, count_cols = lax.axis_size("row"), lax.axis_size("col")

    def info_space(tiles):
        return [pltpu.SMEM((tiles, INFO, LANES), jnp.float32), pltpu.SemaphoreType.DMA((1,))]

    extended = (2, blocks + 1, high, LANES)
    ext, right, below, corner, probe_now, own, measured, tables, info = call(
        halo_kernel,
        [
            extended,
            (2, tall, length),
            (2, length, wide),
            (2, length, length),
            (2, length, length),
            (2, half, length),
            jax.ShapeDtypeStruct(measured.shape, measured.dtype),
            jax.ShapeDtypeStruct(tables.shape, tables.dtype),
            (INFO, LANES),
        ],
        [
            pltpu.SMEM(off_rows.shape, jnp.int32),
            pltpu.SMEM(off_cols.shape, jnp.int32),
            pltpu.SMEM(counts.shape, jnp.int32),
            pltpu.SemaphoreType.DMA((10 + 2 * blocks,)),
        ],
        [object_field, probe_field, measured, tables, off_rows, off_cols, counts],
        space=pltpu.HBM,
    )
    right = shift(right, "col", -1)
    corner = lax.ppermute(
        corner,
        ("row", "col"),
        [
            ((r + 1) * count_cols + c + 1, r * count_cols + c)
            for r in range(count_rows - 1)
            for c in range(count_cols - 1)
        ],
    )
    below = shift(below, "row", -1)
    size = 2 * high
    strip = (size + INFO, LANES)
    partial = (3, half, length)
    deposits = [(blocks + 1, size, LANES), (3, length, length)] + info_space(1)
    ext, keep, send, inner, middle, outer = call(
        first_kernel,
        [extended, partial, partial, strip, (size, LANES), strip],
        deposits,
        [ext, right, below, corner, probe_now, measured, tables, info],
        aliases={0: 0},
    )
    from_inner = swap(inner, "col", 0)
    from_outer = swap(outer, "col", 1)
    new_half, from_inner, from_outer = probe_half(own, keep, send, from_inner, from_outer)
    new_other = flip(new_half, "row", 1)
    edge = (2 * (blocks + 1) * length + 3 * INFO, LANES)
    total, inner, outer, infos = call(
        strips_kernel,
        [(blocks + 1, size, LANES), edge, edge, (3, INFO, LANES)],
        [],
        [inner, middle, outer, from_inner, from_outer],
    )
    from_inner = swap(inner, "row", 0)
    from_outer = swap(outer, "row", 1)
    padded = (blocks + 3, high + 2 * length, LANES)
    tile, patches, infos = call(
        object_kernel,
        [(2, blocks, tall, LANES), (slots, 2, length, length), (9, INFO, LANES)],
        [extended, padded, (length, length)] + info_space(9),
        [ext, probe_now, total, infos, from_inner, from_outer],
    )
    keep, send, left, middle, right = call(
        second_kernel,
        [partial, partial, (size, LANES), (size, LANES), (size, LANES)],
        deposits,
        [patches, new_half, new_other, measured, tables, info],
    )
    from_left = shift(right, "col", 1)
    padded = (blocks + 2, tall + 2 * length, LANES)
    (light,) = call(
        functools.partial(light_kernel, slots),
        [(blocks, tall, LANES)],
        [padded, (length, length)] + info_space(9),
        [infos, new_half, new_other],
    )
    last_half, from_left = probe_half(new_half, keep, send, from_left)
    last_other = flip(last_half, "row", 1)
    left, bottom = call(
        push_kernel, [(size, LANES), (blocks, 2 * length, LANES)], [], [left, middle, from_left]
    )
    from_above = shift(bottom, "row", 1)
    return call(
        final_kernel,
        [(2, tall, wide), (2, length, length)],
        [],
        [tile, light, left, middle, from_above, last_half, last_other],
    )


def solution(mesh):
    placed = (
        P(None, "row", "col"),
        P(),
        P("row", "col", None, None, None),
        P("row", "col", None),
        P("row", "col", None),
        P("row", "col"),
    )
    return jax.shard_map(
        local, mesh=mesh, in_specs=placed, out_specs=(P(None, "row", "col"), P()), check_vma=False
    )
```

time: 111 us -> 91.1 us (0.82)
  the two profiles are of different devices: /device:TPU:20 before, /device:TPU:0 now
where the time goes in v2:
time: 91.1 us; the launch traced here: 89.9 us
  starting transfers between devices  37.6 us (41%)
  waiting for transfers between devices  33.7 us (37%)
  Pallas kernels  11.6 us (13%)
  local copies, waits for them, and re-layouts  5.24 us (6%)
  between operations  1.52 us (2%)
    ppermute x12, starting transfers between devices, flip(): lax.ppermute(value, axis, [(source, source ^ mask) for source in range(co...  27.4 us
    ppermute x12, waiting for transfers between devices, flip(): lax.ppermute(value, axis, [(source, source ^ mask) for source in range(co...  24.9 us
    pallas_call x8, Pallas kernels, call(): pl.pallas_call(kernel, out_shape=[shape_of(spec) for spec in outs], in_sp...  11.6 us
    ppermute x1, waiting for transfers between devices, local(): lax.ppermute(corner, ('row', 'col'), [((r + 1) * count_cols + c + 1, r *...  8.73 us
    ppermute x4, starting transfers between devices, shift(): return lax.ppermute(value, axis, pairs)  5.9 us
    unnamed x12, local copies, waits for them, and re-layouts  5.24 us
    ppermute x4, starting transfers between devices, swap(): return lax.ppermute(value, axis, pairs)  3 us
  transfers between devices with their start and end apart: 21, of which 10 were waited for; matrix products, arithmetic and copies ran while one was open for 0% of the time, Pallas kernels for 5%

profile of v2, /device:TPU:0, one launch (start us, length us, event | category | flops | bytes accessed | tf_op | source)
XLA Modules:
  0.0 89.9 jit_solution(17164179422903027678)
XLA Ops:
  1.3 0.0 copy-start
  1.3 1.0 %copy-done = f32[2,256,256]{2,1,0:T(8,128)S(1)} copy-done((f32[2,256,256]{2,1,0:T(8,128)S(1)}, f32[2,256,256]{2,1,0:T(8,128)}, u32[]{:S(2)}) %copy-start) | copy-done | bytes 524312
  2.3 0.0 copy-start.1
  2.3 1.0 %copy-done.1 = bf16[4,256,256]{2,1,0:T(8,128)(2,1)S(1)} copy-done((bf16[4,256,256]{2,1,0:T(8,128)(2,1)S(1)}, bf16[4,256,256]{2,1,0:T(8,128)(2,1)}, u32[]{:S(2)}) %copy-start.1) | copy-done | bytes 524312
  3.4 0.0 copy-start.2
  3.4 0.9 %copy-done.2 = s32[1,1,4,128,128]{4,3,2,1,0:T(8,128)S(1)} copy-done((s32[1,1,4,128,128]{4,3,2,1,0:T(8,128)S(1)}, s32[1,1,4,128,128]{4,3,2,1,0:T(8,128)}, u32[]{:S(2)}) %copy-start.2) | copy-done | bytes 262168
  4.3 0.0 copy-start.3
  4.3 0.9 %copy-done.3 = f32[2,128,128]{2,1,0:T(8,128)S(1)} copy-done((f32[2,128,128]{2,1,0:T(8,128)S(1)}, f32[2,128,128]{2,1,0:T(8,128)}, u32[]{:S(2)}) %copy-start.3) | copy-done | bytes 131096
  5.2 0.0 copy-start.4
  5.2 0.7 copy-done.4
  5.9 0.0 copy-start.5
  5.9 0.7 copy-done.5
  6.5 0.7 shard_map.86
  7.3 1.3 %collective-permute-start = (f32[2,256,128]{2,1,0:T(8,128)S(1)}, f32[2,256,128]{2,1,0:T(8,128)S(1)}, u32[]{:S(2)}, u32[]{:S(2)}) collective-permute-start(f32[2,256,128]{2,1,0:T(8,128)S(1)} %get-tuple-element.32), channel_id=1, source_target_pairs={{1,0},{2,1},{3,2},{5,4},{6,5},{7,6},{9,8},{10,9},{11,10},{13,12},{... | collective-permute-start | bytes 786440 | tf_op jit(solution)/shard_map/ppermute | solution.py:450
  8.6 1.3 %collective-permute-start.1 = (f32[2,128,256]{2,1,0:T(8,128)S(1)}, f32[2,128,256]{2,1,0:T(8,128)S(1)}, u32[]{:S(2)}, u32[]{:S(2)}) collective-permute-start(f32[2,128,256]{2,1,0:T(8,128)S(1)} %get-tuple-element.33), channel_id=1, source_target_pairs={{4,0},{8,4},{12,8},{16,12},{20,16},{24,20},{28,24},{5,1},{9,5},{13... | collective-permute-start | bytes 786440 | tf_op jit(solution)/shard_map/ppermute | solution.py:450
  9.9 1.3 %collective-permute-start.2 = (f32[2,128,128]{2,1,0:T(8,128)S(1)}, f32[2,128,128]{2,1,0:T(8,128)S(1)}, u32[]{:S(2)}, u32[]{:S(2)}) collective-permute-start(f32[2,128,128]{2,1,0:T(8,128)S(1)} %get-tuple-element.34), channel_id=1, source_target_pairs={{5,0},{6,1},{7,2},{9,4},{10,5},{11,6},{13,8},{14,9},{15,10},{17,12... | collective-permute-start | bytes 393224 | tf_op jit(solution)/shard_map/ppermute | solution.py:536
  11.2 8.7 %collective-permute-done.2.corner_ref = f32[2,128,128]{2,1,0:T(8,128)S(1)} collective-permute-done((f32[2,128,128]{2,1,0:T(8,128)S(1)}, f32[2,128,128]{2,1,0:T(8,128)S(1)}, u32[]{:S(2)}, u32[]{:S(2)}) %collective-permute-start.2) | collective-permute-done | bytes 131104 | tf_op jit(solution)/shard_map/ppermute | solution.py:536
  19.9 0.0 collective-permute-done.right_ref
  19.9 0.0 collective-permute-done.1.below_ref
  19.9 2.7 %shard_map.87 = (f32[2,3,384,128]{3,2,1,0:T(8,128)S(1)}, f32[3,64,128]{2,1,0:T(8,128)S(1)}, f32[3,64,128]{2,1,0:T(8,128)S(1)}, f32[776,128]{1,0:T(8,128)S(1)}, f...) custom-call(f32[2,3,384,128]{3,2,1,0:T(8,128)S(1)} %get-tuple-element.31.start_ref, ...), custom_call_target="tpu_custom_call", output_to_operand_aliasing={{0}: (0, {})} | custom-call | tf_op jit(solution)/shard_map/pallas_call | solution.py:487
  22.6 2.4 %collective-permute-start.7 = (f32[3,64,128]{2,1,0:T(8,128)S(1)}, f32[3,64,128]{2,1,0:T(8,128)S(1)}, u32[]{:S(2)}, u32[]{:S(2)}) collective-permute-start(f32[3,64,128]{2,1,0:T(8,128)S(1)} %get-tuple-element.51), channel_id=1, source_target_pairs={{0,4},{4,0},{8,12},{12,8},{16,20},{20,16},{24,28},{28,24},{1,5},{5... | collective-permute-start | bytes 294920 | tf_op jit(solution)/shard_map/ppermute | solution.py:463
  25.0 1.6 %collective-permute-start.3 = (f32[776,128]{1,0:T(8,128)S(1)}, f32[776,128]{1,0:T(8,128)S(1)}, u32[]{:S(2)}, u32[]{:S(2)}) collective-permute-start(f32[776,128]{1,0:T(8,128)S(1)} %get-tuple-element.40.inner_ref), channel_id=1, source_target_pairs={{0,1},{1,0},{2,3},{3,2},{4,5},{5,4},{6,7},{7,6},{8,9},{9,8},{10,11... | collective-permute-start | bytes 1191944 | tf_op jit(solution)/shard_map/ppermute | solution.py:458
  26.6 0.7 collective-permute-start.4
  27.3 0.0 collective-permute-done.7
  27.3 1.6 %collective-permute-start.8 = (f32[3,64,128]{2,1,0:T(8,128)S(1)}, f32[3,64,128]{2,1,0:T(8,128)S(1)}, u32[]{:S(2)}, u32[]{:S(2)}) collective-permute-start(f32[3,64,128]{2,1,0:T(8,128)S(1)} %add.38), channel_id=1, source_target_pairs={{0,8},{4,12},{8,0},{12,4},{16,24},{20,28},{24,16},{28,20},{1,9},{5... | collective-permute-start | bytes 294920 | tf_op jit(solution)/shard_map/ppermute | solution.py:463
  28.9 3.1 %collective-permute-done.8 = f32[3,64,128]{2,1,0:T(8,128)S(1)} collective-permute-done((f32[3,64,128]{2,1,0:T(8,128)S(1)}, f32[3,64,128]{2,1,0:T(8,128)S(1)}, u32[]{:S(2)}, u32[]{:S(2)}) %collective-permute-start.8) | collective-permute-done | bytes 98336 | tf_op jit(solution)/shard_map/ppermute | solution.py:463
  32.0 1.6 %collective-permute-start.9 = (f32[3,64,128]{2,1,0:T(8,128)S(1)}, f32[3,64,128]{2,1,0:T(8,128)S(1)}, u32[]{:S(2)}, u32[]{:S(2)}) collective-permute-start(f32[3,64,128]{2,1,0:T(8,128)S(1)} %add.39), channel_id=1, source_target_pairs={{0,16},{4,20},{8,24},{12,28},{16,0},{20,4},{24,8},{28,12},{1,17},{... | collective-permute-start | bytes 294920 | tf_op jit(solution)/shard_map/ppermute | solution.py:463
  33.6 3.1 %collective-permute-done.9 = f32[3,64,128]{2,1,0:T(8,128)S(1)} collective-permute-done((f32[3,64,128]{2,1,0:T(8,128)S(1)}, f32[3,64,128]{2,1,0:T(8,128)S(1)}, u32[]{:S(2)}, u32[]{:S(2)}) %collective-permute-start.9) | collective-permute-done | bytes 98336 | tf_op jit(solution)/shard_map/ppermute | solution.py:463
  36.7 2.9 %collective-permute-start.10 = (f32[3,64,128]{2,1,0:T(8,128)S(1)}, f32[3,64,128]{2,1,0:T(8,128)S(1)}, u32[]{:S(2)}, u32[]{:S(2)}) collective-permute-start(f32[3,64,128]{2,1,0:T(8,128)S(1)} %add.40), channel_id=1, source_target_pairs={{0,1},{1,0},{2,3},{3,2},{4,5},{5,4},{6,7},{7,6},{8,9},{9,8},{10,11... | collective-permute-start | bytes 294920 | tf_op jit(solution)/shard_map/ppermute | solution.py:463
  39.6 2.6 %collective-permute-done.10 = f32[3,64,128]{2,1,0:T(8,128)S(1)} collective-permute-done((f32[3,64,128]{2,1,0:T(8,128)S(1)}, f32[3,64,128]{2,1,0:T(8,128)S(1)}, u32[]{:S(2)}, u32[]{:S(2)}) %collective-permute-start.10) | collective-permute-done | bytes 98336 | tf_op jit(solution)/shard_map/ppermute | solution.py:463
  42.2 2.4 %collective-permute-start.11 = (f32[3,64,128]{2,1,0:T(8,128)S(1)}, f32[3,64,128]{2,1,0:T(8,128)S(1)}, u32[]{:S(2)}, u32[]{:S(2)}) collective-permute-start(f32[3,64,128]{2,1,0:T(8,128)S(1)} %add.41), channel_id=1, source_target_pairs={{0,2},{1,3},{2,0},{3,1},{4,6},{5,7},{6,4},{7,5},{8,10},{9,11},{10,... | collective-permute-start | bytes 294920 | tf_op jit(solution)/shard_map/ppermute | solution.py:463
  44.6 0.0 collective-permute-done.3.from_inner
  44.6 0.0 collective-permute-done.4.from_outer
  44.6 0.2 shard_map.88
  44.8 0.1 collective-permute-start.5
  44.9 0.7 collective-permute-start.6
  45.6 2.2 %collective-permute-done.11 = f32[3,64,128]{2,1,0:T(8,128)S(1)} collective-permute-done((f32[3,64,128]{2,1,0:T(8,128)S(1)}, f32[3,64,128]{2,1,0:T(8,128)S(1)}, u32[]{:S(2)}, u32[]{:S(2)}) %collective-permute-start.11) | collective-permute-done | bytes 98336 | tf_op jit(solution)/shard_map/ppermute | solution.py:463
  47.8 0.7 collective-permute-start.12
  48.5 0.0 collective-permute-done.5.from_inner
  48.5 0.0 collective-permute-done.6.from_outer
  48.5 2.6 %shard_map.89 = (f32[2,2,256,128]{3,2,1,0:T(8,128)S(1)}, f32[4,2,128,128]{3,2,1,0:T(8,128)S(1)}, f32[9,8,128]{2,1,0:T(8,128)S(1)}) custom-call(f32[2,3,384,128]{3,2,1,0:T(8,128)S(1)} %get-tuple-element.39.ext_ref, f32[2,128,128]{2,1,0:T(8,128)S(1)} %get-tuple-element.35.probe_ref, f32[3,768,128]{2,1,0:T(8,128)S(1)} %get-tuple-element.43.total_ref, ...), custom_call_target="tpu_custom_call" | custom-call | tf_op jit(solution)/shard_map/pallas_call | solution.py:487
  51.2 0.0 collective-permute-done.12.other_ref
  51.2 2.6 %shard_map.91 = (f32[3,64,128]{2,1,0:T(8,128)S(1)}, f32[3,64,128]{2,1,0:T(8,128)S(1)}, f32[768,128]{1,0:T(8,128)S(1)}, f32[768,128]{1,0:T(8,128)S(1)}, f32[768,128]{1,0:T(8,128)S(1)}) custom-call(f32[4,2,128,128]{3,2,1,0:T(8,128)S(1)} %get-tuple-element.52.patches_ref, f32[2,64,128]{2,1,0:T(8,128)S(1)} %fusion.1.half_ref, ...), custom_call_target="tpu_custom_call" | custom-call | tf_op jit(solution)/shard_map/pallas_call | solution.py:487
  53.8 10.7 %collective-permute-start.15 = (f32[3,64,128]{2,1,0:T(8,128)S(1)}, f32[3,64,128]{2,1,0:T(8,128)S(1)}, u32[]{:S(2)}, u32[]{:S(2)}) collective-permute-start(f32[3,64,128]{2,1,0:T(8,128)S(1)} %get-tuple-element.59), channel_id=1, source_target_pairs={{0,4},{4,0},{8,12},{12,8},{16,20},{20,16},{24,28},{28,24},{1,5},{5... | collective-permute-start | bytes 294920 | tf_op jit(solution)/shard_map/ppermute | solution.py:463
  64.5 0.9 %collective-permute-done.15 = f32[3,64,128]{2,1,0:T(8,128)S(1)} collective-permute-done((f32[3,64,128]{2,1,0:T(8,128)S(1)}, f32[3,64,128]{2,1,0:T(8,128)S(1)}, u32[]{:S(2)}, u32[]{:S(2)}) %collective-permute-start.15) | collective-permute-done | bytes 98336 | tf_op jit(solution)/shard_map/ppermute | solution.py:463
  65.5 1.0 %collective-permute-start.16 = (f32[3,64,128]{2,1,0:T(8,128)S(1)}, f32[3,64,128]{2,1,0:T(8,128)S(1)}, u32[]{:S(2)}, u32[]{:S(2)}) collective-permute-start(f32[3,64,128]{2,1,0:T(8,128)S(1)} %add.44), channel_id=1, source_target_pairs={{0,8},{4,12},{8,0},{12,4},{16,24},{20,28},{24,16},{28,20},{1,9},{5... | collective-permute-start | bytes 294920 | tf_op jit(solution)/shard_map/ppermute | solution.py:463
  66.4 2.0 %collective-permute-start.13 = (f32[768,128]{1,0:T(8,128)S(1)}, f32[768,128]{1,0:T(8,128)S(1)}, u32[]{:S(2)}, u32[]{:S(2)}) collective-permute-start(f32[768,128]{1,0:T(8,128)S(1)} %get-tuple-element.55), channel_id=1, source_target_pairs={{0,1},{1,2},{2,3},{4,5},{5,6},{6,7},{8,9},{9,10},{10,11},{12,13},{... | collective-permute-start | bytes 1179656 | tf_op jit(solution)/shard_map/ppermute | solution.py:450
  68.5 2.2 %collective-permute-done.16 = f32[3,64,128]{2,1,0:T(8,128)S(1)} collective-permute-done((f32[3,64,128]{2,1,0:T(8,128)S(1)}, f32[3,64,128]{2,1,0:T(8,128)S(1)}, u32[]{:S(2)}, u32[]{:S(2)}) %collective-permute-start.16) | collective-permute-done | bytes 98336 | tf_op jit(solution)/shard_map/ppermute | solution.py:463
  70.6 2.1 %collective-permute-start.17 = (f32[3,64,128]{2,1,0:T(8,128)S(1)}, f32[3,64,128]{2,1,0:T(8,128)S(1)}, u32[]{:S(2)}, u32[]{:S(2)}) collective-permute-start(f32[3,64,128]{2,1,0:T(8,128)S(1)} %add.45), channel_id=1, source_target_pairs={{0,16},{4,20},{8,24},{12,28},{16,0},{20,4},{24,8},{28,12},{1,17},{... | collective-permute-start | bytes 294920 | tf_op jit(solution)/shard_map/ppermute | solution.py:463
  72.8 2.6 %collective-permute-done.17 = f32[3,64,128]{2,1,0:T(8,128)S(1)} collective-permute-done((f32[3,64,128]{2,1,0:T(8,128)S(1)}, f32[3,64,128]{2,1,0:T(8,128)S(1)}, u32[]{:S(2)}, u32[]{:S(2)}) %collective-permute-start.17) | collective-permute-done | bytes 98336 | tf_op jit(solution)/shard_map/ppermute | solution.py:463
  75.4 0.3 collective-permute-start.18
  75.7 4.4 %collective-permute-done.18 = f32[3,64,128]{2,1,0:T(8,128)S(1)} collective-permute-done((f32[3,64,128]{2,1,0:T(8,128)S(1)}, f32[3,64,128]{2,1,0:T(8,128)S(1)}, u32[]{:S(2)}, u32[]{:S(2)}) %collective-permute-start.18) | collective-permute-done | bytes 98336 | tf_op jit(solution)/shard_map/ppermute | solution.py:463
  80.1 1.7 %collective-permute-start.19 = (f32[3,64,128]{2,1,0:T(8,128)S(1)}, f32[3,64,128]{2,1,0:T(8,128)S(1)}, u32[]{:S(2)}, u32[]{:S(2)}) collective-permute-start(f32[3,64,128]{2,1,0:T(8,128)S(1)} %add.47), channel_id=1, source_target_pairs={{0,2},{1,3},{2,0},{3,1},{4,6},{5,7},{6,4},{7,5},{8,10},{9,11},{10,... | collective-permute-start | bytes 294920 | tf_op jit(solution)/shard_map/ppermute | solution.py:463
  81.8 0.0 collective-permute-done.13.from_left
  81.8 0.1 shard_map.92
  81.9 1.3 %collective-permute-start.14 = (f32[2,256,128]{2,1,0:T(8,128)S(1)}, f32[2,256,128]{2,1,0:T(8,128)S(1)}, u32[]{:S(2)}, u32[]{:S(2)}) collective-permute-start(f32[2,256,128]{2,1,0:T(8,128)S(1)} %get-tuple-element.57), channel_id=1, source_target_pairs={{0,4},{4,8},{8,12},{12,16},{16,20},{20,24},{24,28},{1,5},{5,9},{9,... | collective-permute-start | bytes 786440 | tf_op jit(solution)/shard_map/ppermute | solution.py:450
  83.2 3.8 %collective-permute-done.19 = f32[3,64,128]{2,1,0:T(8,128)S(1)} collective-permute-done((f32[3,64,128]{2,1,0:T(8,128)S(1)}, f32[3,64,128]{2,1,0:T(8,128)S(1)}, u32[]{:S(2)}, u32[]{:S(2)}) %collective-permute-start.19) | collective-permute-done | bytes 98336 | tf_op jit(solution)/shard_map/ppermute | solution.py:463
  87.1 0.1 collective-permute-start.20
  87.1 1.8 %shard_map.90.light_ref = f32[2,256,128]{2,1,0:T(8,128)S(1)} custom-call(f32[9,8,128]{2,1,0:T(8,128)S(1)} %get-tuple-element.48.infos_ref, f32[2,64,128]{2,1,0:T(8,128)S(1)} %fusion.1.half_ref, f32[2,64,128]{2,1,0:T(8,128)S(1)} %collective-permute-done.12.other_ref), custom_call_target="tpu_custom_call" | custom-call | tf_op jit(solution)/shard_map/pallas_call | solution.py:487
  88.9 0.0 collective-permute-done.20.other_ref
  88.9 0.0 collective-permute-done.14.from_above
  89.0 0.9 %shard_map.93 = (f32[2,256,256]{2,1,0:T(8,128)}, f32[2,128,128]{2,1,0:T(8,128)}) custom-call(f32[2,2,256,128]{3,2,1,0:T(8,128)S(1)} %get-tuple-element.47.tile_ref, f32[2,256,128]{2,1,0:T(8,128)S(1)} %shard_map.90.light_ref, f32[768,128]{1,0:T(8,128)S(1)} %get-tuple-element.56.left_ref, f32[768,128]{1,0:T(8,128)S(1)} %get-tuple-element.54.middle_ref, ...), custom_call_target="tpu_custom_call" | custom-call | tf_op jit(solution)/shard_map/pallas_call | solution.py:487
  (14 shorter events, 0.2 us)
Async XLA Ops:
  1.3 1.0 %copy-start = (f32[2,256,256]{2,1,0:T(8,128)S(1)}, f32[2,256,256]{2,1,0:T(8,128)}, u32[]{:S(2)}) copy-start(f32[2,256,256]{2,1,0:T(8,128)} %field_ref.1) | copy-start | bytes 1572868
  2.3 1.0 %copy-start.1 = (bf16[4,256,256]{2,1,0:T(8,128)(2,1)S(1)}, bf16[4,256,256]{2,1,0:T(8,128)(2,1)}, u32[]{:S(2)}) copy-start(bf16[4,256,256]{2,1,0:T(8,128)(2,1)} %constant.4.clone.tables_ref) | copy-start | bytes 1572868
  3.4 0.9 %copy-start.2 = (s32[1,1,4,128,128]{4,3,2,1,0:T(8,128)S(1)}, s32[1,1,4,128,128]{4,3,2,1,0:T(8,128)}, u32[]{:S(2)}) copy-start(s32[1,1,4,128,128]{4,3,2,1,0:T(8,128)} %param.9) | copy-start | bytes 786436
  4.3 0.9 %copy-start.3 = (f32[2,128,128]{2,1,0:T(8,128)S(1)}, f32[2,128,128]{2,1,0:T(8,128)}, u32[]{:S(2)}) copy-start(f32[2,128,128]{2,1,0:T(8,128)} %probe_ref.1) | copy-start | bytes 393220
  5.2 0.7 copy-start.4
  5.9 0.7 copy-start.5
  7.3 12.6 %collective-permute-start = (f32[2,256,128]{2,1,0:T(8,128)S(1)}, f32[2,256,128]{2,1,0:T(8,128)S(1)}, u32[]{:S(2)}, u32[]{:S(2)}) collective-permute-start(f32[2,256,128]{2,1,0:T(8,128)S(1)} %get-tuple-element.32), channel_id=1, source_target_pairs={{1,0},{2,1},{3,2},{5,4},{6,5},{7,6},{9,8},{10,9},{11,10},{13,12},{... | collective-permute-start | bytes 786440 | tf_op jit(solution)/shard_map/ppermute | solution.py:450
  8.6 11.3 %collective-permute-start.1 = (f32[2,128,256]{2,1,0:T(8,128)S(1)}, f32[2,128,256]{2,1,0:T(8,128)S(1)}, u32[]{:S(2)}, u32[]{:S(2)}) collective-permute-start(f32[2,128,256]{2,1,0:T(8,128)S(1)} %get-tuple-element.33), channel_id=1, source_target_pairs={{4,0},{8,4},{12,8},{16,12},{20,16},{24,20},{28,24},{5,1},{9,5},{13... | collective-permute-start | bytes 786440 | tf_op jit(solution)/shard_map/ppermute | solution.py:450
  9.9 10.0 %collective-permute-start.2 = (f32[2,128,128]{2,1,0:T(8,128)S(1)}, f32[2,128,128]{2,1,0:T(8,128)S(1)}, u32[]{:S(2)}, u32[]{:S(2)}) collective-permute-start(f32[2,128,128]{2,1,0:T(8,128)S(1)} %get-tuple-element.34), channel_id=1, source_target_pairs={{5,0},{6,1},{7,2},{9,4},{10,5},{11,6},{13,8},{14,9},{15,10},{17,12... | collective-permute-start | bytes 393224 | tf_op jit(solution)/shard_map/ppermute | solution.py:536
  22.6 4.6 %collective-permute-start.7 = (f32[3,64,128]{2,1,0:T(8,128)S(1)}, f32[3,64,128]{2,1,0:T(8,128)S(1)}, u32[]{:S(2)}, u32[]{:S(2)}) collective-permute-start(f32[3,64,128]{2,1,0:T(8,128)S(1)} %get-tuple-element.51), channel_id=1, source_target_pairs={{0,4},{4,0},{8,12},{12,8},{16,20},{20,16},{24,28},{28,24},{1,5},{5... | collective-permute-start | bytes 294920 | tf_op jit(solution)/shard_map/ppermute | solution.py:463
  25.0 19.6 %collective-permute-start.3 = (f32[776,128]{1,0:T(8,128)S(1)}, f32[776,128]{1,0:T(8,128)S(1)}, u32[]{:S(2)}, u32[]{:S(2)}) collective-permute-start(f32[776,128]{1,0:T(8,128)S(1)} %get-tuple-element.40.inner_ref), channel_id=1, source_target_pairs={{0,1},{1,0},{2,3},{3,2},{4,5},{5,4},{6,7},{7,6},{8,9},{9,8},{10,11... | collective-permute-start | bytes 1191944 | tf_op jit(solution)/shard_map/ppermute | solution.py:458
  26.6 18.0 %collective-permute-start.4 = (f32[776,128]{1,0:T(8,128)S(1)}, f32[776,128]{1,0:T(8,128)S(1)}, u32[]{:S(2)}, u32[]{:S(2)}) collective-permute-start(f32[776,128]{1,0:T(8,128)S(1)} %get-tuple-element.42.outer_ref), channel_id=1, source_target_pairs={{1,2},{2,1},{5,6},{6,5},{9,10},{10,9},{13,14},{14,13},{17,18},{18,... | collective-permute-start | bytes 1191944 | tf_op jit(solution)/shard_map/ppermute | solution.py:458
  27.3 4.7 %collective-permute-start.8 = (f32[3,64,128]{2,1,0:T(8,128)S(1)}, f32[3,64,128]{2,1,0:T(8,128)S(1)}, u32[]{:S(2)}, u32[]{:S(2)}) collective-permute-start(f32[3,64,128]{2,1,0:T(8,128)S(1)} %add.38), channel_id=1, source_target_pairs={{0,8},{4,12},{8,0},{12,4},{16,24},{20,28},{24,16},{28,20},{1,9},{5... | collective-permute-start | bytes 294920 | tf_op jit(solution)/shard_map/ppermute | solution.py:463
  32.0 4.7 %collective-permute-start.9 = (f32[3,64,128]{2,1,0:T(8,128)S(1)}, f32[3,64,128]{2,1,0:T(8,128)S(1)}, u32[]{:S(2)}, u32[]{:S(2)}) collective-permute-start(f32[3,64,128]{2,1,0:T(8,128)S(1)} %add.39), channel_id=1, source_target_pairs={{0,16},{4,20},{8,24},{12,28},{16,0},{20,4},{24,8},{28,12},{1,17},{... | collective-permute-start | bytes 294920 | tf_op jit(solution)/shard_map/ppermute | solution.py:463
  36.7 5.5 %collective-permute-start.10 = (f32[3,64,128]{2,1,0:T(8,128)S(1)}, f32[3,64,128]{2,1,0:T(8,128)S(1)}, u32[]{:S(2)}, u32[]{:S(2)}) collective-permute-start(f32[3,64,128]{2,1,0:T(8,128)S(1)} %add.40), channel_id=1, source_target_pairs={{0,1},{1,0},{2,3},{3,2},{4,5},{5,4},{6,7},{7,6},{8,9},{9,8},{10,11... | collective-permute-start | bytes 294920 | tf_op jit(solution)/shard_map/ppermute | solution.py:463
  42.2 5.6 %collective-permute-start.11 = (f32[3,64,128]{2,1,0:T(8,128)S(1)}, f32[3,64,128]{2,1,0:T(8,128)S(1)}, u32[]{:S(2)}, u32[]{:S(2)}) collective-permute-start(f32[3,64,128]{2,1,0:T(8,128)S(1)} %add.41), channel_id=1, source_target_pairs={{0,2},{1,3},{2,0},{3,1},{4,6},{5,7},{6,4},{7,5},{8,10},{9,11},{10,... | collective-permute-start | bytes 294920 | tf_op jit(solution)/shard_map/ppermute | solution.py:463
  44.8 3.7 %collective-permute-start.5 = (f32[792,128]{1,0:T(8,128)S(1)}, f32[792,128]{1,0:T(8,128)S(1)}, u32[]{:S(2)}, u32[]{:S(2)}) collective-permute-start(f32[792,128]{1,0:T(8,128)S(1)} %get-tuple-element.45), channel_id=1, source_target_pairs={{0,4},{4,0},{8,12},{12,8},{16,20},{20,16},{24,28},{28,24},{1,5},{5... | collective-permute-start | bytes 1216520 | tf_op jit(solution)/shard_map/ppermute | solution.py:458
  44.9 3.7 %collective-permute-start.6 = (f32[792,128]{1,0:T(8,128)S(1)}, f32[792,128]{1,0:T(8,128)S(1)}, u32[]{:S(2)}, u32[]{:S(2)}) collective-permute-start(f32[792,128]{1,0:T(8,128)S(1)} %get-tuple-element.46), channel_id=1, source_target_pairs={{4,8},{8,4},{12,16},{16,12},{20,24},{24,20},{5,9},{9,5},{13,17},{1... | collective-permute-start | bytes 1216520 | tf_op jit(solution)/shard_map/ppermute | solution.py:458
  47.8 3.4 %collective-permute-start.12 = (f32[2,64,128]{2,1,0:T(8,128)S(1)}, f32[2,64,128]{2,1,0:T(8,128)S(1)}, u32[]{:S(2)}, u32[]{:S(2)}) collective-permute-start(f32[2,64,128]{2,1,0:T(8,128)S(1)} %fusion.1.half_ref), channel_id=1, source_target_pairs={{0,4},{4,0},{8,12},{12,8},{16,20},{20,16},{24,28},{28,24},{1,5},{5... | collective-permute-start | bytes 196616 | tf_op jit(solution)/shard_map/ppermute | solution.py:463
  53.8 11.7 %collective-permute-start.15 = (f32[3,64,128]{2,1,0:T(8,128)S(1)}, f32[3,64,128]{2,1,0:T(8,128)S(1)}, u32[]{:S(2)}, u32[]{:S(2)}) collective-permute-start(f32[3,64,128]{2,1,0:T(8,128)S(1)} %get-tuple-element.59), channel_id=1, source_target_pairs={{0,4},{4,0},{8,12},{12,8},{16,20},{20,16},{24,28},{28,24},{1,5},{5... | collective-permute-start | bytes 294920 | tf_op jit(solution)/shard_map/ppermute | solution.py:463
  65.5 5.1 %collective-permute-start.16 = (f32[3,64,128]{2,1,0:T(8,128)S(1)}, f32[3,64,128]{2,1,0:T(8,128)S(1)}, u32[]{:S(2)}, u32[]{:S(2)}) collective-permute-start(f32[3,64,128]{2,1,0:T(8,128)S(1)} %add.44), channel_id=1, source_target_pairs={{0,8},{4,12},{8,0},{12,4},{16,24},{20,28},{24,16},{28,20},{1,9},{5... | collective-permute-start | bytes 294920 | tf_op jit(solution)/shard_map/ppermute | solution.py:463
  66.4 15.3 %collective-permute-start.13 = (f32[768,128]{1,0:T(8,128)S(1)}, f32[768,128]{1,0:T(8,128)S(1)}, u32[]{:S(2)}, u32[]{:S(2)}) collective-permute-start(f32[768,128]{1,0:T(8,128)S(1)} %get-tuple-element.55), channel_id=1, source_target_pairs={{0,1},{1,2},{2,3},{4,5},{5,6},{6,7},{8,9},{9,10},{10,11},{12,13},{... | collective-permute-start | bytes 1179656 | tf_op jit(solution)/shard_map/ppermute | solution.py:450
  70.6 4.7 %collective-permute-start.17 = (f32[3,64,128]{2,1,0:T(8,128)S(1)}, f32[3,64,128]{2,1,0:T(8,128)S(1)}, u32[]{:S(2)}, u32[]{:S(2)}) collective-permute-start(f32[3,64,128]{2,1,0:T(8,128)S(1)} %add.45), channel_id=1, source_target_pairs={{0,16},{4,20},{8,24},{12,28},{16,0},{20,4},{24,8},{28,12},{1,17},{... | collective-permute-start | bytes 294920 | tf_op jit(solution)/shard_map/ppermute | solution.py:463
  75.4 4.7 %collective-permute-start.18 = (f32[3,64,128]{2,1,0:T(8,128)S(1)}, f32[3,64,128]{2,1,0:T(8,128)S(1)}, u32[]{:S(2)}, u32[]{:S(2)}) collective-permute-start(f32[3,64,128]{2,1,0:T(8,128)S(1)} %add.46), channel_id=1, source_target_pairs={{0,1},{1,0},{2,3},{3,2},{4,5},{5,4},{6,7},{7,6},{8,9},{9,8},{10,11... | collective-permute-start | bytes 294920 | tf_op jit(solution)/shard_map/ppermute | solution.py:463
  80.1 6.9 %collective-permute-start.19 = (f32[3,64,128]{2,1,0:T(8,128)S(1)}, f32[3,64,128]{2,1,0:T(8,128)S(1)}, u32[]{:S(2)}, u32[]{:S(2)}) collective-permute-start(f32[3,64,128]{2,1,0:T(8,128)S(1)} %add.47), channel_id=1, source_target_pairs={{0,2},{1,3},{2,0},{3,1},{4,6},{5,7},{6,4},{7,5},{8,10},{9,11},{10,... | collective-permute-start | bytes 294920 | tf_op jit(solution)/shard_map/ppermute | solution.py:463
  81.9 7.1 %collective-permute-start.14 = (f32[2,256,128]{2,1,0:T(8,128)S(1)}, f32[2,256,128]{2,1,0:T(8,128)S(1)}, u32[]{:S(2)}, u32[]{:S(2)}) collective-permute-start(f32[2,256,128]{2,1,0:T(8,128)S(1)} %get-tuple-element.57), channel_id=1, source_target_pairs={{0,4},{4,8},{8,12},{12,16},{16,20},{20,24},{24,28},{1,5},{5,9},{9,... | collective-permute-start | bytes 786440 | tf_op jit(solution)/shard_map/ppermute | solution.py:450
  87.1 1.9 %collective-permute-start.20 = (f32[2,64,128]{2,1,0:T(8,128)S(1)}, f32[2,64,128]{2,1,0:T(8,128)S(1)}, u32[]{:S(2)}, u32[]{:S(2)}) collective-permute-start(f32[2,64,128]{2,1,0:T(8,128)S(1)} %fusion.half_ref), channel_id=1, source_target_pairs={{0,4},{4,0},{8,12},{12,8},{16,20},{20,16},{24,28},{28,24},{1,5},{5... | collective-permute-start | bytes 196616 | tf_op jit(solution)/shard_map/ppermute | solution.py:463

commit v3 on v2

--- a/solution.py
+++ b/solution.py
@@ -215,27 +215,14 @@
         copy.wait()
 
 
-def halo_kernel(
-    field_ref, probe_ref, measured_ref, tables_ref, rows_ref, cols_ref, counts_ref,
-    ext_ref, right_out, below_out, corner_out, probe_out, half_out, measured_out, tables_out, info_out,
-    rows_at, cols_at, counts_at, sems,
-):
+def halo_kernel(field_ref, ext_ref, right_out, below_out, corner_out, sems):
     length = corner_out.shape[1]
-    half = half_out.shape[1]
     blocks = ext_ref.shape[1] - 1
     tall = field_ref.shape[1]
-    start = pl.multiple_of(parity("row") * half, half)
     pairs = [
-        (rows_ref, rows_at),
-        (cols_ref, cols_at),
-        (counts_ref, counts_at),
         (field_ref.at[:, :, pl.ds(0, length)], right_out),
         (field_ref.at[:, pl.ds(0, length), :], below_out),
         (field_ref.at[:, pl.ds(0, length), pl.ds(0, length)], corner_out),
-        (probe_ref, probe_out),
-        (probe_ref.at[:, pl.ds(start, half), :], half_out),
-        (measured_ref, measured_out),
-        (tables_ref, tables_out),
     ]
     for block in range(blocks):
         for channel in range(2):
@@ -245,6 +232,24 @@
                     ext_ref.at[channel, block, pl.ds(0, tall), :],
                 )
             )
+    wait_all(start_all(pairs, sems))
+
+
+def load_kernel(
+    probe_ref, measured_ref, tables_ref, rows_ref, cols_ref, counts_ref,
+    probe_out, half_out, measured_out, tables_out, info_out, rows_at, cols_at, counts_at, sems,
+):
+    half = half_out.shape[1]
+    start = pl.multiple_of(parity("row") * half, half)
+    pairs = [
+        (rows_ref, rows_at),
+        (cols_ref, cols_at),
+        (counts_ref, counts_at),
+        (probe_ref, probe_out),
+        (probe_ref.at[:, pl.ds(start, half), :], half_out),
+        (measured_ref, measured_out),
+        (tables_ref, tables_out),
+    ]
     copies = start_all(pairs, sems)
     wait_all(copies[:3])
     info_out[...] = fill_info(rows_at, cols_at, counts_at, rows_at.shape[2])
@@ -463,19 +468,20 @@
     return lax.ppermute(value, axis, [(source, source ^ mask) for source in range(count)])
 
 
-def sum_over(value, axis, bit):
-    count = lax.axis_size(axis)
-    while bit < count:
-        value = value + flip(value, axis, bit)
+def tie(*values):
+    return lax.optimization_barrier(values)
+
+
+def butterfly(total, axis, first, stop=None):
+    bit = first
+    while bit < (stop or lax.axis_size(axis)):
+        total = total + flip(total, axis, bit)
         bit *= 2
-    return value
-
-
-def probe_half(half, keep, send, *gates):
-    total = keep + flip(send, "row", 1)
-    total = sum_over(total, "row", 2)
-    total = sum_over(total, "col", 1)
-    return half - PROBE_STEP * total[:2] / (total[2] + REGULARIZER), *gates
+    return total
+
+
+def stepped(half, total):
+    return half - PROBE_STEP * total[:2] / (total[2] + REGULARIZER)
 
 
 def shape_of(spec):
@@ -510,13 +516,16 @@
         return [pltpu.SMEM((tiles, INFO, LANES), jnp.float32), pltpu.SemaphoreType.DMA((1,))]
 
     extended = (2, blocks + 1, high, LANES)
-    ext, right, below, corner, probe_now, own, measured, tables, info = call(
+    ext, right, below, corner = call(
         halo_kernel,
+        [extended, (2, tall, length), (2, length, wide), (2, length, length)],
+        [pltpu.SemaphoreType.DMA((3 + 2 * blocks,))],
+        [object_field],
+        space=pl.ANY,
+    )
+    probe_now, own, measured, tables, info = call(
+        load_kernel,
         [
-            extended,
-            (2, tall, length),
-            (2, length, wide),
-            (2, length, length),
             (2, length, length),
             (2, half, length),
             jax.ShapeDtypeStruct(measured.shape, measured.dtype),
@@ -527,10 +536,10 @@
             pltpu.SMEM(off_rows.shape, jnp.int32),
             pltpu.SMEM(off_cols.shape, jnp.int32),
             pltpu.SMEM(counts.shape, jnp.int32),
-            pltpu.SemaphoreType.DMA((10 + 2 * blocks,)),
+            pltpu.SemaphoreType.DMA((7,)),
         ],
-        [object_field, probe_field, measured, tables, off_rows, off_cols, counts],
-        space=pltpu.HBM,
+        [probe_field, measured, tables, off_rows, off_cols, counts],
+        space=pl.ANY,
     )
     right = shift(right, "col", -1)
     corner = lax.ppermute(
@@ -554,11 +563,15 @@
         [ext, right, below, corner, probe_now, measured, tables, info],
         aliases={0: 0},
     )
+    last_row, last_col = count_rows // 2, count_cols // 2
+    edge = (2 * (blocks + 1) * length + 3 * INFO, LANES)
+    padded = (blocks + 3, high + 2 * length, LANES)
+
     from_inner = swap(inner, "col", 0)
     from_outer = swap(outer, "col", 1)
-    new_half, from_inner, from_outer = probe_half(own, keep, send, from_inner, from_outer)
-    new_other = flip(new_half, "row", 1)
-    edge = (2 * (blocks + 1) * length + 3 * INFO, LANES)
+    part = keep + flip(send, "row", 1)
+    part = butterfly(part, "row", 2, last_row)
+    part = butterfly(part, "row", last_row)
     total, inner, outer, infos = call(
         strips_kernel,
         [(blocks + 1, size, LANES), edge, edge, (3, INFO, LANES)],
@@ -567,20 +580,23 @@
     )
     from_inner = swap(inner, "row", 0)
     from_outer = swap(outer, "row", 1)
-    padded = (blocks + 3, high + 2 * length, LANES)
+    part = butterfly(part, "col", 1, last_col)
+    part = butterfly(part, "col", last_col)
+    new_half = stepped(own, part)
     tile, patches, infos = call(
         object_kernel,
         [(2, blocks, tall, LANES), (slots, 2, length, length), (9, INFO, LANES)],
         [extended, padded, (length, length)] + info_space(9),
         [ext, probe_now, total, infos, from_inner, from_outer],
     )
+    new_other = flip(new_half, "row", 1)
+
     keep, send, left, middle, right = call(
         second_kernel,
         [partial, partial, (size, LANES), (size, LANES), (size, LANES)],
         deposits,
         [patches, new_half, new_other, measured, tables, info],
     )
-    from_left = shift(right, "col", 1)
     padded = (blocks + 2, tall + 2 * length, LANES)
     (light,) = call(
         functools.partial(light_kernel, slots),
@@ -588,12 +604,18 @@
         [padded, (length, length)] + info_space(9),
         [infos, new_half, new_other],
     )
-    last_half, from_left = probe_half(new_half, keep, send, from_left)
-    last_other = flip(last_half, "row", 1)
+    from_left = shift(right, "col", 1)
+    part = keep + flip(send, "row", 1)
+    part = butterfly(part, "row", 2, last_row)
+    part = butterfly(part, "row", last_row)
     left, bottom = call(
         push_kernel, [(size, LANES), (blocks, 2 * length, LANES)], [], [left, middle, from_left]
     )
     from_above = shift(bottom, "row", 1)
+    part = butterfly(part, "col", 1, last_col)
+    part = butterfly(part, "col", last_col)
+    last_half = stepped(new_half, part)
+    last_other = flip(last_half, "row", 1)
     return call(
         final_kernel,
         [(2, tall, wide), (2, length, length)],

time: 91.1 us -> 86.5 us (0.950)
  waiting for transfers between devices: 33.7 us -> 26.9 us
  starting transfers between devices: 37.6 us -> 40.1 us
    ppermute x1, waiting for transfers between devices: 8.73 us -> 3.22 us  [local(): lax.ppermute(corner, ('row', 'col'), [((r + 1) * count_cols + c + 1, r *...]
    ppermute x12, starting transfers between devices: 27.4 us -> 29.1 us  [flip(): lax.ppermute(value, axis, [(source, source ^ mask) for source in range(co...]
    ppermute x12, waiting for transfers between devices: 24.9 us -> 23.6 us  [flip(): lax.ppermute(value, axis, [(source, source ^ mask) for source in range(co...]
    pallas_call x8 -> x9, Pallas kernels: 11.6 us -> 11.8 us  [call(): pl.pallas_call(kernel, out_shape=[shape_of(spec) for spec in outs], in_sp...]
  transfers between devices with their start and end apart: 21 -> 21, of which waited for: 10 -> 10; matrix products, arithmetic and copies ran while one was open for 0% -> 0% of each run, Pallas kernels for 5% -> 6%
where the time goes in v3:
time: 86.5 us; the launch traced here: 85.8 us
  starting transfers between devices  40.1 us (46%)
  waiting for transfers between devices  26.9 us (31%)
  Pallas kernels  11.8 us (14%)
  local copies, waits for them, and re-layouts  5.23 us (6%)
  between operations  1.56 us (2%)
    ppermute x12, starting transfers between devices, flip(): lax.ppermute(value, axis, [(source, source ^ mask) for source in range(co...  29.1 us
    ppermute x12, waiting for transfers between devices, flip(): lax.ppermute(value, axis, [(source, source ^ mask) for source in range(co...  23.6 us
    pallas_call x9, Pallas kernels, call(): pl.pallas_call(kernel, out_shape=[shape_of(spec) for spec in outs], in_sp...  11.8 us
    ppermute x4, starting transfers between devices, shift(): return lax.ppermute(value, axis, pairs)  6.7 us
    unnamed x12, local copies, waits for them, and re-layouts  5.23 us
    ppermute x1, waiting for transfers between devices, local(): lax.ppermute(corner, ('row', 'col'), [((r + 1) * count_cols + c + 1, r *...  3.22 us
    ppermute x4, starting transfers between devices, swap(): return lax.ppermute(value, axis, pairs)  3 us
  transfers between devices with their start and end apart: 21, of which 10 were waited for; matrix products, arithmetic and copies ran while one was open for 0% of the time, Pallas kernels for 6%

profile of v3, /device:TPU:0, one launch (start us, length us, event | category | flops | bytes accessed | tf_op | source)
XLA Modules:
  0.0 85.8 jit_solution(9725142711932184699)
XLA Ops:
  0.6 0.0 copy-start
  0.6 1.0 %copy-done = f32[2,256,256]{2,1,0:T(8,128)S(1)} copy-done((f32[2,256,256]{2,1,0:T(8,128)S(1)}, f32[2,256,256]{2,1,0:T(8,128)}, u32[]{:S(2)}) %copy-start) | copy-done | bytes 524312
  1.7 0.2 shard_map.86
  1.8 1.3 %collective-permute-start = (f32[2,256,128]{2,1,0:T(8,128)S(1)}, f32[2,256,128]{2,1,0:T(8,128)S(1)}, u32[]{:S(2)}, u32[]{:S(2)}) collective-permute-start(f32[2,256,128]{2,1,0:T(8,128)S(1)} %get-tuple-element.32), channel_id=1, source_target_pairs={{1,0},{2,1},{3,2},{5,4},{6,5},{7,6},{9,8},{10,9},{11,10},{13,12},{... | collective-permute-start | bytes 786440 | tf_op jit(solution)/shard_map/ppermute | solution.py:455
  3.1 1.3 %collective-permute-start.1 = (f32[2,128,256]{2,1,0:T(8,128)S(1)}, f32[2,128,256]{2,1,0:T(8,128)S(1)}, u32[]{:S(2)}, u32[]{:S(2)}) collective-permute-start(f32[2,128,256]{2,1,0:T(8,128)S(1)} %get-tuple-element.33), channel_id=1, source_target_pairs={{4,0},{8,4},{12,8},{16,12},{20,16},{24,20},{28,24},{5,1},{9,5},{13... | collective-permute-start | bytes 786440 | tf_op jit(solution)/shard_map/ppermute | solution.py:455
  4.4 1.3 %collective-permute-start.2 = (f32[2,128,128]{2,1,0:T(8,128)S(1)}, f32[2,128,128]{2,1,0:T(8,128)S(1)}, u32[]{:S(2)}, u32[]{:S(2)}) collective-permute-start(f32[2,128,128]{2,1,0:T(8,128)S(1)} %get-tuple-element.34), channel_id=1, source_target_pairs={{5,0},{6,1},{7,2},{9,4},{10,5},{11,6},{13,8},{14,9},{15,10},{17,12... | collective-permute-start | bytes 393224 | tf_op jit(solution)/shard_map/ppermute | solution.py:545
  6.4 0.0 copy-start.1
  6.4 1.0 %copy-done.1 = bf16[4,256,256]{2,1,0:T(8,128)(2,1)S(1)} copy-done((bf16[4,256,256]{2,1,0:T(8,128)(2,1)S(1)}, bf16[4,256,256]{2,1,0:T(8,128)(2,1)}, u32[]{:S(2)}) %copy-start.1) | copy-done | bytes 524312
  7.4 0.0 copy-start.2
  7.4 0.9 %copy-done.2 = s32[1,1,4,128,128]{4,3,2,1,0:T(8,128)S(1)} copy-done((s32[1,1,4,128,128]{4,3,2,1,0:T(8,128)S(1)}, s32[1,1,4,128,128]{4,3,2,1,0:T(8,128)}, u32[]{:S(2)}) %copy-start.2) | copy-done | bytes 262168
  8.4 0.0 copy-start.3
  8.4 0.9 %copy-done.3 = f32[2,128,128]{2,1,0:T(8,128)S(1)} copy-done((f32[2,128,128]{2,1,0:T(8,128)S(1)}, f32[2,128,128]{2,1,0:T(8,128)}, u32[]{:S(2)}) %copy-start.3) | copy-done | bytes 131096
  9.3 0.0 copy-start.4
  9.3 0.7 copy-done.4
  9.9 0.0 copy-start.5
  9.9 0.7 copy-done.5
  10.6 0.6 shard_map.87
  11.2 3.2 %collective-permute-done.2.corner_ref = f32[2,128,128]{2,1,0:T(8,128)S(1)} collective-permute-done((f32[2,128,128]{2,1,0:T(8,128)S(1)}, f32[2,128,128]{2,1,0:T(8,128)S(1)}, u32[]{:S(2)}, u32[]{:S(2)}) %collective-permute-start.2) | collective-permute-done | bytes 131104 | tf_op jit(solution)/shard_map/ppermute | solution.py:545
  14.5 0.0 collective-permute-done.right_ref
  14.5 0.0 collective-permute-done.1.below_ref
  14.5 2.7 %shard_map.88 = (f32[2,3,384,128]{3,2,1,0:T(8,128)S(1)}, f32[3,64,128]{2,1,0:T(8,128)S(1)}, f32[3,64,128]{2,1,0:T(8,128)S(1)}, f32[776,128]{1,0:T(8,128)S(1)}, f...) custom-call(f32[2,3,384,128]{3,2,1,0:T(8,128)S(1)} %get-tuple-element.31.start_ref, ...), custom_call_target="tpu_custom_call", output_to_operand_aliasing={{0}: (0, {})} | custom-call | tf_op jit(solution)/shard_map/pallas_call | solution.py:493
  17.2 2.4 %collective-permute-start.7 = (f32[3,64,128]{2,1,0:T(8,128)S(1)}, f32[3,64,128]{2,1,0:T(8,128)S(1)}, u32[]{:S(2)}, u32[]{:S(2)}) collective-permute-start(f32[3,64,128]{2,1,0:T(8,128)S(1)} %get-tuple-element.51), channel_id=1, source_target_pairs={{0,4},{4,0},{8,12},{12,8},{16,20},{20,16},{24,28},{28,24},{1,5},{5... | collective-permute-start | bytes 294920 | tf_op jit(solution)/shard_map/ppermute | solution.py:468
  19.6 1.6 %collective-permute-start.3 = (f32[776,128]{1,0:T(8,128)S(1)}, f32[776,128]{1,0:T(8,128)S(1)}, u32[]{:S(2)}, u32[]{:S(2)}) collective-permute-start(f32[776,128]{1,0:T(8,128)S(1)} %get-tuple-element.40.inner_ref), channel_id=1, source_target_pairs={{0,1},{1,0},{2,3},{3,2},{4,5},{5,4},{6,7},{7,6},{8,9},{9,8},{10,11... | collective-permute-start | bytes 1191944 | tf_op jit(solution)/shard_map/ppermute | solution.py:463
  21.2 0.7 collective-permute-start.4
  21.8 0.0 collective-permute-done.7
  21.9 1.6 %collective-permute-start.8 = (f32[3,64,128]{2,1,0:T(8,128)S(1)}, f32[3,64,128]{2,1,0:T(8,128)S(1)}, u32[]{:S(2)}, u32[]{:S(2)}) collective-permute-start(f32[3,64,128]{2,1,0:T(8,128)S(1)} %add.38), channel_id=1, source_target_pairs={{0,8},{4,12},{8,0},{12,4},{16,24},{20,28},{24,16},{28,20},{1,9},{5... | collective-permute-start | bytes 294920 | tf_op jit(solution)/shard_map/ppermute | solution.py:468
  23.4 3.1 %collective-permute-done.8 = f32[3,64,128]{2,1,0:T(8,128)S(1)} collective-permute-done((f32[3,64,128]{2,1,0:T(8,128)S(1)}, f32[3,64,128]{2,1,0:T(8,128)S(1)}, u32[]{:S(2)}, u32[]{:S(2)}) %collective-permute-start.8) | collective-permute-done | bytes 98336 | tf_op jit(solution)/shard_map/ppermute | solution.py:468
  26.6 1.6 %collective-permute-start.9 = (f32[3,64,128]{2,1,0:T(8,128)S(1)}, f32[3,64,128]{2,1,0:T(8,128)S(1)}, u32[]{:S(2)}, u32[]{:S(2)}) collective-permute-start(f32[3,64,128]{2,1,0:T(8,128)S(1)} %add.39), channel_id=1, source_target_pairs={{0,16},{4,20},{8,24},{12,28},{16,0},{20,4},{24,8},{28,12},{1,17},{... | collective-permute-start | bytes 294920 | tf_op jit(solution)/shard_map/ppermute | solution.py:468
  28.2 3.1 %collective-permute-done.9 = f32[3,64,128]{2,1,0:T(8,128)S(1)} collective-permute-done((f32[3,64,128]{2,1,0:T(8,128)S(1)}, f32[3,64,128]{2,1,0:T(8,128)S(1)}, u32[]{:S(2)}, u32[]{:S(2)}) %collective-permute-start.9) | collective-permute-done | bytes 98336 | tf_op jit(solution)/shard_map/ppermute | solution.py:468
  31.3 3.7 %collective-permute-start.10 = (f32[3,64,128]{2,1,0:T(8,128)S(1)}, f32[3,64,128]{2,1,0:T(8,128)S(1)}, u32[]{:S(2)}, u32[]{:S(2)}) collective-permute-start(f32[3,64,128]{2,1,0:T(8,128)S(1)} %add.40), channel_id=1, source_target_pairs={{0,1},{1,0},{2,3},{3,2},{4,5},{5,4},{6,7},{7,6},{8,9},{9,8},{10,11... | collective-permute-start | bytes 294920 | tf_op jit(solution)/shard_map/ppermute | solution.py:468
  35.0 2.6 %collective-permute-done.10 = f32[3,64,128]{2,1,0:T(8,128)S(1)} collective-permute-done((f32[3,64,128]{2,1,0:T(8,128)S(1)}, f32[3,64,128]{2,1,0:T(8,128)S(1)}, u32[]{:S(2)}, u32[]{:S(2)}) %collective-permute-start.10) | collective-permute-done | bytes 98336 | tf_op jit(solution)/shard_map/ppermute | solution.py:468
  37.6 1.8 %collective-permute-start.11 = (f32[3,64,128]{2,1,0:T(8,128)S(1)}, f32[3,64,128]{2,1,0:T(8,128)S(1)}, u32[]{:S(2)}, u32[]{:S(2)}) collective-permute-start(f32[3,64,128]{2,1,0:T(8,128)S(1)} %add.41), channel_id=1, source_target_pairs={{0,2},{1,3},{2,0},{3,1},{4,6},{5,7},{6,4},{7,5},{8,10},{9,11},{10,... | collective-permute-start | bytes 294920 | tf_op jit(solution)/shard_map/ppermute | solution.py:468
  39.4 0.0 collective-permute-done.3.from_inner
  39.4 0.0 collective-permute-done.4.from_outer
  39.4 0.2 shard_map.89
  39.6 0.1 collective-permute-start.5
  39.6 0.7 collective-permute-start.6
  40.3 2.8 %collective-permute-done.11 = f32[3,64,128]{2,1,0:T(8,128)S(1)} collective-permute-done((f32[3,64,128]{2,1,0:T(8,128)S(1)}, f32[3,64,128]{2,1,0:T(8,128)S(1)}, u32[]{:S(2)}, u32[]{:S(2)}) %collective-permute-start.11) | collective-permute-done | bytes 98336 | tf_op jit(solution)/shard_map/ppermute | solution.py:468
  43.2 0.1 collective-permute-start.12
  43.3 0.0 collective-permute-done.5.from_inner
  43.3 0.0 collective-permute-done.6.from_outer
  43.3 2.7 %shard_map.90 = (f32[2,2,256,128]{3,2,1,0:T(8,128)S(1)}, f32[4,2,128,128]{3,2,1,0:T(8,128)S(1)}, f32[9,8,128]{2,1,0:T(8,128)S(1)}) custom-call(f32[2,3,384,128]{3,2,1,0:T(8,128)S(1)} %get-tuple-element.39.ext_ref, f32[2,128,128]{2,1,0:T(8,128)S(1)} %get-tuple-element.35.probe_ref, f32[3,768,128]{2,1,0:T(8,128)S(1)} %get-tuple-element.43.total_ref, ...), custom_call_target="tpu_custom_call" | custom-call | tf_op jit(solution)/shard_map/pallas_call | solution.py:493
  46.0 0.0 collective-permute-done.12.other_ref
  46.1 2.6 %shard_map.92 = (f32[3,64,128]{2,1,0:T(8,128)S(1)}, f32[3,64,128]{2,1,0:T(8,128)S(1)}, f32[768,128]{1,0:T(8,128)S(1)}, f32[768,128]{1,0:T(8,128)S(1)}, f32[768,128]{1,0:T(8,128)S(1)}) custom-call(f32[4,2,128,128]{3,2,1,0:T(8,128)S(1)} %get-tuple-element.52.patches_ref, f32[2,64,128]{2,1,0:T(8,128)S(1)} %fusion.1.half_ref, ...), custom_call_target="tpu_custom_call" | custom-call | tf_op jit(solution)/shard_map/pallas_call | solution.py:493
  48.7 9.8 %collective-permute-start.15 = (f32[3,64,128]{2,1,0:T(8,128)S(1)}, f32[3,64,128]{2,1,0:T(8,128)S(1)}, u32[]{:S(2)}, u32[]{:S(2)}) collective-permute-start(f32[3,64,128]{2,1,0:T(8,128)S(1)} %get-tuple-element.59), channel_id=1, source_target_pairs={{0,4},{4,0},{8,12},{12,8},{16,20},{20,16},{24,28},{28,24},{1,5},{5... | collective-permute-start | bytes 294920 | tf_op jit(solution)/shard_map/ppermute | solution.py:468
  58.4 0.9 %collective-permute-done.15 = f32[3,64,128]{2,1,0:T(8,128)S(1)} collective-permute-done((f32[3,64,128]{2,1,0:T(8,128)S(1)}, f32[3,64,128]{2,1,0:T(8,128)S(1)}, u32[]{:S(2)}, u32[]{:S(2)}) %collective-permute-start.15) | collective-permute-done | bytes 98336 | tf_op jit(solution)/shard_map/ppermute | solution.py:468
  59.4 2.3 %collective-permute-start.16 = (f32[3,64,128]{2,1,0:T(8,128)S(1)}, f32[3,64,128]{2,1,0:T(8,128)S(1)}, u32[]{:S(2)}, u32[]{:S(2)}) collective-permute-start(f32[3,64,128]{2,1,0:T(8,128)S(1)} %add.44), channel_id=1, source_target_pairs={{0,8},{4,12},{8,0},{12,4},{16,24},{20,28},{24,16},{28,20},{1,9},{5... | collective-permute-start | bytes 294920 | tf_op jit(solution)/shard_map/ppermute | solution.py:468
  61.7 2.8 %collective-permute-start.13 = (f32[768,128]{1,0:T(8,128)S(1)}, f32[768,128]{1,0:T(8,128)S(1)}, u32[]{:S(2)}, u32[]{:S(2)}) collective-permute-start(f32[768,128]{1,0:T(8,128)S(1)} %get-tuple-element.55), channel_id=1, source_target_pairs={{0,1},{1,2},{2,3},{4,5},{5,6},{6,7},{8,9},{9,10},{10,11},{12,13},{... | collective-permute-start | bytes 1179656 | tf_op jit(solution)/shard_map/ppermute | solution.py:455
  64.5 0.5 collective-permute-done.16
  65.0 2.2 %collective-permute-start.17 = (f32[3,64,128]{2,1,0:T(8,128)S(1)}, f32[3,64,128]{2,1,0:T(8,128)S(1)}, u32[]{:S(2)}, u32[]{:S(2)}) collective-permute-start(f32[3,64,128]{2,1,0:T(8,128)S(1)} %add.45), channel_id=1, source_target_pairs={{0,16},{4,20},{8,24},{12,28},{16,0},{20,4},{24,8},{28,12},{1,17},{... | collective-permute-start | bytes 294920 | tf_op jit(solution)/shard_map/ppermute | solution.py:468
  67.2 2.6 %collective-permute-done.17 = f32[3,64,128]{2,1,0:T(8,128)S(1)} collective-permute-done((f32[3,64,128]{2,1,0:T(8,128)S(1)}, f32[3,64,128]{2,1,0:T(8,128)S(1)}, u32[]{:S(2)}, u32[]{:S(2)}) %collective-permute-start.17) | collective-permute-done | bytes 98336 | tf_op jit(solution)/shard_map/ppermute | solution.py:468
  69.8 0.8 collective-permute-start.18
  70.7 4.5 %collective-permute-done.18 = f32[3,64,128]{2,1,0:T(8,128)S(1)} collective-permute-done((f32[3,64,128]{2,1,0:T(8,128)S(1)}, f32[3,64,128]{2,1,0:T(8,128)S(1)}, u32[]{:S(2)}, u32[]{:S(2)}) %collective-permute-start.18) | collective-permute-done | bytes 98336 | tf_op jit(solution)/shard_map/ppermute | solution.py:468
  75.2 2.9 %collective-permute-start.19 = (f32[3,64,128]{2,1,0:T(8,128)S(1)}, f32[3,64,128]{2,1,0:T(8,128)S(1)}, u32[]{:S(2)}, u32[]{:S(2)}) collective-permute-start(f32[3,64,128]{2,1,0:T(8,128)S(1)} %add.47), channel_id=1, source_target_pairs={{0,2},{1,3},{2,0},{3,1},{4,6},{5,7},{6,4},{7,5},{8,10},{9,11},{10,... | collective-permute-start | bytes 294920 | tf_op jit(solution)/shard_map/ppermute | solution.py:468
  78.1 0.0 collective-permute-done.13.from_left
  78.1 0.1 shard_map.93
  78.1 1.3 %collective-permute-start.14 = (f32[2,256,128]{2,1,0:T(8,128)S(1)}, f32[2,256,128]{2,1,0:T(8,128)S(1)}, u32[]{:S(2)}, u32[]{:S(2)}) collective-permute-start(f32[2,256,128]{2,1,0:T(8,128)S(1)} %get-tuple-element.57), channel_id=1, source_target_pairs={{0,4},{4,8},{8,12},{12,16},{16,20},{20,24},{24,28},{1,5},{5,9},{9,... | collective-permute-start | bytes 786440 | tf_op jit(solution)/shard_map/ppermute | solution.py:455
  79.5 3.4 %collective-permute-done.19 = f32[3,64,128]{2,1,0:T(8,128)S(1)} collective-permute-done((f32[3,64,128]{2,1,0:T(8,128)S(1)}, f32[3,64,128]{2,1,0:T(8,128)S(1)}, u32[]{:S(2)}, u32[]{:S(2)}) %collective-permute-start.19) | collective-permute-done | bytes 98336 | tf_op jit(solution)/shard_map/ppermute | solution.py:468
  82.9 0.1 collective-permute-start.20
  83.0 1.8 %shard_map.91.light_ref = f32[2,256,128]{2,1,0:T(8,128)S(1)} custom-call(f32[9,8,128]{2,1,0:T(8,128)S(1)} %get-tuple-element.48.infos_ref, f32[2,64,128]{2,1,0:T(8,128)S(1)} %fusion.1.half_ref, f32[2,64,128]{2,1,0:T(8,128)S(1)} %collective-permute-done.12.other_ref), custom_call_target="tpu_custom_call" | custom-call | tf_op jit(solution)/shard_map/pallas_call | solution.py:493
  84.8 0.0 collective-permute-done.20.other_ref
  84.8 0.0 collective-permute-done.14.from_above
  84.8 0.9 %shard_map.94 = (f32[2,256,256]{2,1,0:T(8,128)}, f32[2,128,128]{2,1,0:T(8,128)}) custom-call(f32[2,2,256,128]{3,2,1,0:T(8,128)S(1)} %get-tuple-element.47.tile_ref, f32[2,256,128]{2,1,0:T(8,128)S(1)} %shard_map.91.light_ref, f32[768,128]{1,0:T(8,128)S(1)} %get-tuple-element.56.left_ref, f32[768,128]{1,0:T(8,128)S(1)} %get-tuple-element.54.middle_ref, ...), custom_call_target="tpu_custom_call" | custom-call | tf_op jit(solution)/shard_map/pallas_call | solution.py:493
  (14 shorter events, 0.2 us)
Async XLA Ops:
  0.6 1.0 %copy-start = (f32[2,256,256]{2,1,0:T(8,128)S(1)}, f32[2,256,256]{2,1,0:T(8,128)}, u32[]{:S(2)}) copy-start(f32[2,256,256]{2,1,0:T(8,128)} %field_ref.1) | copy-start | bytes 1572868
  1.8 12.6 %collective-permute-start = (f32[2,256,128]{2,1,0:T(8,128)S(1)}, f32[2,256,128]{2,1,0:T(8,128)S(1)}, u32[]{:S(2)}, u32[]{:S(2)}) collective-permute-start(f32[2,256,128]{2,1,0:T(8,128)S(1)} %get-tuple-element.32), channel_id=1, source_target_pairs={{1,0},{2,1},{3,2},{5,4},{6,5},{7,6},{9,8},{10,9},{11,10},{13,12},{... | collective-permute-start | bytes 786440 | tf_op jit(solution)/shard_map/ppermute | solution.py:455
  3.1 11.3 %collective-permute-start.1 = (f32[2,128,256]{2,1,0:T(8,128)S(1)}, f32[2,128,256]{2,1,0:T(8,128)S(1)}, u32[]{:S(2)}, u32[]{:S(2)}) collective-permute-start(f32[2,128,256]{2,1,0:T(8,128)S(1)} %get-tuple-element.33), channel_id=1, source_target_pairs={{4,0},{8,4},{12,8},{16,12},{20,16},{24,20},{28,24},{5,1},{9,5},{13... | collective-permute-start | bytes 786440 | tf_op jit(solution)/shard_map/ppermute | solution.py:455
  4.4 10.0 %collective-permute-start.2 = (f32[2,128,128]{2,1,0:T(8,128)S(1)}, f32[2,128,128]{2,1,0:T(8,128)S(1)}, u32[]{:S(2)}, u32[]{:S(2)}) collective-permute-start(f32[2,128,128]{2,1,0:T(8,128)S(1)} %get-tuple-element.34), channel_id=1, source_target_pairs={{5,0},{6,1},{7,2},{9,4},{10,5},{11,6},{13,8},{14,9},{15,10},{17,12... | collective-permute-start | bytes 393224 | tf_op jit(solution)/shard_map/ppermute | solution.py:545
  6.4 1.0 %copy-start.1 = (bf16[4,256,256]{2,1,0:T(8,128)(2,1)S(1)}, bf16[4,256,256]{2,1,0:T(8,128)(2,1)}, u32[]{:S(2)}) copy-start(bf16[4,256,256]{2,1,0:T(8,128)(2,1)} %constant.4.clone.tables_ref) | copy-start | bytes 1572868
  7.4 0.9 %copy-start.2 = (s32[1,1,4,128,128]{4,3,2,1,0:T(8,128)S(1)}, s32[1,1,4,128,128]{4,3,2,1,0:T(8,128)}, u32[]{:S(2)}) copy-start(s32[1,1,4,128,128]{4,3,2,1,0:T(8,128)} %param.9) | copy-start | bytes 786436
  8.4 0.9 %copy-start.3 = (f32[2,128,128]{2,1,0:T(8,128)S(1)}, f32[2,128,128]{2,1,0:T(8,128)}, u32[]{:S(2)}) copy-start(f32[2,128,128]{2,1,0:T(8,128)} %probe_ref.1) | copy-start | bytes 393220
  9.3 0.7 copy-start.4
  9.9 0.7 copy-start.5
  17.2 4.6 %collective-permute-start.7 = (f32[3,64,128]{2,1,0:T(8,128)S(1)}, f32[3,64,128]{2,1,0:T(8,128)S(1)}, u32[]{:S(2)}, u32[]{:S(2)}) collective-permute-start(f32[3,64,128]{2,1,0:T(8,128)S(1)} %get-tuple-element.51), channel_id=1, source_target_pairs={{0,4},{4,0},{8,12},{12,8},{16,20},{20,16},{24,28},{28,24},{1,5},{5... | collective-permute-start | bytes 294920 | tf_op jit(solution)/shard_map/ppermute | solution.py:468
  19.6 19.8 %collective-permute-start.3 = (f32[776,128]{1,0:T(8,128)S(1)}, f32[776,128]{1,0:T(8,128)S(1)}, u32[]{:S(2)}, u32[]{:S(2)}) collective-permute-start(f32[776,128]{1,0:T(8,128)S(1)} %get-tuple-element.40.inner_ref), channel_id=1, source_target_pairs={{0,1},{1,0},{2,3},{3,2},{4,5},{5,4},{6,7},{7,6},{8,9},{9,8},{10,11... | collective-permute-start | bytes 1191944 | tf_op jit(solution)/shard_map/ppermute | solution.py:463
  21.2 18.2 %collective-permute-start.4 = (f32[776,128]{1,0:T(8,128)S(1)}, f32[776,128]{1,0:T(8,128)S(1)}, u32[]{:S(2)}, u32[]{:S(2)}) collective-permute-start(f32[776,128]{1,0:T(8,128)S(1)} %get-tuple-element.42.outer_ref), channel_id=1, source_target_pairs={{1,2},{2,1},{5,6},{6,5},{9,10},{10,9},{13,14},{14,13},{17,18},{18,... | collective-permute-start | bytes 1191944 | tf_op jit(solution)/shard_map/ppermute | solution.py:463
  21.9 4.7 %collective-permute-start.8 = (f32[3,64,128]{2,1,0:T(8,128)S(1)}, f32[3,64,128]{2,1,0:T(8,128)S(1)}, u32[]{:S(2)}, u32[]{:S(2)}) collective-permute-start(f32[3,64,128]{2,1,0:T(8,128)S(1)} %add.38), channel_id=1, source_target_pairs={{0,8},{4,12},{8,0},{12,4},{16,24},{20,28},{24,16},{28,20},{1,9},{5... | collective-permute-start | bytes 294920 | tf_op jit(solution)/shard_map/ppermute | solution.py:468
  26.6 4.7 %collective-permute-start.9 = (f32[3,64,128]{2,1,0:T(8,128)S(1)}, f32[3,64,128]{2,1,0:T(8,128)S(1)}, u32[]{:S(2)}, u32[]{:S(2)}) collective-permute-start(f32[3,64,128]{2,1,0:T(8,128)S(1)} %add.39), channel_id=1, source_target_pairs={{0,16},{4,20},{8,24},{12,28},{16,0},{20,4},{24,8},{28,12},{1,17},{... | collective-permute-start | bytes 294920 | tf_op jit(solution)/shard_map/ppermute | solution.py:468
  31.3 6.3 %collective-permute-start.10 = (f32[3,64,128]{2,1,0:T(8,128)S(1)}, f32[3,64,128]{2,1,0:T(8,128)S(1)}, u32[]{:S(2)}, u32[]{:S(2)}) collective-permute-start(f32[3,64,128]{2,1,0:T(8,128)S(1)} %add.40), channel_id=1, source_target_pairs={{0,1},{1,0},{2,3},{3,2},{4,5},{5,4},{6,7},{7,6},{8,9},{9,8},{10,11... | collective-permute-start | bytes 294920 | tf_op jit(solution)/shard_map/ppermute | solution.py:468
  37.6 5.6 %collective-permute-start.11 = (f32[3,64,128]{2,1,0:T(8,128)S(1)}, f32[3,64,128]{2,1,0:T(8,128)S(1)}, u32[]{:S(2)}, u32[]{:S(2)}) collective-permute-start(f32[3,64,128]{2,1,0:T(8,128)S(1)} %add.41), channel_id=1, source_target_pairs={{0,2},{1,3},{2,0},{3,1},{4,6},{5,7},{6,4},{7,5},{8,10},{9,11},{10,... | collective-permute-start | bytes 294920 | tf_op jit(solution)/shard_map/ppermute | solution.py:468
  39.6 3.7 %collective-permute-start.5 = (f32[792,128]{1,0:T(8,128)S(1)}, f32[792,128]{1,0:T(8,128)S(1)}, u32[]{:S(2)}, u32[]{:S(2)}) collective-permute-start(f32[792,128]{1,0:T(8,128)S(1)} %get-tuple-element.45), channel_id=1, source_target_pairs={{0,4},{4,0},{8,12},{12,8},{16,20},{20,16},{24,28},{28,24},{1,5},{5... | collective-permute-start | bytes 1216520 | tf_op jit(solution)/shard_map/ppermute | solution.py:463
  39.6 3.7 %collective-permute-start.6 = (f32[792,128]{1,0:T(8,128)S(1)}, f32[792,128]{1,0:T(8,128)S(1)}, u32[]{:S(2)}, u32[]{:S(2)}) collective-permute-start(f32[792,128]{1,0:T(8,128)S(1)} %get-tuple-element.46), channel_id=1, source_target_pairs={{4,8},{8,4},{12,16},{16,12},{20,24},{24,20},{5,9},{9,5},{13,17},{1... | collective-permute-start | bytes 1216520 | tf_op jit(solution)/shard_map/ppermute | solution.py:463
  43.2 2.8 %collective-permute-start.12 = (f32[2,64,128]{2,1,0:T(8,128)S(1)}, f32[2,64,128]{2,1,0:T(8,128)S(1)}, u32[]{:S(2)}, u32[]{:S(2)}) collective-permute-start(f32[2,64,128]{2,1,0:T(8,128)S(1)} %fusion.1.half_ref), channel_id=1, source_target_pairs={{0,4},{4,0},{8,12},{12,8},{16,20},{20,16},{24,28},{28,24},{1,5},{5... | collective-permute-start | bytes 196616 | tf_op jit(solution)/shard_map/ppermute | solution.py:468
  48.7 10.7 %collective-permute-start.15 = (f32[3,64,128]{2,1,0:T(8,128)S(1)}, f32[3,64,128]{2,1,0:T(8,128)S(1)}, u32[]{:S(2)}, u32[]{:S(2)}) collective-permute-start(f32[3,64,128]{2,1,0:T(8,128)S(1)} %get-tuple-element.59), channel_id=1, source_target_pairs={{0,4},{4,0},{8,12},{12,8},{16,20},{20,16},{24,28},{28,24},{1,5},{5... | collective-permute-start | bytes 294920 | tf_op jit(solution)/shard_map/ppermute | solution.py:468
  59.4 5.6 %collective-permute-start.16 = (f32[3,64,128]{2,1,0:T(8,128)S(1)}, f32[3,64,128]{2,1,0:T(8,128)S(1)}, u32[]{:S(2)}, u32[]{:S(2)}) collective-permute-start(f32[3,64,128]{2,1,0:T(8,128)S(1)} %add.44), channel_id=1, source_target_pairs={{0,8},{4,12},{8,0},{12,4},{16,24},{20,28},{24,16},{28,20},{1,9},{5... | collective-permute-start | bytes 294920 | tf_op jit(solution)/shard_map/ppermute | solution.py:468
  61.7 16.4 %collective-permute-start.13 = (f32[768,128]{1,0:T(8,128)S(1)}, f32[768,128]{1,0:T(8,128)S(1)}, u32[]{:S(2)}, u32[]{:S(2)}) collective-permute-start(f32[768,128]{1,0:T(8,128)S(1)} %get-tuple-element.55), channel_id=1, source_target_pairs={{0,1},{1,2},{2,3},{4,5},{5,6},{6,7},{8,9},{9,10},{10,11},{12,13},{... | collective-permute-start | bytes 1179656 | tf_op jit(solution)/shard_map/ppermute | solution.py:455
  65.0 4.8 %collective-permute-start.17 = (f32[3,64,128]{2,1,0:T(8,128)S(1)}, f32[3,64,128]{2,1,0:T(8,128)S(1)}, u32[]{:S(2)}, u32[]{:S(2)}) collective-permute-start(f32[3,64,128]{2,1,0:T(8,128)S(1)} %add.45), channel_id=1, source_target_pairs={{0,16},{4,20},{8,24},{12,28},{16,0},{20,4},{24,8},{28,12},{1,17},{... | collective-permute-start | bytes 294920 | tf_op jit(solution)/shard_map/ppermute | solution.py:468
  69.8 5.3 %collective-permute-start.18 = (f32[3,64,128]{2,1,0:T(8,128)S(1)}, f32[3,64,128]{2,1,0:T(8,128)S(1)}, u32[]{:S(2)}, u32[]{:S(2)}) collective-permute-start(f32[3,64,128]{2,1,0:T(8,128)S(1)} %add.46), channel_id=1, source_target_pairs={{0,1},{1,0},{2,3},{3,2},{4,5},{5,4},{6,7},{7,6},{8,9},{9,8},{10,11... | collective-permute-start | bytes 294920 | tf_op jit(solution)/shard_map/ppermute | solution.py:468
  75.2 7.7 %collective-permute-start.19 = (f32[3,64,128]{2,1,0:T(8,128)S(1)}, f32[3,64,128]{2,1,0:T(8,128)S(1)}, u32[]{:S(2)}, u32[]{:S(2)}) collective-permute-start(f32[3,64,128]{2,1,0:T(8,128)S(1)} %add.47), channel_id=1, source_target_pairs={{0,2},{1,3},{2,0},{3,1},{4,6},{5,7},{6,4},{7,5},{8,10},{9,11},{10,... | collective-permute-start | bytes 294920 | tf_op jit(solution)/shard_map/ppermute | solution.py:468
  78.1 6.7 %collective-permute-start.14 = (f32[2,256,128]{2,1,0:T(8,128)S(1)}, f32[2,256,128]{2,1,0:T(8,128)S(1)}, u32[]{:S(2)}, u32[]{:S(2)}) collective-permute-start(f32[2,256,128]{2,1,0:T(8,128)S(1)} %get-tuple-element.57), channel_id=1, source_target_pairs={{0,4},{4,8},{8,12},{12,16},{16,20},{20,24},{24,28},{1,5},{5,9},{9,... | collective-permute-start | bytes 786440 | tf_op jit(solution)/shard_map/ppermute | solution.py:455
  82.9 1.9 %collective-permute-start.20 = (f32[2,64,128]{2,1,0:T(8,128)S(1)}, f32[2,64,128]{2,1,0:T(8,128)S(1)}, u32[]{:S(2)}, u32[]{:S(2)}) collective-permute-start(f32[2,64,128]{2,1,0:T(8,128)S(1)} %fusion.half_ref), channel_id=1, source_target_pairs={{0,4},{4,0},{8,12},{12,8},{16,20},{20,16},{24,28},{28,24},{1,5},{5... | collective-permute-start | bytes 196616 | tf_op jit(solution)/shard_map/ppermute | solution.py:468

commit v4 on v3

--- a/solution.py
+++ b/solution.py
@@ -480,6 +480,15 @@
     return total
 
 
+def quad(total, axis, first):
+    bit = first
+    while 2 * bit < lax.axis_size(axis):
+        one, two, three = (flip(total, axis, bit * mask) for mask in (1, 2, 3))
+        total = (total + one) + (two + three)
+        bit *= 4
+    return butterfly(total, axis, bit)
+
+
 def stepped(half, total):
     return half - PROBE_STEP * total[:2] / (total[2] + REGULARIZER)
 
@@ -569,18 +578,19 @@
 
     from_inner = swap(inner, "col", 0)
     from_outer = swap(outer, "col", 1)
-    part = keep + flip(send, "row", 1)
-    part = butterfly(part, "row", 2, last_row)
-    part = butterfly(part, "row", last_row)
     total, inner, outer, infos = call(
         strips_kernel,
         [(blocks + 1, size, LANES), edge, edge, (3, INFO, LANES)],
         [],
         [inner, middle, outer, from_inner, from_outer],
     )
+    part = keep + flip(send, "row", 1)
+    part = quad(part, "row", 2)
+    part, inner, outer = tie(part, inner, outer)
     from_inner = swap(inner, "row", 0)
     from_outer = swap(outer, "row", 1)
     part = butterfly(part, "col", 1, last_col)
+    part, from_inner = tie(part, from_inner)
     part = butterfly(part, "col", last_col)
     new_half = stepped(own, part)
     tile, patches, infos = call(
@@ -589,6 +599,7 @@
         [extended, padded, (length, length)] + info_space(9),
         [ext, probe_now, total, infos, from_inner, from_outer],
     )
+    new_half, patches = tie(new_half, patches)
     new_other = flip(new_half, "row", 1)
 
     keep, send, left, middle, right = call(
@@ -608,6 +619,7 @@
     part = keep + flip(send, "row", 1)
     part = butterfly(part, "row", 2, last_row)
     part = butterfly(part, "row", last_row)
+    part, light = tie(part, light)
     left, bottom = call(
         push_kernel, [(size, LANES), (blocks, 2 * length, LANES)], [], [left, middle, from_left]
     )

time: 86.5 us -> 81.9 us (0.947)
  starting transfers between devices: 40.1 us -> 36.8 us
  waiting for transfers between devices: 26.9 us -> 25.5 us
    ppermute x12 -> x13, starting transfers between devices: 29.1 us -> 23.1 us  [flip(): lax.ppermute(value, axis, [(source, source ^ mask) for source in range(co...]
    ppermute x4, starting transfers between devices: 6.7 us -> 9.38 us  [shift(): return lax.ppermute(value, axis, pairs)]
    ppermute x12 -> x13, waiting for transfers between devices: 23.6 us -> 21.2 us  [flip(): lax.ppermute(value, axis, [(source, source ^ mask) for source in range(co...]
    ppermute x4, waiting for transfers between devices: 0.01 us -> 1.13 us  [swap(): return lax.ppermute(value, axis, pairs)]
  transfers between devices with their start and end apart: 21 -> 22, of which waited for: 10 -> 12; matrix products, arithmetic and copies ran while one was open for 0% -> 0% of each run, Pallas kernels for 6% -> 7%
where the time goes in v4:
time: 81.9 us; the launch traced here: 81.2 us
  starting transfers between devices  36.8 us (45%)
  waiting for transfers between devices  25.5 us (31%)
  Pallas kernels  11.9 us (15%)
  local copies, waits for them, and re-layouts  5.23 us (6%)
  between operations  1.53 us (2%)
    ppermute x13, starting transfers between devices, flip(): lax.ppermute(value, axis, [(source, source ^ mask) for source in range(co...  23.1 us
    ppermute x13, waiting for transfers between devices, flip(): lax.ppermute(value, axis, [(source, source ^ mask) for source in range(co...  21.2 us
    pallas_call x9, Pallas kernels, call(): pl.pallas_call(kernel, out_shape=[shape_of(spec) for spec in outs], in_sp...  11.9 us
    ppermute x4, starting transfers between devices, shift(): return lax.ppermute(value, axis, pairs)  9.38 us
    unnamed x12, local copies, waits for them, and re-layouts  5.23 us
    ppermute x1, waiting for transfers between devices, local(): lax.ppermute(corner, ('row', 'col'), [((r + 1) * count_cols + c + 1, r *...  3.22 us
    ppermute x4, starting transfers between devices, swap(): return lax.ppermute(value, axis, pairs)  3.01 us
  transfers between devices with their start and end apart: 22, of which 12 were waited for; matrix products, arithmetic and copies ran while one was open for 0% of the time, Pallas kernels for 7%

profile of v4, /device:TPU:0, one launch (start us, length us, event | category | flops | bytes accessed | tf_op | source)
XLA Modules:
  0.0 81.2 jit_solution(58115287003965585)
XLA Ops:
  0.6 0.0 copy-start
  0.6 1.0 %copy-done = f32[2,256,256]{2,1,0:T(8,128)S(1)} copy-done((f32[2,256,256]{2,1,0:T(8,128)S(1)}, f32[2,256,256]{2,1,0:T(8,128)}, u32[]{:S(2)}) %copy-start) | copy-done | bytes 524312
  1.7 0.2 shard_map.86
  1.8 1.3 %collective-permute-start = (f32[2,256,128]{2,1,0:T(8,128)S(1)}, f32[2,256,128]{2,1,0:T(8,128)S(1)}, u32[]{:S(2)}, u32[]{:S(2)}) collective-permute-start(f32[2,256,128]{2,1,0:T(8,128)S(1)} %get-tuple-element.41), channel_id=1, source_target_pairs={{1,0},{2,1},{3,2},{5,4},{6,5},{7,6},{9,8},{10,9},{11,10},{13,12},{... | collective-permute-start | bytes 786440 | tf_op jit(solution)/shard_map/ppermute | solution.py:455
  3.1 1.3 %collective-permute-start.1 = (f32[2,128,256]{2,1,0:T(8,128)S(1)}, f32[2,128,256]{2,1,0:T(8,128)S(1)}, u32[]{:S(2)}, u32[]{:S(2)}) collective-permute-start(f32[2,128,256]{2,1,0:T(8,128)S(1)} %get-tuple-element.42), channel_id=1, source_target_pairs={{4,0},{8,4},{12,8},{16,12},{20,16},{24,20},{28,24},{5,1},{9,5},{13... | collective-permute-start | bytes 786440 | tf_op jit(solution)/shard_map/ppermute | solution.py:455
  4.4 1.3 %collective-permute-start.2 = (f32[2,128,128]{2,1,0:T(8,128)S(1)}, f32[2,128,128]{2,1,0:T(8,128)S(1)}, u32[]{:S(2)}, u32[]{:S(2)}) collective-permute-start(f32[2,128,128]{2,1,0:T(8,128)S(1)} %get-tuple-element.43), channel_id=1, source_target_pairs={{5,0},{6,1},{7,2},{9,4},{10,5},{11,6},{13,8},{14,9},{15,10},{17,12... | collective-permute-start | bytes 393224 | tf_op jit(solution)/shard_map/ppermute | solution.py:554
  6.4 0.0 copy-start.1
  6.4 1.0 %copy-done.1 = bf16[4,256,256]{2,1,0:T(8,128)(2,1)S(1)} copy-done((bf16[4,256,256]{2,1,0:T(8,128)(2,1)S(1)}, bf16[4,256,256]{2,1,0:T(8,128)(2,1)}, u32[]{:S(2)}) %copy-start.1) | copy-done | bytes 524312
  7.4 0.0 copy-start.2
  7.4 0.9 %copy-done.2 = s32[1,1,4,128,128]{4,3,2,1,0:T(8,128)S(1)} copy-done((s32[1,1,4,128,128]{4,3,2,1,0:T(8,128)S(1)}, s32[1,1,4,128,128]{4,3,2,1,0:T(8,128)}, u32[]{:S(2)}) %copy-start.2) | copy-done | bytes 262168
  8.4 0.0 copy-start.3
  8.4 0.9 %copy-done.3 = f32[2,128,128]{2,1,0:T(8,128)S(1)} copy-done((f32[2,128,128]{2,1,0:T(8,128)S(1)}, f32[2,128,128]{2,1,0:T(8,128)}, u32[]{:S(2)}) %copy-start.3) | copy-done | bytes 131096
  9.3 0.0 copy-start.4
  9.3 0.7 copy-done.4
  9.9 0.7 copy-done.5
  10.6 0.6 shard_map.87
  11.2 3.2 %collective-permute-done.2.corner_ref = f32[2,128,128]{2,1,0:T(8,128)S(1)} collective-permute-done((f32[2,128,128]{2,1,0:T(8,128)S(1)}, f32[2,128,128]{2,1,0:T(8,128)S(1)}, u32[]{:S(2)}, u32[]{:S(2)}) %collective-permute-start.2) | collective-permute-done | bytes 131104 | tf_op jit(solution)/shard_map/ppermute | solution.py:554
  14.5 0.0 collective-permute-done.right_ref
  14.5 0.0 collective-permute-done.1.below_ref
  14.5 2.7 %shard_map.88 = (f32[2,3,384,128]{3,2,1,0:T(8,128)S(1)}, f32[3,64,128]{2,1,0:T(8,128)S(1)}, f32[3,64,128]{2,1,0:T(8,128)S(1)}, f32[776,128]{1,0:T(8,128)S(1)}, f...) custom-call(f32[2,3,384,128]{3,2,1,0:T(8,128)S(1)} %get-tuple-element.40.start_ref, ...), custom_call_target="tpu_custom_call", output_to_operand_aliasing={{0}: (0, {})} | custom-call | tf_op jit(solution)/shard_map/pallas_call | solution.py:502
  17.2 2.4 %collective-permute-start.5 = (f32[3,64,128]{2,1,0:T(8,128)S(1)}, f32[3,64,128]{2,1,0:T(8,128)S(1)}, u32[]{:S(2)}, u32[]{:S(2)}) collective-permute-start(f32[3,64,128]{2,1,0:T(8,128)S(1)} %get-tuple-element.55), channel_id=1, source_target_pairs={{0,4},{4,0},{8,12},{12,8},{16,20},{20,16},{24,28},{28,24},{1,5},{5... | collective-permute-start | bytes 294920 | tf_op jit(solution)/shard_map/ppermute | solution.py:468
  19.6 1.6 %collective-permute-start.3 = (f32[776,128]{1,0:T(8,128)S(1)}, f32[776,128]{1,0:T(8,128)S(1)}, u32[]{:S(2)}, u32[]{:S(2)}) collective-permute-start(f32[776,128]{1,0:T(8,128)S(1)} %get-tuple-element.49.inner_ref), channel_id=1, source_target_pairs={{0,1},{1,0},{2,3},{3,2},{4,5},{5,4},{6,7},{7,6},{8,9},{9,8},{10,11... | collective-permute-start | bytes 1191944 | tf_op jit(solution)/shard_map/ppermute | solution.py:463
  21.2 0.7 collective-permute-start.4
  21.8 0.0 collective-permute-done.5
  21.9 1.1 %collective-permute-start.8 = (f32[3,64,128]{2,1,0:T(8,128)S(1)}, f32[3,64,128]{2,1,0:T(8,128)S(1)}, u32[]{:S(2)}, u32[]{:S(2)}) collective-permute-start(f32[3,64,128]{2,1,0:T(8,128)S(1)} %add.41), channel_id=1, source_target_pairs={{0,24},{4,28},{8,16},{12,20},{16,8},{20,12},{24,0},{28,4},{1,25},{... | collective-permute-start | bytes 294920 | tf_op jit(solution)/shard_map/ppermute | solution.py:468
  23.0 1.9 %collective-permute-start.7 = (f32[3,64,128]{2,1,0:T(8,128)S(1)}, f32[3,64,128]{2,1,0:T(8,128)S(1)}, u32[]{:S(2)}, u32[]{:S(2)}) collective-permute-start(f32[3,64,128]{2,1,0:T(8,128)S(1)} %add.41), channel_id=1, source_target_pairs={{0,16},{4,20},{8,24},{12,28},{16,0},{20,4},{24,8},{28,12},{1,17},{... | collective-permute-start | bytes 294920 | tf_op jit(solution)/shard_map/ppermute | solution.py:468
  24.9 0.5 collective-permute-start.6
  25.4 2.8 %collective-permute-done.8 = f32[3,64,128]{2,1,0:T(8,128)S(1)} collective-permute-done((f32[3,64,128]{2,1,0:T(8,128)S(1)}, f32[3,64,128]{2,1,0:T(8,128)S(1)}, u32[]{:S(2)}, u32[]{:S(2)}) %collective-permute-start.8) | collective-permute-done | bytes 98336 | tf_op jit(solution)/shard_map/ppermute | solution.py:468
  28.2 1.2 %collective-permute-done.7 = f32[3,64,128]{2,1,0:T(8,128)S(1)} collective-permute-done((f32[3,64,128]{2,1,0:T(8,128)S(1)}, f32[3,64,128]{2,1,0:T(8,128)S(1)}, u32[]{:S(2)}, u32[]{:S(2)}) %collective-permute-start.7) | collective-permute-done | bytes 98336 | tf_op jit(solution)/shard_map/ppermute | solution.py:468
  29.4 0.2 collective-permute-done.6
  29.7 1.1 %collective-permute-done.3.from_inner = f32[776,128]{1,0:T(8,128)S(1)} collective-permute-done((f32[776,128]{1,0:T(8,128)S(1)}, f32[776,128]{1,0:T(8,128)S(1)}, u32[]{:S(2)}, u32[]{:S(2)}) %collective-permute-start.3) | collective-permute-done | bytes 397344 | tf_op jit(solution)/shard_map/ppermute | solution.py:463
  30.8 0.0 collective-permute-done.4.from_outer
  30.8 0.2 shard_map.89
  31.0 0.1 collective-permute-start.10
  31.0 0.7 collective-permute-start.11
  31.7 3.7 %collective-permute-start.9 = (f32[3,64,128]{2,1,0:T(8,128)S(1)}, f32[3,64,128]{2,1,0:T(8,128)S(1)}, u32[]{:S(2)}, u32[]{:S(2)}) collective-permute-start(f32[3,64,128]{2,1,0:T(8,128)S(1)} %add_add_fusion), channel_id=1, source_target_pairs={{0,1},{1,0},{2,3},{3,2},{4,5},{5,4},{6,7},{7,6},{8,9},{9,8},{10,11... | collective-permute-start | bytes 294920 | tf_op jit(solution)/shard_map/ppermute | solution.py:468
  35.4 2.6 %collective-permute-done.9 = f32[3,64,128]{2,1,0:T(8,128)S(1)} collective-permute-done((f32[3,64,128]{2,1,0:T(8,128)S(1)}, f32[3,64,128]{2,1,0:T(8,128)S(1)}, u32[]{:S(2)}, u32[]{:S(2)}) %collective-permute-start.9) | collective-permute-done | bytes 98336 | tf_op jit(solution)/shard_map/ppermute | solution.py:468
  38.0 0.0 collective-permute-done.10.from_inner
  38.0 2.9 %collective-permute-start.12 = (f32[3,64,128]{2,1,0:T(8,128)S(1)}, f32[3,64,128]{2,1,0:T(8,128)S(1)}, u32[]{:S(2)}, u32[]{:S(2)}) collective-permute-start(f32[3,64,128]{2,1,0:T(8,128)S(1)} %add.45), channel_id=1, source_target_pairs={{0,2},{1,3},{2,0},{3,1},{4,6},{5,7},{6,4},{7,5},{8,10},{9,11},{10,... | collective-permute-start | bytes 294920 | tf_op jit(solution)/shard_map/ppermute | solution.py:468
  41.0 0.0 collective-permute-done.11.from_outer
  41.0 2.8 %shard_map.90 = (f32[2,2,256,128]{3,2,1,0:T(8,128)S(1)}, f32[4,2,128,128]{3,2,1,0:T(8,128)S(1)}, f32[9,8,128]{2,1,0:T(8,128)S(1)}) custom-call(f32[2,3,384,128]{3,2,1,0:T(8,128)S(1)} %get-tuple-element.48.ext_ref, f32[2,128,128]{2,1,0:T(8,128)S(1)} %get-tuple-element.44.probe_ref, f32[3,768,128]{2,1,0:T(8,128)S(1)} %get-tuple-element.52.total_ref, ...), custom_call_target="tpu_custom_call" | custom-call | tf_op jit(solution)/shard_map/pallas_call | solution.py:502
  43.8 0.0 collective-permute-done.12
  43.9 4.0 %collective-permute-start.13 = (f32[2,64,128]{2,1,0:T(8,128)S(1)}, f32[2,64,128]{2,1,0:T(8,128)S(1)}, u32[]{:S(2)}, u32[]{:S(2)}) collective-permute-start(f32[2,64,128]{2,1,0:T(8,128)S(1)} %fusion.1.half_ref), channel_id=1, source_target_pairs={{0,4},{4,0},{8,12},{12,8},{16,20},{20,16},{24,28},{28,24},{1,5},{5... | collective-permute-start | bytes 196616 | tf_op jit(solution)/shard_map/ppermute | solution.py:468
  47.9 0.9 %collective-permute-done.13.other_ref = f32[2,64,128]{2,1,0:T(8,128)S(1)} collective-permute-done((f32[2,64,128]{2,1,0:T(8,128)S(1)}, f32[2,64,128]{2,1,0:T(8,128)S(1)}, u32[]{:S(2)}, u32[]{:S(2)}) %collective-permute-start.13) | collective-permute-done | bytes 65568 | tf_op jit(solution)/shard_map/ppermute | solution.py:468
  48.8 2.6 %shard_map.91 = (f32[3,64,128]{2,1,0:T(8,128)S(1)}, f32[3,64,128]{2,1,0:T(8,128)S(1)}, f32[768,128]{1,0:T(8,128)S(1)}, f32[768,128]{1,0:T(8,128)S(1)}, f32[768,128]{1,0:T(8,128)S(1)}) custom-call(f32[4,2,128,128]{3,2,1,0:T(8,128)S(1)} %get-tuple-element.66.patches_ref, f32[2,64,128]{2,1,0:T(8,128)S(1)} %fusion.1.half_ref, ...), custom_call_target="tpu_custom_call" | custom-call | tf_op jit(solution)/shard_map/pallas_call | solution.py:502
  51.4 0.4 collective-permute-start.14
  51.8 1.0 %collective-permute-done.14 = f32[3,64,128]{2,1,0:T(8,128)S(1)} collective-permute-done((f32[3,64,128]{2,1,0:T(8,128)S(1)}, f32[3,64,128]{2,1,0:T(8,128)S(1)}, u32[]{:S(2)}, u32[]{:S(2)}) %collective-permute-start.14) | collective-permute-done | bytes 98336 | tf_op jit(solution)/shard_map/ppermute | solution.py:468
  52.8 2.2 %collective-permute-start.15 = (f32[3,64,128]{2,1,0:T(8,128)S(1)}, f32[3,64,128]{2,1,0:T(8,128)S(1)}, u32[]{:S(2)}, u32[]{:S(2)}) collective-permute-start(f32[3,64,128]{2,1,0:T(8,128)S(1)} %add.48), channel_id=1, source_target_pairs={{0,8},{4,12},{8,0},{12,4},{16,24},{20,28},{24,16},{28,20},{1,9},{5... | collective-permute-start | bytes 294920 | tf_op jit(solution)/shard_map/ppermute | solution.py:468
  55.0 5.5 %collective-permute-start.17 = (f32[768,128]{1,0:T(8,128)S(1)}, f32[768,128]{1,0:T(8,128)S(1)}, u32[]{:S(2)}, u32[]{:S(2)}) collective-permute-start(f32[768,128]{1,0:T(8,128)S(1)} %get-tuple-element.74), channel_id=1, source_target_pairs={{0,1},{1,2},{2,3},{4,5},{5,6},{6,7},{8,9},{9,10},{10,11},{12,13},{... | collective-permute-start | bytes 1179656 | tf_op jit(solution)/shard_map/ppermute | solution.py:455
  60.5 0.0 collective-permute-done.15
  60.6 0.9 %collective-permute-start.16 = (f32[3,64,128]{2,1,0:T(8,128)S(1)}, f32[3,64,128]{2,1,0:T(8,128)S(1)}, u32[]{:S(2)}, u32[]{:S(2)}) collective-permute-start(f32[3,64,128]{2,1,0:T(8,128)S(1)} %add.49), channel_id=1, source_target_pairs={{0,16},{4,20},{8,24},{12,28},{16,0},{20,4},{24,8},{28,12},{1,17},{... | collective-permute-start | bytes 294920 | tf_op jit(solution)/shard_map/ppermute | solution.py:468
  61.4 1.8 %shard_map.92.light_ref = f32[2,256,128]{2,1,0:T(8,128)S(1)} custom-call(f32[9,8,128]{2,1,0:T(8,128)S(1)} %get-tuple-element.70.infos_ref, f32[2,64,128]{2,1,0:T(8,128)S(1)} %fusion.1.half_ref, f32[2,64,128]{2,1,0:T(8,128)S(1)} %collective-permute-done.13.other_ref), custom_call_target="tpu_custom_call" | custom-call | tf_op jit(solution)/shard_map/pallas_call | solution.py:502
  63.2 2.0 %collective-permute-done.16 = f32[3,64,128]{2,1,0:T(8,128)S(1)} collective-permute-done((f32[3,64,128]{2,1,0:T(8,128)S(1)}, f32[3,64,128]{2,1,0:T(8,128)S(1)}, u32[]{:S(2)}, u32[]{:S(2)}) %collective-permute-start.16) | collective-permute-done | bytes 98336 | tf_op jit(solution)/shard_map/ppermute | solution.py:468
  65.3 1.6 %collective-permute-start.19 = (f32[3,64,128]{2,1,0:T(8,128)S(1)}, f32[3,64,128]{2,1,0:T(8,128)S(1)}, u32[]{:S(2)}, u32[]{:S(2)}) collective-permute-start(f32[3,64,128]{2,1,0:T(8,128)S(1)} %add.50), channel_id=1, source_target_pairs={{0,1},{1,0},{2,3},{3,2},{4,5},{5,4},{6,7},{7,6},{8,9},{9,8},{10,11... | collective-permute-start | bytes 294920 | tf_op jit(solution)/shard_map/ppermute | solution.py:468
  66.9 4.3 %collective-permute-done.19 = f32[3,64,128]{2,1,0:T(8,128)S(1)} collective-permute-done((f32[3,64,128]{2,1,0:T(8,128)S(1)}, f32[3,64,128]{2,1,0:T(8,128)S(1)}, u32[]{:S(2)}, u32[]{:S(2)}) %collective-permute-start.19) | collective-permute-done | bytes 98336 | tf_op jit(solution)/shard_map/ppermute | solution.py:468
  71.2 1.4 %collective-permute-start.20 = (f32[3,64,128]{2,1,0:T(8,128)S(1)}, f32[3,64,128]{2,1,0:T(8,128)S(1)}, u32[]{:S(2)}, u32[]{:S(2)}) collective-permute-start(f32[3,64,128]{2,1,0:T(8,128)S(1)} %add.51), channel_id=1, source_target_pairs={{0,2},{1,3},{2,0},{3,1},{4,6},{5,7},{6,4},{7,5},{8,10},{9,11},{10,... | collective-permute-start | bytes 294920 | tf_op jit(solution)/shard_map/ppermute | solution.py:468
  72.6 0.0 collective-permute-done.17.from_left
  72.6 0.1 shard_map.93
  72.6 1.3 %collective-permute-start.18 = (f32[2,256,128]{2,1,0:T(8,128)S(1)}, f32[2,256,128]{2,1,0:T(8,128)S(1)}, u32[]{:S(2)}, u32[]{:S(2)}) collective-permute-start(f32[2,256,128]{2,1,0:T(8,128)S(1)} %get-tuple-element.76), channel_id=1, source_target_pairs={{0,4},{4,8},{8,12},{12,16},{16,20},{20,24},{24,28},{1,5},{5,9},{9,... | collective-permute-start | bytes 786440 | tf_op jit(solution)/shard_map/ppermute | solution.py:455
  74.0 4.9 %collective-permute-done.20 = f32[3,64,128]{2,1,0:T(8,128)S(1)} collective-permute-done((f32[3,64,128]{2,1,0:T(8,128)S(1)}, f32[3,64,128]{2,1,0:T(8,128)S(1)}, u32[]{:S(2)}, u32[]{:S(2)}) %collective-permute-start.20) | collective-permute-done | bytes 98336 | tf_op jit(solution)/shard_map/ppermute | solution.py:468
  79.0 0.1 collective-permute-start.21
  79.0 1.2 %collective-permute-done.21.other_ref = f32[2,64,128]{2,1,0:T(8,128)S(1)} collective-permute-done((f32[2,64,128]{2,1,0:T(8,128)S(1)}, f32[2,64,128]{2,1,0:T(8,128)S(1)}, u32[]{:S(2)}, u32[]{:S(2)}) %collective-permute-start.21) | collective-permute-done | bytes 65568 | tf_op jit(solution)/shard_map/ppermute | solution.py:468
  80.3 0.0 collective-permute-done.18.from_above
  80.3 0.9 %shard_map.94 = (f32[2,256,256]{2,1,0:T(8,128)}, f32[2,128,128]{2,1,0:T(8,128)}) custom-call(f32[2,2,256,128]{3,2,1,0:T(8,128)S(1)} %get-tuple-element.62.tile_ref, f32[2,256,128]{2,1,0:T(8,128)S(1)} %shard_map.92.light_ref, f32[768,128]{1,0:T(8,128)S(1)} %get-tuple-element.75.left_ref, f32[768,128]{1,0:T(8,128)S(1)} %get-tuple-element.73.middle_ref, ...), custom_call_target="tpu_custom_call" | custom-call | tf_op jit(solution)/shard_map/pallas_call | solution.py:502
  (14 shorter events, 0.2 us)
Async XLA Ops:
  0.6 1.0 %copy-start = (f32[2,256,256]{2,1,0:T(8,128)S(1)}, f32[2,256,256]{2,1,0:T(8,128)}, u32[]{:S(2)}) copy-start(f32[2,256,256]{2,1,0:T(8,128)} %field_ref.1) | copy-start | bytes 1572868
  1.8 12.6 %collective-permute-start = (f32[2,256,128]{2,1,0:T(8,128)S(1)}, f32[2,256,128]{2,1,0:T(8,128)S(1)}, u32[]{:S(2)}, u32[]{:S(2)}) collective-permute-start(f32[2,256,128]{2,1,0:T(8,128)S(1)} %get-tuple-element.41), channel_id=1, source_target_pairs={{1,0},{2,1},{3,2},{5,4},{6,5},{7,6},{9,8},{10,9},{11,10},{13,12},{... | collective-permute-start | bytes 786440 | tf_op jit(solution)/shard_map/ppermute | solution.py:455
  3.1 11.3 %collective-permute-start.1 = (f32[2,128,256]{2,1,0:T(8,128)S(1)}, f32[2,128,256]{2,1,0:T(8,128)S(1)}, u32[]{:S(2)}, u32[]{:S(2)}) collective-permute-start(f32[2,128,256]{2,1,0:T(8,128)S(1)} %get-tuple-element.42), channel_id=1, source_target_pairs={{4,0},{8,4},{12,8},{16,12},{20,16},{24,20},{28,24},{5,1},{9,5},{13... | collective-permute-start | bytes 786440 | tf_op jit(solution)/shard_map/ppermute | solution.py:455
  4.4 10.0 %collective-permute-start.2 = (f32[2,128,128]{2,1,0:T(8,128)S(1)}, f32[2,128,128]{2,1,0:T(8,128)S(1)}, u32[]{:S(2)}, u32[]{:S(2)}) collective-permute-start(f32[2,128,128]{2,1,0:T(8,128)S(1)} %get-tuple-element.43), channel_id=1, source_target_pairs={{5,0},{6,1},{7,2},{9,4},{10,5},{11,6},{13,8},{14,9},{15,10},{17,12... | collective-permute-start | bytes 393224 | tf_op jit(solution)/shard_map/ppermute | solution.py:554
  6.4 1.0 %copy-start.1 = (bf16[4,256,256]{2,1,0:T(8,128)(2,1)S(1)}, bf16[4,256,256]{2,1,0:T(8,128)(2,1)}, u32[]{:S(2)}) copy-start(bf16[4,256,256]{2,1,0:T(8,128)(2,1)} %constant.4.clone.tables_ref) | copy-start | bytes 1572868
  7.4 0.9 %copy-start.2 = (s32[1,1,4,128,128]{4,3,2,1,0:T(8,128)S(1)}, s32[1,1,4,128,128]{4,3,2,1,0:T(8,128)}, u32[]{:S(2)}) copy-start(s32[1,1,4,128,128]{4,3,2,1,0:T(8,128)} %param.9) | copy-start | bytes 786436
  8.4 0.9 %copy-start.3 = (f32[2,128,128]{2,1,0:T(8,128)S(1)}, f32[2,128,128]{2,1,0:T(8,128)}, u32[]{:S(2)}) copy-start(f32[2,128,128]{2,1,0:T(8,128)} %probe_ref.1) | copy-start | bytes 393220
  9.3 0.7 copy-start.4
  9.9 0.7 copy-start.5
  17.2 4.6 %collective-permute-start.5 = (f32[3,64,128]{2,1,0:T(8,128)S(1)}, f32[3,64,128]{2,1,0:T(8,128)S(1)}, u32[]{:S(2)}, u32[]{:S(2)}) collective-permute-start(f32[3,64,128]{2,1,0:T(8,128)S(1)} %get-tuple-element.55), channel_id=1, source_target_pairs={{0,4},{4,0},{8,12},{12,8},{16,20},{20,16},{24,28},{28,24},{1,5},{5... | collective-permute-start | bytes 294920 | tf_op jit(solution)/shard_map/ppermute | solution.py:468
  19.6 11.2 %collective-permute-start.3 = (f32[776,128]{1,0:T(8,128)S(1)}, f32[776,128]{1,0:T(8,128)S(1)}, u32[]{:S(2)}, u32[]{:S(2)}) collective-permute-start(f32[776,128]{1,0:T(8,128)S(1)} %get-tuple-element.49.inner_ref), channel_id=1, source_target_pairs={{0,1},{1,0},{2,3},{3,2},{4,5},{5,4},{6,7},{7,6},{8,9},{9,8},{10,11... | collective-permute-start | bytes 1191944 | tf_op jit(solution)/shard_map/ppermute | solution.py:463
  21.2 9.6 %collective-permute-start.4 = (f32[776,128]{1,0:T(8,128)S(1)}, f32[776,128]{1,0:T(8,128)S(1)}, u32[]{:S(2)}, u32[]{:S(2)}) collective-permute-start(f32[776,128]{1,0:T(8,128)S(1)} %get-tuple-element.51.outer_ref), channel_id=1, source_target_pairs={{1,2},{2,1},{5,6},{6,5},{9,10},{10,9},{13,14},{14,13},{17,18},{18,... | collective-permute-start | bytes 1191944 | tf_op jit(solution)/shard_map/ppermute | solution.py:463
  21.9 6.4 %collective-permute-start.8 = (f32[3,64,128]{2,1,0:T(8,128)S(1)}, f32[3,64,128]{2,1,0:T(8,128)S(1)}, u32[]{:S(2)}, u32[]{:S(2)}) collective-permute-start(f32[3,64,128]{2,1,0:T(8,128)S(1)} %add.41), channel_id=1, source_target_pairs={{0,24},{4,28},{8,16},{12,20},{16,8},{20,12},{24,0},{28,4},{1,25},{... | collective-permute-start | bytes 294920 | tf_op jit(solution)/shard_map/ppermute | solution.py:468
  23.0 6.4 %collective-permute-start.7 = (f32[3,64,128]{2,1,0:T(8,128)S(1)}, f32[3,64,128]{2,1,0:T(8,128)S(1)}, u32[]{:S(2)}, u32[]{:S(2)}) collective-permute-start(f32[3,64,128]{2,1,0:T(8,128)S(1)} %add.41), channel_id=1, source_target_pairs={{0,16},{4,20},{8,24},{12,28},{16,0},{20,4},{24,8},{28,12},{1,17},{... | collective-permute-start | bytes 294920 | tf_op jit(solution)/shard_map/ppermute | solution.py:468
  24.9 4.7 %collective-permute-start.6 = (f32[3,64,128]{2,1,0:T(8,128)S(1)}, f32[3,64,128]{2,1,0:T(8,128)S(1)}, u32[]{:S(2)}, u32[]{:S(2)}) collective-permute-start(f32[3,64,128]{2,1,0:T(8,128)S(1)} %add.41), channel_id=1, source_target_pairs={{0,8},{4,12},{8,0},{12,4},{16,24},{20,28},{24,16},{28,20},{1,9},{5... | collective-permute-start | bytes 294920 | tf_op jit(solution)/shard_map/ppermute | solution.py:468
  31.0 7.1 %collective-permute-start.10 = (f32[792,128]{1,0:T(8,128)S(1)}, f32[792,128]{1,0:T(8,128)S(1)}, u32[]{:S(2)}, u32[]{:S(2)}) collective-permute-start(f32[792,128]{1,0:T(8,128)S(1)} %get-tuple-element.59), channel_id=1, source_target_pairs={{0,4},{4,0},{8,12},{12,8},{16,20},{20,16},{24,28},{28,24},{1,5},{5... | collective-permute-start | bytes 1216520 | tf_op jit(solution)/shard_map/ppermute | solution.py:463
  31.0 10.0 %collective-permute-start.11 = (f32[792,128]{1,0:T(8,128)S(1)}, f32[792,128]{1,0:T(8,128)S(1)}, u32[]{:S(2)}, u32[]{:S(2)}) collective-permute-start(f32[792,128]{1,0:T(8,128)S(1)} %get-tuple-element.61), channel_id=1, source_target_pairs={{4,8},{8,4},{12,16},{16,12},{20,24},{24,20},{5,9},{9,5},{13,17},{1... | collective-permute-start | bytes 1216520 | tf_op jit(solution)/shard_map/ppermute | solution.py:463
  31.7 6.3 %collective-permute-start.9 = (f32[3,64,128]{2,1,0:T(8,128)S(1)}, f32[3,64,128]{2,1,0:T(8,128)S(1)}, u32[]{:S(2)}, u32[]{:S(2)}) collective-permute-start(f32[3,64,128]{2,1,0:T(8,128)S(1)} %add_add_fusion), channel_id=1, source_target_pairs={{0,1},{1,0},{2,3},{3,2},{4,5},{5,4},{6,7},{7,6},{8,9},{9,8},{10,11... | collective-permute-start | bytes 294920 | tf_op jit(solution)/shard_map/ppermute | solution.py:468
  38.0 5.8 %collective-permute-start.12 = (f32[3,64,128]{2,1,0:T(8,128)S(1)}, f32[3,64,128]{2,1,0:T(8,128)S(1)}, u32[]{:S(2)}, u32[]{:S(2)}) collective-permute-start(f32[3,64,128]{2,1,0:T(8,128)S(1)} %add.45), channel_id=1, source_target_pairs={{0,2},{1,3},{2,0},{3,1},{4,6},{5,7},{6,4},{7,5},{8,10},{9,11},{10,... | collective-permute-start | bytes 294920 | tf_op jit(solution)/shard_map/ppermute | solution.py:468
  43.9 4.9 %collective-permute-start.13 = (f32[2,64,128]{2,1,0:T(8,128)S(1)}, f32[2,64,128]{2,1,0:T(8,128)S(1)}, u32[]{:S(2)}, u32[]{:S(2)}) collective-permute-start(f32[2,64,128]{2,1,0:T(8,128)S(1)} %fusion.1.half_ref), channel_id=1, source_target_pairs={{0,4},{4,0},{8,12},{12,8},{16,20},{20,16},{24,28},{28,24},{1,5},{5... | collective-permute-start | bytes 196616 | tf_op jit(solution)/shard_map/ppermute | solution.py:468
  51.4 1.4 %collective-permute-start.14 = (f32[3,64,128]{2,1,0:T(8,128)S(1)}, f32[3,64,128]{2,1,0:T(8,128)S(1)}, u32[]{:S(2)}, u32[]{:S(2)}) collective-permute-start(f32[3,64,128]{2,1,0:T(8,128)S(1)} %get-tuple-element.69), channel_id=1, source_target_pairs={{0,4},{4,0},{8,12},{12,8},{16,20},{20,16},{24,28},{28,24},{1,5},{5... | collective-permute-start | bytes 294920 | tf_op jit(solution)/shard_map/ppermute | solution.py:468
  52.8 7.7 %collective-permute-start.15 = (f32[3,64,128]{2,1,0:T(8,128)S(1)}, f32[3,64,128]{2,1,0:T(8,128)S(1)}, u32[]{:S(2)}, u32[]{:S(2)}) collective-permute-start(f32[3,64,128]{2,1,0:T(8,128)S(1)} %add.48), channel_id=1, source_target_pairs={{0,8},{4,12},{8,0},{12,4},{16,24},{20,28},{24,16},{28,20},{1,9},{5... | collective-permute-start | bytes 294920 | tf_op jit(solution)/shard_map/ppermute | solution.py:468
  55.0 17.6 %collective-permute-start.17 = (f32[768,128]{1,0:T(8,128)S(1)}, f32[768,128]{1,0:T(8,128)S(1)}, u32[]{:S(2)}, u32[]{:S(2)}) collective-permute-start(f32[768,128]{1,0:T(8,128)S(1)} %get-tuple-element.74), channel_id=1, source_target_pairs={{0,1},{1,2},{2,3},{4,5},{5,6},{6,7},{8,9},{9,10},{10,11},{12,13},{... | collective-permute-start | bytes 1179656 | tf_op jit(solution)/shard_map/ppermute | solution.py:455
  60.6 4.7 %collective-permute-start.16 = (f32[3,64,128]{2,1,0:T(8,128)S(1)}, f32[3,64,128]{2,1,0:T(8,128)S(1)}, u32[]{:S(2)}, u32[]{:S(2)}) collective-permute-start(f32[3,64,128]{2,1,0:T(8,128)S(1)} %add.49), channel_id=1, source_target_pairs={{0,16},{4,20},{8,24},{12,28},{16,0},{20,4},{24,8},{28,12},{1,17},{... | collective-permute-start | bytes 294920 | tf_op jit(solution)/shard_map/ppermute | solution.py:468
  65.3 5.9 %collective-permute-start.19 = (f32[3,64,128]{2,1,0:T(8,128)S(1)}, f32[3,64,128]{2,1,0:T(8,128)S(1)}, u32[]{:S(2)}, u32[]{:S(2)}) collective-permute-start(f32[3,64,128]{2,1,0:T(8,128)S(1)} %add.50), channel_id=1, source_target_pairs={{0,1},{1,0},{2,3},{3,2},{4,5},{5,4},{6,7},{7,6},{8,9},{9,8},{10,11... | collective-permute-start | bytes 294920 | tf_op jit(solution)/shard_map/ppermute | solution.py:468
  71.2 7.7 %collective-permute-start.20 = (f32[3,64,128]{2,1,0:T(8,128)S(1)}, f32[3,64,128]{2,1,0:T(8,128)S(1)}, u32[]{:S(2)}, u32[]{:S(2)}) collective-permute-start(f32[3,64,128]{2,1,0:T(8,128)S(1)} %add.51), channel_id=1, source_target_pairs={{0,2},{1,3},{2,0},{3,1},{4,6},{5,7},{6,4},{7,5},{8,10},{9,11},{10,... | collective-permute-start | bytes 294920 | tf_op jit(solution)/shard_map/ppermute | solution.py:468
  72.6 7.6 %collective-permute-start.18 = (f32[2,256,128]{2,1,0:T(8,128)S(1)}, f32[2,256,128]{2,1,0:T(8,128)S(1)}, u32[]{:S(2)}, u32[]{:S(2)}) collective-permute-start(f32[2,256,128]{2,1,0:T(8,128)S(1)} %get-tuple-element.76), channel_id=1, source_target_pairs={{0,4},{4,8},{8,12},{12,16},{16,20},{20,24},{24,28},{1,5},{5,9},{9,... | collective-permute-start | bytes 786440 | tf_op jit(solution)/shard_map/ppermute | solution.py:455
  79.0 1.3 %collective-permute-start.21 = (f32[2,64,128]{2,1,0:T(8,128)S(1)}, f32[2,64,128]{2,1,0:T(8,128)S(1)}, u32[]{:S(2)}, u32[]{:S(2)}) collective-permute-start(f32[2,64,128]{2,1,0:T(8,128)S(1)} %fusion.half_ref), channel_id=1, source_target_pairs={{0,4},{4,0},{8,12},{12,8},{16,20},{20,16},{24,28},{28,24},{1,5},{5... | collective-permute-start | bytes 196616 | tf_op jit(solution)/shard_map/ppermute | solution.py:468

commit v5 on v4

--- a/solution.py
+++ b/solution.py
@@ -94,12 +94,13 @@
         add_patch(light_ref, row, col, power_ref[...], length)
 
 
-def all_light(light_ref, power_ref, info_ref, tall, wide, slots, length):
+def add_tiles(light_ref, power_ref, info_ref, tiles, tall, wide, slots, length):
     across = 1 - 2 * parity("col")
     down = 1 - 2 * parity("row")
     places = [(0, 0), (0, across), (0, -across)]
     places += [(down, step) for step in (-1, 0, 1)] + [(-down, step) for step in (-1, 0, 1)]
-    for index, (row_step, col_step) in enumerate(places):
+    for index in tiles:
+        row_step, col_step = places[index]
         for s in range(slots):
             row, col, weight = slot_place(info_ref, index, s, slots)
             add_light(light_ref, power_ref, row + row_step * tall, col + col_step * wide, weight, length)
@@ -325,15 +326,46 @@
         outer_out[rows] = info
 
 
+def update_rows(new_ref, ext_ref, light_ref, total_ref, extra, block, start, stop, length, inside):
+    high = ext_ref.shape[2]
+    scale = STEP_SIZE / (light_ref[block + 1, start + length : stop + length, :] + REGULARIZER)
+    if inside is not None:
+        scale = scale * inside
+    for channel in range(2):
+        total = total_ref[block, channel * high + start : channel * high + stop]
+        if extra is not None:
+            total = total + extra(2 * block + channel)
+        new_ref[channel, block, start:stop, :] = ext_ref[channel, block, start:stop, :] - scale * total
+
+
+def inside_mesh(axis):
+    return jnp.where(lax.axis_index(axis) < lax.axis_size(axis) - 1, 1.0, 0.0).astype(jnp.float32)
+
+
+def near_light_kernel(
+    slots, tall, ext_ref, infos_ref, probe_ref, total_ref, new_ref, light_out, power_ref, info_at, sems
+):
+    copies = start_all([(infos_ref, info_at)], sems)
+    length = power_ref.shape[0]
+    power_ref[...] = probe_ref[0] * probe_ref[0] + probe_ref[1] * probe_ref[1]
+    light_out[...] = jnp.zeros_like(light_out)
+    wait_all(copies)
+    wide = (light_out.shape[0] - 3) * LANES
+    add_tiles(light_out, power_ref, info_at, range(3), tall, wide, slots, length)
+    blocks = ext_ref.shape[1] - 1
+    for block in range(blocks + 1):
+        inside = inside_mesh("col") if block == blocks else None
+        update_rows(new_ref, ext_ref, light_out, total_ref, None, block, length, tall, length, inside)
+
+
 def object_kernel(
-    ext_ref, probe_ref, total_ref, infos_ref, from_inner, from_outer,
-    tile_out, patches_out, info_out, new_ref, light_ref, power_ref, info_at, sems,
+    slots, ext_ref, light_in, probe_ref, total_ref, infos_ref, from_inner, from_outer,
+    new_ref, light_ref, info_out, power_ref, info_at, sems,
 ):
-    length = patches_out.shape[2]
-    slots = patches_out.shape[0]
+    length = power_ref.shape[0]
     high = ext_ref.shape[2]
     tall = high - length
-    blocks = tile_out.shape[1]
+    blocks = ext_ref.shape[1] - 1
     edge = 6 * length
     info_out[0:3] = infos_ref[...]
     for index in range(3):
@@ -341,34 +373,34 @@
         info_out[6 + index] = from_outer[edge + index * INFO : edge + (index + 1) * INFO]
     copies = start_all([(info_out, info_at)], sems)
     power_ref[...] = probe_ref[0] * probe_ref[0] + probe_ref[1] * probe_ref[1]
-    light_ref[...] = jnp.zeros_like(light_ref)
     wait_all(copies)
-    all_light(light_ref, power_ref, info_at, tall, blocks * LANES, slots, length)
-    inside_row = jnp.where(lax.axis_index("row") < lax.axis_size("row") - 1, 1.0, 0.0).astype(jnp.float32)
-    inside_col = jnp.where(lax.axis_index("col") < lax.axis_size("col") - 1, 1.0, 0.0).astype(jnp.float32)
+    add_tiles(light_ref, power_ref, info_at, range(3, 9), tall, blocks * LANES, slots, length)
     even = parity("row") == 0
+
+    def rows_of(part, index):
+        return part[index * length : (index + 1) * length]
+
+    def from_above(index):
+        return jnp.where(even, rows_of(from_outer, index), rows_of(from_inner, index))
+
+    def from_below(index):
+        return jnp.where(even, rows_of(from_inner, index), rows_of(from_outer, index))
+
     for block in range(blocks + 1):
-        for piece, start, stop in ((0, 0, length), (1, length, tall), (2, tall, high)):
-            light = light_ref[block + 1, start + length : stop + length, :]
-            scale = STEP_SIZE / (light + REGULARIZER)
-            if piece == 2:
-                scale = scale * inside_row
-            if block == blocks:
-                scale = scale * inside_col
-            for channel in range(2):
-                total = total_ref[block, channel * high + start : channel * high + stop]
-                rows = slice((2 * block + channel) * length, (2 * block + channel + 1) * length)
-                if piece == 0:
-                    total = total + jnp.where(even, from_outer[rows], from_inner[rows])
-                if piece == 2:
-                    total = total + jnp.where(even, from_inner[rows], from_outer[rows])
-                new_ref[channel, block, start:stop, :] = ext_ref[channel, block, start:stop, :] - scale * total
-    for channel in range(2):
-        tile_out[channel] = new_ref[channel, :blocks, :tall, :]
+        inside = inside_mesh("col") if block == blocks else None
+        update_rows(new_ref, ext_ref, light_ref, total_ref, from_above, block, 0, length, length, inside)
+        last = inside_mesh("row") if inside is None else inside * inside_mesh("row")
+        update_rows(new_ref, ext_ref, light_ref, total_ref, from_below, block, tall, high, length, last)
+
+
+def patch_kernel(ext_ref, info_ref, patches_out, info_at, sems):
+    copies = start_all([(info_ref, info_at.at[0])], sems)
+    slots, _, length, _ = patches_out.shape
+    wait_all(copies)
     for s in range(slots):
         row, col, _ = slot_place(info_at, 0, s, slots)
         for channel in range(2):
-            patches_out[s, channel] = take_patch(new_ref, channel, row, col, length)
+            patches_out[s, channel] = take_patch(ext_ref, channel, row, col, length)
 
 
 def assemble_probe(half_ref, other_ref, side):
@@ -387,7 +419,7 @@
 
 def second_kernel(
     patches_ref, half_ref, other_ref, measured_ref, tables_ref, info_ref,
-    keep_ref, send_ref, left_out, middle_out, right_out, dep_ref, sum_ref, info_at, sems,
+    keep_ref, send_ref, body_out, bottom_out, dep_ref, sum_ref, info_at, sems,
 ):
     copies = start_all([(info_ref, info_at.at[0])], sems)
     slots = measured_ref.shape[0]
@@ -401,9 +433,12 @@
         patches, probe_real, probe_imag, measured_ref, tables_ref, weights, slots, length
     )
     finish_terms(patches, updates, probe_real, probe_imag, places, keep_ref, send_ref, dep_ref, sum_ref, length)
-    left_out[...] = dep_ref[0]
-    middle_out[...] = dep_ref[1]
-    right_out[...] = dep_ref[2]
+    high = dep_ref.shape[1] // 2
+    tall = body_out.shape[1] // 2
+    for channel in range(2):
+        start = channel * high
+        body_out[:, channel * tall : (channel + 1) * tall] = dep_ref[:, start : start + tall, :]
+        bottom_out[:, channel * length : (channel + 1) * length] = dep_ref[:, start + tall : start + high, :]
 
 
 def light_kernel(slots, infos_ref, half_ref, other_ref, light_out, light_ref, power_ref, info_at, sems):
@@ -415,34 +450,35 @@
     power_ref[...] = probe_real * probe_real + probe_imag * probe_imag
     light_ref[...] = jnp.zeros_like(light_ref)
     wait_all(copies)
-    all_light(light_ref, power_ref, info_at, tall, blocks * LANES, slots, length)
+    add_tiles(light_ref, power_ref, info_at, range(9), tall, blocks * LANES, slots, length)
     light_out[...] = STEP_SIZE / (light_ref[1 : 1 + blocks, length : length + tall, :] + REGULARIZER)
 
 
-def push_kernel(left_ref, middle_ref, from_left, left_out, bottom_out):
-    size = middle_ref.shape[0]
-    high = size // 2
-    length = bottom_out.shape[1] // 2
-    tall = high - length
-    left_out[...] = left_ref[...] + from_left[...]
-    for block, part in enumerate((left_out, middle_ref)):
-        for channel in range(2):
-            bottom_out[block, channel * length : (channel + 1) * length] = part[
-                channel * high + tall : (channel + 1) * high
-            ]
-
-
-def final_kernel(tile_ref, light_ref, left_ref, middle_ref, from_above, half_ref, other_ref, object_out, probe_out):
-    tall = tile_ref.shape[2]
+def push_kernel(body_ref, from_above, right_out):
+    tall = body_ref.shape[1] // 2
     length = from_above.shape[1] // 2
-    high = tall + length
-    for block, part in enumerate((left_ref, middle_ref)):
+    last = body_ref.shape[0] - 1
+    for channel in range(2):
+        start = channel * tall
+        right_out[start : start + length] = (
+            body_ref[last, start : start + length] + from_above[last, channel * length : (channel + 1) * length]
+        )
+        right_out[start + length : start + tall] = body_ref[last, start + length : start + tall]
+
+
+def final_kernel(tile_ref, light_ref, body_ref, from_above, from_left, half_ref, other_ref, object_out, probe_out):
+    tall = body_ref.shape[1] // 2
+    length = from_above.shape[1] // 2
+    for block in range(light_ref.shape[0]):
         lanes = slice(block * LANES, (block + 1) * LANES)
         for channel in range(2):
             for start, stop in ((0, length), (length, tall)):
-                total = part[channel * high + start : channel * high + stop]
+                rows = slice(channel * tall + start, channel * tall + stop)
+                total = body_ref[block, rows]
                 if start == 0:
                     total = total + from_above[block, channel * length : (channel + 1) * length]
+                if block == 0:
+                    total = total + from_left[rows]
                 object_out[channel, start:stop, lanes] = (
                     tile_ref[channel, block, start:stop, :] - light_ref[block, start:stop, :] * total
                 )
@@ -586,25 +622,36 @@
     )
     part = keep + flip(send, "row", 1)
     part = quad(part, "row", 2)
+    ext, light = call(
+        functools.partial(near_light_kernel, slots, tall),
+        [extended, padded],
+        [(length, length)] + info_space(3),
+        [ext, infos, probe_now, total],
+        aliases={0: 0},
+    )
     part, inner, outer = tie(part, inner, outer)
     from_inner = swap(inner, "row", 0)
     from_outer = swap(outer, "row", 1)
     part = butterfly(part, "col", 1, last_col)
-    part, from_inner = tie(part, from_inner)
+    part, from_inner, light = tie(part, from_inner, light)
     part = butterfly(part, "col", last_col)
     new_half = stepped(own, part)
-    tile, patches, infos = call(
-        object_kernel,
-        [(2, blocks, tall, LANES), (slots, 2, length, length), (9, INFO, LANES)],
-        [extended, padded, (length, length)] + info_space(9),
-        [ext, probe_now, total, infos, from_inner, from_outer],
-    )
-    new_half, patches = tie(new_half, patches)
+    tile, _, infos = call(
+        functools.partial(object_kernel, slots),
+        [extended, padded, (9, INFO, LANES)],
+        [(length, length)] + info_space(9),
+        [ext, light, probe_now, total, infos, from_inner, from_outer],
+        aliases={0: 0, 1: 1},
+    )
+    new_half, tile = tie(new_half, tile)
+    (patches,) = call(patch_kernel, [(slots, 2, length, length)], info_space(1), [tile, info])
     new_other = flip(new_half, "row", 1)
 
-    keep, send, left, middle, right = call(
+    body_shape = (blocks + 1, 2 * tall, LANES)
+    bottom_shape = (blocks + 1, 2 * length, LANES)
+    keep, send, body, bottom = call(
         second_kernel,
-        [partial, partial, (size, LANES), (size, LANES), (size, LANES)],
+        [partial, partial, body_shape, bottom_shape],
         deposits,
         [patches, new_half, new_other, measured, tables, info],
     )
@@ -615,24 +662,21 @@
         [padded, (length, length)] + info_space(9),
         [infos, new_half, new_other],
     )
+    from_above = shift(bottom, "row", 1)
+    (right,) = call(push_kernel, [(2 * tall, LANES)], [], [body, from_above])
+    part = keep + flip(send, "row", 1)
+    part = butterfly(part, "col", 1, last_col)
+    part = butterfly(part, "col", last_col)
     from_left = shift(right, "col", 1)
-    part = keep + flip(send, "row", 1)
     part = butterfly(part, "row", 2, last_row)
     part = butterfly(part, "row", last_row)
-    part, light = tie(part, light)
-    left, bottom = call(
-        push_kernel, [(size, LANES), (blocks, 2 * length, LANES)], [], [left, middle, from_left]
-    )
-    from_above = shift(bottom, "row", 1)
-    part = butterfly(part, "col", 1, last_col)
-    part = butterfly(part, "col", last_col)
     last_half = stepped(new_half, part)
     last_other = flip(last_half, "row", 1)
     return call(
         final_kernel,
         [(2, tall, wide), (2, length, length)],
         [],
-        [tile, light, left, middle, from_above, last_half, last_other],
+        [tile, light, body, from_above, from_left, last_half, last_other],
     )
 
 

time: 81.9 us -> 80.5 us (0.983)
  waiting for transfers between devices: 25.5 us -> 20.4 us
  starting transfers between devices: 36.8 us -> 39.4 us
  Pallas kernels: 11.9 us -> 13.3 us
    ppermute x13, starting transfers between devices: 23.1 us -> 28.9 us  [flip(): lax.ppermute(value, axis, [(source, source ^ mask) for source in range(co...]
    ppermute x13, waiting for transfers between devices: 21.2 us -> 15.8 us  [flip(): lax.ppermute(value, axis, [(source, source ^ mask) for source in range(co...]
    ppermute x4, starting transfers between devices: 9.38 us -> 6.23 us  [shift(): return lax.ppermute(value, axis, pairs)]
    pallas_call x9 -> x11, Pallas kernels: 11.9 us -> 13.3 us  [call(): pl.pallas_call(kernel, out_shape=[shape_of(spec) for spec in outs], in_sp...]
  transfers between devices with their start and end apart: 22 -> 22, of which waited for: 12 -> 13; matrix products, arithmetic and copies ran while one was open for 0% -> 0% of each run, Pallas kernels for 7% -> 8%
where the time goes in v5:
time: 80.5 us; the launch traced here: 80.1 us
  starting transfers between devices  39.4 us (49%)
  waiting for transfers between devices  20.4 us (25%)
  Pallas kernels  13.3 us (17%)
  local copies, waits for them, and re-layouts  5.23 us (6%)
  between operations  1.54 us (2%)
    ppermute x13, starting transfers between devices, flip(): lax.ppermute(value, axis, [(source, source ^ mask) for source in range(co...  28.9 us
    ppermute x13, waiting for transfers between devices, flip(): lax.ppermute(value, axis, [(source, source ^ mask) for source in range(co...  15.8 us
    pallas_call x11, Pallas kernels, call(): pl.pallas_call(kernel, out_shape=[shape_of(spec) for spec in outs], in_sp...  13.3 us
    ppermute x4, starting transfers between devices, shift(): return lax.ppermute(value, axis, pairs)  6.23 us
    unnamed x12, local copies, waits for them, and re-layouts  5.23 us
    ppermute x1, waiting for transfers between devices, local(): lax.ppermute(corner, ('row', 'col'), [((r + 1) * count_cols + c + 1, r *...  3.22 us
    ppermute x4, starting transfers between devices, swap(): return lax.ppermute(value, axis, pairs)  3.01 us
  transfers between devices with their start and end apart: 22, of which 13 were waited for; matrix products, arithmetic and copies ran while one was open for 0% of the time, Pallas kernels for 8%

profile of v5, /device:TPU:0, one launch (start us, length us, event | category | flops | bytes accessed | tf_op | source)
XLA Modules:
  0.0 80.1 jit_solution(10117811178016140137)
XLA Ops:
  0.6 0.0 copy-start
  0.6 1.0 %copy-done = f32[2,256,256]{2,1,0:T(8,128)S(1)} copy-done((f32[2,256,256]{2,1,0:T(8,128)S(1)}, f32[2,256,256]{2,1,0:T(8,128)}, u32[]{:S(2)}) %copy-start) | copy-done | bytes 524312
  1.7 0.2 shard_map.87
  1.8 1.3 %collective-permute-start = (f32[2,256,128]{2,1,0:T(8,128)S(1)}, f32[2,256,128]{2,1,0:T(8,128)S(1)}, u32[]{:S(2)}, u32[]{:S(2)}) collective-permute-start(f32[2,256,128]{2,1,0:T(8,128)S(1)} %get-tuple-element.39), channel_id=1, source_target_pairs={{1,0},{2,1},{3,2},{5,4},{6,5},{7,6},{9,8},{10,9},{11,10},{13,12},{... | collective-permute-start | bytes 786440 | tf_op jit(solution)/shard_map/ppermute | solution.py:491
  3.1 1.3 %collective-permute-start.1 = (f32[2,128,256]{2,1,0:T(8,128)S(1)}, f32[2,128,256]{2,1,0:T(8,128)S(1)}, u32[]{:S(2)}, u32[]{:S(2)}) collective-permute-start(f32[2,128,256]{2,1,0:T(8,128)S(1)} %get-tuple-element.40), channel_id=1, source_target_pairs={{4,0},{8,4},{12,8},{16,12},{20,16},{24,20},{28,24},{5,1},{9,5},{13... | collective-permute-start | bytes 786440 | tf_op jit(solution)/shard_map/ppermute | solution.py:491
  4.4 1.3 %collective-permute-start.2 = (f32[2,128,128]{2,1,0:T(8,128)S(1)}, f32[2,128,128]{2,1,0:T(8,128)S(1)}, u32[]{:S(2)}, u32[]{:S(2)}) collective-permute-start(f32[2,128,128]{2,1,0:T(8,128)S(1)} %get-tuple-element.41), channel_id=1, source_target_pairs={{5,0},{6,1},{7,2},{9,4},{10,5},{11,6},{13,8},{14,9},{15,10},{17,12... | collective-permute-start | bytes 393224 | tf_op jit(solution)/shard_map/ppermute | solution.py:590
  6.4 0.0 copy-start.1
  6.4 1.0 %copy-done.1 = bf16[4,256,256]{2,1,0:T(8,128)(2,1)S(1)} copy-done((bf16[4,256,256]{2,1,0:T(8,128)(2,1)S(1)}, bf16[4,256,256]{2,1,0:T(8,128)(2,1)}, u32[]{:S(2)}) %copy-start.1) | copy-done | bytes 524312
  7.4 0.0 copy-start.2
  7.4 0.9 %copy-done.2 = s32[1,1,4,128,128]{4,3,2,1,0:T(8,128)S(1)} copy-done((s32[1,1,4,128,128]{4,3,2,1,0:T(8,128)S(1)}, s32[1,1,4,128,128]{4,3,2,1,0:T(8,128)}, u32[]{:S(2)}) %copy-start.2) | copy-done | bytes 262168
  8.4 0.0 copy-start.3
  8.4 0.9 %copy-done.3 = f32[2,128,128]{2,1,0:T(8,128)S(1)} copy-done((f32[2,128,128]{2,1,0:T(8,128)S(1)}, f32[2,128,128]{2,1,0:T(8,128)}, u32[]{:S(2)}) %copy-start.3) | copy-done | bytes 131096
  9.3 0.7 copy-done.4
  9.9 0.7 copy-done.5
  10.6 0.6 shard_map.86
  11.2 3.2 %collective-permute-done.2.corner_ref = f32[2,128,128]{2,1,0:T(8,128)S(1)} collective-permute-done((f32[2,128,128]{2,1,0:T(8,128)S(1)}, f32[2,128,128]{2,1,0:T(8,128)S(1)}, u32[]{:S(2)}, u32[]{:S(2)}) %collective-permute-start.2) | collective-permute-done | bytes 131104 | tf_op jit(solution)/shard_map/ppermute | solution.py:590
  14.5 0.0 collective-permute-done.right_ref
  14.5 0.0 collective-permute-done.1.below_ref
  14.5 2.7 %shard_map.88 = (f32[2,3,384,128]{3,2,1,0:T(8,128)S(1)}, f32[3,64,128]{2,1,0:T(8,128)S(1)}, f32[3,64,128]{2,1,0:T(8,128)S(1)}, f32[776,128]{1,0:T(8,128)S(1)}, f...) custom-call(f32[2,3,384,128]{3,2,1,0:T(8,128)S(1)} %get-tuple-element.38.start_ref, ...), custom_call_target="tpu_custom_call", output_to_operand_aliasing={{0}: (0, {})} | custom-call | tf_op jit(solution)/shard_map/pallas_call | solution.py:538
  17.2 2.4 %collective-permute-start.3 = (f32[3,64,128]{2,1,0:T(8,128)S(1)}, f32[3,64,128]{2,1,0:T(8,128)S(1)}, u32[]{:S(2)}, u32[]{:S(2)}) collective-permute-start(f32[3,64,128]{2,1,0:T(8,128)S(1)} %get-tuple-element.47), channel_id=1, source_target_pairs={{0,4},{4,0},{8,12},{12,8},{16,20},{20,16},{24,28},{28,24},{1,5},{5... | collective-permute-start | bytes 294920 | tf_op jit(solution)/shard_map/ppermute | solution.py:504
  19.6 1.6 %collective-permute-start.7 = (f32[776,128]{1,0:T(8,128)S(1)}, f32[776,128]{1,0:T(8,128)S(1)}, u32[]{:S(2)}, u32[]{:S(2)}) collective-permute-start(f32[776,128]{1,0:T(8,128)S(1)} %get-tuple-element.48.inner_ref), channel_id=1, source_target_pairs={{0,1},{1,0},{2,3},{3,2},{4,5},{5,4},{6,7},{7,6},{8,9},{9,8},{10,11... | collective-permute-start | bytes 1191944 | tf_op jit(solution)/shard_map/ppermute | solution.py:499
  21.2 0.7 collective-permute-start.8
  21.9 0.0 collective-permute-done.3
  21.9 1.6 %collective-permute-start.5 = (f32[3,64,128]{2,1,0:T(8,128)S(1)}, f32[3,64,128]{2,1,0:T(8,128)S(1)}, u32[]{:S(2)}, u32[]{:S(2)}) collective-permute-start(f32[3,64,128]{2,1,0:T(8,128)S(1)} %add.41), channel_id=1, source_target_pairs={{0,16},{4,20},{8,24},{12,28},{16,0},{20,4},{24,8},{28,12},{1,17},{... | collective-permute-start | bytes 294920 | tf_op jit(solution)/shard_map/ppermute | solution.py:504
  23.5 1.4 %collective-permute-start.6 = (f32[3,64,128]{2,1,0:T(8,128)S(1)}, f32[3,64,128]{2,1,0:T(8,128)S(1)}, u32[]{:S(2)}, u32[]{:S(2)}) collective-permute-start(f32[3,64,128]{2,1,0:T(8,128)S(1)} %add.41), channel_id=1, source_target_pairs={{0,24},{4,28},{8,16},{12,20},{16,8},{20,12},{24,0},{28,4},{1,25},{... | collective-permute-start | bytes 294920 | tf_op jit(solution)/shard_map/ppermute | solution.py:504
  24.9 0.5 collective-permute-start.4
  25.4 1.7 %collective-permute-done.5 = f32[3,64,128]{2,1,0:T(8,128)S(1)} collective-permute-done((f32[3,64,128]{2,1,0:T(8,128)S(1)}, f32[3,64,128]{2,1,0:T(8,128)S(1)}, u32[]{:S(2)}, u32[]{:S(2)}) %collective-permute-start.5) | collective-permute-done | bytes 98336 | tf_op jit(solution)/shard_map/ppermute | solution.py:504
  27.1 2.6 %collective-permute-done.6 = f32[3,64,128]{2,1,0:T(8,128)S(1)} collective-permute-done((f32[3,64,128]{2,1,0:T(8,128)S(1)}, f32[3,64,128]{2,1,0:T(8,128)S(1)}, u32[]{:S(2)}, u32[]{:S(2)}) %collective-permute-start.6) | collective-permute-done | bytes 98336 | tf_op jit(solution)/shard_map/ppermute | solution.py:504
  29.7 0.2 collective-permute-done.4
  29.9 0.9 %collective-permute-done.7.from_inner = f32[776,128]{1,0:T(8,128)S(1)} collective-permute-done((f32[776,128]{1,0:T(8,128)S(1)}, f32[776,128]{1,0:T(8,128)S(1)}, u32[]{:S(2)}, u32[]{:S(2)}) %collective-permute-start.7) | collective-permute-done | bytes 397344 | tf_op jit(solution)/shard_map/ppermute | solution.py:499
  30.8 0.0 collective-permute-done.8.from_outer
  30.8 0.2 shard_map.89
  31.0 0.1 collective-permute-start.10
  31.0 0.7 collective-permute-start.12
  31.7 3.7 %collective-permute-start.9 = (f32[3,64,128]{2,1,0:T(8,128)S(1)}, f32[3,64,128]{2,1,0:T(8,128)S(1)}, u32[]{:S(2)}, u32[]{:S(2)}) collective-permute-start(f32[3,64,128]{2,1,0:T(8,128)S(1)} %add_add_fusion), channel_id=1, source_target_pairs={{0,1},{1,0},{2,3},{3,2},{4,5},{5,4},{6,7},{7,6},{8,9},{9,8},{10,11... | collective-permute-start | bytes 294920 | tf_op jit(solution)/shard_map/ppermute | solution.py:504
  35.4 1.1 %shard_map.90 = (f32[2,3,384,128]{3,2,1,0:T(8,128)S(1)}, f32[5,640,128]{2,1,0:T(8,128)S(1)}) custom-call(f32[2,3,384,128]{3,2,1,0:T(8,128)S(1)} %get-tuple-element.55.ext_ref, f32[3,8,128]{2,1,0:T(8,128)S(1)} %get-tuple-element.56.infos_ref, f32[2,128,128]{2,1,0:T(8,128)S(1)} %get-tuple-element.42.probe_ref, ...), custom_call_target="tpu_custom_call", output_to_operand_aliasing={{0}: (0, {})} | custom-call | tf_op jit(solution)/shard_map/pallas_call | solution.py:538
  36.5 1.5 %collective-permute-done.9 = f32[3,64,128]{2,1,0:T(8,128)S(1)} collective-permute-done((f32[3,64,128]{2,1,0:T(8,128)S(1)}, f32[3,64,128]{2,1,0:T(8,128)S(1)}, u32[]{:S(2)}, u32[]{:S(2)}) %collective-permute-start.9) | collective-permute-done | bytes 98336 | tf_op jit(solution)/shard_map/ppermute | solution.py:504
  38.0 0.0 collective-permute-done.10.from_inner
  38.1 2.9 %collective-permute-start.11 = (f32[3,64,128]{2,1,0:T(8,128)S(1)}, f32[3,64,128]{2,1,0:T(8,128)S(1)}, u32[]{:S(2)}, u32[]{:S(2)}) collective-permute-start(f32[3,64,128]{2,1,0:T(8,128)S(1)} %add.45), channel_id=1, source_target_pairs={{0,2},{1,3},{2,0},{3,1},{4,6},{5,7},{6,4},{7,5},{8,10},{9,11},{10,... | collective-permute-start | bytes 294920 | tf_op jit(solution)/shard_map/ppermute | solution.py:504
  41.0 0.0 collective-permute-done.12.from_outer
  41.0 2.2 %shard_map.91 = (f32[2,3,384,128]{3,2,1,0:T(8,128)S(1)}, f32[5,640,128]{2,1,0:T(8,128)S(1)}, f32[9,8,128]{2,1,0:T(8,128)S(1)}) custom-call(f32[2,3,384,128]{3,2,1,0:T(8,128)S(1)} %get-tuple-element.60.ext_ref, f32[5,640,128]{2,1,0:T(8,128)S(1)} %get-tuple-element.61.light_in, ...), custom_call_target="tpu_custom_call", output_to_operand_aliasing={{0}: (0, {}), {1}: (1, {})} | custom-call | tf_op jit(solution)/shard_map/pallas_call | solution.py:538
  43.2 0.4 collective-permute-done.11
  43.7 3.4 %collective-permute-start.13 = (f32[2,64,128]{2,1,0:T(8,128)S(1)}, f32[2,64,128]{2,1,0:T(8,128)S(1)}, u32[]{:S(2)}, u32[]{:S(2)}) collective-permute-start(f32[2,64,128]{2,1,0:T(8,128)S(1)} %fusion.1.half_ref), channel_id=1, source_target_pairs={{0,4},{4,0},{8,12},{12,8},{16,20},{20,16},{24,28},{28,24},{1,5},{5... | collective-permute-start | bytes 196616 | tf_op jit(solution)/shard_map/ppermute | solution.py:504
  47.1 1.0 %shard_map.93.patches_ref = f32[4,2,128,128]{3,2,1,0:T(8,128)S(1)} custom-call(f32[2,3,384,128]{3,2,1,0:T(8,128)S(1)} %get-tuple-element.65.ext_ref.tile_ref, f32[8,128]{1,0:T(8,128)S(1)} %get-tuple-element.45.info_ref), custom_call_target="tpu_custom_call" | custom-call | tf_op jit(solution)/shard_map/pallas_call | solution.py:538
  48.1 0.0 collective-permute-done.13.other_ref
  48.1 2.6 %shard_map.94 = (f32[3,64,128]{2,1,0:T(8,128)S(1)}, f32[3,64,128]{2,1,0:T(8,128)S(1)}, f32[3,512,128]{2,1,0:T(8,128)S(1)}, f32[3,256,128]{2,1,0:T(8,128)S(1)}) custom-call(f32[4,2,128,128]{3,2,1,0:T(8,128)S(1)} %shard_map.93.patches_ref, f32[2,64,128]{2,1,0:T(8,128)S(1)} %fusion.1.half_ref, f32[2,64,128]{2,1,0:T(8,128)S(1)} %collective-permute-done.13.other_ref, ...), custom_call_target="tpu_custom_call" | custom-call | tf_op jit(solution)/shard_map/pallas_call | solution.py:538
  50.7 0.3 collective-permute-start.16
  51.1 1.0 %collective-permute-done.16 = f32[3,64,128]{2,1,0:T(8,128)S(1)} collective-permute-done((f32[3,64,128]{2,1,0:T(8,128)S(1)}, f32[3,64,128]{2,1,0:T(8,128)S(1)}, u32[]{:S(2)}, u32[]{:S(2)}) %collective-permute-start.16) | collective-permute-done | bytes 98336 | tf_op jit(solution)/shard_map/ppermute | solution.py:504
  52.1 2.5 %collective-permute-start.17 = (f32[3,64,128]{2,1,0:T(8,128)S(1)}, f32[3,64,128]{2,1,0:T(8,128)S(1)}, u32[]{:S(2)}, u32[]{:S(2)}) collective-permute-start(f32[3,64,128]{2,1,0:T(8,128)S(1)} %add.48), channel_id=1, source_target_pairs={{0,1},{1,0},{2,3},{3,2},{4,5},{5,4},{6,7},{7,6},{8,9},{9,8},{10,11... | collective-permute-start | bytes 294920 | tf_op jit(solution)/shard_map/ppermute | solution.py:504
  54.6 1.9 %collective-permute-start.14 = (f32[3,256,128]{2,1,0:T(8,128)S(1)}, f32[3,256,128]{2,1,0:T(8,128)S(1)}, u32[]{:S(2)}, u32[]{:S(2)}) collective-permute-start(f32[3,256,128]{2,1,0:T(8,128)S(1)} %get-tuple-element.69), channel_id=1, source_target_pairs={{0,4},{4,8},{8,12},{12,16},{16,20},{20,24},{24,28},{1,5},{5,9},{9,... | collective-permute-start | bytes 1179656 | tf_op jit(solution)/shard_map/ppermute | solution.py:491
  56.5 1.3 %collective-permute-done.17 = f32[3,64,128]{2,1,0:T(8,128)S(1)} collective-permute-done((f32[3,64,128]{2,1,0:T(8,128)S(1)}, f32[3,64,128]{2,1,0:T(8,128)S(1)}, u32[]{:S(2)}, u32[]{:S(2)}) %collective-permute-start.17) | collective-permute-done | bytes 98336 | tf_op jit(solution)/shard_map/ppermute | solution.py:504
  57.8 2.5 %collective-permute-start.18 = (f32[3,64,128]{2,1,0:T(8,128)S(1)}, f32[3,64,128]{2,1,0:T(8,128)S(1)}, u32[]{:S(2)}, u32[]{:S(2)}) collective-permute-start(f32[3,64,128]{2,1,0:T(8,128)S(1)} %add.49), channel_id=1, source_target_pairs={{0,2},{1,3},{2,0},{3,1},{4,6},{5,7},{6,4},{7,5},{8,10},{9,11},{10,... | collective-permute-start | bytes 294920 | tf_op jit(solution)/shard_map/ppermute | solution.py:504
  60.3 3.1 %collective-permute-done.18 = f32[3,64,128]{2,1,0:T(8,128)S(1)} collective-permute-done((f32[3,64,128]{2,1,0:T(8,128)S(1)}, f32[3,64,128]{2,1,0:T(8,128)S(1)}, u32[]{:S(2)}, u32[]{:S(2)}) %collective-permute-start.18) | collective-permute-done | bytes 98336 | tf_op jit(solution)/shard_map/ppermute | solution.py:504
  63.4 5.9 %collective-permute-start.19 = (f32[3,64,128]{2,1,0:T(8,128)S(1)}, f32[3,64,128]{2,1,0:T(8,128)S(1)}, u32[]{:S(2)}, u32[]{:S(2)}) collective-permute-start(f32[3,64,128]{2,1,0:T(8,128)S(1)} %add.50), channel_id=1, source_target_pairs={{0,8},{4,12},{8,0},{12,4},{16,24},{20,28},{24,16},{28,20},{1,9},{5... | collective-permute-start | bytes 294920 | tf_op jit(solution)/shard_map/ppermute | solution.py:504
  69.4 2.6 %collective-permute-done.19 = f32[3,64,128]{2,1,0:T(8,128)S(1)} collective-permute-done((f32[3,64,128]{2,1,0:T(8,128)S(1)}, f32[3,64,128]{2,1,0:T(8,128)S(1)}, u32[]{:S(2)}, u32[]{:S(2)}) %collective-permute-start.19) | collective-permute-done | bytes 98336 | tf_op jit(solution)/shard_map/ppermute | solution.py:504
  72.0 1.5 %collective-permute-start.20 = (f32[3,64,128]{2,1,0:T(8,128)S(1)}, f32[3,64,128]{2,1,0:T(8,128)S(1)}, u32[]{:S(2)}, u32[]{:S(2)}) collective-permute-start(f32[3,64,128]{2,1,0:T(8,128)S(1)} %add.51), channel_id=1, source_target_pairs={{0,16},{4,20},{8,24},{12,28},{16,0},{20,4},{24,8},{28,12},{1,17},{... | collective-permute-start | bytes 294920 | tf_op jit(solution)/shard_map/ppermute | solution.py:504
  73.5 0.0 collective-permute-done.14.from_above
  73.6 1.7 %collective-permute-start.15 = (f32[512,128]{1,0:T(8,128)S(1)}, f32[512,128]{1,0:T(8,128)S(1)}, u32[]{:S(2)}, u32[]{:S(2)}) collective-permute-start(f32[512,128]{1,0:T(8,128)S(1)} %shard_map.95), channel_id=1, source_target_pairs={{0,1},{1,2},{2,3},{4,5},{5,6},{6,7},{8,9},{9,10},{10,11},{12,13},{... | collective-permute-start | bytes 786440 | tf_op jit(solution)/shard_map/ppermute | solution.py:491
  75.3 1.4 %collective-permute-done.20 = f32[3,64,128]{2,1,0:T(8,128)S(1)} collective-permute-done((f32[3,64,128]{2,1,0:T(8,128)S(1)}, f32[3,64,128]{2,1,0:T(8,128)S(1)}, u32[]{:S(2)}, u32[]{:S(2)}) %collective-permute-start.20) | collective-permute-done | bytes 98336 | tf_op jit(solution)/shard_map/ppermute | solution.py:504
  76.7 0.1 collective-permute-start.21
  76.8 1.8 %shard_map.92.light_ref = f32[2,256,128]{2,1,0:T(8,128)S(1)} custom-call(f32[9,8,128]{2,1,0:T(8,128)S(1)} %get-tuple-element.66.infos_ref, f32[2,64,128]{2,1,0:T(8,128)S(1)} %fusion.1.half_ref, f32[2,64,128]{2,1,0:T(8,128)S(1)} %collective-permute-done.13.other_ref), custom_call_target="tpu_custom_call" | custom-call | tf_op jit(solution)/shard_map/pallas_call | solution.py:538
  78.6 0.0 collective-permute-done.21.other_ref
  78.6 0.5 collective-permute-done.15.from_left
  79.1 1.0 %shard_map.96 = (f32[2,256,256]{2,1,0:T(8,128)}, f32[2,128,128]{2,1,0:T(8,128)}) custom-call(f32[2,3,384,128]{3,2,1,0:T(8,128)S(1)} %get-tuple-element.65.ext_ref.tile_ref, f32[2,256,128]{2,1,0:T(8,128)S(1)} %shard_map.92.light_ref, f32[3,512,128]{2,1,0:T(8,128)S(1)} %get-tuple-element.68.body_ref, f32[3,256,128]{2,1,0:T(8,128)S(1)} %collective-permute-done.14.from_above, ...), custom_call_target="tpu_custom_call" | custom-call | tf_op jit(solution)/shard_map/pallas_call | solution.py:538
  (16 shorter events, 0.2 us)
Async XLA Ops:
  0.6 1.0 %copy-start = (f32[2,256,256]{2,1,0:T(8,128)S(1)}, f32[2,256,256]{2,1,0:T(8,128)}, u32[]{:S(2)}) copy-start(f32[2,256,256]{2,1,0:T(8,128)} %field_ref.1) | copy-start | bytes 1572868
  1.8 12.6 %collective-permute-start = (f32[2,256,128]{2,1,0:T(8,128)S(1)}, f32[2,256,128]{2,1,0:T(8,128)S(1)}, u32[]{:S(2)}, u32[]{:S(2)}) collective-permute-start(f32[2,256,128]{2,1,0:T(8,128)S(1)} %get-tuple-element.39), channel_id=1, source_target_pairs={{1,0},{2,1},{3,2},{5,4},{6,5},{7,6},{9,8},{10,9},{11,10},{13,12},{... | collective-permute-start | bytes 786440 | tf_op jit(solution)/shard_map/ppermute | solution.py:491
  3.1 11.3 %collective-permute-start.1 = (f32[2,128,256]{2,1,0:T(8,128)S(1)}, f32[2,128,256]{2,1,0:T(8,128)S(1)}, u32[]{:S(2)}, u32[]{:S(2)}) collective-permute-start(f32[2,128,256]{2,1,0:T(8,128)S(1)} %get-tuple-element.40), channel_id=1, source_target_pairs={{4,0},{8,4},{12,8},{16,12},{20,16},{24,20},{28,24},{5,1},{9,5},{13... | collective-permute-start | bytes 786440 | tf_op jit(solution)/shard_map/ppermute | solution.py:491
  4.4 10.0 %collective-permute-start.2 = (f32[2,128,128]{2,1,0:T(8,128)S(1)}, f32[2,128,128]{2,1,0:T(8,128)S(1)}, u32[]{:S(2)}, u32[]{:S(2)}) collective-permute-start(f32[2,128,128]{2,1,0:T(8,128)S(1)} %get-tuple-element.41), channel_id=1, source_target_pairs={{5,0},{6,1},{7,2},{9,4},{10,5},{11,6},{13,8},{14,9},{15,10},{17,12... | collective-permute-start | bytes 393224 | tf_op jit(solution)/shard_map/ppermute | solution.py:590
  6.4 1.0 %copy-start.1 = (bf16[4,256,256]{2,1,0:T(8,128)(2,1)S(1)}, bf16[4,256,256]{2,1,0:T(8,128)(2,1)}, u32[]{:S(2)}) copy-start(bf16[4,256,256]{2,1,0:T(8,128)(2,1)} %constant.4.clone.tables_ref) | copy-start | bytes 1572868
  7.4 0.9 %copy-start.2 = (s32[1,1,4,128,128]{4,3,2,1,0:T(8,128)S(1)}, s32[1,1,4,128,128]{4,3,2,1,0:T(8,128)}, u32[]{:S(2)}) copy-start(s32[1,1,4,128,128]{4,3,2,1,0:T(8,128)} %param.9) | copy-start | bytes 786436
  8.4 0.9 %copy-start.3 = (f32[2,128,128]{2,1,0:T(8,128)S(1)}, f32[2,128,128]{2,1,0:T(8,128)}, u32[]{:S(2)}) copy-start(f32[2,128,128]{2,1,0:T(8,128)} %probe_ref.1) | copy-start | bytes 393220
  9.3 0.7 copy-start.4
  9.9 0.7 copy-start.5
  17.2 4.6 %collective-permute-start.3 = (f32[3,64,128]{2,1,0:T(8,128)S(1)}, f32[3,64,128]{2,1,0:T(8,128)S(1)}, u32[]{:S(2)}, u32[]{:S(2)}) collective-permute-start(f32[3,64,128]{2,1,0:T(8,128)S(1)} %get-tuple-element.47), channel_id=1, source_target_pairs={{0,4},{4,0},{8,12},{12,8},{16,20},{20,16},{24,28},{28,24},{1,5},{5... | collective-permute-start | bytes 294920 | tf_op jit(solution)/shard_map/ppermute | solution.py:504
  19.6 11.2 %collective-permute-start.7 = (f32[776,128]{1,0:T(8,128)S(1)}, f32[776,128]{1,0:T(8,128)S(1)}, u32[]{:S(2)}, u32[]{:S(2)}) collective-permute-start(f32[776,128]{1,0:T(8,128)S(1)} %get-tuple-element.48.inner_ref), channel_id=1, source_target_pairs={{0,1},{1,0},{2,3},{3,2},{4,5},{5,4},{6,7},{7,6},{8,9},{9,8},{10,11... | collective-permute-start | bytes 1191944 | tf_op jit(solution)/shard_map/ppermute | solution.py:499
  21.2 9.6 %collective-permute-start.8 = (f32[776,128]{1,0:T(8,128)S(1)}, f32[776,128]{1,0:T(8,128)S(1)}, u32[]{:S(2)}, u32[]{:S(2)}) collective-permute-start(f32[776,128]{1,0:T(8,128)S(1)} %get-tuple-element.50.outer_ref), channel_id=1, source_target_pairs={{1,2},{2,1},{5,6},{6,5},{9,10},{10,9},{13,14},{14,13},{17,18},{18,... | collective-permute-start | bytes 1191944 | tf_op jit(solution)/shard_map/ppermute | solution.py:499
  21.9 5.2 %collective-permute-start.5 = (f32[3,64,128]{2,1,0:T(8,128)S(1)}, f32[3,64,128]{2,1,0:T(8,128)S(1)}, u32[]{:S(2)}, u32[]{:S(2)}) collective-permute-start(f32[3,64,128]{2,1,0:T(8,128)S(1)} %add.41), channel_id=1, source_target_pairs={{0,16},{4,20},{8,24},{12,28},{16,0},{20,4},{24,8},{28,12},{1,17},{... | collective-permute-start | bytes 294920 | tf_op jit(solution)/shard_map/ppermute | solution.py:504
  23.5 6.2 %collective-permute-start.6 = (f32[3,64,128]{2,1,0:T(8,128)S(1)}, f32[3,64,128]{2,1,0:T(8,128)S(1)}, u32[]{:S(2)}, u32[]{:S(2)}) collective-permute-start(f32[3,64,128]{2,1,0:T(8,128)S(1)} %add.41), channel_id=1, source_target_pairs={{0,24},{4,28},{8,16},{12,20},{16,8},{20,12},{24,0},{28,4},{1,25},{... | collective-permute-start | bytes 294920 | tf_op jit(solution)/shard_map/ppermute | solution.py:504
  24.9 5.0 %collective-permute-start.4 = (f32[3,64,128]{2,1,0:T(8,128)S(1)}, f32[3,64,128]{2,1,0:T(8,128)S(1)}, u32[]{:S(2)}, u32[]{:S(2)}) collective-permute-start(f32[3,64,128]{2,1,0:T(8,128)S(1)} %add.41), channel_id=1, source_target_pairs={{0,8},{4,12},{8,0},{12,4},{16,24},{20,28},{24,16},{28,20},{1,9},{5... | collective-permute-start | bytes 294920 | tf_op jit(solution)/shard_map/ppermute | solution.py:504
  31.0 7.1 %collective-permute-start.10 = (f32[792,128]{1,0:T(8,128)S(1)}, f32[792,128]{1,0:T(8,128)S(1)}, u32[]{:S(2)}, u32[]{:S(2)}) collective-permute-start(f32[792,128]{1,0:T(8,128)S(1)} %get-tuple-element.54), channel_id=1, source_target_pairs={{0,4},{4,0},{8,12},{12,8},{16,20},{20,16},{24,28},{28,24},{1,5},{5... | collective-permute-start | bytes 1216520 | tf_op jit(solution)/shard_map/ppermute | solution.py:499
  31.0 10.0 %collective-permute-start.12 = (f32[792,128]{1,0:T(8,128)S(1)}, f32[792,128]{1,0:T(8,128)S(1)}, u32[]{:S(2)}, u32[]{:S(2)}) collective-permute-start(f32[792,128]{1,0:T(8,128)S(1)} %get-tuple-element.63), channel_id=1, source_target_pairs={{4,8},{8,4},{12,16},{16,12},{20,24},{24,20},{5,9},{9,5},{13,17},{1... | collective-permute-start | bytes 1216520 | tf_op jit(solution)/shard_map/ppermute | solution.py:499
  31.7 6.3 %collective-permute-start.9 = (f32[3,64,128]{2,1,0:T(8,128)S(1)}, f32[3,64,128]{2,1,0:T(8,128)S(1)}, u32[]{:S(2)}, u32[]{:S(2)}) collective-permute-start(f32[3,64,128]{2,1,0:T(8,128)S(1)} %add_add_fusion), channel_id=1, source_target_pairs={{0,1},{1,0},{2,3},{3,2},{4,5},{5,4},{6,7},{7,6},{8,9},{9,8},{10,11... | collective-permute-start | bytes 294920 | tf_op jit(solution)/shard_map/ppermute | solution.py:504
  38.1 5.6 %collective-permute-start.11 = (f32[3,64,128]{2,1,0:T(8,128)S(1)}, f32[3,64,128]{2,1,0:T(8,128)S(1)}, u32[]{:S(2)}, u32[]{:S(2)}) collective-permute-start(f32[3,64,128]{2,1,0:T(8,128)S(1)} %add.45), channel_id=1, source_target_pairs={{0,2},{1,3},{2,0},{3,1},{4,6},{5,7},{6,4},{7,5},{8,10},{9,11},{10,... | collective-permute-start | bytes 294920 | tf_op jit(solution)/shard_map/ppermute | solution.py:504
  43.7 4.4 %collective-permute-start.13 = (f32[2,64,128]{2,1,0:T(8,128)S(1)}, f32[2,64,128]{2,1,0:T(8,128)S(1)}, u32[]{:S(2)}, u32[]{:S(2)}) collective-permute-start(f32[2,64,128]{2,1,0:T(8,128)S(1)} %fusion.1.half_ref), channel_id=1, source_target_pairs={{0,4},{4,0},{8,12},{12,8},{16,20},{20,16},{24,28},{28,24},{1,5},{5... | collective-permute-start | bytes 196616 | tf_op jit(solution)/shard_map/ppermute | solution.py:504
  50.7 1.4 %collective-permute-start.16 = (f32[3,64,128]{2,1,0:T(8,128)S(1)}, f32[3,64,128]{2,1,0:T(8,128)S(1)}, u32[]{:S(2)}, u32[]{:S(2)}) collective-permute-start(f32[3,64,128]{2,1,0:T(8,128)S(1)} %get-tuple-element.71), channel_id=1, source_target_pairs={{0,4},{4,0},{8,12},{12,8},{16,20},{20,16},{24,28},{28,24},{1,5},{5... | collective-permute-start | bytes 294920 | tf_op jit(solution)/shard_map/ppermute | solution.py:504
  52.1 5.7 %collective-permute-start.17 = (f32[3,64,128]{2,1,0:T(8,128)S(1)}, f32[3,64,128]{2,1,0:T(8,128)S(1)}, u32[]{:S(2)}, u32[]{:S(2)}) collective-permute-start(f32[3,64,128]{2,1,0:T(8,128)S(1)} %add.48), channel_id=1, source_target_pairs={{0,1},{1,0},{2,3},{3,2},{4,5},{5,4},{6,7},{7,6},{8,9},{9,8},{10,11... | collective-permute-start | bytes 294920 | tf_op jit(solution)/shard_map/ppermute | solution.py:504
  54.6 19.0 %collective-permute-start.14 = (f32[3,256,128]{2,1,0:T(8,128)S(1)}, f32[3,256,128]{2,1,0:T(8,128)S(1)}, u32[]{:S(2)}, u32[]{:S(2)}) collective-permute-start(f32[3,256,128]{2,1,0:T(8,128)S(1)} %get-tuple-element.69), channel_id=1, source_target_pairs={{0,4},{4,8},{8,12},{12,16},{16,20},{20,24},{24,28},{1,5},{5,9},{9,... | collective-permute-start | bytes 1179656 | tf_op jit(solution)/shard_map/ppermute | solution.py:491
  57.8 5.6 %collective-permute-start.18 = (f32[3,64,128]{2,1,0:T(8,128)S(1)}, f32[3,64,128]{2,1,0:T(8,128)S(1)}, u32[]{:S(2)}, u32[]{:S(2)}) collective-permute-start(f32[3,64,128]{2,1,0:T(8,128)S(1)} %add.49), channel_id=1, source_target_pairs={{0,2},{1,3},{2,0},{3,1},{4,6},{5,7},{6,4},{7,5},{8,10},{9,11},{10,... | collective-permute-start | bytes 294920 | tf_op jit(solution)/shard_map/ppermute | solution.py:504
  63.4 8.5 %collective-permute-start.19 = (f32[3,64,128]{2,1,0:T(8,128)S(1)}, f32[3,64,128]{2,1,0:T(8,128)S(1)}, u32[]{:S(2)}, u32[]{:S(2)}) collective-permute-start(f32[3,64,128]{2,1,0:T(8,128)S(1)} %add.50), channel_id=1, source_target_pairs={{0,8},{4,12},{8,0},{12,4},{16,24},{20,28},{24,16},{28,20},{1,9},{5... | collective-permute-start | bytes 294920 | tf_op jit(solution)/shard_map/ppermute | solution.py:504
  72.0 4.7 %collective-permute-start.20 = (f32[3,64,128]{2,1,0:T(8,128)S(1)}, f32[3,64,128]{2,1,0:T(8,128)S(1)}, u32[]{:S(2)}, u32[]{:S(2)}) collective-permute-start(f32[3,64,128]{2,1,0:T(8,128)S(1)} %add.51), channel_id=1, source_target_pairs={{0,16},{4,20},{8,24},{12,28},{16,0},{20,4},{24,8},{28,12},{1,17},{... | collective-permute-start | bytes 294920 | tf_op jit(solution)/shard_map/ppermute | solution.py:504
  73.6 5.6 %collective-permute-start.15 = (f32[512,128]{1,0:T(8,128)S(1)}, f32[512,128]{1,0:T(8,128)S(1)}, u32[]{:S(2)}, u32[]{:S(2)}) collective-permute-start(f32[512,128]{1,0:T(8,128)S(1)} %shard_map.95), channel_id=1, source_target_pairs={{0,1},{1,2},{2,3},{4,5},{5,6},{6,7},{8,9},{9,10},{10,11},{12,13},{... | collective-permute-start | bytes 786440 | tf_op jit(solution)/shard_map/ppermute | solution.py:491
  76.7 1.9 %collective-permute-start.21 = (f32[2,64,128]{2,1,0:T(8,128)S(1)}, f32[2,64,128]{2,1,0:T(8,128)S(1)}, u32[]{:S(2)}, u32[]{:S(2)}) collective-permute-start(f32[2,64,128]{2,1,0:T(8,128)S(1)} %fusion.half_ref), channel_id=1, source_target_pairs={{0,4},{4,0},{8,12},{12,8},{16,20},{20,16},{24,28},{28,24},{1,5},{5... | collective-permute-start | bytes 196616 | tf_op jit(solution)/shard_map/ppermute | solution.py:504

commit v6 on v5

--- a/solution.py
+++ b/solution.py
@@ -49,7 +49,9 @@
 
 def left_table(table_high, table_low, values):
     high, low = split(values)
-    return dot(table_high, high) + (dot(table_low, high) + dot(table_high, low))
+    rows = table_high.shape[0]
+    both = dot(jnp.concatenate([table_high, table_low], axis=0), high)
+    return both[:rows] + (both[rows:] + dot(table_high, low))
 
 
 def parity(axis):
@@ -178,7 +180,7 @@
     return updates
 
 
-def finish_terms(patches, updates, probe_real, probe_imag, places, keep_ref, send_ref, dep_ref, sum_ref, length):
+def probe_sums(patches, updates, weights, keep_ref, send_ref, sum_ref, length):
     slots = len(patches)
     grad_real = jnp.zeros((length, length), jnp.float32)
     grad_imag = grad_real
@@ -187,7 +189,7 @@
         (patch_real, patch_imag), (back_real, back_imag) = patches[s], updates[s]
         grad_real += patch_real * back_real + patch_imag * back_imag
         grad_imag += patch_real * back_imag - patch_imag * back_real
-        light += places[s][2] * (patch_real * patch_real + patch_imag * patch_imag)
+        light += weights[s] * (patch_real * patch_real + patch_imag * patch_imag)
     sum_ref[0] = grad_real
     sum_ref[1] = grad_imag
     sum_ref[2] = light
@@ -195,9 +197,12 @@
     side = parity("row")
     keep_ref[...] = sum_ref[:, pl.ds(pl.multiple_of(side * half, half), half), :]
     send_ref[...] = sum_ref[:, pl.ds(pl.multiple_of((1 - side) * half, half), half), :]
+
+
+def deposit(updates, probe_real, probe_imag, places, dep_ref, length):
     dep_ref[...] = jnp.zeros_like(dep_ref)
     high = dep_ref.shape[1] // 2
-    for s in range(slots):
+    for s in range(len(updates)):
         back_real, back_imag = updates[s]
         row, col, _ = places[s]
         add_patch(dep_ref, row, col, probe_real * back_real + probe_imag * back_imag, length)
@@ -289,7 +294,8 @@
     updates = position_terms(
         patches, probe_real, probe_imag, measured_ref, tables_ref, weights, slots, length
     )
-    finish_terms(patches, updates, probe_real, probe_imag, places, keep_ref, send_ref, dep_ref, sum_ref, length)
+    probe_sums(patches, updates, weights, keep_ref, send_ref, sum_ref, length)
+    deposit(updates, probe_real, probe_imag, places, dep_ref, length)
     size = dep_ref.shape[1]
     middle_out[...] = dep_ref[1]
     split_sides(inner_out, outer_out, dep_ref)
@@ -359,38 +365,33 @@
 
 
 def object_kernel(
-    slots, ext_ref, light_in, probe_ref, total_ref, infos_ref, from_inner, from_outer,
-    new_ref, light_ref, info_out, power_ref, info_at, sems,
+    slots, outer, ext_ref, light_in, probe_ref, total_ref, strip_ref, new_ref, light_ref, info_out, power_ref, info_at, sems
 ):
     length = power_ref.shape[0]
     high = ext_ref.shape[2]
     tall = high - length
     blocks = ext_ref.shape[1] - 1
     edge = 6 * length
-    info_out[0:3] = infos_ref[...]
     for index in range(3):
-        info_out[3 + index] = from_inner[edge + index * INFO : edge + (index + 1) * INFO]
-        info_out[6 + index] = from_outer[edge + index * INFO : edge + (index + 1) * INFO]
-    copies = start_all([(info_out, info_at)], sems)
+        info_out[index] = strip_ref[edge + index * INFO : edge + (index + 1) * INFO]
+    copies = start_all([(info_out, info_at.at[pl.ds(3 + 3 * outer, 3)])], sems)
     power_ref[...] = probe_ref[0] * probe_ref[0] + probe_ref[1] * probe_ref[1]
+    side = parity("row")
+    below = side if outer else 1 - side
+    start = below * tall
+    inside_row = jnp.where(below == 1, inside_mesh("row"), 1.0)
     wait_all(copies)
-    add_tiles(light_ref, power_ref, info_at, range(3, 9), tall, blocks * LANES, slots, length)
-    even = parity("row") == 0
-
-    def rows_of(part, index):
-        return part[index * length : (index + 1) * length]
-
-    def from_above(index):
-        return jnp.where(even, rows_of(from_outer, index), rows_of(from_inner, index))
-
-    def from_below(index):
-        return jnp.where(even, rows_of(from_inner, index), rows_of(from_outer, index))
-
+    add_tiles(light_ref, power_ref, info_at, range(3 + 3 * outer, 6 + 3 * outer), tall, blocks * LANES, slots, length)
+    window = pl.ds(pl.multiple_of(start, 8), length)
     for block in range(blocks + 1):
-        inside = inside_mesh("col") if block == blocks else None
-        update_rows(new_ref, ext_ref, light_ref, total_ref, from_above, block, 0, length, length, inside)
-        last = inside_mesh("row") if inside is None else inside * inside_mesh("row")
-        update_rows(new_ref, ext_ref, light_ref, total_ref, from_below, block, tall, high, length, last)
+        light = light_ref[block + 1, pl.ds(pl.multiple_of(start + length, 8), length), :]
+        inside = inside_row * inside_mesh("col") if block == blocks else inside_row
+        scale = inside * (STEP_SIZE / (light + REGULARIZER))
+        for channel in range(2):
+            index = 2 * block + channel
+            total = total_ref[block, pl.ds(pl.multiple_of(start + channel * high, 8), length), :]
+            total = total + strip_ref[index * length : (index + 1) * length]
+            new_ref[channel, block, window, :] = ext_ref[channel, block, window, :] - scale * total
 
 
 def patch_kernel(ext_ref, info_ref, patches_out, info_at, sems):
@@ -419,7 +420,7 @@
 
 def second_kernel(
     patches_ref, half_ref, other_ref, measured_ref, tables_ref, info_ref,
-    keep_ref, send_ref, body_out, bottom_out, dep_ref, sum_ref, info_at, sems,
+    keep_ref, send_ref, updates_out, sum_ref, info_at, sems,
 ):
     copies = start_all([(info_ref, info_at.at[0])], sems)
     slots = measured_ref.shape[0]
@@ -427,12 +428,23 @@
     probe_real, probe_imag = assemble_probe(half_ref, other_ref, parity("row"))
     patches = [[patches_ref[s, channel] for channel in range(2)] for s in range(slots)]
     wait_all(copies)
-    places = [slot_place(info_at, 0, s, slots) for s in range(slots)]
-    weights = [place[2] for place in places]
+    weights = [slot_place(info_at, 0, s, slots)[2] for s in range(slots)]
     updates = position_terms(
         patches, probe_real, probe_imag, measured_ref, tables_ref, weights, slots, length
     )
-    finish_terms(patches, updates, probe_real, probe_imag, places, keep_ref, send_ref, dep_ref, sum_ref, length)
+    probe_sums(patches, updates, weights, keep_ref, send_ref, sum_ref, length)
+    for s in range(slots):
+        updates_out[s, 0], updates_out[s, 1] = updates[s]
+
+
+def deposit_kernel(updates_ref, half_ref, other_ref, info_ref, body_out, bottom_out, dep_ref, info_at, sems):
+    copies = start_all([(info_ref, info_at.at[0])], sems)
+    slots, _, length, _ = updates_ref.shape
+    probe_real, probe_imag = assemble_probe(half_ref, other_ref, parity("row"))
+    wait_all(copies)
+    places = [slot_place(info_at, 0, s, slots) for s in range(slots)]
+    updates = [(updates_ref[s, 0], updates_ref[s, 1]) for s in range(slots)]
+    deposit(updates, probe_real, probe_imag, places, dep_ref, length)
     high = dep_ref.shape[1] // 2
     tall = body_out.shape[1] // 2
     for channel in range(2):
@@ -441,8 +453,11 @@
         bottom_out[:, channel * length : (channel + 1) * length] = dep_ref[:, start + tall : start + high, :]
 
 
-def light_kernel(slots, infos_ref, half_ref, other_ref, light_out, light_ref, power_ref, info_at, sems):
-    copies = start_all([(infos_ref, info_at)], sems)
+def light_kernel(
+    slots, near_ref, inner_ref, outer_ref, half_ref, other_ref, light_out, light_ref, power_ref, info_at, sems
+):
+    parts = (near_ref, inner_ref, outer_ref)
+    copies = start_all([(part, info_at.at[pl.ds(3 * index, 3)]) for index, part in enumerate(parts)], sems)
     length = power_ref.shape[0]
     tall = light_out.shape[1]
     blocks = light_out.shape[0]
@@ -558,7 +573,7 @@
     count_rows, count_cols = lax.axis_size("row"), lax.axis_size("col")
 
     def info_space(tiles):
-        return [pltpu.SMEM((tiles, INFO, LANES), jnp.float32), pltpu.SemaphoreType.DMA((1,))]
+        return [pltpu.SMEM((tiles, INFO, LANES), jnp.float32), pltpu.SemaphoreType.DMA((3,))]
 
     extended = (2, blocks + 1, high, LANES)
     ext, right, below, corner = call(
@@ -632,39 +647,54 @@
     part, inner, outer = tie(part, inner, outer)
     from_inner = swap(inner, "row", 0)
     from_outer = swap(outer, "row", 1)
+    row_infos = []
+
+    def update(ext, light, strip, outer):
+        ext, light, info_rows = call(
+            functools.partial(object_kernel, slots, outer),
+            [extended, padded, (3, INFO, LANES)],
+            [(length, length)] + info_space(9),
+            [ext, light, probe_now, total, strip],
+            aliases={0: 0, 1: 1},
+        )
+        row_infos.append(info_rows)
+        return ext, light
+
     part = butterfly(part, "col", 1, last_col)
     part, from_inner, light = tie(part, from_inner, light)
+    ext, light = update(ext, light, from_inner, 0)
     part = butterfly(part, "col", last_col)
     new_half = stepped(own, part)
-    tile, _, infos = call(
-        functools.partial(object_kernel, slots),
-        [extended, padded, (9, INFO, LANES)],
-        [(length, length)] + info_space(9),
-        [ext, light, probe_now, total, infos, from_inner, from_outer],
-        aliases={0: 0, 1: 1},
-    )
+    tile, _ = update(ext, light, from_outer, 1)
     new_half, tile = tie(new_half, tile)
     (patches,) = call(patch_kernel, [(slots, 2, length, length)], info_space(1), [tile, info])
     new_other = flip(new_half, "row", 1)
 
     body_shape = (blocks + 1, 2 * tall, LANES)
     bottom_shape = (blocks + 1, 2 * length, LANES)
-    keep, send, body, bottom = call(
+    keep, send, updates = call(
         second_kernel,
-        [partial, partial, body_shape, bottom_shape],
-        deposits,
+        [partial, partial, (slots, 2, length, length)],
+        [(3, length, length)] + info_space(1),
         [patches, new_half, new_other, measured, tables, info],
+    )
+    body, bottom = call(
+        deposit_kernel,
+        [body_shape, bottom_shape],
+        [(blocks + 1, size, LANES)] + info_space(1),
+        [updates, new_half, new_other, info],
     )
     padded = (blocks + 2, tall + 2 * length, LANES)
     (light,) = call(
         functools.partial(light_kernel, slots),
         [(blocks, tall, LANES)],
         [padded, (length, length)] + info_space(9),
-        [infos, new_half, new_other],
+        [infos, *row_infos, new_half, new_other],
     )
     from_above = shift(bottom, "row", 1)
     (right,) = call(push_kernel, [(2 * tall, LANES)], [], [body, from_above])
     part = keep + flip(send, "row", 1)
+    part, bottom = tie(part, bottom)
     part = butterfly(part, "col", 1, last_col)
     part = butterfly(part, "col", last_col)
     from_left = shift(right, "col", 1)

time: 80.5 us -> 79.7 us (0.990)
  starting transfers between devices: 39.4 us -> 35.6 us
  waiting for transfers between devices: 20.4 us -> 22.2 us
  Pallas kernels: 13.3 us -> 14.2 us
    ppermute x13, starting transfers between devices: 28.9 us -> 25.1 us  [flip(): lax.ppermute(value, axis, [(source, source ^ mask) for source in range(co...]
    ppermute x13, waiting for transfers between devices: 15.8 us -> 17.7 us  [flip(): lax.ppermute(value, axis, [(source, source ^ mask) for source in range(co...]
    pallas_call x11 -> x13, Pallas kernels: 13.3 us -> 14.2 us  [call(): pl.pallas_call(kernel, out_shape=[shape_of(spec) for spec in outs], in_sp...]
  transfers between devices with their start and end apart: 22 -> 22, of which waited for: 13 -> 12; matrix products, arithmetic and copies ran while one was open for 0% -> 0% of each run, Pallas kernels for 8% -> 10%
where the time goes in v6:
time: 79.7 us; the launch traced here: 79 us
  starting transfers between devices  35.6 us (45%)
  waiting for transfers between devices  22.2 us (28%)
  Pallas kernels  14.2 us (18%)
  local copies, waits for them, and re-layouts  5.23 us (7%)
  between operations  1.57 us (2%)
    ppermute x13, starting transfers between devices, flip(): lax.ppermute(value, axis, [(source, source ^ mask) for source in range(co...  25.1 us
    ppermute x13, waiting for transfers between devices, flip(): lax.ppermute(value, axis, [(source, source ^ mask) for source in range(co...  17.7 us
    pallas_call x13, Pallas kernels, call(): pl.pallas_call(kernel, out_shape=[shape_of(spec) for spec in outs], in_sp...  14.2 us
    ppermute x4, starting transfers between devices, shift(): return lax.ppermute(value, axis, pairs)  6.26 us
    unnamed x12, local copies, waits for them, and re-layouts  5.23 us
    ppermute x1, waiting for transfers between devices, local(): lax.ppermute(corner, ('row', 'col'), [((r + 1) * count_cols + c + 1, r *...  3.22 us
    ppermute x4, starting transfers between devices, swap(): return lax.ppermute(value, axis, pairs)  3.03 us
  transfers between devices with their start and end apart: 22, of which 12 were waited for; matrix products, arithmetic and copies ran while one was open for 0% of the time, Pallas kernels for 10%

profile of v6, /device:TPU:0, one launch (start us, length us, event | category | flops | bytes accessed | tf_op | source)
XLA Modules:
  0.0 79.0 jit_solution(17911962019811819507)
XLA Ops:
  0.6 0.0 copy-start
  0.6 1.0 %copy-done = f32[2,256,256]{2,1,0:T(8,128)S(1)} copy-done((f32[2,256,256]{2,1,0:T(8,128)S(1)}, f32[2,256,256]{2,1,0:T(8,128)}, u32[]{:S(2)}) %copy-start) | copy-done | bytes 524312
  1.7 0.2 shard_map.87
  1.8 1.3 %collective-permute-start = (f32[2,256,128]{2,1,0:T(8,128)S(1)}, f32[2,256,128]{2,1,0:T(8,128)S(1)}, u32[]{:S(2)}, u32[]{:S(2)}) collective-permute-start(f32[2,256,128]{2,1,0:T(8,128)S(1)} %get-tuple-element.44), channel_id=1, source_target_pairs={{1,0},{2,1},{3,2},{5,4},{6,5},{7,6},{9,8},{10,9},{11,10},{13,12},{... | collective-permute-start | bytes 786440 | tf_op jit(solution)/shard_map/ppermute | solution.py:506
  3.1 1.3 %collective-permute-start.1 = (f32[2,128,256]{2,1,0:T(8,128)S(1)}, f32[2,128,256]{2,1,0:T(8,128)S(1)}, u32[]{:S(2)}, u32[]{:S(2)}) collective-permute-start(f32[2,128,256]{2,1,0:T(8,128)S(1)} %get-tuple-element.45), channel_id=1, source_target_pairs={{4,0},{8,4},{12,8},{16,12},{20,16},{24,20},{28,24},{5,1},{9,5},{13... | collective-permute-start | bytes 786440 | tf_op jit(solution)/shard_map/ppermute | solution.py:506
  4.4 1.3 %collective-permute-start.2 = (f32[2,128,128]{2,1,0:T(8,128)S(1)}, f32[2,128,128]{2,1,0:T(8,128)S(1)}, u32[]{:S(2)}, u32[]{:S(2)}) collective-permute-start(f32[2,128,128]{2,1,0:T(8,128)S(1)} %get-tuple-element.46), channel_id=1, source_target_pairs={{5,0},{6,1},{7,2},{9,4},{10,5},{11,6},{13,8},{14,9},{15,10},{17,12... | collective-permute-start | bytes 393224 | tf_op jit(solution)/shard_map/ppermute | solution.py:605
  6.4 0.0 copy-start.1
  6.4 1.0 %copy-done.1 = bf16[4,256,256]{2,1,0:T(8,128)(2,1)S(1)} copy-done((bf16[4,256,256]{2,1,0:T(8,128)(2,1)S(1)}, bf16[4,256,256]{2,1,0:T(8,128)(2,1)}, u32[]{:S(2)}) %copy-start.1) | copy-done | bytes 524312
  7.4 0.9 %copy-done.2 = s32[1,1,4,128,128]{4,3,2,1,0:T(8,128)S(1)} copy-done((s32[1,1,4,128,128]{4,3,2,1,0:T(8,128)S(1)}, s32[1,1,4,128,128]{4,3,2,1,0:T(8,128)}, u32[]{:S(2)}) %copy-start.2) | copy-done | bytes 262168
  8.4 0.9 %copy-done.3 = f32[2,128,128]{2,1,0:T(8,128)S(1)} copy-done((f32[2,128,128]{2,1,0:T(8,128)S(1)}, f32[2,128,128]{2,1,0:T(8,128)}, u32[]{:S(2)}) %copy-start.3) | copy-done | bytes 131096
  9.3 0.7 copy-done.4
  9.9 0.7 copy-done.5
  10.6 0.6 shard_map.86
  11.2 3.2 %collective-permute-done.2.corner_ref = f32[2,128,128]{2,1,0:T(8,128)S(1)} collective-permute-done((f32[2,128,128]{2,1,0:T(8,128)S(1)}, f32[2,128,128]{2,1,0:T(8,128)S(1)}, u32[]{:S(2)}, u32[]{:S(2)}) %collective-permute-start.2) | collective-permute-done | bytes 131104 | tf_op jit(solution)/shard_map/ppermute | solution.py:605
  14.5 0.0 collective-permute-done.right_ref
  14.5 0.0 collective-permute-done.1.below_ref
  14.5 2.7 %shard_map.88 = (f32[2,3,384,128]{3,2,1,0:T(8,128)S(1)}, f32[3,64,128]{2,1,0:T(8,128)S(1)}, f32[3,64,128]{2,1,0:T(8,128)S(1)}, f32[776,128]{1,0:T(8,128)S(1)}, f...) custom-call(f32[2,3,384,128]{3,2,1,0:T(8,128)S(1)} %get-tuple-element.43.start_ref, ...), custom_call_target="tpu_custom_call", output_to_operand_aliasing={{0}: (0, {})} | custom-call | tf_op jit(solution)/shard_map/pallas_call | solution.py:553
  17.2 2.4 %collective-permute-start.3 = (f32[3,64,128]{2,1,0:T(8,128)S(1)}, f32[3,64,128]{2,1,0:T(8,128)S(1)}, u32[]{:S(2)}, u32[]{:S(2)}) collective-permute-start(f32[3,64,128]{2,1,0:T(8,128)S(1)} %get-tuple-element.52), channel_id=1, source_target_pairs={{0,4},{4,0},{8,12},{12,8},{16,20},{20,16},{24,28},{28,24},{1,5},{5... | collective-permute-start | bytes 294920 | tf_op jit(solution)/shard_map/ppermute | solution.py:519
  19.5 1.6 %collective-permute-start.7 = (f32[776,128]{1,0:T(8,128)S(1)}, f32[776,128]{1,0:T(8,128)S(1)}, u32[]{:S(2)}, u32[]{:S(2)}) collective-permute-start(f32[776,128]{1,0:T(8,128)S(1)} %get-tuple-element.53.inner_ref), channel_id=1, source_target_pairs={{0,1},{1,0},{2,3},{3,2},{4,5},{5,4},{6,7},{7,6},{8,9},{9,8},{10,11... | collective-permute-start | bytes 1191944 | tf_op jit(solution)/shard_map/ppermute | solution.py:514
  21.1 0.7 collective-permute-start.8
  21.8 0.0 collective-permute-done.3
  21.8 1.6 %collective-permute-start.5 = (f32[3,64,128]{2,1,0:T(8,128)S(1)}, f32[3,64,128]{2,1,0:T(8,128)S(1)}, u32[]{:S(2)}, u32[]{:S(2)}) collective-permute-start(f32[3,64,128]{2,1,0:T(8,128)S(1)} %add.41), channel_id=1, source_target_pairs={{0,16},{4,20},{8,24},{12,28},{16,0},{20,4},{24,8},{28,12},{1,17},{... | collective-permute-start | bytes 294920 | tf_op jit(solution)/shard_map/ppermute | solution.py:519
  23.4 1.4 %collective-permute-start.6 = (f32[3,64,128]{2,1,0:T(8,128)S(1)}, f32[3,64,128]{2,1,0:T(8,128)S(1)}, u32[]{:S(2)}, u32[]{:S(2)}) collective-permute-start(f32[3,64,128]{2,1,0:T(8,128)S(1)} %add.41), channel_id=1, source_target_pairs={{0,24},{4,28},{8,16},{12,20},{16,8},{20,12},{24,0},{28,4},{1,25},{... | collective-permute-start | bytes 294920 | tf_op jit(solution)/shard_map/ppermute | solution.py:519
  24.8 0.5 collective-permute-start.4
  25.4 1.7 %collective-permute-done.5 = f32[3,64,128]{2,1,0:T(8,128)S(1)} collective-permute-done((f32[3,64,128]{2,1,0:T(8,128)S(1)}, f32[3,64,128]{2,1,0:T(8,128)S(1)}, u32[]{:S(2)}, u32[]{:S(2)}) %collective-permute-start.5) | collective-permute-done | bytes 98336 | tf_op jit(solution)/shard_map/ppermute | solution.py:519
  27.1 2.5 %collective-permute-done.6 = f32[3,64,128]{2,1,0:T(8,128)S(1)} collective-permute-done((f32[3,64,128]{2,1,0:T(8,128)S(1)}, f32[3,64,128]{2,1,0:T(8,128)S(1)}, u32[]{:S(2)}, u32[]{:S(2)}) %collective-permute-start.6) | collective-permute-done | bytes 98336 | tf_op jit(solution)/shard_map/ppermute | solution.py:519
  29.6 0.2 collective-permute-done.4
  29.9 0.8 %collective-permute-done.7.from_inner = f32[776,128]{1,0:T(8,128)S(1)} collective-permute-done((f32[776,128]{1,0:T(8,128)S(1)}, f32[776,128]{1,0:T(8,128)S(1)}, u32[]{:S(2)}, u32[]{:S(2)}) %collective-permute-start.7) | collective-permute-done | bytes 397344 | tf_op jit(solution)/shard_map/ppermute | solution.py:514
  30.7 0.0 collective-permute-done.8.from_outer
  30.7 0.2 shard_map.89
  30.9 0.1 collective-permute-start.10
  31.0 0.7 collective-permute-start.12
  31.7 3.7 %collective-permute-start.9 = (f32[3,64,128]{2,1,0:T(8,128)S(1)}, f32[3,64,128]{2,1,0:T(8,128)S(1)}, u32[]{:S(2)}, u32[]{:S(2)}) collective-permute-start(f32[3,64,128]{2,1,0:T(8,128)S(1)} %add_add_fusion), channel_id=1, source_target_pairs={{0,1},{1,0},{2,3},{3,2},{4,5},{5,4},{6,7},{7,6},{8,9},{9,8},{10,11... | collective-permute-start | bytes 294920 | tf_op jit(solution)/shard_map/ppermute | solution.py:519
  35.4 1.2 %shard_map.90 = (f32[2,3,384,128]{3,2,1,0:T(8,128)S(1)}, f32[5,640,128]{2,1,0:T(8,128)S(1)}) custom-call(f32[2,3,384,128]{3,2,1,0:T(8,128)S(1)} %get-tuple-element.60.ext_ref, f32[3,8,128]{2,1,0:T(8,128)S(1)} %get-tuple-element.61.infos_ref.near_ref, f32[2,128,128]{2,1,0:T(8,128)S(1)} %get-tuple-element.47.probe_ref, ...), custom_call_target="tpu_custom_call", output_to_operand_aliasing={{0}: (0, {})} | custom-call | tf_op jit(solution)/shard_map/pallas_call | solution.py:553
  36.5 1.4 %collective-permute-done.9 = f32[3,64,128]{2,1,0:T(8,128)S(1)} collective-permute-done((f32[3,64,128]{2,1,0:T(8,128)S(1)}, f32[3,64,128]{2,1,0:T(8,128)S(1)}, u32[]{:S(2)}, u32[]{:S(2)}) %collective-permute-start.9) | collective-permute-done | bytes 98336 | tf_op jit(solution)/shard_map/ppermute | solution.py:519
  38.0 0.0 collective-permute-done.10.strip_ref
  38.0 3.0 %collective-permute-start.11 = (f32[3,64,128]{2,1,0:T(8,128)S(1)}, f32[3,64,128]{2,1,0:T(8,128)S(1)}, u32[]{:S(2)}, u32[]{:S(2)}) collective-permute-start(f32[3,64,128]{2,1,0:T(8,128)S(1)} %add.45), channel_id=1, source_target_pairs={{0,2},{1,3},{2,0},{3,1},{4,6},{5,7},{6,4},{7,5},{8,10},{9,11},{10,... | collective-permute-start | bytes 294920 | tf_op jit(solution)/shard_map/ppermute | solution.py:519
  41.0 1.2 %shard_map.91 = (f32[2,3,384,128]{3,2,1,0:T(8,128)S(1)}, f32[5,640,128]{2,1,0:T(8,128)S(1)}, f32[3,8,128]{2,1,0:T(8,128)S(1)}) custom-call(f32[2,3,384,128]{3,2,1,0:T(8,128)S(1)} %get-tuple-element.65.ext_ref, f32[5,640,128]{2,1,0:T(8,128)S(1)} %get-tuple-element.66.light_in, ...), custom_call_target="tpu_custom_call", output_to_operand_aliasing={{0}: (0, {}), {1}: (1, {})} | custom-call | tf_op jit(solution)/shard_map/pallas_call | solution.py:553
  42.1 0.0 collective-permute-done.12.strip_ref
  42.1 1.1 %shard_map.92 = (f32[2,3,384,128]{3,2,1,0:T(8,128)S(1)}, f32[5,640,128]{2,1,0:T(8,128)S(1)}, f32[3,8,128]{2,1,0:T(8,128)S(1)}) custom-call(f32[2,3,384,128]{3,2,1,0:T(8,128)S(1)} %get-tuple-element.68.ext_ref, f32[5,640,128]{2,1,0:T(8,128)S(1)} %get-tuple-element.69.light_in, ...), custom_call_target="tpu_custom_call", output_to_operand_aliasing={{0}: (0, {}), {1}: (1, {})} | custom-call | tf_op jit(solution)/shard_map/pallas_call | solution.py:553
  43.2 0.3 collective-permute-done.11
  43.6 3.4 %collective-permute-start.13 = (f32[2,64,128]{2,1,0:T(8,128)S(1)}, f32[2,64,128]{2,1,0:T(8,128)S(1)}, u32[]{:S(2)}, u32[]{:S(2)}) collective-permute-start(f32[2,64,128]{2,1,0:T(8,128)S(1)} %fusion.1.half_ref), channel_id=1, source_target_pairs={{0,4},{4,0},{8,12},{12,8},{16,20},{20,16},{24,28},{28,24},{1,5},{5... | collective-permute-start | bytes 196616 | tf_op jit(solution)/shard_map/ppermute | solution.py:519
  47.1 1.0 %shard_map.94.patches_ref = f32[4,2,128,128]{3,2,1,0:T(8,128)S(1)} custom-call(f32[2,3,384,128]{3,2,1,0:T(8,128)S(1)} %get-tuple-element.72.ext_ref.tile_ref, f32[8,128]{1,0:T(8,128)S(1)} %get-tuple-element.50.info_ref), custom_call_target="tpu_custom_call" | custom-call | tf_op jit(solution)/shard_map/pallas_call | solution.py:553
  48.0 0.0 collective-permute-done.13.other_ref
  48.1 2.3 %shard_map.95 = (f32[3,64,128]{2,1,0:T(8,128)S(1)}, f32[3,64,128]{2,1,0:T(8,128)S(1)}, f32[4,2,128,128]{3,2,1,0:T(8,128)S(1)}) custom-call(f32[4,2,128,128]{3,2,1,0:T(8,128)S(1)} %shard_map.94.patches_ref, f32[2,64,128]{2,1,0:T(8,128)S(1)} %fusion.1.half_ref, f32[2,64,128]{2,1,0:T(8,128)S(1)} %collective-permute-done.13.other_ref, ...), custom_call_target="tpu_custom_call" | custom-call | tf_op jit(solution)/shard_map/pallas_call | solution.py:553
  50.4 0.3 collective-permute-start.16
  50.7 1.0 %shard_map.96 = (f32[3,512,128]{2,1,0:T(8,128)S(1)}, f32[3,256,128]{2,1,0:T(8,128)S(1)}) custom-call(f32[4,2,128,128]{3,2,1,0:T(8,128)S(1)} %get-tuple-element.76.updates_ref, f32[2,64,128]{2,1,0:T(8,128)S(1)} %fusion.1.half_ref, f32[2,64,128]{2,1,0:T(8,128)S(1)} %collective-permute-done.13.other_ref, f32[8,128]{1,0:T(8,128)S(1)} %get-tuple-element.50.info_ref), custom_call_target="tpu_custom_call" | custom-call | tf_op jit(solution)/shard_map/pallas_call | solution.py:553
  51.7 0.0 collective-permute-done.16
  51.8 1.5 %collective-permute-start.17 = (f32[3,64,128]{2,1,0:T(8,128)S(1)}, f32[3,64,128]{2,1,0:T(8,128)S(1)}, u32[]{:S(2)}, u32[]{:S(2)}) collective-permute-start(f32[3,64,128]{2,1,0:T(8,128)S(1)} %add.48), channel_id=1, source_target_pairs={{0,1},{1,0},{2,3},{3,2},{4,5},{5,4},{6,7},{7,6},{8,9},{9,8},{10,11... | collective-permute-start | bytes 294920 | tf_op jit(solution)/shard_map/ppermute | solution.py:519
  53.3 1.9 %collective-permute-start.14 = (f32[3,256,128]{2,1,0:T(8,128)S(1)}, f32[3,256,128]{2,1,0:T(8,128)S(1)}, u32[]{:S(2)}, u32[]{:S(2)}) collective-permute-start(f32[3,256,128]{2,1,0:T(8,128)S(1)} %get-tuple-element.78), channel_id=1, source_target_pairs={{0,4},{4,8},{8,12},{12,16},{16,20},{20,24},{24,28},{1,5},{5,9},{9,... | collective-permute-start | bytes 1179656 | tf_op jit(solution)/shard_map/ppermute | solution.py:506
  55.2 1.6 %collective-permute-done.17 = f32[3,64,128]{2,1,0:T(8,128)S(1)} collective-permute-done((f32[3,64,128]{2,1,0:T(8,128)S(1)}, f32[3,64,128]{2,1,0:T(8,128)S(1)}, u32[]{:S(2)}, u32[]{:S(2)}) %collective-permute-start.17) | collective-permute-done | bytes 98336 | tf_op jit(solution)/shard_map/ppermute | solution.py:519
  56.8 2.0 %collective-permute-start.18 = (f32[3,64,128]{2,1,0:T(8,128)S(1)}, f32[3,64,128]{2,1,0:T(8,128)S(1)}, u32[]{:S(2)}, u32[]{:S(2)}) collective-permute-start(f32[3,64,128]{2,1,0:T(8,128)S(1)} %add.49), channel_id=1, source_target_pairs={{0,2},{1,3},{2,0},{3,1},{4,6},{5,7},{6,4},{7,5},{8,10},{9,11},{10,... | collective-permute-start | bytes 294920 | tf_op jit(solution)/shard_map/ppermute | solution.py:519
  58.8 5.7 %collective-permute-done.18 = f32[3,64,128]{2,1,0:T(8,128)S(1)} collective-permute-done((f32[3,64,128]{2,1,0:T(8,128)S(1)}, f32[3,64,128]{2,1,0:T(8,128)S(1)}, u32[]{:S(2)}, u32[]{:S(2)}) %collective-permute-start.18) | collective-permute-done | bytes 98336 | tf_op jit(solution)/shard_map/ppermute | solution.py:519
  64.6 3.7 %collective-permute-start.19 = (f32[3,64,128]{2,1,0:T(8,128)S(1)}, f32[3,64,128]{2,1,0:T(8,128)S(1)}, u32[]{:S(2)}, u32[]{:S(2)}) collective-permute-start(f32[3,64,128]{2,1,0:T(8,128)S(1)} %add.50), channel_id=1, source_target_pairs={{0,8},{4,12},{8,0},{12,4},{16,24},{20,28},{24,16},{28,20},{1,9},{5... | collective-permute-start | bytes 294920 | tf_op jit(solution)/shard_map/ppermute | solution.py:519
  68.2 2.7 %collective-permute-done.19 = f32[3,64,128]{2,1,0:T(8,128)S(1)} collective-permute-done((f32[3,64,128]{2,1,0:T(8,128)S(1)}, f32[3,64,128]{2,1,0:T(8,128)S(1)}, u32[]{:S(2)}, u32[]{:S(2)}) %collective-permute-start.19) | collective-permute-done | bytes 98336 | tf_op jit(solution)/shard_map/ppermute | solution.py:519
  70.9 1.4 %collective-permute-start.20 = (f32[3,64,128]{2,1,0:T(8,128)S(1)}, f32[3,64,128]{2,1,0:T(8,128)S(1)}, u32[]{:S(2)}, u32[]{:S(2)}) collective-permute-start(f32[3,64,128]{2,1,0:T(8,128)S(1)} %add.51), channel_id=1, source_target_pairs={{0,16},{4,20},{8,24},{12,28},{16,0},{20,4},{24,8},{28,12},{1,17},{... | collective-permute-start | bytes 294920 | tf_op jit(solution)/shard_map/ppermute | solution.py:519
  72.4 0.0 collective-permute-done.14.from_above
  72.4 1.8 %collective-permute-start.15 = (f32[512,128]{1,0:T(8,128)S(1)}, f32[512,128]{1,0:T(8,128)S(1)}, u32[]{:S(2)}, u32[]{:S(2)}) collective-permute-start(f32[512,128]{1,0:T(8,128)S(1)} %shard_map.97), channel_id=1, source_target_pairs={{0,1},{1,2},{2,3},{4,5},{5,6},{6,7},{8,9},{9,10},{10,11},{12,13},{... | collective-permute-start | bytes 786440 | tf_op jit(solution)/shard_map/ppermute | solution.py:506
  74.2 1.4 %collective-permute-done.20 = f32[3,64,128]{2,1,0:T(8,128)S(1)} collective-permute-done((f32[3,64,128]{2,1,0:T(8,128)S(1)}, f32[3,64,128]{2,1,0:T(8,128)S(1)}, u32[]{:S(2)}, u32[]{:S(2)}) %collective-permute-start.20) | collective-permute-done | bytes 98336 | tf_op jit(solution)/shard_map/ppermute | solution.py:519
  75.7 0.1 collective-permute-start.21
  75.7 1.8 %shard_map.93.light_ref = f32[2,256,128]{2,1,0:T(8,128)S(1)} custom-call(f32[3,8,128]{2,1,0:T(8,128)S(1)} %get-tuple-element.61.infos_ref.near_ref, f32[3,8,128]{2,1,0:T(8,128)S(1)} %get-tuple-element.73.inner_ref, f32[3,8,128]{2,1,0:T(8,128)S(1)} %get-tuple-element.74.outer_ref, f32[2,64,128]{2,1,0:T(8,128)S(1)} %fusion.1.half_ref, ...), custom_call_target="tpu_custom_call" | custom-call | tf_op jit(solution)/shard_map/pallas_call | solution.py:553
  77.6 0.0 collective-permute-done.21.other_ref
  77.6 0.5 collective-permute-done.15.from_left
  78.0 1.0 %shard_map.98 = (f32[2,256,256]{2,1,0:T(8,128)}, f32[2,128,128]{2,1,0:T(8,128)}) custom-call(f32[2,3,384,128]{3,2,1,0:T(8,128)S(1)} %get-tuple-element.72.ext_ref.tile_ref, f32[2,256,128]{2,1,0:T(8,128)S(1)} %shard_map.93.light_ref, f32[3,512,128]{2,1,0:T(8,128)S(1)} %get-tuple-element.77.body_ref, f32[3,256,128]{2,1,0:T(8,128)S(1)} %collective-permute-done.14.from_above, ...), custom_call_target="tpu_custom_call" | custom-call | tf_op jit(solution)/shard_map/pallas_call | solution.py:553
  (18 shorter events, 0.2 us)
Async XLA Ops:
  0.6 1.0 %copy-start = (f32[2,256,256]{2,1,0:T(8,128)S(1)}, f32[2,256,256]{2,1,0:T(8,128)}, u32[]{:S(2)}) copy-start(f32[2,256,256]{2,1,0:T(8,128)} %field_ref.1) | copy-start | bytes 1572868
  1.8 12.6 %collective-permute-start = (f32[2,256,128]{2,1,0:T(8,128)S(1)}, f32[2,256,128]{2,1,0:T(8,128)S(1)}, u32[]{:S(2)}, u32[]{:S(2)}) collective-permute-start(f32[2,256,128]{2,1,0:T(8,128)S(1)} %get-tuple-element.44), channel_id=1, source_target_pairs={{1,0},{2,1},{3,2},{5,4},{6,5},{7,6},{9,8},{10,9},{11,10},{13,12},{... | collective-permute-start | bytes 786440 | tf_op jit(solution)/shard_map/ppermute | solution.py:506
  3.1 11.3 %collective-permute-start.1 = (f32[2,128,256]{2,1,0:T(8,128)S(1)}, f32[2,128,256]{2,1,0:T(8,128)S(1)}, u32[]{:S(2)}, u32[]{:S(2)}) collective-permute-start(f32[2,128,256]{2,1,0:T(8,128)S(1)} %get-tuple-element.45), channel_id=1, source_target_pairs={{4,0},{8,4},{12,8},{16,12},{20,16},{24,20},{28,24},{5,1},{9,5},{13... | collective-permute-start | bytes 786440 | tf_op jit(solution)/shard_map/ppermute | solution.py:506
  4.4 10.0 %collective-permute-start.2 = (f32[2,128,128]{2,1,0:T(8,128)S(1)}, f32[2,128,128]{2,1,0:T(8,128)S(1)}, u32[]{:S(2)}, u32[]{:S(2)}) collective-permute-start(f32[2,128,128]{2,1,0:T(8,128)S(1)} %get-tuple-element.46), channel_id=1, source_target_pairs={{5,0},{6,1},{7,2},{9,4},{10,5},{11,6},{13,8},{14,9},{15,10},{17,12... | collective-permute-start | bytes 393224 | tf_op jit(solution)/shard_map/ppermute | solution.py:605
  6.4 1.0 %copy-start.1 = (bf16[4,256,256]{2,1,0:T(8,128)(2,1)S(1)}, bf16[4,256,256]{2,1,0:T(8,128)(2,1)}, u32[]{:S(2)}) copy-start(bf16[4,256,256]{2,1,0:T(8,128)(2,1)} %constant.4.clone.tables_ref) | copy-start | bytes 1572868
  7.4 0.9 %copy-start.2 = (s32[1,1,4,128,128]{4,3,2,1,0:T(8,128)S(1)}, s32[1,1,4,128,128]{4,3,2,1,0:T(8,128)}, u32[]{:S(2)}) copy-start(s32[1,1,4,128,128]{4,3,2,1,0:T(8,128)} %param.9) | copy-start | bytes 786436
  8.4 0.9 %copy-start.3 = (f32[2,128,128]{2,1,0:T(8,128)S(1)}, f32[2,128,128]{2,1,0:T(8,128)}, u32[]{:S(2)}) copy-start(f32[2,128,128]{2,1,0:T(8,128)} %probe_ref.1) | copy-start | bytes 393220
  9.3 0.7 copy-start.4
  9.9 0.7 copy-start.5
  17.2 4.7 %collective-permute-start.3 = (f32[3,64,128]{2,1,0:T(8,128)S(1)}, f32[3,64,128]{2,1,0:T(8,128)S(1)}, u32[]{:S(2)}, u32[]{:S(2)}) collective-permute-start(f32[3,64,128]{2,1,0:T(8,128)S(1)} %get-tuple-element.52), channel_id=1, source_target_pairs={{0,4},{4,0},{8,12},{12,8},{16,20},{20,16},{24,28},{28,24},{1,5},{5... | collective-permute-start | bytes 294920 | tf_op jit(solution)/shard_map/ppermute | solution.py:519
  19.5 11.2 %collective-permute-start.7 = (f32[776,128]{1,0:T(8,128)S(1)}, f32[776,128]{1,0:T(8,128)S(1)}, u32[]{:S(2)}, u32[]{:S(2)}) collective-permute-start(f32[776,128]{1,0:T(8,128)S(1)} %get-tuple-element.53.inner_ref), channel_id=1, source_target_pairs={{0,1},{1,0},{2,3},{3,2},{4,5},{5,4},{6,7},{7,6},{8,9},{9,8},{10,11... | collective-permute-start | bytes 1191944 | tf_op jit(solution)/shard_map/ppermute | solution.py:514
  21.1 9.6 %collective-permute-start.8 = (f32[776,128]{1,0:T(8,128)S(1)}, f32[776,128]{1,0:T(8,128)S(1)}, u32[]{:S(2)}, u32[]{:S(2)}) collective-permute-start(f32[776,128]{1,0:T(8,128)S(1)} %get-tuple-element.55.outer_ref), channel_id=1, source_target_pairs={{1,2},{2,1},{5,6},{6,5},{9,10},{10,9},{13,14},{14,13},{17,18},{18,... | collective-permute-start | bytes 1191944 | tf_op jit(solution)/shard_map/ppermute | solution.py:514
  21.8 5.2 %collective-permute-start.5 = (f32[3,64,128]{2,1,0:T(8,128)S(1)}, f32[3,64,128]{2,1,0:T(8,128)S(1)}, u32[]{:S(2)}, u32[]{:S(2)}) collective-permute-start(f32[3,64,128]{2,1,0:T(8,128)S(1)} %add.41), channel_id=1, source_target_pairs={{0,16},{4,20},{8,24},{12,28},{16,0},{20,4},{24,8},{28,12},{1,17},{... | collective-permute-start | bytes 294920 | tf_op jit(solution)/shard_map/ppermute | solution.py:519
  23.4 6.2 %collective-permute-start.6 = (f32[3,64,128]{2,1,0:T(8,128)S(1)}, f32[3,64,128]{2,1,0:T(8,128)S(1)}, u32[]{:S(2)}, u32[]{:S(2)}) collective-permute-start(f32[3,64,128]{2,1,0:T(8,128)S(1)} %add.41), channel_id=1, source_target_pairs={{0,24},{4,28},{8,16},{12,20},{16,8},{20,12},{24,0},{28,4},{1,25},{... | collective-permute-start | bytes 294920 | tf_op jit(solution)/shard_map/ppermute | solution.py:519
  24.8 5.0 %collective-permute-start.4 = (f32[3,64,128]{2,1,0:T(8,128)S(1)}, f32[3,64,128]{2,1,0:T(8,128)S(1)}, u32[]{:S(2)}, u32[]{:S(2)}) collective-permute-start(f32[3,64,128]{2,1,0:T(8,128)S(1)} %add.41), channel_id=1, source_target_pairs={{0,8},{4,12},{8,0},{12,4},{16,24},{20,28},{24,16},{28,20},{1,9},{5... | collective-permute-start | bytes 294920 | tf_op jit(solution)/shard_map/ppermute | solution.py:519
  30.9 7.1 %collective-permute-start.10 = (f32[792,128]{1,0:T(8,128)S(1)}, f32[792,128]{1,0:T(8,128)S(1)}, u32[]{:S(2)}, u32[]{:S(2)}) collective-permute-start(f32[792,128]{1,0:T(8,128)S(1)} %get-tuple-element.59), channel_id=1, source_target_pairs={{0,4},{4,0},{8,12},{12,8},{16,20},{20,16},{24,28},{28,24},{1,5},{5... | collective-permute-start | bytes 1216520 | tf_op jit(solution)/shard_map/ppermute | solution.py:514
  31.0 11.1 %collective-permute-start.12 = (f32[792,128]{1,0:T(8,128)S(1)}, f32[792,128]{1,0:T(8,128)S(1)}, u32[]{:S(2)}, u32[]{:S(2)}) collective-permute-start(f32[792,128]{1,0:T(8,128)S(1)} %get-tuple-element.70), channel_id=1, source_target_pairs={{4,8},{8,4},{12,16},{16,12},{20,24},{24,20},{5,9},{9,5},{13,17},{1... | collective-permute-start | bytes 1216520 | tf_op jit(solution)/shard_map/ppermute | solution.py:514
  31.7 6.3 %collective-permute-start.9 = (f32[3,64,128]{2,1,0:T(8,128)S(1)}, f32[3,64,128]{2,1,0:T(8,128)S(1)}, u32[]{:S(2)}, u32[]{:S(2)}) collective-permute-start(f32[3,64,128]{2,1,0:T(8,128)S(1)} %add_add_fusion), channel_id=1, source_target_pairs={{0,1},{1,0},{2,3},{3,2},{4,5},{5,4},{6,7},{7,6},{8,9},{9,8},{10,11... | collective-permute-start | bytes 294920 | tf_op jit(solution)/shard_map/ppermute | solution.py:519
  38.0 5.6 %collective-permute-start.11 = (f32[3,64,128]{2,1,0:T(8,128)S(1)}, f32[3,64,128]{2,1,0:T(8,128)S(1)}, u32[]{:S(2)}, u32[]{:S(2)}) collective-permute-start(f32[3,64,128]{2,1,0:T(8,128)S(1)} %add.45), channel_id=1, source_target_pairs={{0,2},{1,3},{2,0},{3,1},{4,6},{5,7},{6,4},{7,5},{8,10},{9,11},{10,... | collective-permute-start | bytes 294920 | tf_op jit(solution)/shard_map/ppermute | solution.py:519
  43.6 4.4 %collective-permute-start.13 = (f32[2,64,128]{2,1,0:T(8,128)S(1)}, f32[2,64,128]{2,1,0:T(8,128)S(1)}, u32[]{:S(2)}, u32[]{:S(2)}) collective-permute-start(f32[2,64,128]{2,1,0:T(8,128)S(1)} %fusion.1.half_ref), channel_id=1, source_target_pairs={{0,4},{4,0},{8,12},{12,8},{16,20},{20,16},{24,28},{28,24},{1,5},{5... | collective-permute-start | bytes 196616 | tf_op jit(solution)/shard_map/ppermute | solution.py:519
  50.4 1.4 %collective-permute-start.16 = (f32[3,64,128]{2,1,0:T(8,128)S(1)}, f32[3,64,128]{2,1,0:T(8,128)S(1)}, u32[]{:S(2)}, u32[]{:S(2)}) collective-permute-start(f32[3,64,128]{2,1,0:T(8,128)S(1)} %get-tuple-element.80), channel_id=1, source_target_pairs={{0,4},{4,0},{8,12},{12,8},{16,20},{20,16},{24,28},{28,24},{1,5},{5... | collective-permute-start | bytes 294920 | tf_op jit(solution)/shard_map/ppermute | solution.py:519
  51.8 5.0 %collective-permute-start.17 = (f32[3,64,128]{2,1,0:T(8,128)S(1)}, f32[3,64,128]{2,1,0:T(8,128)S(1)}, u32[]{:S(2)}, u32[]{:S(2)}) collective-permute-start(f32[3,64,128]{2,1,0:T(8,128)S(1)} %add.48), channel_id=1, source_target_pairs={{0,1},{1,0},{2,3},{3,2},{4,5},{5,4},{6,7},{7,6},{8,9},{9,8},{10,11... | collective-permute-start | bytes 294920 | tf_op jit(solution)/shard_map/ppermute | solution.py:519
  53.3 19.1 %collective-permute-start.14 = (f32[3,256,128]{2,1,0:T(8,128)S(1)}, f32[3,256,128]{2,1,0:T(8,128)S(1)}, u32[]{:S(2)}, u32[]{:S(2)}) collective-permute-start(f32[3,256,128]{2,1,0:T(8,128)S(1)} %get-tuple-element.78), channel_id=1, source_target_pairs={{0,4},{4,8},{8,12},{12,16},{16,20},{20,24},{24,28},{1,5},{5,9},{9,... | collective-permute-start | bytes 1179656 | tf_op jit(solution)/shard_map/ppermute | solution.py:506
  56.8 7.7 %collective-permute-start.18 = (f32[3,64,128]{2,1,0:T(8,128)S(1)}, f32[3,64,128]{2,1,0:T(8,128)S(1)}, u32[]{:S(2)}, u32[]{:S(2)}) collective-permute-start(f32[3,64,128]{2,1,0:T(8,128)S(1)} %add.49), channel_id=1, source_target_pairs={{0,2},{1,3},{2,0},{3,1},{4,6},{5,7},{6,4},{7,5},{8,10},{9,11},{10,... | collective-permute-start | bytes 294920 | tf_op jit(solution)/shard_map/ppermute | solution.py:519
  64.6 6.4 %collective-permute-start.19 = (f32[3,64,128]{2,1,0:T(8,128)S(1)}, f32[3,64,128]{2,1,0:T(8,128)S(1)}, u32[]{:S(2)}, u32[]{:S(2)}) collective-permute-start(f32[3,64,128]{2,1,0:T(8,128)S(1)} %add.50), channel_id=1, source_target_pairs={{0,8},{4,12},{8,0},{12,4},{16,24},{20,28},{24,16},{28,20},{1,9},{5... | collective-permute-start | bytes 294920 | tf_op jit(solution)/shard_map/ppermute | solution.py:519
  70.9 4.7 %collective-permute-start.20 = (f32[3,64,128]{2,1,0:T(8,128)S(1)}, f32[3,64,128]{2,1,0:T(8,128)S(1)}, u32[]{:S(2)}, u32[]{:S(2)}) collective-permute-start(f32[3,64,128]{2,1,0:T(8,128)S(1)} %add.51), channel_id=1, source_target_pairs={{0,16},{4,20},{8,24},{12,28},{16,0},{20,4},{24,8},{28,12},{1,17},{... | collective-permute-start | bytes 294920 | tf_op jit(solution)/shard_map/ppermute | solution.py:519
  72.4 5.6 %collective-permute-start.15 = (f32[512,128]{1,0:T(8,128)S(1)}, f32[512,128]{1,0:T(8,128)S(1)}, u32[]{:S(2)}, u32[]{:S(2)}) collective-permute-start(f32[512,128]{1,0:T(8,128)S(1)} %shard_map.97), channel_id=1, source_target_pairs={{0,1},{1,2},{2,3},{4,5},{5,6},{6,7},{8,9},{9,10},{10,11},{12,13},{... | collective-permute-start | bytes 786440 | tf_op jit(solution)/shard_map/ppermute | solution.py:506
  75.7 1.9 %collective-permute-start.21 = (f32[2,64,128]{2,1,0:T(8,128)S(1)}, f32[2,64,128]{2,1,0:T(8,128)S(1)}, u32[]{:S(2)}, u32[]{:S(2)}) collective-permute-start(f32[2,64,128]{2,1,0:T(8,128)S(1)} %fusion.half_ref), channel_id=1, source_target_pairs={{0,4},{4,0},{8,12},{12,8},{16,20},{20,16},{24,28},{28,24},{1,5},{5... | collective-permute-start | bytes 196616 | tf_op jit(solution)/shard_map/ppermute | solution.py:519

commit v7 on v6

--- a/solution.py
+++ b/solution.py
@@ -96,16 +96,19 @@
         add_patch(light_ref, row, col, power_ref[...], length)
 
 
+def add_tile(light_ref, power_ref, info_ref, index, down, across, tall, wide, slots, length):
+    for s in range(slots):
+        row, col, weight = slot_place(info_ref, index, s, slots)
+        add_light(light_ref, power_ref, row + down * tall, col + across * wide, weight, length)
+
+
 def add_tiles(light_ref, power_ref, info_ref, tiles, tall, wide, slots, length):
     across = 1 - 2 * parity("col")
     down = 1 - 2 * parity("row")
     places = [(0, 0), (0, across), (0, -across)]
     places += [(down, step) for step in (-1, 0, 1)] + [(-down, step) for step in (-1, 0, 1)]
     for index in tiles:
-        row_step, col_step = places[index]
-        for s in range(slots):
-            row, col, weight = slot_place(info_ref, index, s, slots)
-            add_light(light_ref, power_ref, row + row_step * tall, col + col_step * wide, weight, length)
+        add_tile(light_ref, power_ref, info_ref, index, *places[index], tall, wide, slots, length)
 
 
 def fill_info(rows_ref, cols_ref, counts_ref, slots):
@@ -465,7 +468,9 @@
     power_ref[...] = probe_real * probe_real + probe_imag * probe_imag
     light_ref[...] = jnp.zeros_like(light_ref)
     wait_all(copies)
-    add_tiles(light_ref, power_ref, info_at, range(9), tall, blocks * LANES, slots, length)
+    left, above = 2 - parity("col"), 6 - 3 * parity("row")
+    for index, down, across in ((0, 0, 0), (left, 0, -1), (above, -1, -1), (above + 1, -1, 0)):
+        add_tile(light_ref, power_ref, info_at, index, down, across, tall, blocks * LANES, slots, length)
     light_out[...] = STEP_SIZE / (light_ref[1 : 1 + blocks, length : length + tall, :] + REGULARIZER)
 
 
@@ -699,6 +704,7 @@
     part = butterfly(part, "col", last_col)
     from_left = shift(right, "col", 1)
     part = butterfly(part, "row", 2, last_row)
+    part, light = tie(part, light)
     part = butterfly(part, "row", last_row)
     last_half = stepped(new_half, part)
     last_other = flip(last_half, "row", 1)

time: 79.7 us -> 79.6 us (level)
  starting transfers between devices: 35.6 us -> 38 us
  waiting for transfers between devices: 22.2 us -> 20.2 us
    ppermute x13, waiting for transfers between devices: 17.7 us -> 15 us  [flip(): lax.ppermute(value, axis, [(source, source ^ mask) for source in range(co...]
    ppermute x13, starting transfers between devices: 25.1 us -> 27.4 us  [flip(): lax.ppermute(value, axis, [(source, source ^ mask) for source in range(co...]
  transfers between devices with their start and end apart: 22 -> 22, of which waited for: 12 -> 13; matrix products, arithmetic and copies ran while one was open for 0% -> 0% of each run, Pallas kernels for 10% -> 10%
where the time goes in v7:
time: 79.6 us; the launch traced here: 79 us
  starting transfers between devices  38 us (48%)
  waiting for transfers between devices  20.2 us (25%)
  Pallas kernels  13.8 us (17%)
  local copies, waits for them, and re-layouts  5.23 us (7%)
  between operations  1.56 us (2%)
    ppermute x13, starting transfers between devices, flip(): lax.ppermute(value, axis, [(source, source ^ mask) for source in range(co...  27.4 us
    ppermute x13, waiting for transfers between devices, flip(): lax.ppermute(value, axis, [(source, source ^ mask) for source in range(co...  15 us
    pallas_call x13, Pallas kernels, call(): pl.pallas_call(kernel, out_shape=[shape_of(spec) for spec in outs], in_sp...  13.8 us
    ppermute x4, starting transfers between devices, shift(): return lax.ppermute(value, axis, pairs)  6.29 us
    unnamed x12, local copies, waits for them, and re-layouts  5.23 us
    ppermute x1, waiting for transfers between devices, local(): lax.ppermute(corner, ('row', 'col'), [((r + 1) * count_cols + c + 1, r *...  3.22 us
    ppermute x4, starting transfers between devices, swap(): return lax.ppermute(value, axis, pairs)  3 us
  transfers between devices with their start and end apart: 22, of which 13 were waited for; matrix products, arithmetic and copies ran while one was open for 0% of the time, Pallas kernels for 10%

profile of v7, /device:TPU:0, one launch (start us, length us, event | category | flops | bytes accessed | tf_op | source)
XLA Modules:
  0.0 79.0 jit_solution(12056240214724464804)
XLA Ops:
  0.6 0.0 copy-start
  0.6 1.0 %copy-done = f32[2,256,256]{2,1,0:T(8,128)S(1)} copy-done((f32[2,256,256]{2,1,0:T(8,128)S(1)}, f32[2,256,256]{2,1,0:T(8,128)}, u32[]{:S(2)}) %copy-start) | copy-done | bytes 524312
  1.7 0.2 shard_map.87
  1.8 1.3 %collective-permute-start = (f32[2,256,128]{2,1,0:T(8,128)S(1)}, f32[2,256,128]{2,1,0:T(8,128)S(1)}, u32[]{:S(2)}, u32[]{:S(2)}) collective-permute-start(f32[2,256,128]{2,1,0:T(8,128)S(1)} %get-tuple-element.46), channel_id=1, source_target_pairs={{1,0},{2,1},{3,2},{5,4},{6,5},{7,6},{9,8},{10,9},{11,10},{13,12},{... | collective-permute-start | bytes 786440 | tf_op jit(solution)/shard_map/ppermute | solution.py:511
  3.1 1.3 %collective-permute-start.1 = (f32[2,128,256]{2,1,0:T(8,128)S(1)}, f32[2,128,256]{2,1,0:T(8,128)S(1)}, u32[]{:S(2)}, u32[]{:S(2)}) collective-permute-start(f32[2,128,256]{2,1,0:T(8,128)S(1)} %get-tuple-element.47), channel_id=1, source_target_pairs={{4,0},{8,4},{12,8},{16,12},{20,16},{24,20},{28,24},{5,1},{9,5},{13... | collective-permute-start | bytes 786440 | tf_op jit(solution)/shard_map/ppermute | solution.py:511
  4.4 1.3 %collective-permute-start.2 = (f32[2,128,128]{2,1,0:T(8,128)S(1)}, f32[2,128,128]{2,1,0:T(8,128)S(1)}, u32[]{:S(2)}, u32[]{:S(2)}) collective-permute-start(f32[2,128,128]{2,1,0:T(8,128)S(1)} %get-tuple-element.48), channel_id=1, source_target_pairs={{5,0},{6,1},{7,2},{9,4},{10,5},{11,6},{13,8},{14,9},{15,10},{17,12... | collective-permute-start | bytes 393224 | tf_op jit(solution)/shard_map/ppermute | solution.py:610
  6.4 0.0 copy-start.1
  6.4 1.0 %copy-done.1 = bf16[4,256,256]{2,1,0:T(8,128)(2,1)S(1)} copy-done((bf16[4,256,256]{2,1,0:T(8,128)(2,1)S(1)}, bf16[4,256,256]{2,1,0:T(8,128)(2,1)}, u32[]{:S(2)}) %copy-start.1) | copy-done | bytes 524312
  7.4 0.9 %copy-done.2 = s32[1,1,4,128,128]{4,3,2,1,0:T(8,128)S(1)} copy-done((s32[1,1,4,128,128]{4,3,2,1,0:T(8,128)S(1)}, s32[1,1,4,128,128]{4,3,2,1,0:T(8,128)}, u32[]{:S(2)}) %copy-start.2) | copy-done | bytes 262168
  8.4 0.9 %copy-done.3 = f32[2,128,128]{2,1,0:T(8,128)S(1)} copy-done((f32[2,128,128]{2,1,0:T(8,128)S(1)}, f32[2,128,128]{2,1,0:T(8,128)}, u32[]{:S(2)}) %copy-start.3) | copy-done | bytes 131096
  9.3 0.7 copy-done.4
  9.9 0.7 copy-done.5
  10.6 0.6 shard_map.86
  11.2 3.2 %collective-permute-done.2.corner_ref = f32[2,128,128]{2,1,0:T(8,128)S(1)} collective-permute-done((f32[2,128,128]{2,1,0:T(8,128)S(1)}, f32[2,128,128]{2,1,0:T(8,128)S(1)}, u32[]{:S(2)}, u32[]{:S(2)}) %collective-permute-start.2) | collective-permute-done | bytes 131104 | tf_op jit(solution)/shard_map/ppermute | solution.py:610
  14.5 0.0 collective-permute-done.right_ref
  14.5 0.0 collective-permute-done.1.below_ref
  14.5 2.7 %shard_map.88 = (f32[2,3,384,128]{3,2,1,0:T(8,128)S(1)}, f32[3,64,128]{2,1,0:T(8,128)S(1)}, f32[3,64,128]{2,1,0:T(8,128)S(1)}, f32[776,128]{1,0:T(8,128)S(1)}, f...) custom-call(f32[2,3,384,128]{3,2,1,0:T(8,128)S(1)} %get-tuple-element.45.start_ref, ...), custom_call_target="tpu_custom_call", output_to_operand_aliasing={{0}: (0, {})} | custom-call | tf_op jit(solution)/shard_map/pallas_call | solution.py:558
  17.2 2.4 %collective-permute-start.3 = (f32[3,64,128]{2,1,0:T(8,128)S(1)}, f32[3,64,128]{2,1,0:T(8,128)S(1)}, u32[]{:S(2)}, u32[]{:S(2)}) collective-permute-start(f32[3,64,128]{2,1,0:T(8,128)S(1)} %get-tuple-element.54), channel_id=1, source_target_pairs={{0,4},{4,0},{8,12},{12,8},{16,20},{20,16},{24,28},{28,24},{1,5},{5... | collective-permute-start | bytes 294920 | tf_op jit(solution)/shard_map/ppermute | solution.py:524
  19.5 1.6 %collective-permute-start.7 = (f32[776,128]{1,0:T(8,128)S(1)}, f32[776,128]{1,0:T(8,128)S(1)}, u32[]{:S(2)}, u32[]{:S(2)}) collective-permute-start(f32[776,128]{1,0:T(8,128)S(1)} %get-tuple-element.55.inner_ref), channel_id=1, source_target_pairs={{0,1},{1,0},{2,3},{3,2},{4,5},{5,4},{6,7},{7,6},{8,9},{9,8},{10,11... | collective-permute-start | bytes 1191944 | tf_op jit(solution)/shard_map/ppermute | solution.py:519
  21.1 0.7 collective-permute-start.8
  21.8 0.0 collective-permute-done.3
  21.8 1.6 %collective-permute-start.5 = (f32[3,64,128]{2,1,0:T(8,128)S(1)}, f32[3,64,128]{2,1,0:T(8,128)S(1)}, u32[]{:S(2)}, u32[]{:S(2)}) collective-permute-start(f32[3,64,128]{2,1,0:T(8,128)S(1)} %add.41), channel_id=1, source_target_pairs={{0,16},{4,20},{8,24},{12,28},{16,0},{20,4},{24,8},{28,12},{1,17},{... | collective-permute-start | bytes 294920 | tf_op jit(solution)/shard_map/ppermute | solution.py:524
  23.4 1.4 %collective-permute-start.6 = (f32[3,64,128]{2,1,0:T(8,128)S(1)}, f32[3,64,128]{2,1,0:T(8,128)S(1)}, u32[]{:S(2)}, u32[]{:S(2)}) collective-permute-start(f32[3,64,128]{2,1,0:T(8,128)S(1)} %add.41), channel_id=1, source_target_pairs={{0,24},{4,28},{8,16},{12,20},{16,8},{20,12},{24,0},{28,4},{1,25},{... | collective-permute-start | bytes 294920 | tf_op jit(solution)/shard_map/ppermute | solution.py:524
  24.8 0.5 collective-permute-start.4
  25.4 1.7 %collective-permute-done.5 = f32[3,64,128]{2,1,0:T(8,128)S(1)} collective-permute-done((f32[3,64,128]{2,1,0:T(8,128)S(1)}, f32[3,64,128]{2,1,0:T(8,128)S(1)}, u32[]{:S(2)}, u32[]{:S(2)}) %collective-permute-start.5) | collective-permute-done | bytes 98336 | tf_op jit(solution)/shard_map/ppermute | solution.py:524
  27.1 2.5 %collective-permute-done.6 = f32[3,64,128]{2,1,0:T(8,128)S(1)} collective-permute-done((f32[3,64,128]{2,1,0:T(8,128)S(1)}, f32[3,64,128]{2,1,0:T(8,128)S(1)}, u32[]{:S(2)}, u32[]{:S(2)}) %collective-permute-start.6) | collective-permute-done | bytes 98336 | tf_op jit(solution)/shard_map/ppermute | solution.py:524
  29.6 0.2 collective-permute-done.4
  29.9 0.9 %collective-permute-done.7.from_inner = f32[776,128]{1,0:T(8,128)S(1)} collective-permute-done((f32[776,128]{1,0:T(8,128)S(1)}, f32[776,128]{1,0:T(8,128)S(1)}, u32[]{:S(2)}, u32[]{:S(2)}) %collective-permute-start.7) | collective-permute-done | bytes 397344 | tf_op jit(solution)/shard_map/ppermute | solution.py:519
  30.7 0.0 collective-permute-done.8.from_outer
  30.7 0.2 shard_map.89
  30.9 0.1 collective-permute-start.10
  31.0 0.7 collective-permute-start.12
  31.7 3.7 %collective-permute-start.9 = (f32[3,64,128]{2,1,0:T(8,128)S(1)}, f32[3,64,128]{2,1,0:T(8,128)S(1)}, u32[]{:S(2)}, u32[]{:S(2)}) collective-permute-start(f32[3,64,128]{2,1,0:T(8,128)S(1)} %add_add_fusion), channel_id=1, source_target_pairs={{0,1},{1,0},{2,3},{3,2},{4,5},{5,4},{6,7},{7,6},{8,9},{9,8},{10,11... | collective-permute-start | bytes 294920 | tf_op jit(solution)/shard_map/ppermute | solution.py:524
  35.4 1.2 %shard_map.90 = (f32[2,3,384,128]{3,2,1,0:T(8,128)S(1)}, f32[5,640,128]{2,1,0:T(8,128)S(1)}) custom-call(f32[2,3,384,128]{3,2,1,0:T(8,128)S(1)} %get-tuple-element.62.ext_ref, f32[3,8,128]{2,1,0:T(8,128)S(1)} %get-tuple-element.63.infos_ref.near_ref, f32[2,128,128]{2,1,0:T(8,128)S(1)} %get-tuple-element.49.probe_ref, ...), custom_call_target="tpu_custom_call", output_to_operand_aliasing={{0}: (0, {})} | custom-call | tf_op jit(solution)/shard_map/pallas_call | solution.py:558
  36.6 1.4 %collective-permute-done.9 = f32[3,64,128]{2,1,0:T(8,128)S(1)} collective-permute-done((f32[3,64,128]{2,1,0:T(8,128)S(1)}, f32[3,64,128]{2,1,0:T(8,128)S(1)}, u32[]{:S(2)}, u32[]{:S(2)}) %collective-permute-start.9) | collective-permute-done | bytes 98336 | tf_op jit(solution)/shard_map/ppermute | solution.py:524
  38.0 0.0 collective-permute-done.10.strip_ref
  38.0 2.9 %collective-permute-start.11 = (f32[3,64,128]{2,1,0:T(8,128)S(1)}, f32[3,64,128]{2,1,0:T(8,128)S(1)}, u32[]{:S(2)}, u32[]{:S(2)}) collective-permute-start(f32[3,64,128]{2,1,0:T(8,128)S(1)} %add.45), channel_id=1, source_target_pairs={{0,2},{1,3},{2,0},{3,1},{4,6},{5,7},{6,4},{7,5},{8,10},{9,11},{10,... | collective-permute-start | bytes 294920 | tf_op jit(solution)/shard_map/ppermute | solution.py:524
  41.0 1.2 %shard_map.91 = (f32[2,3,384,128]{3,2,1,0:T(8,128)S(1)}, f32[5,640,128]{2,1,0:T(8,128)S(1)}, f32[3,8,128]{2,1,0:T(8,128)S(1)}) custom-call(f32[2,3,384,128]{3,2,1,0:T(8,128)S(1)} %get-tuple-element.67.ext_ref, f32[5,640,128]{2,1,0:T(8,128)S(1)} %get-tuple-element.68.light_in, ...), custom_call_target="tpu_custom_call", output_to_operand_aliasing={{0}: (0, {}), {1}: (1, {})} | custom-call | tf_op jit(solution)/shard_map/pallas_call | solution.py:558
  42.1 0.0 collective-permute-done.12.strip_ref
  42.1 1.1 %shard_map.92 = (f32[2,3,384,128]{3,2,1,0:T(8,128)S(1)}, f32[5,640,128]{2,1,0:T(8,128)S(1)}, f32[3,8,128]{2,1,0:T(8,128)S(1)}) custom-call(f32[2,3,384,128]{3,2,1,0:T(8,128)S(1)} %get-tuple-element.70.ext_ref, f32[5,640,128]{2,1,0:T(8,128)S(1)} %get-tuple-element.71.light_in, ...), custom_call_target="tpu_custom_call", output_to_operand_aliasing={{0}: (0, {}), {1}: (1, {})} | custom-call | tf_op jit(solution)/shard_map/pallas_call | solution.py:558
  43.2 0.4 collective-permute-done.11
  43.6 3.4 %collective-permute-start.13 = (f32[2,64,128]{2,1,0:T(8,128)S(1)}, f32[2,64,128]{2,1,0:T(8,128)S(1)}, u32[]{:S(2)}, u32[]{:S(2)}) collective-permute-start(f32[2,64,128]{2,1,0:T(8,128)S(1)} %fusion.1.half_ref), channel_id=1, source_target_pairs={{0,4},{4,0},{8,12},{12,8},{16,20},{20,16},{24,28},{28,24},{1,5},{5... | collective-permute-start | bytes 196616 | tf_op jit(solution)/shard_map/ppermute | solution.py:524
  47.1 1.0 %shard_map.93.patches_ref = f32[4,2,128,128]{3,2,1,0:T(8,128)S(1)} custom-call(f32[2,3,384,128]{3,2,1,0:T(8,128)S(1)} %get-tuple-element.74.ext_ref.tile_ref, f32[8,128]{1,0:T(8,128)S(1)} %get-tuple-element.52.info_ref), custom_call_target="tpu_custom_call" | custom-call | tf_op jit(solution)/shard_map/pallas_call | solution.py:558
  48.1 0.0 collective-permute-done.13.other_ref
  48.1 2.3 %shard_map.94 = (f32[3,64,128]{2,1,0:T(8,128)S(1)}, f32[3,64,128]{2,1,0:T(8,128)S(1)}, f32[4,2,128,128]{3,2,1,0:T(8,128)S(1)}) custom-call(f32[4,2,128,128]{3,2,1,0:T(8,128)S(1)} %shard_map.93.patches_ref, f32[2,64,128]{2,1,0:T(8,128)S(1)} %fusion.1.half_ref, f32[2,64,128]{2,1,0:T(8,128)S(1)} %collective-permute-done.13.other_ref, ...), custom_call_target="tpu_custom_call" | custom-call | tf_op jit(solution)/shard_map/pallas_call | solution.py:558
  50.4 0.3 collective-permute-start.14
  50.7 1.0 %shard_map.95 = (f32[3,512,128]{2,1,0:T(8,128)S(1)}, f32[3,256,128]{2,1,0:T(8,128)S(1)}) custom-call(f32[4,2,128,128]{3,2,1,0:T(8,128)S(1)} %get-tuple-element.78.updates_ref, f32[2,64,128]{2,1,0:T(8,128)S(1)} %fusion.1.half_ref, f32[2,64,128]{2,1,0:T(8,128)S(1)} %collective-permute-done.13.other_ref, f32[8,128]{1,0:T(8,128)S(1)} %get-tuple-element.52.info_ref), custom_call_target="tpu_custom_call" | custom-call | tf_op jit(solution)/shard_map/pallas_call | solution.py:558
  51.7 0.0 collective-permute-done.14
  51.8 1.6 %collective-permute-start.15 = (f32[3,64,128]{2,1,0:T(8,128)S(1)}, f32[3,64,128]{2,1,0:T(8,128)S(1)}, u32[]{:S(2)}, u32[]{:S(2)}) collective-permute-start(f32[3,64,128]{2,1,0:T(8,128)S(1)} %add.48), channel_id=1, source_target_pairs={{0,1},{1,0},{2,3},{3,2},{4,5},{5,4},{6,7},{7,6},{8,9},{9,8},{10,11... | collective-permute-start | bytes 294920 | tf_op jit(solution)/shard_map/ppermute | solution.py:524
  53.4 1.9 %collective-permute-start.18 = (f32[3,256,128]{2,1,0:T(8,128)S(1)}, f32[3,256,128]{2,1,0:T(8,128)S(1)}, u32[]{:S(2)}, u32[]{:S(2)}) collective-permute-start(f32[3,256,128]{2,1,0:T(8,128)S(1)} %get-tuple-element.79), channel_id=1, source_target_pairs={{0,4},{4,8},{8,12},{12,16},{16,20},{20,24},{24,28},{1,5},{5,9},{9,... | collective-permute-start | bytes 1179656 | tf_op jit(solution)/shard_map/ppermute | solution.py:511
  55.3 1.5 %collective-permute-done.15 = f32[3,64,128]{2,1,0:T(8,128)S(1)} collective-permute-done((f32[3,64,128]{2,1,0:T(8,128)S(1)}, f32[3,64,128]{2,1,0:T(8,128)S(1)}, u32[]{:S(2)}, u32[]{:S(2)}) %collective-permute-start.15) | collective-permute-done | bytes 98336 | tf_op jit(solution)/shard_map/ppermute | solution.py:524
  56.8 2.1 %collective-permute-start.16 = (f32[3,64,128]{2,1,0:T(8,128)S(1)}, f32[3,64,128]{2,1,0:T(8,128)S(1)}, u32[]{:S(2)}, u32[]{:S(2)}) collective-permute-start(f32[3,64,128]{2,1,0:T(8,128)S(1)} %add.49), channel_id=1, source_target_pairs={{0,2},{1,3},{2,0},{3,1},{4,6},{5,7},{6,4},{7,5},{8,10},{9,11},{10,... | collective-permute-start | bytes 294920 | tf_op jit(solution)/shard_map/ppermute | solution.py:524
  58.9 3.5 %collective-permute-done.16 = f32[3,64,128]{2,1,0:T(8,128)S(1)} collective-permute-done((f32[3,64,128]{2,1,0:T(8,128)S(1)}, f32[3,64,128]{2,1,0:T(8,128)S(1)}, u32[]{:S(2)}, u32[]{:S(2)}) %collective-permute-start.16) | collective-permute-done | bytes 98336 | tf_op jit(solution)/shard_map/ppermute | solution.py:524
  62.4 5.8 %collective-permute-start.17 = (f32[3,64,128]{2,1,0:T(8,128)S(1)}, f32[3,64,128]{2,1,0:T(8,128)S(1)}, u32[]{:S(2)}, u32[]{:S(2)}) collective-permute-start(f32[3,64,128]{2,1,0:T(8,128)S(1)} %add.50), channel_id=1, source_target_pairs={{0,8},{4,12},{8,0},{12,4},{16,24},{20,28},{24,16},{28,20},{1,9},{5... | collective-permute-start | bytes 294920 | tf_op jit(solution)/shard_map/ppermute | solution.py:524
  68.3 1.5 %shard_map.96.light_ref = f32[2,256,128]{2,1,0:T(8,128)S(1)} custom-call(f32[3,8,128]{2,1,0:T(8,128)S(1)} %get-tuple-element.63.infos_ref.near_ref, f32[3,8,128]{2,1,0:T(8,128)S(1)} %get-tuple-element.81.inner_ref, f32[3,8,128]{2,1,0:T(8,128)S(1)} %get-tuple-element.82.outer_ref, f32[2,64,128]{2,1,0:T(8,128)S(1)} %fusion.1.half_ref, ...), custom_call_target="tpu_custom_call" | custom-call | tf_op jit(solution)/shard_map/pallas_call | solution.py:558
  69.7 1.1 %collective-permute-done.17 = f32[3,64,128]{2,1,0:T(8,128)S(1)} collective-permute-done((f32[3,64,128]{2,1,0:T(8,128)S(1)}, f32[3,64,128]{2,1,0:T(8,128)S(1)}, u32[]{:S(2)}, u32[]{:S(2)}) %collective-permute-start.17) | collective-permute-done | bytes 98336 | tf_op jit(solution)/shard_map/ppermute | solution.py:524
  70.9 1.5 %collective-permute-start.20 = (f32[3,64,128]{2,1,0:T(8,128)S(1)}, f32[3,64,128]{2,1,0:T(8,128)S(1)}, u32[]{:S(2)}, u32[]{:S(2)}) collective-permute-start(f32[3,64,128]{2,1,0:T(8,128)S(1)} %add.51), channel_id=1, source_target_pairs={{0,16},{4,20},{8,24},{12,28},{16,0},{20,4},{24,8},{28,12},{1,17},{... | collective-permute-start | bytes 294920 | tf_op jit(solution)/shard_map/ppermute | solution.py:524
  72.3 0.0 collective-permute-done.18.from_above
  72.4 1.8 %collective-permute-start.19 = (f32[512,128]{1,0:T(8,128)S(1)}, f32[512,128]{1,0:T(8,128)S(1)}, u32[]{:S(2)}, u32[]{:S(2)}) collective-permute-start(f32[512,128]{1,0:T(8,128)S(1)} %shard_map.97), channel_id=1, source_target_pairs={{0,1},{1,2},{2,3},{4,5},{5,6},{6,7},{8,9},{9,10},{10,11},{12,13},{... | collective-permute-start | bytes 786440 | tf_op jit(solution)/shard_map/ppermute | solution.py:511
  74.2 1.4 %collective-permute-done.20 = f32[3,64,128]{2,1,0:T(8,128)S(1)} collective-permute-done((f32[3,64,128]{2,1,0:T(8,128)S(1)}, f32[3,64,128]{2,1,0:T(8,128)S(1)}, u32[]{:S(2)}, u32[]{:S(2)}) %collective-permute-start.20) | collective-permute-done | bytes 98336 | tf_op jit(solution)/shard_map/ppermute | solution.py:524
  75.6 0.1 collective-permute-start.21
  75.7 1.2 %collective-permute-done.21.other_ref = f32[2,64,128]{2,1,0:T(8,128)S(1)} collective-permute-done((f32[2,64,128]{2,1,0:T(8,128)S(1)}, f32[2,64,128]{2,1,0:T(8,128)S(1)}, u32[]{:S(2)}, u32[]{:S(2)}) %collective-permute-start.21) | collective-permute-done | bytes 65568 | tf_op jit(solution)/shard_map/ppermute | solution.py:524
  76.9 1.1 %collective-permute-done.19.from_left = f32[512,128]{1,0:T(8,128)S(1)} collective-permute-done((f32[512,128]{1,0:T(8,128)S(1)}, f32[512,128]{1,0:T(8,128)S(1)}, u32[]{:S(2)}, u32[]{:S(2)}) %collective-permute-start.19) | collective-permute-done | bytes 262176 | tf_op jit(solution)/shard_map/ppermute | solution.py:511
  78.1 1.0 %shard_map.98 = (f32[2,256,256]{2,1,0:T(8,128)}, f32[2,128,128]{2,1,0:T(8,128)}) custom-call(f32[2,3,384,128]{3,2,1,0:T(8,128)S(1)} %get-tuple-element.74.ext_ref.tile_ref, f32[2,256,128]{2,1,0:T(8,128)S(1)} %shard_map.96.light_ref, f32[3,512,128]{2,1,0:T(8,128)S(1)} %get-tuple-element.84.body_ref, f32[3,256,128]{2,1,0:T(8,128)S(1)} %collective-permute-done.18.from_above, ...), custom_call_target="tpu_custom_call" | custom-call | tf_op jit(solution)/shard_map/pallas_call | solution.py:558
  (18 shorter events, 0.2 us)
Async XLA Ops:
  0.6 1.0 %copy-start = (f32[2,256,256]{2,1,0:T(8,128)S(1)}, f32[2,256,256]{2,1,0:T(8,128)}, u32[]{:S(2)}) copy-start(f32[2,256,256]{2,1,0:T(8,128)} %field_ref.1) | copy-start | bytes 1572868
  1.8 12.6 %collective-permute-start = (f32[2,256,128]{2,1,0:T(8,128)S(1)}, f32[2,256,128]{2,1,0:T(8,128)S(1)}, u32[]{:S(2)}, u32[]{:S(2)}) collective-permute-start(f32[2,256,128]{2,1,0:T(8,128)S(1)} %get-tuple-element.46), channel_id=1, source_target_pairs={{1,0},{2,1},{3,2},{5,4},{6,5},{7,6},{9,8},{10,9},{11,10},{13,12},{... | collective-permute-start | bytes 786440 | tf_op jit(solution)/shard_map/ppermute | solution.py:511
  3.1 11.3 %collective-permute-start.1 = (f32[2,128,256]{2,1,0:T(8,128)S(1)}, f32[2,128,256]{2,1,0:T(8,128)S(1)}, u32[]{:S(2)}, u32[]{:S(2)}) collective-permute-start(f32[2,128,256]{2,1,0:T(8,128)S(1)} %get-tuple-element.47), channel_id=1, source_target_pairs={{4,0},{8,4},{12,8},{16,12},{20,16},{24,20},{28,24},{5,1},{9,5},{13... | collective-permute-start | bytes 786440 | tf_op jit(solution)/shard_map/ppermute | solution.py:511
  4.4 10.0 %collective-permute-start.2 = (f32[2,128,128]{2,1,0:T(8,128)S(1)}, f32[2,128,128]{2,1,0:T(8,128)S(1)}, u32[]{:S(2)}, u32[]{:S(2)}) collective-permute-start(f32[2,128,128]{2,1,0:T(8,128)S(1)} %get-tuple-element.48), channel_id=1, source_target_pairs={{5,0},{6,1},{7,2},{9,4},{10,5},{11,6},{13,8},{14,9},{15,10},{17,12... | collective-permute-start | bytes 393224 | tf_op jit(solution)/shard_map/ppermute | solution.py:610
  6.4 1.0 %copy-start.1 = (bf16[4,256,256]{2,1,0:T(8,128)(2,1)S(1)}, bf16[4,256,256]{2,1,0:T(8,128)(2,1)}, u32[]{:S(2)}) copy-start(bf16[4,256,256]{2,1,0:T(8,128)(2,1)} %constant.4.clone.tables_ref) | copy-start | bytes 1572868
  7.4 0.9 %copy-start.2 = (s32[1,1,4,128,128]{4,3,2,1,0:T(8,128)S(1)}, s32[1,1,4,128,128]{4,3,2,1,0:T(8,128)}, u32[]{:S(2)}) copy-start(s32[1,1,4,128,128]{4,3,2,1,0:T(8,128)} %param.9) | copy-start | bytes 786436
  8.4 0.9 %copy-start.3 = (f32[2,128,128]{2,1,0:T(8,128)S(1)}, f32[2,128,128]{2,1,0:T(8,128)}, u32[]{:S(2)}) copy-start(f32[2,128,128]{2,1,0:T(8,128)} %probe_ref.1) | copy-start | bytes 393220
  9.3 0.7 copy-start.4
  9.9 0.7 copy-start.5
  17.2 4.6 %collective-permute-start.3 = (f32[3,64,128]{2,1,0:T(8,128)S(1)}, f32[3,64,128]{2,1,0:T(8,128)S(1)}, u32[]{:S(2)}, u32[]{:S(2)}) collective-permute-start(f32[3,64,128]{2,1,0:T(8,128)S(1)} %get-tuple-element.54), channel_id=1, source_target_pairs={{0,4},{4,0},{8,12},{12,8},{16,20},{20,16},{24,28},{28,24},{1,5},{5... | collective-permute-start | bytes 294920 | tf_op jit(solution)/shard_map/ppermute | solution.py:524
  19.5 11.2 %collective-permute-start.7 = (f32[776,128]{1,0:T(8,128)S(1)}, f32[776,128]{1,0:T(8,128)S(1)}, u32[]{:S(2)}, u32[]{:S(2)}) collective-permute-start(f32[776,128]{1,0:T(8,128)S(1)} %get-tuple-element.55.inner_ref), channel_id=1, source_target_pairs={{0,1},{1,0},{2,3},{3,2},{4,5},{5,4},{6,7},{7,6},{8,9},{9,8},{10,11... | collective-permute-start | bytes 1191944 | tf_op jit(solution)/shard_map/ppermute | solution.py:519
  21.1 9.6 %collective-permute-start.8 = (f32[776,128]{1,0:T(8,128)S(1)}, f32[776,128]{1,0:T(8,128)S(1)}, u32[]{:S(2)}, u32[]{:S(2)}) collective-permute-start(f32[776,128]{1,0:T(8,128)S(1)} %get-tuple-element.57.outer_ref), channel_id=1, source_target_pairs={{1,2},{2,1},{5,6},{6,5},{9,10},{10,9},{13,14},{14,13},{17,18},{18,... | collective-permute-start | bytes 1191944 | tf_op jit(solution)/shard_map/ppermute | solution.py:519
  21.8 5.2 %collective-permute-start.5 = (f32[3,64,128]{2,1,0:T(8,128)S(1)}, f32[3,64,128]{2,1,0:T(8,128)S(1)}, u32[]{:S(2)}, u32[]{:S(2)}) collective-permute-start(f32[3,64,128]{2,1,0:T(8,128)S(1)} %add.41), channel_id=1, source_target_pairs={{0,16},{4,20},{8,24},{12,28},{16,0},{20,4},{24,8},{28,12},{1,17},{... | collective-permute-start | bytes 294920 | tf_op jit(solution)/shard_map/ppermute | solution.py:524
  23.4 6.2 %collective-permute-start.6 = (f32[3,64,128]{2,1,0:T(8,128)S(1)}, f32[3,64,128]{2,1,0:T(8,128)S(1)}, u32[]{:S(2)}, u32[]{:S(2)}) collective-permute-start(f32[3,64,128]{2,1,0:T(8,128)S(1)} %add.41), channel_id=1, source_target_pairs={{0,24},{4,28},{8,16},{12,20},{16,8},{20,12},{24,0},{28,4},{1,25},{... | collective-permute-start | bytes 294920 | tf_op jit(solution)/shard_map/ppermute | solution.py:524
  24.8 5.0 %collective-permute-start.4 = (f32[3,64,128]{2,1,0:T(8,128)S(1)}, f32[3,64,128]{2,1,0:T(8,128)S(1)}, u32[]{:S(2)}, u32[]{:S(2)}) collective-permute-start(f32[3,64,128]{2,1,0:T(8,128)S(1)} %add.41), channel_id=1, source_target_pairs={{0,8},{4,12},{8,0},{12,4},{16,24},{20,28},{24,16},{28,20},{1,9},{5... | collective-permute-start | bytes 294920 | tf_op jit(solution)/shard_map/ppermute | solution.py:524
  30.9 7.1 %collective-permute-start.10 = (f32[792,128]{1,0:T(8,128)S(1)}, f32[792,128]{1,0:T(8,128)S(1)}, u32[]{:S(2)}, u32[]{:S(2)}) collective-permute-start(f32[792,128]{1,0:T(8,128)S(1)} %get-tuple-element.61), channel_id=1, source_target_pairs={{0,4},{4,0},{8,12},{12,8},{16,20},{20,16},{24,28},{28,24},{1,5},{5... | collective-permute-start | bytes 1216520 | tf_op jit(solution)/shard_map/ppermute | solution.py:519
  31.0 11.1 %collective-permute-start.12 = (f32[792,128]{1,0:T(8,128)S(1)}, f32[792,128]{1,0:T(8,128)S(1)}, u32[]{:S(2)}, u32[]{:S(2)}) collective-permute-start(f32[792,128]{1,0:T(8,128)S(1)} %get-tuple-element.72), channel_id=1, source_target_pairs={{4,8},{8,4},{12,16},{16,12},{20,24},{24,20},{5,9},{9,5},{13,17},{1... | collective-permute-start | bytes 1216520 | tf_op jit(solution)/shard_map/ppermute | solution.py:519
  31.7 6.3 %collective-permute-start.9 = (f32[3,64,128]{2,1,0:T(8,128)S(1)}, f32[3,64,128]{2,1,0:T(8,128)S(1)}, u32[]{:S(2)}, u32[]{:S(2)}) collective-permute-start(f32[3,64,128]{2,1,0:T(8,128)S(1)} %add_add_fusion), channel_id=1, source_target_pairs={{0,1},{1,0},{2,3},{3,2},{4,5},{5,4},{6,7},{7,6},{8,9},{9,8},{10,11... | collective-permute-start | bytes 294920 | tf_op jit(solution)/shard_map/ppermute | solution.py:524
  38.0 5.6 %collective-permute-start.11 = (f32[3,64,128]{2,1,0:T(8,128)S(1)}, f32[3,64,128]{2,1,0:T(8,128)S(1)}, u32[]{:S(2)}, u32[]{:S(2)}) collective-permute-start(f32[3,64,128]{2,1,0:T(8,128)S(1)} %add.45), channel_id=1, source_target_pairs={{0,2},{1,3},{2,0},{3,1},{4,6},{5,7},{6,4},{7,5},{8,10},{9,11},{10,... | collective-permute-start | bytes 294920 | tf_op jit(solution)/shard_map/ppermute | solution.py:524
  43.6 4.4 %collective-permute-start.13 = (f32[2,64,128]{2,1,0:T(8,128)S(1)}, f32[2,64,128]{2,1,0:T(8,128)S(1)}, u32[]{:S(2)}, u32[]{:S(2)}) collective-permute-start(f32[2,64,128]{2,1,0:T(8,128)S(1)} %fusion.1.half_ref), channel_id=1, source_target_pairs={{0,4},{4,0},{8,12},{12,8},{16,20},{20,16},{24,28},{28,24},{1,5},{5... | collective-permute-start | bytes 196616 | tf_op jit(solution)/shard_map/ppermute | solution.py:524
  50.4 1.4 %collective-permute-start.14 = (f32[3,64,128]{2,1,0:T(8,128)S(1)}, f32[3,64,128]{2,1,0:T(8,128)S(1)}, u32[]{:S(2)}, u32[]{:S(2)}) collective-permute-start(f32[3,64,128]{2,1,0:T(8,128)S(1)} %get-tuple-element.77), channel_id=1, source_target_pairs={{0,4},{4,0},{8,12},{12,8},{16,20},{20,16},{24,28},{28,24},{1,5},{5... | collective-permute-start | bytes 294920 | tf_op jit(solution)/shard_map/ppermute | solution.py:524
  51.8 5.0 %collective-permute-start.15 = (f32[3,64,128]{2,1,0:T(8,128)S(1)}, f32[3,64,128]{2,1,0:T(8,128)S(1)}, u32[]{:S(2)}, u32[]{:S(2)}) collective-permute-start(f32[3,64,128]{2,1,0:T(8,128)S(1)} %add.48), channel_id=1, source_target_pairs={{0,1},{1,0},{2,3},{3,2},{4,5},{5,4},{6,7},{7,6},{8,9},{9,8},{10,11... | collective-permute-start | bytes 294920 | tf_op jit(solution)/shard_map/ppermute | solution.py:524
  53.4 18.9 %collective-permute-start.18 = (f32[3,256,128]{2,1,0:T(8,128)S(1)}, f32[3,256,128]{2,1,0:T(8,128)S(1)}, u32[]{:S(2)}, u32[]{:S(2)}) collective-permute-start(f32[3,256,128]{2,1,0:T(8,128)S(1)} %get-tuple-element.79), channel_id=1, source_target_pairs={{0,4},{4,8},{8,12},{12,16},{16,20},{20,24},{24,28},{1,5},{5,9},{9,... | collective-permute-start | bytes 1179656 | tf_op jit(solution)/shard_map/ppermute | solution.py:511
  56.8 5.6 %collective-permute-start.16 = (f32[3,64,128]{2,1,0:T(8,128)S(1)}, f32[3,64,128]{2,1,0:T(8,128)S(1)}, u32[]{:S(2)}, u32[]{:S(2)}) collective-permute-start(f32[3,64,128]{2,1,0:T(8,128)S(1)} %add.49), channel_id=1, source_target_pairs={{0,2},{1,3},{2,0},{3,1},{4,6},{5,7},{6,4},{7,5},{8,10},{9,11},{10,... | collective-permute-start | bytes 294920 | tf_op jit(solution)/shard_map/ppermute | solution.py:524
  62.4 8.4 %collective-permute-start.17 = (f32[3,64,128]{2,1,0:T(8,128)S(1)}, f32[3,64,128]{2,1,0:T(8,128)S(1)}, u32[]{:S(2)}, u32[]{:S(2)}) collective-permute-start(f32[3,64,128]{2,1,0:T(8,128)S(1)} %add.50), channel_id=1, source_target_pairs={{0,8},{4,12},{8,0},{12,4},{16,24},{20,28},{24,16},{28,20},{1,9},{5... | collective-permute-start | bytes 294920 | tf_op jit(solution)/shard_map/ppermute | solution.py:524
  70.9 4.7 %collective-permute-start.20 = (f32[3,64,128]{2,1,0:T(8,128)S(1)}, f32[3,64,128]{2,1,0:T(8,128)S(1)}, u32[]{:S(2)}, u32[]{:S(2)}) collective-permute-start(f32[3,64,128]{2,1,0:T(8,128)S(1)} %add.51), channel_id=1, source_target_pairs={{0,16},{4,20},{8,24},{12,28},{16,0},{20,4},{24,8},{28,12},{1,17},{... | collective-permute-start | bytes 294920 | tf_op jit(solution)/shard_map/ppermute | solution.py:524
  72.4 5.7 %collective-permute-start.19 = (f32[512,128]{1,0:T(8,128)S(1)}, f32[512,128]{1,0:T(8,128)S(1)}, u32[]{:S(2)}, u32[]{:S(2)}) collective-permute-start(f32[512,128]{1,0:T(8,128)S(1)} %shard_map.97), channel_id=1, source_target_pairs={{0,1},{1,2},{2,3},{4,5},{5,6},{6,7},{8,9},{9,10},{10,11},{12,13},{... | collective-permute-start | bytes 786440 | tf_op jit(solution)/shard_map/ppermute | solution.py:511
  75.6 1.3 %collective-permute-start.21 = (f32[2,64,128]{2,1,0:T(8,128)S(1)}, f32[2,64,128]{2,1,0:T(8,128)S(1)}, u32[]{:S(2)}, u32[]{:S(2)}) collective-permute-start(f32[2,64,128]{2,1,0:T(8,128)S(1)} %fusion.half_ref), channel_id=1, source_target_pairs={{0,4},{4,0},{8,12},{12,8},{16,20},{20,16},{24,28},{28,24},{1,5},{5... | collective-permute-start | bytes 196616 | tf_op jit(solution)/shard_map/ppermute | solution.py:524

commit v8 on v7

--- a/solution.py
+++ b/solution.py
@@ -665,10 +665,10 @@
         row_infos.append(info_rows)
         return ext, light
 
-    part = butterfly(part, "col", 1, last_col)
+    part = butterfly(part, "col", last_col)
     part, from_inner, light = tie(part, from_inner, light)
     ext, light = update(ext, light, from_inner, 0)
-    part = butterfly(part, "col", last_col)
+    part = butterfly(part, "col", 1, last_col)
     new_half = stepped(own, part)
     tile, _ = update(ext, light, from_outer, 1)
     new_half, tile = tie(new_half, tile)
@@ -704,7 +704,6 @@
     part = butterfly(part, "col", last_col)
     from_left = shift(right, "col", 1)
     part = butterfly(part, "row", 2, last_row)
-    part, light = tie(part, light)
     part = butterfly(part, "row", last_row)
     last_half = stepped(new_half, part)
     last_other = flip(last_half, "row", 1)

time: 79.6 us -> 79.8 us (level)
    ppermute x13, starting transfers between devices: 27.4 us -> 28.6 us  [flip(): lax.ppermute(value, axis, [(source, source ^ mask) for source in range(co...]
  transfers between devices with their start and end apart: 22 -> 22, of which waited for: 13 -> 12; matrix products, arithmetic and copies ran while one was open for 0% -> 0% of each run, Pallas kernels for 10% -> 10%
where the time goes in v8:
time: 79.8 us; the launch traced here: 79.4 us
  starting transfers between devices  38.7 us (48%)
  waiting for transfers between devices  19.6 us (25%)
  Pallas kernels  14.1 us (18%)
  local copies, waits for them, and re-layouts  5.23 us (7%)
  between operations  1.57 us (2%)
    ppermute x13, starting transfers between devices, flip(): lax.ppermute(value, axis, [(source, source ^ mask) for source in range(co...  28.6 us
    ppermute x13, waiting for transfers between devices, flip(): lax.ppermute(value, axis, [(source, source ^ mask) for source in range(co...  14.3 us
    pallas_call x13, Pallas kernels, call(): pl.pallas_call(kernel, out_shape=[shape_of(spec) for spec in outs], in_sp...  14.1 us
    ppermute x4, starting transfers between devices, shift(): return lax.ppermute(value, axis, pairs)  5.78 us
    unnamed x12, local copies, waits for them, and re-layouts  5.23 us
    ppermute x1, waiting for transfers between devices, local(): lax.ppermute(corner, ('row', 'col'), [((r + 1) * count_cols + c + 1, r *...  3.22 us
    ppermute x4, starting transfers between devices, swap(): return lax.ppermute(value, axis, pairs)  3.02 us
  transfers between devices with their start and end apart: 22, of which 12 were waited for; matrix products, arithmetic and copies ran while one was open for 0% of the time, Pallas kernels for 10%

profile of v8, /device:TPU:0, one launch (start us, length us, event | category | flops | bytes accessed | tf_op | source)
XLA Modules:
  0.0 79.4 jit_solution(3256308954393177399)
XLA Ops:
  0.6 0.0 copy-start
  0.6 1.0 %copy-done = f32[2,256,256]{2,1,0:T(8,128)S(1)} copy-done((f32[2,256,256]{2,1,0:T(8,128)S(1)}, f32[2,256,256]{2,1,0:T(8,128)}, u32[]{:S(2)}) %copy-start) | copy-done | bytes 524312
  1.7 0.2 shard_map.87
  1.8 1.3 %collective-permute-start = (f32[2,256,128]{2,1,0:T(8,128)S(1)}, f32[2,256,128]{2,1,0:T(8,128)S(1)}, u32[]{:S(2)}, u32[]{:S(2)}) collective-permute-start(f32[2,256,128]{2,1,0:T(8,128)S(1)} %get-tuple-element.44), channel_id=1, source_target_pairs={{1,0},{2,1},{3,2},{5,4},{6,5},{7,6},{9,8},{10,9},{11,10},{13,12},{... | collective-permute-start | bytes 786440 | tf_op jit(solution)/shard_map/ppermute | solution.py:511
  3.1 1.3 %collective-permute-start.1 = (f32[2,128,256]{2,1,0:T(8,128)S(1)}, f32[2,128,256]{2,1,0:T(8,128)S(1)}, u32[]{:S(2)}, u32[]{:S(2)}) collective-permute-start(f32[2,128,256]{2,1,0:T(8,128)S(1)} %get-tuple-element.45), channel_id=1, source_target_pairs={{4,0},{8,4},{12,8},{16,12},{20,16},{24,20},{28,24},{5,1},{9,5},{13... | collective-permute-start | bytes 786440 | tf_op jit(solution)/shard_map/ppermute | solution.py:511
  4.4 1.3 %collective-permute-start.2 = (f32[2,128,128]{2,1,0:T(8,128)S(1)}, f32[2,128,128]{2,1,0:T(8,128)S(1)}, u32[]{:S(2)}, u32[]{:S(2)}) collective-permute-start(f32[2,128,128]{2,1,0:T(8,128)S(1)} %get-tuple-element.46), channel_id=1, source_target_pairs={{5,0},{6,1},{7,2},{9,4},{10,5},{11,6},{13,8},{14,9},{15,10},{17,12... | collective-permute-start | bytes 393224 | tf_op jit(solution)/shard_map/ppermute | solution.py:610
  6.4 0.0 copy-start.1
  6.4 1.0 %copy-done.1 = bf16[4,256,256]{2,1,0:T(8,128)(2,1)S(1)} copy-done((bf16[4,256,256]{2,1,0:T(8,128)(2,1)S(1)}, bf16[4,256,256]{2,1,0:T(8,128)(2,1)}, u32[]{:S(2)}) %copy-start.1) | copy-done | bytes 524312
  7.4 0.9 %copy-done.2 = s32[1,1,4,128,128]{4,3,2,1,0:T(8,128)S(1)} copy-done((s32[1,1,4,128,128]{4,3,2,1,0:T(8,128)S(1)}, s32[1,1,4,128,128]{4,3,2,1,0:T(8,128)}, u32[]{:S(2)}) %copy-start.2) | copy-done | bytes 262168
  8.4 0.9 %copy-done.3 = f32[2,128,128]{2,1,0:T(8,128)S(1)} copy-done((f32[2,128,128]{2,1,0:T(8,128)S(1)}, f32[2,128,128]{2,1,0:T(8,128)}, u32[]{:S(2)}) %copy-start.3) | copy-done | bytes 131096
  9.3 0.7 copy-done.4
  9.9 0.7 copy-done.5
  10.6 0.6 shard_map.86
  11.2 3.2 %collective-permute-done.2.corner_ref = f32[2,128,128]{2,1,0:T(8,128)S(1)} collective-permute-done((f32[2,128,128]{2,1,0:T(8,128)S(1)}, f32[2,128,128]{2,1,0:T(8,128)S(1)}, u32[]{:S(2)}, u32[]{:S(2)}) %collective-permute-start.2) | collective-permute-done | bytes 131104 | tf_op jit(solution)/shard_map/ppermute | solution.py:610
  14.5 0.0 collective-permute-done.right_ref
  14.5 0.0 collective-permute-done.1.below_ref
  14.5 2.7 %shard_map.88 = (f32[2,3,384,128]{3,2,1,0:T(8,128)S(1)}, f32[3,64,128]{2,1,0:T(8,128)S(1)}, f32[3,64,128]{2,1,0:T(8,128)S(1)}, f32[776,128]{1,0:T(8,128)S(1)}, f...) custom-call(f32[2,3,384,128]{3,2,1,0:T(8,128)S(1)} %get-tuple-element.43.start_ref, ...), custom_call_target="tpu_custom_call", output_to_operand_aliasing={{0}: (0, {})} | custom-call | tf_op jit(solution)/shard_map/pallas_call | solution.py:558
  17.2 2.4 %collective-permute-start.3 = (f32[3,64,128]{2,1,0:T(8,128)S(1)}, f32[3,64,128]{2,1,0:T(8,128)S(1)}, u32[]{:S(2)}, u32[]{:S(2)}) collective-permute-start(f32[3,64,128]{2,1,0:T(8,128)S(1)} %get-tuple-element.52), channel_id=1, source_target_pairs={{0,4},{4,0},{8,12},{12,8},{16,20},{20,16},{24,28},{28,24},{1,5},{5... | collective-permute-start | bytes 294920 | tf_op jit(solution)/shard_map/ppermute | solution.py:524
  19.5 1.6 %collective-permute-start.7 = (f32[776,128]{1,0:T(8,128)S(1)}, f32[776,128]{1,0:T(8,128)S(1)}, u32[]{:S(2)}, u32[]{:S(2)}) collective-permute-start(f32[776,128]{1,0:T(8,128)S(1)} %get-tuple-element.53.inner_ref), channel_id=1, source_target_pairs={{0,1},{1,0},{2,3},{3,2},{4,5},{5,4},{6,7},{7,6},{8,9},{9,8},{10,11... | collective-permute-start | bytes 1191944 | tf_op jit(solution)/shard_map/ppermute | solution.py:519
  21.1 0.7 collective-permute-start.8
  21.8 0.0 collective-permute-done.3
  21.8 1.6 %collective-permute-start.5 = (f32[3,64,128]{2,1,0:T(8,128)S(1)}, f32[3,64,128]{2,1,0:T(8,128)S(1)}, u32[]{:S(2)}, u32[]{:S(2)}) collective-permute-start(f32[3,64,128]{2,1,0:T(8,128)S(1)} %add.41), channel_id=1, source_target_pairs={{0,16},{4,20},{8,24},{12,28},{16,0},{20,4},{24,8},{28,12},{1,17},{... | collective-permute-start | bytes 294920 | tf_op jit(solution)/shard_map/ppermute | solution.py:524
  23.4 1.4 %collective-permute-start.6 = (f32[3,64,128]{2,1,0:T(8,128)S(1)}, f32[3,64,128]{2,1,0:T(8,128)S(1)}, u32[]{:S(2)}, u32[]{:S(2)}) collective-permute-start(f32[3,64,128]{2,1,0:T(8,128)S(1)} %add.41), channel_id=1, source_target_pairs={{0,24},{4,28},{8,16},{12,20},{16,8},{20,12},{24,0},{28,4},{1,25},{... | collective-permute-start | bytes 294920 | tf_op jit(solution)/shard_map/ppermute | solution.py:524
  24.8 0.5 collective-permute-start.4
  25.4 1.7 %collective-permute-done.5 = f32[3,64,128]{2,1,0:T(8,128)S(1)} collective-permute-done((f32[3,64,128]{2,1,0:T(8,128)S(1)}, f32[3,64,128]{2,1,0:T(8,128)S(1)}, u32[]{:S(2)}, u32[]{:S(2)}) %collective-permute-start.5) | collective-permute-done | bytes 98336 | tf_op jit(solution)/shard_map/ppermute | solution.py:524
  27.1 2.6 %collective-permute-done.6 = f32[3,64,128]{2,1,0:T(8,128)S(1)} collective-permute-done((f32[3,64,128]{2,1,0:T(8,128)S(1)}, f32[3,64,128]{2,1,0:T(8,128)S(1)}, u32[]{:S(2)}, u32[]{:S(2)}) %collective-permute-start.6) | collective-permute-done | bytes 98336 | tf_op jit(solution)/shard_map/ppermute | solution.py:524
  29.6 0.2 collective-permute-done.4
  29.9 0.8 %collective-permute-done.7.from_inner = f32[776,128]{1,0:T(8,128)S(1)} collective-permute-done((f32[776,128]{1,0:T(8,128)S(1)}, f32[776,128]{1,0:T(8,128)S(1)}, u32[]{:S(2)}, u32[]{:S(2)}) %collective-permute-start.7) | collective-permute-done | bytes 397344 | tf_op jit(solution)/shard_map/ppermute | solution.py:519
  30.7 0.0 collective-permute-done.8.from_outer
  30.7 0.2 shard_map.89
  30.9 0.1 collective-permute-start.10
  31.0 0.7 collective-permute-start.12
  31.7 4.6 %collective-permute-start.9 = (f32[3,64,128]{2,1,0:T(8,128)S(1)}, f32[3,64,128]{2,1,0:T(8,128)S(1)}, u32[]{:S(2)}, u32[]{:S(2)}) collective-permute-start(f32[3,64,128]{2,1,0:T(8,128)S(1)} %add_add_fusion), channel_id=1, source_target_pairs={{0,2},{1,3},{2,0},{3,1},{4,6},{5,7},{6,4},{7,5},{8,10},{9,11},{10,... | collective-permute-start | bytes 294920 | tf_op jit(solution)/shard_map/ppermute | solution.py:524
  36.2 1.2 %shard_map.90 = (f32[2,3,384,128]{3,2,1,0:T(8,128)S(1)}, f32[5,640,128]{2,1,0:T(8,128)S(1)}) custom-call(f32[2,3,384,128]{3,2,1,0:T(8,128)S(1)} %get-tuple-element.60.ext_ref, f32[3,8,128]{2,1,0:T(8,128)S(1)} %get-tuple-element.61.infos_ref.near_ref, f32[2,128,128]{2,1,0:T(8,128)S(1)} %get-tuple-element.47.probe_ref, ...), custom_call_target="tpu_custom_call", output_to_operand_aliasing={{0}: (0, {})} | custom-call | tf_op jit(solution)/shard_map/pallas_call | solution.py:558
  37.4 1.4 %collective-permute-done.9 = f32[3,64,128]{2,1,0:T(8,128)S(1)} collective-permute-done((f32[3,64,128]{2,1,0:T(8,128)S(1)}, f32[3,64,128]{2,1,0:T(8,128)S(1)}, u32[]{:S(2)}, u32[]{:S(2)}) %collective-permute-start.9) | collective-permute-done | bytes 98336 | tf_op jit(solution)/shard_map/ppermute | solution.py:524
  38.9 0.0 collective-permute-done.10.strip_ref
  38.9 2.1 %collective-permute-start.11 = (f32[3,64,128]{2,1,0:T(8,128)S(1)}, f32[3,64,128]{2,1,0:T(8,128)S(1)}, u32[]{:S(2)}, u32[]{:S(2)}) collective-permute-start(f32[3,64,128]{2,1,0:T(8,128)S(1)} %add.45), channel_id=1, source_target_pairs={{0,1},{1,0},{2,3},{3,2},{4,5},{5,4},{6,7},{7,6},{8,9},{9,8},{10,11... | collective-permute-start | bytes 294920 | tf_op jit(solution)/shard_map/ppermute | solution.py:524
  41.0 1.4 %shard_map.91 = (f32[2,3,384,128]{3,2,1,0:T(8,128)S(1)}, f32[5,640,128]{2,1,0:T(8,128)S(1)}, f32[3,8,128]{2,1,0:T(8,128)S(1)}) custom-call(f32[2,3,384,128]{3,2,1,0:T(8,128)S(1)} %get-tuple-element.65.ext_ref, f32[5,640,128]{2,1,0:T(8,128)S(1)} %get-tuple-element.66.light_in, ...), custom_call_target="tpu_custom_call", output_to_operand_aliasing={{0}: (0, {}), {1}: (1, {})} | custom-call | tf_op jit(solution)/shard_map/pallas_call | solution.py:558
  42.4 0.0 collective-permute-done.12.strip_ref
  42.4 1.1 %shard_map.92 = (f32[2,3,384,128]{3,2,1,0:T(8,128)S(1)}, f32[5,640,128]{2,1,0:T(8,128)S(1)}, f32[3,8,128]{2,1,0:T(8,128)S(1)}) custom-call(f32[2,3,384,128]{3,2,1,0:T(8,128)S(1)} %get-tuple-element.68.ext_ref, f32[5,640,128]{2,1,0:T(8,128)S(1)} %get-tuple-element.69.light_in, ...), custom_call_target="tpu_custom_call", output_to_operand_aliasing={{0}: (0, {}), {1}: (1, {})} | custom-call | tf_op jit(solution)/shard_map/pallas_call | solution.py:558
  43.5 0.1 collective-permute-done.11
  43.6 2.4 %collective-permute-start.13 = (f32[2,64,128]{2,1,0:T(8,128)S(1)}, f32[2,64,128]{2,1,0:T(8,128)S(1)}, u32[]{:S(2)}, u32[]{:S(2)}) collective-permute-start(f32[2,64,128]{2,1,0:T(8,128)S(1)} %fusion.1.half_ref), channel_id=1, source_target_pairs={{0,4},{4,0},{8,12},{12,8},{16,20},{20,16},{24,28},{28,24},{1,5},{5... | collective-permute-start | bytes 196616 | tf_op jit(solution)/shard_map/ppermute | solution.py:524
  46.0 1.0 %shard_map.94.patches_ref = f32[4,2,128,128]{3,2,1,0:T(8,128)S(1)} custom-call(f32[2,3,384,128]{3,2,1,0:T(8,128)S(1)} %get-tuple-element.72.ext_ref.tile_ref, f32[8,128]{1,0:T(8,128)S(1)} %get-tuple-element.50.info_ref), custom_call_target="tpu_custom_call" | custom-call | tf_op jit(solution)/shard_map/pallas_call | solution.py:558
  47.0 0.0 collective-permute-done.13.other_ref
  47.0 2.3 %shard_map.95 = (f32[3,64,128]{2,1,0:T(8,128)S(1)}, f32[3,64,128]{2,1,0:T(8,128)S(1)}, f32[4,2,128,128]{3,2,1,0:T(8,128)S(1)}) custom-call(f32[4,2,128,128]{3,2,1,0:T(8,128)S(1)} %shard_map.94.patches_ref, f32[2,64,128]{2,1,0:T(8,128)S(1)} %fusion.1.half_ref, f32[2,64,128]{2,1,0:T(8,128)S(1)} %collective-permute-done.13.other_ref, ...), custom_call_target="tpu_custom_call" | custom-call | tf_op jit(solution)/shard_map/pallas_call | solution.py:558
  49.3 0.3 collective-permute-start.16
  49.7 1.0 %shard_map.96 = (f32[3,512,128]{2,1,0:T(8,128)S(1)}, f32[3,256,128]{2,1,0:T(8,128)S(1)}) custom-call(f32[4,2,128,128]{3,2,1,0:T(8,128)S(1)} %get-tuple-element.76.updates_ref, f32[2,64,128]{2,1,0:T(8,128)S(1)} %fusion.1.half_ref, f32[2,64,128]{2,1,0:T(8,128)S(1)} %collective-permute-done.13.other_ref, f32[8,128]{1,0:T(8,128)S(1)} %get-tuple-element.50.info_ref), custom_call_target="tpu_custom_call" | custom-call | tf_op jit(solution)/shard_map/pallas_call | solution.py:558
  50.7 0.0 collective-permute-done.16
  50.7 2.5 %collective-permute-start.17 = (f32[3,64,128]{2,1,0:T(8,128)S(1)}, f32[3,64,128]{2,1,0:T(8,128)S(1)}, u32[]{:S(2)}, u32[]{:S(2)}) collective-permute-start(f32[3,64,128]{2,1,0:T(8,128)S(1)} %add.48), channel_id=1, source_target_pairs={{0,1},{1,0},{2,3},{3,2},{4,5},{5,4},{6,7},{7,6},{8,9},{9,8},{10,11... | collective-permute-start | bytes 294920 | tf_op jit(solution)/shard_map/ppermute | solution.py:524
  53.2 1.9 %collective-permute-start.14 = (f32[3,256,128]{2,1,0:T(8,128)S(1)}, f32[3,256,128]{2,1,0:T(8,128)S(1)}, u32[]{:S(2)}, u32[]{:S(2)}) collective-permute-start(f32[3,256,128]{2,1,0:T(8,128)S(1)} %get-tuple-element.78), channel_id=1, source_target_pairs={{0,4},{4,8},{8,12},{12,16},{16,20},{20,24},{24,28},{1,5},{5,9},{9,... | collective-permute-start | bytes 1179656 | tf_op jit(solution)/shard_map/ppermute | solution.py:511
  55.1 1.3 %collective-permute-done.17 = f32[3,64,128]{2,1,0:T(8,128)S(1)} collective-permute-done((f32[3,64,128]{2,1,0:T(8,128)S(1)}, f32[3,64,128]{2,1,0:T(8,128)S(1)}, u32[]{:S(2)}, u32[]{:S(2)}) %collective-permute-start.17) | collective-permute-done | bytes 98336 | tf_op jit(solution)/shard_map/ppermute | solution.py:524
  56.4 2.6 %collective-permute-start.18 = (f32[3,64,128]{2,1,0:T(8,128)S(1)}, f32[3,64,128]{2,1,0:T(8,128)S(1)}, u32[]{:S(2)}, u32[]{:S(2)}) collective-permute-start(f32[3,64,128]{2,1,0:T(8,128)S(1)} %add.49), channel_id=1, source_target_pairs={{0,2},{1,3},{2,0},{3,1},{4,6},{5,7},{6,4},{7,5},{8,10},{9,11},{10,... | collective-permute-start | bytes 294920 | tf_op jit(solution)/shard_map/ppermute | solution.py:524
  59.0 3.1 %collective-permute-done.18 = f32[3,64,128]{2,1,0:T(8,128)S(1)} collective-permute-done((f32[3,64,128]{2,1,0:T(8,128)S(1)}, f32[3,64,128]{2,1,0:T(8,128)S(1)}, u32[]{:S(2)}, u32[]{:S(2)}) %collective-permute-start.18) | collective-permute-done | bytes 98336 | tf_op jit(solution)/shard_map/ppermute | solution.py:524
  62.1 6.0 %collective-permute-start.19 = (f32[3,64,128]{2,1,0:T(8,128)S(1)}, f32[3,64,128]{2,1,0:T(8,128)S(1)}, u32[]{:S(2)}, u32[]{:S(2)}) collective-permute-start(f32[3,64,128]{2,1,0:T(8,128)S(1)} %add.50), channel_id=1, source_target_pairs={{0,8},{4,12},{8,0},{12,4},{16,24},{20,28},{24,16},{28,20},{1,9},{5... | collective-permute-start | bytes 294920 | tf_op jit(solution)/shard_map/ppermute | solution.py:524
  68.1 2.6 %collective-permute-done.19 = f32[3,64,128]{2,1,0:T(8,128)S(1)} collective-permute-done((f32[3,64,128]{2,1,0:T(8,128)S(1)}, f32[3,64,128]{2,1,0:T(8,128)S(1)}, u32[]{:S(2)}, u32[]{:S(2)}) %collective-permute-start.19) | collective-permute-done | bytes 98336 | tf_op jit(solution)/shard_map/ppermute | solution.py:524
  70.7 2.3 %collective-permute-start.20 = (f32[3,64,128]{2,1,0:T(8,128)S(1)}, f32[3,64,128]{2,1,0:T(8,128)S(1)}, u32[]{:S(2)}, u32[]{:S(2)}) collective-permute-start(f32[3,64,128]{2,1,0:T(8,128)S(1)} %add.51), channel_id=1, source_target_pairs={{0,16},{4,20},{8,24},{12,28},{16,0},{20,4},{24,8},{28,12},{1,17},{... | collective-permute-start | bytes 294920 | tf_op jit(solution)/shard_map/ppermute | solution.py:524
  73.0 0.0 collective-permute-done.14.from_above
  73.0 1.3 %collective-permute-start.15 = (f32[512,128]{1,0:T(8,128)S(1)}, f32[512,128]{1,0:T(8,128)S(1)}, u32[]{:S(2)}, u32[]{:S(2)}) collective-permute-start(f32[512,128]{1,0:T(8,128)S(1)} %shard_map.97), channel_id=1, source_target_pairs={{0,1},{1,2},{2,3},{4,5},{5,6},{6,7},{8,9},{9,10},{10,11},{12,13},{... | collective-permute-start | bytes 786440 | tf_op jit(solution)/shard_map/ppermute | solution.py:511
  74.3 1.3 %collective-permute-done.20 = f32[3,64,128]{2,1,0:T(8,128)S(1)} collective-permute-done((f32[3,64,128]{2,1,0:T(8,128)S(1)}, f32[3,64,128]{2,1,0:T(8,128)S(1)}, u32[]{:S(2)}, u32[]{:S(2)}) %collective-permute-start.20) | collective-permute-done | bytes 98336 | tf_op jit(solution)/shard_map/ppermute | solution.py:524
  75.6 0.1 collective-permute-start.21
  75.7 1.5 %shard_map.93.light_ref = f32[2,256,128]{2,1,0:T(8,128)S(1)} custom-call(f32[3,8,128]{2,1,0:T(8,128)S(1)} %get-tuple-element.61.infos_ref.near_ref, f32[3,8,128]{2,1,0:T(8,128)S(1)} %get-tuple-element.73.inner_ref, f32[3,8,128]{2,1,0:T(8,128)S(1)} %get-tuple-element.74.outer_ref, f32[2,64,128]{2,1,0:T(8,128)S(1)} %fusion.1.half_ref, ...), custom_call_target="tpu_custom_call" | custom-call | tf_op jit(solution)/shard_map/pallas_call | solution.py:558
  77.2 0.0 collective-permute-done.21.other_ref
  77.2 1.2 %collective-permute-done.15.from_left = f32[512,128]{1,0:T(8,128)S(1)} collective-permute-done((f32[512,128]{1,0:T(8,128)S(1)}, f32[512,128]{1,0:T(8,128)S(1)}, u32[]{:S(2)}, u32[]{:S(2)}) %collective-permute-start.15) | collective-permute-done | bytes 262176 | tf_op jit(solution)/shard_map/ppermute | solution.py:511
  78.4 1.0 %shard_map.98 = (f32[2,256,256]{2,1,0:T(8,128)}, f32[2,128,128]{2,1,0:T(8,128)}) custom-call(f32[2,3,384,128]{3,2,1,0:T(8,128)S(1)} %get-tuple-element.72.ext_ref.tile_ref, f32[2,256,128]{2,1,0:T(8,128)S(1)} %shard_map.93.light_ref, f32[3,512,128]{2,1,0:T(8,128)S(1)} %get-tuple-element.77.body_ref, f32[3,256,128]{2,1,0:T(8,128)S(1)} %collective-permute-done.14.from_above, ...), custom_call_target="tpu_custom_call" | custom-call | tf_op jit(solution)/shard_map/pallas_call | solution.py:558
  (18 shorter events, 0.2 us)
Async XLA Ops:
  0.6 1.0 %copy-start = (f32[2,256,256]{2,1,0:T(8,128)S(1)}, f32[2,256,256]{2,1,0:T(8,128)}, u32[]{:S(2)}) copy-start(f32[2,256,256]{2,1,0:T(8,128)} %field_ref.1) | copy-start | bytes 1572868
  1.8 12.6 %collective-permute-start = (f32[2,256,128]{2,1,0:T(8,128)S(1)}, f32[2,256,128]{2,1,0:T(8,128)S(1)}, u32[]{:S(2)}, u32[]{:S(2)}) collective-permute-start(f32[2,256,128]{2,1,0:T(8,128)S(1)} %get-tuple-element.44), channel_id=1, source_target_pairs={{1,0},{2,1},{3,2},{5,4},{6,5},{7,6},{9,8},{10,9},{11,10},{13,12},{... | collective-permute-start | bytes 786440 | tf_op jit(solution)/shard_map/ppermute | solution.py:511
  3.1 11.3 %collective-permute-start.1 = (f32[2,128,256]{2,1,0:T(8,128)S(1)}, f32[2,128,256]{2,1,0:T(8,128)S(1)}, u32[]{:S(2)}, u32[]{:S(2)}) collective-permute-start(f32[2,128,256]{2,1,0:T(8,128)S(1)} %get-tuple-element.45), channel_id=1, source_target_pairs={{4,0},{8,4},{12,8},{16,12},{20,16},{24,20},{28,24},{5,1},{9,5},{13... | collective-permute-start | bytes 786440 | tf_op jit(solution)/shard_map/ppermute | solution.py:511
  4.4 10.0 %collective-permute-start.2 = (f32[2,128,128]{2,1,0:T(8,128)S(1)}, f32[2,128,128]{2,1,0:T(8,128)S(1)}, u32[]{:S(2)}, u32[]{:S(2)}) collective-permute-start(f32[2,128,128]{2,1,0:T(8,128)S(1)} %get-tuple-element.46), channel_id=1, source_target_pairs={{5,0},{6,1},{7,2},{9,4},{10,5},{11,6},{13,8},{14,9},{15,10},{17,12... | collective-permute-start | bytes 393224 | tf_op jit(solution)/shard_map/ppermute | solution.py:610
  6.4 1.0 %copy-start.1 = (bf16[4,256,256]{2,1,0:T(8,128)(2,1)S(1)}, bf16[4,256,256]{2,1,0:T(8,128)(2,1)}, u32[]{:S(2)}) copy-start(bf16[4,256,256]{2,1,0:T(8,128)(2,1)} %constant.4.clone.tables_ref) | copy-start | bytes 1572868
  7.4 0.9 %copy-start.2 = (s32[1,1,4,128,128]{4,3,2,1,0:T(8,128)S(1)}, s32[1,1,4,128,128]{4,3,2,1,0:T(8,128)}, u32[]{:S(2)}) copy-start(s32[1,1,4,128,128]{4,3,2,1,0:T(8,128)} %param.9) | copy-start | bytes 786436
  8.4 0.9 %copy-start.3 = (f32[2,128,128]{2,1,0:T(8,128)S(1)}, f32[2,128,128]{2,1,0:T(8,128)}, u32[]{:S(2)}) copy-start(f32[2,128,128]{2,1,0:T(8,128)} %probe_ref.1) | copy-start | bytes 393220
  9.3 0.7 copy-start.4
  9.9 0.7 copy-start.5
  17.2 4.6 %collective-permute-start.3 = (f32[3,64,128]{2,1,0:T(8,128)S(1)}, f32[3,64,128]{2,1,0:T(8,128)S(1)}, u32[]{:S(2)}, u32[]{:S(2)}) collective-permute-start(f32[3,64,128]{2,1,0:T(8,128)S(1)} %get-tuple-element.52), channel_id=1, source_target_pairs={{0,4},{4,0},{8,12},{12,8},{16,20},{20,16},{24,28},{28,24},{1,5},{5... | collective-permute-start | bytes 294920 | tf_op jit(solution)/shard_map/ppermute | solution.py:524
  19.5 11.2 %collective-permute-start.7 = (f32[776,128]{1,0:T(8,128)S(1)}, f32[776,128]{1,0:T(8,128)S(1)}, u32[]{:S(2)}, u32[]{:S(2)}) collective-permute-start(f32[776,128]{1,0:T(8,128)S(1)} %get-tuple-element.53.inner_ref), channel_id=1, source_target_pairs={{0,1},{1,0},{2,3},{3,2},{4,5},{5,4},{6,7},{7,6},{8,9},{9,8},{10,11... | collective-permute-start | bytes 1191944 | tf_op jit(solution)/shard_map/ppermute | solution.py:519
  21.1 9.6 %collective-permute-start.8 = (f32[776,128]{1,0:T(8,128)S(1)}, f32[776,128]{1,0:T(8,128)S(1)}, u32[]{:S(2)}, u32[]{:S(2)}) collective-permute-start(f32[776,128]{1,0:T(8,128)S(1)} %get-tuple-element.55.outer_ref), channel_id=1, source_target_pairs={{1,2},{2,1},{5,6},{6,5},{9,10},{10,9},{13,14},{14,13},{17,18},{18,... | collective-permute-start | bytes 1191944 | tf_op jit(solution)/shard_map/ppermute | solution.py:519
  21.8 5.2 %collective-permute-start.5 = (f32[3,64,128]{2,1,0:T(8,128)S(1)}, f32[3,64,128]{2,1,0:T(8,128)S(1)}, u32[]{:S(2)}, u32[]{:S(2)}) collective-permute-start(f32[3,64,128]{2,1,0:T(8,128)S(1)} %add.41), channel_id=1, source_target_pairs={{0,16},{4,20},{8,24},{12,28},{16,0},{20,4},{24,8},{28,12},{1,17},{... | collective-permute-start | bytes 294920 | tf_op jit(solution)/shard_map/ppermute | solution.py:524
  23.4 6.2 %collective-permute-start.6 = (f32[3,64,128]{2,1,0:T(8,128)S(1)}, f32[3,64,128]{2,1,0:T(8,128)S(1)}, u32[]{:S(2)}, u32[]{:S(2)}) collective-permute-start(f32[3,64,128]{2,1,0:T(8,128)S(1)} %add.41), channel_id=1, source_target_pairs={{0,24},{4,28},{8,16},{12,20},{16,8},{20,12},{24,0},{28,4},{1,25},{... | collective-permute-start | bytes 294920 | tf_op jit(solution)/shard_map/ppermute | solution.py:524
  24.8 5.0 %collective-permute-start.4 = (f32[3,64,128]{2,1,0:T(8,128)S(1)}, f32[3,64,128]{2,1,0:T(8,128)S(1)}, u32[]{:S(2)}, u32[]{:S(2)}) collective-permute-start(f32[3,64,128]{2,1,0:T(8,128)S(1)} %add.41), channel_id=1, source_target_pairs={{0,8},{4,12},{8,0},{12,4},{16,24},{20,28},{24,16},{28,20},{1,9},{5... | collective-permute-start | bytes 294920 | tf_op jit(solution)/shard_map/ppermute | solution.py:524
  30.9 8.0 %collective-permute-start.10 = (f32[792,128]{1,0:T(8,128)S(1)}, f32[792,128]{1,0:T(8,128)S(1)}, u32[]{:S(2)}, u32[]{:S(2)}) collective-permute-start(f32[792,128]{1,0:T(8,128)S(1)} %get-tuple-element.59), channel_id=1, source_target_pairs={{0,4},{4,0},{8,12},{12,8},{16,20},{20,16},{24,28},{28,24},{1,5},{5... | collective-permute-start | bytes 1216520 | tf_op jit(solution)/shard_map/ppermute | solution.py:519
  31.0 11.4 %collective-permute-start.12 = (f32[792,128]{1,0:T(8,128)S(1)}, f32[792,128]{1,0:T(8,128)S(1)}, u32[]{:S(2)}, u32[]{:S(2)}) collective-permute-start(f32[792,128]{1,0:T(8,128)S(1)} %get-tuple-element.70), channel_id=1, source_target_pairs={{4,8},{8,4},{12,16},{16,12},{20,24},{24,20},{5,9},{9,5},{13,17},{1... | collective-permute-start | bytes 1216520 | tf_op jit(solution)/shard_map/ppermute | solution.py:519
  31.7 7.2 %collective-permute-start.9 = (f32[3,64,128]{2,1,0:T(8,128)S(1)}, f32[3,64,128]{2,1,0:T(8,128)S(1)}, u32[]{:S(2)}, u32[]{:S(2)}) collective-permute-start(f32[3,64,128]{2,1,0:T(8,128)S(1)} %add_add_fusion), channel_id=1, source_target_pairs={{0,2},{1,3},{2,0},{3,1},{4,6},{5,7},{6,4},{7,5},{8,10},{9,11},{10,... | collective-permute-start | bytes 294920 | tf_op jit(solution)/shard_map/ppermute | solution.py:524
  38.9 4.7 %collective-permute-start.11 = (f32[3,64,128]{2,1,0:T(8,128)S(1)}, f32[3,64,128]{2,1,0:T(8,128)S(1)}, u32[]{:S(2)}, u32[]{:S(2)}) collective-permute-start(f32[3,64,128]{2,1,0:T(8,128)S(1)} %add.45), channel_id=1, source_target_pairs={{0,1},{1,0},{2,3},{3,2},{4,5},{5,4},{6,7},{7,6},{8,9},{9,8},{10,11... | collective-permute-start | bytes 294920 | tf_op jit(solution)/shard_map/ppermute | solution.py:524
  43.6 3.4 %collective-permute-start.13 = (f32[2,64,128]{2,1,0:T(8,128)S(1)}, f32[2,64,128]{2,1,0:T(8,128)S(1)}, u32[]{:S(2)}, u32[]{:S(2)}) collective-permute-start(f32[2,64,128]{2,1,0:T(8,128)S(1)} %fusion.1.half_ref), channel_id=1, source_target_pairs={{0,4},{4,0},{8,12},{12,8},{16,20},{20,16},{24,28},{28,24},{1,5},{5... | collective-permute-start | bytes 196616 | tf_op jit(solution)/shard_map/ppermute | solution.py:524
  49.3 1.4 %collective-permute-start.16 = (f32[3,64,128]{2,1,0:T(8,128)S(1)}, f32[3,64,128]{2,1,0:T(8,128)S(1)}, u32[]{:S(2)}, u32[]{:S(2)}) collective-permute-start(f32[3,64,128]{2,1,0:T(8,128)S(1)} %get-tuple-element.80), channel_id=1, source_target_pairs={{0,4},{4,0},{8,12},{12,8},{16,20},{20,16},{24,28},{28,24},{1,5},{5... | collective-permute-start | bytes 294920 | tf_op jit(solution)/shard_map/ppermute | solution.py:524
  50.7 5.7 %collective-permute-start.17 = (f32[3,64,128]{2,1,0:T(8,128)S(1)}, f32[3,64,128]{2,1,0:T(8,128)S(1)}, u32[]{:S(2)}, u32[]{:S(2)}) collective-permute-start(f32[3,64,128]{2,1,0:T(8,128)S(1)} %add.48), channel_id=1, source_target_pairs={{0,1},{1,0},{2,3},{3,2},{4,5},{5,4},{6,7},{7,6},{8,9},{9,8},{10,11... | collective-permute-start | bytes 294920 | tf_op jit(solution)/shard_map/ppermute | solution.py:524
  53.2 19.8 %collective-permute-start.14 = (f32[3,256,128]{2,1,0:T(8,128)S(1)}, f32[3,256,128]{2,1,0:T(8,128)S(1)}, u32[]{:S(2)}, u32[]{:S(2)}) collective-permute-start(f32[3,256,128]{2,1,0:T(8,128)S(1)} %get-tuple-element.78), channel_id=1, source_target_pairs={{0,4},{4,8},{8,12},{12,16},{16,20},{20,24},{24,28},{1,5},{5,9},{9,... | collective-permute-start | bytes 1179656 | tf_op jit(solution)/shard_map/ppermute | solution.py:511
  56.4 5.7 %collective-permute-start.18 = (f32[3,64,128]{2,1,0:T(8,128)S(1)}, f32[3,64,128]{2,1,0:T(8,128)S(1)}, u32[]{:S(2)}, u32[]{:S(2)}) collective-permute-start(f32[3,64,128]{2,1,0:T(8,128)S(1)} %add.49), channel_id=1, source_target_pairs={{0,2},{1,3},{2,0},{3,1},{4,6},{5,7},{6,4},{7,5},{8,10},{9,11},{10,... | collective-permute-start | bytes 294920 | tf_op jit(solution)/shard_map/ppermute | solution.py:524
  62.1 8.6 %collective-permute-start.19 = (f32[3,64,128]{2,1,0:T(8,128)S(1)}, f32[3,64,128]{2,1,0:T(8,128)S(1)}, u32[]{:S(2)}, u32[]{:S(2)}) collective-permute-start(f32[3,64,128]{2,1,0:T(8,128)S(1)} %add.50), channel_id=1, source_target_pairs={{0,8},{4,12},{8,0},{12,4},{16,24},{20,28},{24,16},{28,20},{1,9},{5... | collective-permute-start | bytes 294920 | tf_op jit(solution)/shard_map/ppermute | solution.py:524
  70.7 4.9 %collective-permute-start.20 = (f32[3,64,128]{2,1,0:T(8,128)S(1)}, f32[3,64,128]{2,1,0:T(8,128)S(1)}, u32[]{:S(2)}, u32[]{:S(2)}) collective-permute-start(f32[3,64,128]{2,1,0:T(8,128)S(1)} %add.51), channel_id=1, source_target_pairs={{0,16},{4,20},{8,24},{12,28},{16,0},{20,4},{24,8},{28,12},{1,17},{... | collective-permute-start | bytes 294920 | tf_op jit(solution)/shard_map/ppermute | solution.py:524
  73.0 5.4 %collective-permute-start.15 = (f32[512,128]{1,0:T(8,128)S(1)}, f32[512,128]{1,0:T(8,128)S(1)}, u32[]{:S(2)}, u32[]{:S(2)}) collective-permute-start(f32[512,128]{1,0:T(8,128)S(1)} %shard_map.97), channel_id=1, source_target_pairs={{0,1},{1,2},{2,3},{4,5},{5,6},{6,7},{8,9},{9,10},{10,11},{12,13},{... | collective-permute-start | bytes 786440 | tf_op jit(solution)/shard_map/ppermute | solution.py:511
  75.6 1.6 %collective-permute-start.21 = (f32[2,64,128]{2,1,0:T(8,128)S(1)}, f32[2,64,128]{2,1,0:T(8,128)S(1)}, u32[]{:S(2)}, u32[]{:S(2)}) collective-permute-start(f32[2,64,128]{2,1,0:T(8,128)S(1)} %fusion.half_ref), channel_id=1, source_target_pairs={{0,4},{4,0},{8,12},{12,8},{16,20},{20,16},{24,28},{28,24},{1,5},{5... | collective-permute-start | bytes 196616 | tf_op jit(solution)/shard_map/ppermute | solution.py:524
